TPU v7x, 256 devices: a whole 4x4x8 slice. The times are simulated.
256 devices in a mesh: seq: 32 (over z, x), win: 4 (over y), wout: 2 (over core).
Axes of the slice: x: 4, y: 4, z: 8, core: 2. Of those that a mesh axis runs over, the one named last changes fastest.
Arguments:
- qkv_in: bfloat16 [8192, 3, 2048], P('seq', None, ('win', 'wout')), may hold values from -6 to 6
- conv_w: float32 [3, 4, 2048], P(None, None, ('win', 'wout')), may hold values from -3 to 3
- beta_logits: float32 [16, 8192], P(('win', 'wout'), 'seq'), may hold values from -10 to 3
- lengths: int32 [4], replicated, may hold values from 1 to 3968, as said below
- out_gain: float32 [128], replicated, may hold values from 0.1 to 1.9
- w_out: bfloat16 [2048, 2048], P(('win', 'wout')), may hold values from -0.125 to 0.125
- hidden_in: bfloat16 [8192, 2048], P(('seq', 'win', 'wout')), may hold values from -6 to 6
- norm_gain: float32 [2048], replicated, may hold values from 0.1 to 1.9
- w_qkv: bfloat16 [2048, 6144], P('win', 'wout'), may hold values from -0.125 to 0.125
Outputs:
- qkv_next: bfloat16 [8192, 6144], P(('seq', 'win'), 'wout')
- stream_out: bfloat16 [8192, 2048], P(('seq', 'win', 'wout'))
- final_states: float32 [4, 16, 128, 128], P(None, ('win', 'wout'))
- conv_edges: bfloat16 [4, 3, 3, 2048], P(None, None, None, ('win', 'wout'))
Inputs may be any that keep to these rules, and one draw needn't show every extreme that they name: The lengths sum to 8192; the largest is exactly 3968.
All inputs are finite; a program needn't handle non-finite values.
Results may differ from a plain program's by a relative error of at most 0.022.
Values may be sent and summed in bfloat16 or wider, within the bound.
No kernel may reach another device: no remote copies, remote signals or barrier semaphores. Data moves between devices by JAX's collectives and lax.ppermute only.
A program may use at most 64 MiB of HBM per device.

v0:
```python
import jax
import jax.numpy as jnp
from jax import lax
from jax.sharding import PartitionSpec as P

DK = 128
CONV = 4
SPAN = 64
REQS = 4


def from_behind(value, axis, steps):
    count = lax.axis_size(axis)
    leading, last = (max(0, -steps), min(count, count - steps))
    return lax.ppermute(value, axis, [(source, source + steps) for source in range(leading, last)])


def segment_ids(positions, seg_ends):
    counts = jnp.sum((positions[:, None] >= seg_ends[None, :]).astype(jnp.int32), axis=1)
    return jnp.where(positions < 0, -1, counts)


def unit_rows(values):
    return values / jnp.sqrt(jnp.sum(values * values, axis=-1, keepdims=True) + 1e-06)


def outer_product(form, left, right):
    return jnp.einsum(form, left, right, precision=lax.Precision.HIGHEST)


def body(qkv_in, conv_w, beta_logits, lengths, out_gain, w_out, hidden_in, norm_gain, w_qkv):
    row_count = qkv_in.shape[0]
    local_width = qkv_in.shape[2]
    head_count = local_width // DK
    rim_rows = CONV - 1
    first_position = lax.axis_index("seq") * row_count
    seg_ends = jnp.cumsum(lengths)
    preceding_entries = from_behind(qkv_in[row_count - rim_rows :], "seq", 1)
    extended = jnp.concatenate([preceding_entries, qkv_in], axis=0)
    ext_pos = first_position - rim_rows + jnp.arange(row_count + rim_rows, dtype=jnp.int32)
    ext_seg = segment_ids(ext_pos, seg_ends)
    own_seg = ext_seg[rim_rows:]
    pre = jnp.zeros((row_count, 3, local_width), jnp.float32)
    for offset in range(CONV):
        same_request = (ext_seg[offset : offset + row_count] == own_seg).astype(jnp.float32)
        window = extended[offset : offset + row_count].astype(jnp.float32)
        pre = pre + conv_w[:, offset, :][None] * window * same_request[:, None, None]
    activated = jax.nn.silu(pre).astype(jnp.bfloat16)
    span_count = row_count // SPAN

    def blocks(values):
        return values.reshape(span_count, SPAN, head_count, DK).transpose(0, 2, 1, 3)

    query = blocks(
        unit_rows(activated[:, 0].astype(jnp.float32).reshape(row_count, head_count, DK))
    )
    keys_b = blocks(
        unit_rows(activated[:, 1].astype(jnp.float32).reshape(row_count, head_count, DK))
    )
    values_b = blocks(activated[:, 2].astype(jnp.float32).reshape(row_count, head_count, DK))
    beta_coefficient = (
        jax.nn.sigmoid(beta_logits).reshape(head_count, span_count, SPAN).transpose(1, 0, 2)
    )
    seg_blocks = own_seg.reshape(span_count, SPAN)
    before_seg = segment_ids(
        first_position + jnp.arange(span_count, dtype=jnp.int32) * SPAN - 1, seg_ends
    )
    coupled_entries = (seg_blocks == before_seg[:, None]).astype(jnp.float32)
    same = seg_blocks[:, :, None] == seg_blocks[:, None, :]
    row_ids = jnp.arange(SPAN)[:, None]
    col_ids = jnp.arange(SPAN)[None, :]
    strict = (same & (row_ids > col_ids)).astype(jnp.float32)
    causal = (same & (row_ids >= col_ids)).astype(jnp.float32)
    gram = outer_product("nhik,nhjk->nhij", keys_b, keys_b)
    system = (
        jnp.eye(SPAN, dtype=jnp.float32) + beta_coefficient[..., :, None] * gram * strict[:, None]
    )
    targets = jnp.concatenate(
        [
            beta_coefficient[..., None] * values_b,
            (beta_coefficient * coupled_entries[:, None])[..., None] * keys_b,
        ],
        axis=-1,
    )
    solved = lax.linalg.triangular_solve(
        system, targets, left_side=True, lower=True, unit_diagonal=True
    )
    u_local = solved[..., :DK]
    w_link = solved[..., DK:]
    scores = outer_product("nhik,nhjk->nhij", query, keys_b) * causal[:, None]
    out_local = outer_product("nhij,nhjv->nhiv", scores, u_local)
    query_link = coupled_entries[:, None, :, None] * query - outer_product(
        "nhij,nhjk->nhik", scores, w_link
    )
    eye_keys = jnp.eye(DK, dtype=jnp.float32)
    last_link = coupled_entries[:, -1]
    in_last = (seg_blocks == seg_blocks[:, -1:]).astype(jnp.float32)
    trans = last_link[:, None, None, None] * (
        eye_keys - outer_product("nhjk,nhjl->nhkl", keys_b, w_link)
    )
    write = outer_product("nhjk,nhjv->nhkv", keys_b * in_last[:, None, :, None], u_local)

    def fold_span(carried_state, state_pair):
        return (
            (
                outer_product("hkl,hlm->hkm", state_pair[0], carried_state[0]),
                outer_product("eat,eto->eao", state_pair[0], carried_state[1]) + state_pair[1],
            ),
            None,
        )

    identity_maps = (
        jnp.broadcast_to(eye_keys, (head_count, DK, DK)),
        jnp.zeros((head_count, DK, DK), jnp.float32),
    )
    (device_transition, device_update), unused = lax.scan(fold_span, identity_maps, (trans, write))

    def chain_step(hop_index, incoming_state):
        outgoing_state = (
            outer_product("eat,eto->eao", device_transition, incoming_state) + device_update
        )
        return from_behind(outgoing_state, "seq", 1)

    state_in = lax.fori_loop(0, lax.axis_size("seq") - 1, chain_step, jnp.zeros_like(device_update))

    def advance(memory_state, state_pair):
        return (
            outer_product("eat,eto->eao", state_pair[0], memory_state) + state_pair[1],
            memory_state,
        )

    unused_end, entry_states = lax.scan(advance, state_in, (trans, write))
    attended = out_local + outer_product("nhik,nhkv->nhiv", query_link, entry_states)
    corrected_values = u_local - outer_product("nhik,nhkv->nhiv", w_link, entry_states)
    positions = (first_position + jnp.arange(row_count, dtype=jnp.int32)).reshape(span_count, SPAN)
    last_tok = seg_ends - 1
    at_end = (positions[None] == last_tok[:, None, None]).astype(jnp.float32)
    ends_here = jnp.sum(at_end, axis=2)
    request_ids = jnp.arange(REQS, dtype=jnp.int32)
    member = (seg_blocks[None] == request_ids[:, None, None]).astype(jnp.float32) * ends_here[
        ..., None
    ]
    carried = jnp.sum(at_end * coupled_entries[None], axis=2)
    req_states = outer_product("rn,nhkv->rhkv", carried, entry_states)
    req_states = req_states + jnp.einsum(
        "rnj,nhjk,nhjv->rhkv", member, keys_b, corrected_values, precision=lax.Precision.HIGHEST
    )
    owned = (last_tok >= first_position) & (last_tok < first_position + row_count)
    wanted = last_tok[:, None] - rim_rows + 1 + jnp.arange(rim_rows, dtype=jnp.int32)[None, :]
    select = (
        (ext_pos[None, None, :] == wanted[:, :, None])
        & (ext_seg[None, None, :] == request_ids[:, None, None])
        & owned[:, None, None]
    )
    edge_vals = jnp.einsum(
        "rim,mcj->ricj", select.astype(jnp.bfloat16), extended, preferred_element_type=jnp.float32
    )
    totals = (
        lax.psum(req_states.astype(jnp.bfloat16), "seq").astype(jnp.float32),
        lax.psum(edge_vals.astype(jnp.bfloat16), "seq").astype(jnp.float32),
    )
    final_states = totals[0]
    conv_edges = totals[1].astype(jnp.bfloat16)
    heads_rows = attended.transpose(0, 2, 1, 3).reshape(row_count, head_count, DK)
    scale_heads = jnp.sqrt(jnp.mean(heads_rows * heads_rows, axis=-1, keepdims=True) + 1e-05)
    normed_heads = (
        (heads_rows / scale_heads * out_gain).reshape(row_count, local_width).astype(jnp.bfloat16)
    )
    mixed = lax.psum_scatter(
        jnp.dot(normed_heads, w_out, preferred_element_type=jnp.float32).astype(jnp.bfloat16),
        ("win", "wout"),
        scatter_dimension=0,
        tiled=True,
    ).astype(jnp.float32)
    summed = hidden_in.astype(jnp.float32) + mixed
    stream_out = summed.astype(jnp.bfloat16)
    scale_stream = jnp.sqrt(jnp.mean(summed * summed, axis=-1, keepdims=True) + 1e-05)
    normed_stream = (summed / scale_stream * norm_gain).astype(jnp.bfloat16)
    in_block = w_qkv.shape[0]
    all_rows = lax.all_gather(normed_stream, ("win", "wout"), axis=0, tiled=True)
    columns = lax.dynamic_slice_in_dim(all_rows, lax.axis_index("win") * in_block, in_block, 1)
    projected = lax.psum_scatter(
        jnp.dot(columns, w_qkv, preferred_element_type=jnp.float32).astype(jnp.bfloat16),
        "win",
        scatter_dimension=0,
        tiled=True,
    )
    return (projected, stream_out, final_states, conv_edges)


def solution(mesh):
    return jax.shard_map(
        body,
        mesh=mesh,
        in_specs=(
            P("seq", None, ("win", "wout")),
            P(None, None, ("win", "wout")),
            P(("win", "wout"), "seq"),
            P(),
            P(),
            P(("win", "wout"), None),
            P(("seq", "win", "wout"), None),
            P(),
            P("win", "wout"),
        ),
        out_specs=(
            P(("seq", "win"), "wout"),
            P(("seq", "win", "wout"), None),
            P(None, ("win", "wout"), None, None),
            P(None, None, None, ("win", "wout")),
        ),
        check_vma=False,
    )
```

profile of v0, /device:TPU:24, one launch (start us, length us, event | category | flops | bytes accessed | tf_op | source)
XLA Modules:
  0.0 698.6 jit_solution(7639928728784033836)
XLA Ops:
  8.9 3.5 collective-permute-start.1
  45.6 40.7 %custom-call.3 = f32[4,2,1,64,64]{3,4,2,1,0:T(8,128)} custom-call(f32[4,2,1,64,64]{4,3,2,1,0:T(8,128)} %fusion.23), custom_call_target="InvertDiagBlocksLowerTriangular" | custom-call | tf_op jit(solution)/shard_map/triangular_solve | solution.py:85
  98.1 9.9 %while.37 = (s32[]{:T(128)}, f32[2,128,128]{2,1,0:T(8,128)S(1)}, f32[2,128,128]{2,1,0:T(8,128)S(1)}, f32[4,2,128,128]{3,2,1,0:T(8,128)}, f32[4,2,128,128]{3,2,1,0:T(8,128)}, /*index=5*/s32[]{:T(128)}, s32[]{:T(128)}) while((s32[]{:T(128)}, f32[2,128,128]{2,1,0:T(8,128)S(1)}, f32[2,128,128]{2,1,0:T(8,128)S(1)}, ...), condition=%wide.region_6.7_spmd.clone, body=%wide.region_5.6_spmd.clone.sunk | while | flops 100728832 | bytes 1443426 | solution.py:116
  108.1 306.8 %while.35 = (s32[]{:T(128)}, f32[2,128,128]{2,1,0:T(8,128)S(1)}, f32[2,128,128]{2,1,0:T(8,128)S(1)}, f32[2,128,128]{2,1,0:T(8,128)S(1)}, s32[]{:T(128)}) while((s32[]{:T(128)}, f32[2,128,128]{2,1,0:T(8,128)S(1)}, f32[2,128,128]{2,1,0:T(8,128)S(1)}, f32[2,128,128]{2,1,0:T(8,128)S(1)}, s32[]{:T(128)}) %tuple.81), condition=%wide.region_8.9_spmd, body=%wide.region_7.8_spmd.sunk | while | flops 50364416 | bytes 1048677 | solution.py:124
  109.0 3.4 collective-permute-start
  116.2 4.2 collective-permute-start
  124.2 4.2 collective-permute-start
  132.2 4.2 collective-permute-start
  140.1 4.2 collective-permute-start
  148.1 6.0 collective-permute-start
  157.8 6.3 collective-permute-start
  167.9 6.5 collective-permute-start
  174.4 3.9 collective-permute-done
  179.2 6.9 collective-permute-start
  186.1 3.4 collective-permute-done
  190.5 6.1 collective-permute-start
  200.3 5.9 collective-permute-start
  210.0 6.4 collective-permute-start
  220.1 6.4 collective-permute-start
  230.3 6.3 collective-permute-start
  240.4 6.3 collective-permute-start
  250.5 6.3 collective-permute-start
  256.8 3.5 collective-permute-done
  261.3 6.7 collective-permute-start
  268.0 3.7 collective-permute-done
  272.6 6.7 collective-permute-start
  283.0 6.0 collective-permute-start
  292.8 6.4 collective-permute-start
  302.9 6.4 collective-permute-start
  313.1 6.3 collective-permute-start
  323.2 6.3 collective-permute-start
  333.3 6.3 collective-permute-start
  339.6 3.1 collective-permute-done
  343.7 6.7 collective-permute-start
  350.4 4.0 collective-permute-done
  355.3 6.4 collective-permute-start
  361.7 3.0 collective-permute-done
  365.6 6.2 collective-permute-start
  375.6 6.2 collective-permute-start
  385.5 6.4 collective-permute-start
  395.7 6.3 collective-permute-start
  405.8 6.3 collective-permute-start
  414.9 7.7 %while.36 = (s32[]{:T(128)}, f32[2,128,128]{2,1,0:T(8,128)S(1)}, f32[4,2,128,128]{3,2,1,0:T(8,128)}, f32[4,2,128,128]{3,2,1,0:T(8,128)}, f32[4,2,128,128]{3,2,1,0:T(8,128)}, /*index=5*/s32[]{:T(128)}) while((s32[]{:T(128)}, f32[2,128,128]{2,1,0:T(8,128)S(1)}, f32[4,2,128,128]{3,2,1,0:T(8,128)}, f32[4,2,128,128]{3,2,1,0:T(8,128)}, ...), condition=%wide.region_10.11_spmd, body=%wide.region_9.10_spmd.sunk | while | flops 50364416 | bytes 1049681 | solution.py:132
  431.1 80.9 %reduce-scatter.3.cloned.1.call-done = bf16[32,2048]{1,0:T(8,128)(2,1)} async-done(((bf16[256,2048]{1,0:T(8,128)(2,1)}), bf16[32,2048]{1,0:T(8,128)(2,1)}) %reduce-scatter.3.cloned.1.call-update) | async-done | bytes 131088 | tf_op jit(solution)/shard_map/reduce_scatter | solution.py:169
  520.2 3.2 fusion.16
  523.6 17.6 %all-gather.2.cloned.1.call-done = bf16[256,2048]{1,0:T(8,128)(2,1)} async-done(((bf16[32,2048]{1,0:T(8,128)(2,1)}), bf16[256,2048]{1,0:T(8,128)(2,1)}) %all-gather.2.cloned.1.call-update) | async-done | bytes 1048592 | tf_op jit(solution)/shard_map/all_gather | solution.py:180
  541.2 3.1 convolution_convert_fusion
  546.5 143.2 %psum.15 = bf16[4,3,3,256]{3,0,2,1:T(4,128)(2,1)} all-reduce(bf16[4,3,3,256]{3,0,2,1:T(4,128)(2,1)} %convolution_convert_fusion.2), channel_id=1, replica_groups=mesh['seq'=32,'win'=4,'wout'=2] {'seq'}, use_global_device_ids=true, to_apply=%region_18.19 | all-reduce | flops 9216 | bytes 36864 | tf_op jit(solution)/shard_map/psum | solution.py:160
  (195 shorter events, 179.8 us)
Async XLA Ops:
  8.0 533.2 %copy-start = (bf16[512,3072]{1,0:T(8,128)(2,1)S(1)}, bf16[512,3072]{1,0:T(8,128)(2,1)}, u32[]{:S(2)}) copy-start(bf16[512,3072]{1,0:T(8,128)(2,1)} %param.23) | copy-start | bytes 9437188
  8.0 504.0 %reduce-scatter.3.cloned.1.call-start = ((), (), s32[]{:S(2)}) async-start(), calls=%async_computation.2 | async-start | bytes 1179648 | tf_op jit(solution)/shard_map/reduce_scatter | solution.py:169
  8.9 12.8 %collective-permute-start.1 = (bf16[3,3,256]{2,0,1:T(4,128)(2,1)S(1)}, bf16[3,3,256]{2,0,1:T(4,128)(2,1)S(1)}, u32[]{:S(2)}, u32[]{:S(2)}) collective-permute-start(bf16[3,3,256]{2,0,1:T(4,128)(2,1)S(1)} %slice.63), channel_id=1, source_target_pairs={{0,8},{8,16},{16,24},{24,32},{32,40},{40,48},{48,56},{56,64},{64,7... | collective-permute-start | bytes 13832 | tf_op jit(solution)/shard_map/ppermute | solution.py:15
  12.5 4.0 copy-start.8
  13.3 3.9 copy-start.12
  43.4 52.3 %copy-start.1 = (f32[4,64,2,128]{3,1,2,0:T(8,128)}, f32[4,64,2,128]{3,1,2,0:T(8,128)S(1)}, u32[]{:S(2)}) copy-start(f32[4,64,2,128]{3,1,2,0:T(8,128)S(1)} %get-tuple-element.164) | copy-start | bytes 786436
  86.3 9.3 %copy-start.5 = (f32[128,128]{1,0:T(8,128)S(1)}, f32[128,128]{1,0:T(8,128)}, u32[]{:S(2)}) copy-start(f32[128,128]{1,0:T(8,128)} %fusion.63) | copy-start | bytes 196612
  88.1 10.0 %copy-start.3 = (f32[4,2,64,256]{3,2,1,0:T(8,128)}, f32[4,2,64,256]{3,2,1,0:T(8,128)S(1)}, u32[]{:S(2)}) copy-start(f32[4,2,64,256]{3,2,1,0:T(8,128)S(1)} %fusion.28) | copy-start | bytes 1572868
  109.0 6.2 collective-permute-start
  116.2 7.1 %collective-permute-start = (f32[2,128,128]{2,1,0:T(8,128)}, f32[2,128,128]{2,1,0:T(8,128)S(1)}, u32[]{:S(2)}, u32[]{:S(2)}) collective-permute-start(f32[2,128,128]{2,1,0:T(8,128)} %convolution_add_fusion.8), channel_id=1, source_target_pairs={{0,8},{8,16},{16,24},{24,32},{32,40},{40,48},{48,56},{56,64},{64,7... | collective-permute-start | bytes 393224 | tf_op jit(solution)/shard_map/while/body/eval_jaxpr/ppermute | solution.py:15
  124.2 7.1 %collective-permute-start = (f32[2,128,128]{2,1,0:T(8,128)}, f32[2,128,128]{2,1,0:T(8,128)S(1)}, u32[]{:S(2)}, u32[]{:S(2)}) collective-permute-start(f32[2,128,128]{2,1,0:T(8,128)} %convolution_add_fusion.8), channel_id=1, source_target_pairs={{0,8},{8,16},{16,24},{24,32},{32,40},{40,48},{48,56},{56,64},{64,7... | collective-permute-start | bytes 393224 | tf_op jit(solution)/shard_map/while/body/eval_jaxpr/ppermute | solution.py:15
  132.2 7.1 %collective-permute-start = (f32[2,128,128]{2,1,0:T(8,128)}, f32[2,128,128]{2,1,0:T(8,128)S(1)}, u32[]{:S(2)}, u32[]{:S(2)}) collective-permute-start(f32[2,128,128]{2,1,0:T(8,128)} %convolution_add_fusion.8), channel_id=1, source_target_pairs={{0,8},{8,16},{16,24},{24,32},{32,40},{40,48},{48,56},{56,64},{64,7... | collective-permute-start | bytes 393224 | tf_op jit(solution)/shard_map/while/body/eval_jaxpr/ppermute | solution.py:15
  140.1 7.1 %collective-permute-start = (f32[2,128,128]{2,1,0:T(8,128)}, f32[2,128,128]{2,1,0:T(8,128)S(1)}, u32[]{:S(2)}, u32[]{:S(2)}) collective-permute-start(f32[2,128,128]{2,1,0:T(8,128)} %convolution_add_fusion.8), channel_id=1, source_target_pairs={{0,8},{8,16},{16,24},{24,32},{32,40},{40,48},{48,56},{56,64},{64,7... | collective-permute-start | bytes 393224 | tf_op jit(solution)/shard_map/while/body/eval_jaxpr/ppermute | solution.py:15
  148.1 8.8 %collective-permute-start = (f32[2,128,128]{2,1,0:T(8,128)}, f32[2,128,128]{2,1,0:T(8,128)S(1)}, u32[]{:S(2)}, u32[]{:S(2)}) collective-permute-start(f32[2,128,128]{2,1,0:T(8,128)} %convolution_add_fusion.8), channel_id=1, source_target_pairs={{0,8},{8,16},{16,24},{24,32},{32,40},{40,48},{48,56},{56,64},{64,7... | collective-permute-start | bytes 393224 | tf_op jit(solution)/shard_map/while/body/eval_jaxpr/ppermute | solution.py:15
  157.8 9.2 %collective-permute-start = (f32[2,128,128]{2,1,0:T(8,128)}, f32[2,128,128]{2,1,0:T(8,128)S(1)}, u32[]{:S(2)}, u32[]{:S(2)}) collective-permute-start(f32[2,128,128]{2,1,0:T(8,128)} %convolution_add_fusion.8), channel_id=1, source_target_pairs={{0,8},{8,16},{16,24},{24,32},{32,40},{40,48},{48,56},{56,64},{64,7... | collective-permute-start | bytes 393224 | tf_op jit(solution)/shard_map/while/body/eval_jaxpr/ppermute | solution.py:15
  167.9 10.3 %collective-permute-start = (f32[2,128,128]{2,1,0:T(8,128)}, f32[2,128,128]{2,1,0:T(8,128)S(1)}, u32[]{:S(2)}, u32[]{:S(2)}) collective-permute-start(f32[2,128,128]{2,1,0:T(8,128)} %convolution_add_fusion.8), channel_id=1, source_target_pairs={{0,8},{8,16},{16,24},{24,32},{32,40},{40,48},{48,56},{56,64},{64,7... | collective-permute-start | bytes 393224 | tf_op jit(solution)/shard_map/while/body/eval_jaxpr/ppermute | solution.py:15
  179.2 10.4 %collective-permute-start = (f32[2,128,128]{2,1,0:T(8,128)}, f32[2,128,128]{2,1,0:T(8,128)S(1)}, u32[]{:S(2)}, u32[]{:S(2)}) collective-permute-start(f32[2,128,128]{2,1,0:T(8,128)} %convolution_add_fusion.8), channel_id=1, source_target_pairs={{0,8},{8,16},{16,24},{24,32},{32,40},{40,48},{48,56},{56,64},{64,7... | collective-permute-start | bytes 393224 | tf_op jit(solution)/shard_map/while/body/eval_jaxpr/ppermute | solution.py:15
  190.5 8.9 %collective-permute-start = (f32[2,128,128]{2,1,0:T(8,128)}, f32[2,128,128]{2,1,0:T(8,128)S(1)}, u32[]{:S(2)}, u32[]{:S(2)}) collective-permute-start(f32[2,128,128]{2,1,0:T(8,128)} %convolution_add_fusion.8), channel_id=1, source_target_pairs={{0,8},{8,16},{16,24},{24,32},{32,40},{40,48},{48,56},{56,64},{64,7... | collective-permute-start | bytes 393224 | tf_op jit(solution)/shard_map/while/body/eval_jaxpr/ppermute | solution.py:15
  200.3 8.7 %collective-permute-start = (f32[2,128,128]{2,1,0:T(8,128)}, f32[2,128,128]{2,1,0:T(8,128)S(1)}, u32[]{:S(2)}, u32[]{:S(2)}) collective-permute-start(f32[2,128,128]{2,1,0:T(8,128)} %convolution_add_fusion.8), channel_id=1, source_target_pairs={{0,8},{8,16},{16,24},{24,32},{32,40},{40,48},{48,56},{56,64},{64,7... | collective-permute-start | bytes 393224 | tf_op jit(solution)/shard_map/while/body/eval_jaxpr/ppermute | solution.py:15
  210.0 9.2 %collective-permute-start = (f32[2,128,128]{2,1,0:T(8,128)}, f32[2,128,128]{2,1,0:T(8,128)S(1)}, u32[]{:S(2)}, u32[]{:S(2)}) collective-permute-start(f32[2,128,128]{2,1,0:T(8,128)} %convolution_add_fusion.8), channel_id=1, source_target_pairs={{0,8},{8,16},{16,24},{24,32},{32,40},{40,48},{48,56},{56,64},{64,7... | collective-permute-start | bytes 393224 | tf_op jit(solution)/shard_map/while/body/eval_jaxpr/ppermute | solution.py:15
  220.1 9.2 %collective-permute-start = (f32[2,128,128]{2,1,0:T(8,128)}, f32[2,128,128]{2,1,0:T(8,128)S(1)}, u32[]{:S(2)}, u32[]{:S(2)}) collective-permute-start(f32[2,128,128]{2,1,0:T(8,128)} %convolution_add_fusion.8), channel_id=1, source_target_pairs={{0,8},{8,16},{16,24},{24,32},{32,40},{40,48},{48,56},{56,64},{64,7... | collective-permute-start | bytes 393224 | tf_op jit(solution)/shard_map/while/body/eval_jaxpr/ppermute | solution.py:15
  230.3 9.2 %collective-permute-start = (f32[2,128,128]{2,1,0:T(8,128)}, f32[2,128,128]{2,1,0:T(8,128)S(1)}, u32[]{:S(2)}, u32[]{:S(2)}) collective-permute-start(f32[2,128,128]{2,1,0:T(8,128)} %convolution_add_fusion.8), channel_id=1, source_target_pairs={{0,8},{8,16},{16,24},{24,32},{32,40},{40,48},{48,56},{56,64},{64,7... | collective-permute-start | bytes 393224 | tf_op jit(solution)/shard_map/while/body/eval_jaxpr/ppermute | solution.py:15
  240.4 9.2 %collective-permute-start = (f32[2,128,128]{2,1,0:T(8,128)}, f32[2,128,128]{2,1,0:T(8,128)S(1)}, u32[]{:S(2)}, u32[]{:S(2)}) collective-permute-start(f32[2,128,128]{2,1,0:T(8,128)} %convolution_add_fusion.8), channel_id=1, source_target_pairs={{0,8},{8,16},{16,24},{24,32},{32,40},{40,48},{48,56},{56,64},{64,7... | collective-permute-start | bytes 393224 | tf_op jit(solution)/shard_map/while/body/eval_jaxpr/ppermute | solution.py:15
  250.5 9.9 %collective-permute-start = (f32[2,128,128]{2,1,0:T(8,128)}, f32[2,128,128]{2,1,0:T(8,128)S(1)}, u32[]{:S(2)}, u32[]{:S(2)}) collective-permute-start(f32[2,128,128]{2,1,0:T(8,128)} %convolution_add_fusion.8), channel_id=1, source_target_pairs={{0,8},{8,16},{16,24},{24,32},{32,40},{40,48},{48,56},{56,64},{64,7... | collective-permute-start | bytes 393224 | tf_op jit(solution)/shard_map/while/body/eval_jaxpr/ppermute | solution.py:15
  261.3 10.4 %collective-permute-start = (f32[2,128,128]{2,1,0:T(8,128)}, f32[2,128,128]{2,1,0:T(8,128)S(1)}, u32[]{:S(2)}, u32[]{:S(2)}) collective-permute-start(f32[2,128,128]{2,1,0:T(8,128)} %convolution_add_fusion.8), channel_id=1, source_target_pairs={{0,8},{8,16},{16,24},{24,32},{32,40},{40,48},{48,56},{56,64},{64,7... | collective-permute-start | bytes 393224 | tf_op jit(solution)/shard_map/while/body/eval_jaxpr/ppermute | solution.py:15
  272.6 9.5 %collective-permute-start = (f32[2,128,128]{2,1,0:T(8,128)}, f32[2,128,128]{2,1,0:T(8,128)S(1)}, u32[]{:S(2)}, u32[]{:S(2)}) collective-permute-start(f32[2,128,128]{2,1,0:T(8,128)} %convolution_add_fusion.8), channel_id=1, source_target_pairs={{0,8},{8,16},{16,24},{24,32},{32,40},{40,48},{48,56},{56,64},{64,7... | collective-permute-start | bytes 393224 | tf_op jit(solution)/shard_map/while/body/eval_jaxpr/ppermute | solution.py:15
  283.0 8.8 %collective-permute-start = (f32[2,128,128]{2,1,0:T(8,128)}, f32[2,128,128]{2,1,0:T(8,128)S(1)}, u32[]{:S(2)}, u32[]{:S(2)}) collective-permute-start(f32[2,128,128]{2,1,0:T(8,128)} %convolution_add_fusion.8), channel_id=1, source_target_pairs={{0,8},{8,16},{16,24},{24,32},{32,40},{40,48},{48,56},{56,64},{64,7... | collective-permute-start | bytes 393224 | tf_op jit(solution)/shard_map/while/body/eval_jaxpr/ppermute | solution.py:15
  292.8 9.2 %collective-permute-start = (f32[2,128,128]{2,1,0:T(8,128)}, f32[2,128,128]{2,1,0:T(8,128)S(1)}, u32[]{:S(2)}, u32[]{:S(2)}) collective-permute-start(f32[2,128,128]{2,1,0:T(8,128)} %convolution_add_fusion.8), channel_id=1, source_target_pairs={{0,8},{8,16},{16,24},{24,32},{32,40},{40,48},{48,56},{56,64},{64,7... | collective-permute-start | bytes 393224 | tf_op jit(solution)/shard_map/while/body/eval_jaxpr/ppermute | solution.py:15
  302.9 9.2 %collective-permute-start = (f32[2,128,128]{2,1,0:T(8,128)}, f32[2,128,128]{2,1,0:T(8,128)S(1)}, u32[]{:S(2)}, u32[]{:S(2)}) collective-permute-start(f32[2,128,128]{2,1,0:T(8,128)} %convolution_add_fusion.8), channel_id=1, source_target_pairs={{0,8},{8,16},{16,24},{24,32},{32,40},{40,48},{48,56},{56,64},{64,7... | collective-permute-start | bytes 393224 | tf_op jit(solution)/shard_map/while/body/eval_jaxpr/ppermute | solution.py:15
  313.1 9.2 %collective-permute-start = (f32[2,128,128]{2,1,0:T(8,128)}, f32[2,128,128]{2,1,0:T(8,128)S(1)}, u32[]{:S(2)}, u32[]{:S(2)}) collective-permute-start(f32[2,128,128]{2,1,0:T(8,128)} %convolution_add_fusion.8), channel_id=1, source_target_pairs={{0,8},{8,16},{16,24},{24,32},{32,40},{40,48},{48,56},{56,64},{64,7... | collective-permute-start | bytes 393224 | tf_op jit(solution)/shard_map/while/body/eval_jaxpr/ppermute | solution.py:15
  323.2 9.2 %collective-permute-start = (f32[2,128,128]{2,1,0:T(8,128)}, f32[2,128,128]{2,1,0:T(8,128)S(1)}, u32[]{:S(2)}, u32[]{:S(2)}) collective-permute-start(f32[2,128,128]{2,1,0:T(8,128)} %convolution_add_fusion.8), channel_id=1, source_target_pairs={{0,8},{8,16},{16,24},{24,32},{32,40},{40,48},{48,56},{56,64},{64,7... | collective-permute-start | bytes 393224 | tf_op jit(solution)/shard_map/while/body/eval_jaxpr/ppermute | solution.py:15
  333.3 9.5 %collective-permute-start = (f32[2,128,128]{2,1,0:T(8,128)}, f32[2,128,128]{2,1,0:T(8,128)S(1)}, u32[]{:S(2)}, u32[]{:S(2)}) collective-permute-start(f32[2,128,128]{2,1,0:T(8,128)} %convolution_add_fusion.8), channel_id=1, source_target_pairs={{0,8},{8,16},{16,24},{24,32},{32,40},{40,48},{48,56},{56,64},{64,7... | collective-permute-start | bytes 393224 | tf_op jit(solution)/shard_map/while/body/eval_jaxpr/ppermute | solution.py:15
  343.7 10.7 %collective-permute-start = (f32[2,128,128]{2,1,0:T(8,128)}, f32[2,128,128]{2,1,0:T(8,128)S(1)}, u32[]{:S(2)}, u32[]{:S(2)}) collective-permute-start(f32[2,128,128]{2,1,0:T(8,128)} %convolution_add_fusion.8), channel_id=1, source_target_pairs={{0,8},{8,16},{16,24},{24,32},{32,40},{40,48},{48,56},{56,64},{64,7... | collective-permute-start | bytes 393224 | tf_op jit(solution)/shard_map/while/body/eval_jaxpr/ppermute | solution.py:15
  355.3 9.4 %collective-permute-start = (f32[2,128,128]{2,1,0:T(8,128)}, f32[2,128,128]{2,1,0:T(8,128)S(1)}, u32[]{:S(2)}, u32[]{:S(2)}) collective-permute-start(f32[2,128,128]{2,1,0:T(8,128)} %convolution_add_fusion.8), channel_id=1, source_target_pairs={{0,8},{8,16},{16,24},{24,32},{32,40},{40,48},{48,56},{56,64},{64,7... | collective-permute-start | bytes 393224 | tf_op jit(solution)/shard_map/while/body/eval_jaxpr/ppermute | solution.py:15
  365.6 9.1 %collective-permute-start = (f32[2,128,128]{2,1,0:T(8,128)}, f32[2,128,128]{2,1,0:T(8,128)S(1)}, u32[]{:S(2)}, u32[]{:S(2)}) collective-permute-start(f32[2,128,128]{2,1,0:T(8,128)} %convolution_add_fusion.8), channel_id=1, source_target_pairs={{0,8},{8,16},{16,24},{24,32},{32,40},{40,48},{48,56},{56,64},{64,7... | collective-permute-start | bytes 393224 | tf_op jit(solution)/shard_map/while/body/eval_jaxpr/ppermute | solution.py:15
  375.6 9.0 %collective-permute-start = (f32[2,128,128]{2,1,0:T(8,128)}, f32[2,128,128]{2,1,0:T(8,128)S(1)}, u32[]{:S(2)}, u32[]{:S(2)}) collective-permute-start(f32[2,128,128]{2,1,0:T(8,128)} %convolution_add_fusion.8), channel_id=1, source_target_pairs={{0,8},{8,16},{16,24},{24,32},{32,40},{40,48},{48,56},{56,64},{64,7... | collective-permute-start | bytes 393224 | tf_op jit(solution)/shard_map/while/body/eval_jaxpr/ppermute | solution.py:15
  385.5 9.2 %collective-permute-start = (f32[2,128,128]{2,1,0:T(8,128)}, f32[2,128,128]{2,1,0:T(8,128)S(1)}, u32[]{:S(2)}, u32[]{:S(2)}) collective-permute-start(f32[2,128,128]{2,1,0:T(8,128)} %convolution_add_fusion.8), channel_id=1, source_target_pairs={{0,8},{8,16},{16,24},{24,32},{32,40},{40,48},{48,56},{56,64},{64,7... | collective-permute-start | bytes 393224 | tf_op jit(solution)/shard_map/while/body/eval_jaxpr/ppermute | solution.py:15
  395.7 9.2 %collective-permute-start = (f32[2,128,128]{2,1,0:T(8,128)}, f32[2,128,128]{2,1,0:T(8,128)S(1)}, u32[]{:S(2)}, u32[]{:S(2)}) collective-permute-start(f32[2,128,128]{2,1,0:T(8,128)} %convolution_add_fusion.8), channel_id=1, source_target_pairs={{0,8},{8,16},{16,24},{24,32},{32,40},{40,48},{48,56},{56,64},{64,7... | collective-permute-start | bytes 393224 | tf_op jit(solution)/shard_map/while/body/eval_jaxpr/ppermute | solution.py:15
  405.8 9.2 %collective-permute-start = (f32[2,128,128]{2,1,0:T(8,128)}, f32[2,128,128]{2,1,0:T(8,128)S(1)}, u32[]{:S(2)}, u32[]{:S(2)}) collective-permute-start(f32[2,128,128]{2,1,0:T(8,128)} %convolution_add_fusion.8), channel_id=1, source_target_pairs={{0,8},{8,16},{16,24},{24,32},{32,40},{40,48},{48,56},{56,64},{64,7... | collective-permute-start | bytes 393224 | tf_op jit(solution)/shard_map/while/body/eval_jaxpr/ppermute | solution.py:15
  414.9 7.7 %copy-start.4 = (f32[4,2,64,128]{3,2,1,0:T(8,128)S(1)}, f32[4,2,64,128]{3,2,1,0:T(8,128)}, u32[]{:S(2)}) copy-start(f32[4,2,64,128]{3,2,1,0:T(8,128)} %fusion.56) | copy-start | bytes 786436
  422.7 89.4 %copy-start.6 = (bf16[32,2048]{1,0:T(8,128)(2,1)S(1)}, bf16[32,2048]{1,0:T(8,128)(2,1)}, u32[]{:S(2)}) copy-start(bf16[32,2048]{1,0:T(8,128)(2,1)} %param.21) | copy-start | bytes 393220
  427.1 91.1 %copy-start.2 = (f32[4,64,2,128]{3,1,2,0:T(8,128)S(1)}, f32[4,64,2,128]{3,1,2,0:T(8,128)}, u32[]{:S(2)}) copy-start(f32[4,64,2,128]{3,1,2,0:T(8,128)} %copy-done.1) | copy-start | bytes 786436
  431.0 110.1 %all-gather.2.cloned.1.call-start = ((), (), s32[]{:S(2)}) async-start(), calls=%async_computation.3 | async-start | bytes 1179648 | tf_op jit(solution)/shard_map/all_gather | solution.py:180
  514.8 174.9 %all-reduce.2.cloned.1.call-start = ((), (), s32[]{:S(2)}) async-start(), calls=%async_computation.5 | async-start | bytes 524288 | tf_op jit(solution)/shard_map/psum | solution.py:159
  523.5 22.1 %copy-start.7 = (bf16[256,3,256]{2,0,1:T(8,128)(2,1)S(1)}, bf16[256,3,256]{2,0,1:T(8,128)(2,1)}, u32[]{:S(2)}) copy-start(bf16[256,3,256]{2,0,1:T(8,128)(2,1)} %param.15) | copy-start | bytes 1179652
  523.5 22.1 %copy-start.9 = (s32[259]{0:T(512)S(1)}, s32[259]{0:T(512)}, u32[]{:S(2)}) copy-start(s32[259]{0:T(512)} %copy-done.8) | copy-start | bytes 3112
  523.5 22.1 %copy-start.11 = (bf16[3,3,256]{2,0,1:T(4,128)(2,1)S(1)}, bf16[3,3,256]{2,0,1:T(4,128)(2,1)}, u32[]{:S(2)}) copy-start(bf16[3,3,256]{2,0,1:T(4,128)(2,1)} %copy-done.10) | copy-start | bytes 13828
  523.5 167.9 %reduce-scatter.5.cloned.1.call-start = ((), (), s32[]{:S(2)}) async-start(), calls=%async_computation.4 | async-start | bytes 1966080 | tf_op jit(solution)/shard_map/reduce_scatter | solution.py:182
  (1 other events, 0.6 us)
Sparse Core Ops, SparseCore 0:
  431.2 80.7 reduce-scatter.2
  514.9 26.2 all-gather.1
  544.4 28.4 reduce-scatter.4
Sparse Core Ops, SparseCore 1:
  523.6 145.8 all-reduce.1
where the time goes:
time: 701 us; the launch traced here: 699 us
  waiting for transfers between devices  191 us (27%)
  starting transfers between devices  190 us (27%)
  blocking collectives  143 us (20%)
  matrix products  73.4 us (10%)
  other arithmetic  63.6 us (9%)
  local copies, waits for them, and re-layouts  22.1 us (3%)
  between operations  15.5 us (2%)
    ppermute x32, starting transfers between devices, from_behind(): lax.ppermute(value, axis, [(source, source + steps) for source in range(l...  189 us
    psum x1, blocking collectives, body(): lax.psum(edge_vals.astype(jnp.bfloat16), 'seq').astype(jnp.float32)  143 us
    ppermute x32, waiting for transfers between devices, from_behind(): lax.ppermute(value, axis, [(source, source + steps) for source in range(l...  92 us
    reduce_scatter x1, waiting for transfers between devices, body(): lax.psum_scatter(jnp.dot(normed_heads, w_out, preferred_element_type=jnp....  80.9 us
    dot_general x52, matrix products, outer_product(): return jnp.einsum(form, left, right, precision=lax.Precision.HIGHEST)  63 us
    another operation x4, other arithmetic, body(): lax.linalg.triangular_solve(system, targets, left_side=True, lower=True,...  42 us
    all_gather x1, waiting for transfers between devices, body(): lax.all_gather(normed_stream, ('win', 'wout'), axis=0, tiled=True)  17.6 us
  transfers between devices with their start and end apart: 36, of which 33 were waited for; matrix products, arithmetic and copies ran while one was open for 4% of the time, Pallas kernels for 0%

commit v1 on v0

v1 whole, which is shorter than its diff:
```python
import functools

import jax
import jax.numpy as jnp
from jax import lax
from jax.experimental import pallas as pl
from jax.experimental.pallas import tpu as pltpu
from jax.sharding import PartitionSpec as P

DK = 128
CONV = 4
REQS = 4
HALO = 16
EDGE_ROWS = 16
INTERPRET = False
F32 = jnp.float32
BF16 = jnp.bfloat16
NN = ((1,), (0,))
NT = ((1,), (1,))
TN = ((0,), (0,))
VMEM = pl.BlockSpec(memory_space=pltpu.VMEM)
SMEM = pl.BlockSpec(memory_space=pltpu.SMEM)


def shift(value, axis, steps):
    count = lax.axis_size(axis)
    return lax.ppermute(value, axis, [(s, s + steps) for s in range(count - steps)])


def rotate(value, axis, steps):
    count = lax.axis_size(axis)
    return lax.ppermute(value, axis, [(s, (s + steps) % count) for s in range(count)])


def exchange(value, axis, bit):
    return lax.ppermute(value, axis, [(s, s ^ bit) for s in range(lax.axis_size(axis))])


def dot(left, right, dims=NN):
    return lax.dot_general(left, right, (dims, ((), ())), preferred_element_type=F32)


def split(value):
    high = value.astype(BF16)
    return high, (value - high.astype(F32)).astype(BF16)


def dot_split(left, right, dims=NN):
    lh, ll = left
    rh, rl = right
    return dot(lh, rh, dims) + (dot(lh, rl, dims) + dot(ll, rh, dims))


def dot32(left, right, dims=NN):
    return dot_split(split(left), split(right), dims)


def call(kernel, outs, name, flops, *args, scratch=(), smem=1):
    size = sum(a.size * a.dtype.itemsize for a in args) + sum(
        o.size * o.dtype.itemsize for o in outs
    )
    return pl.pallas_call(
        kernel,
        out_shape=outs,
        in_specs=[SMEM] * smem + [VMEM] * (len(args) - smem),
        out_specs=[VMEM] * len(outs),
        scratch_shapes=list(scratch),
        name=name,
        interpret=INTERPRET,
        cost_estimate=pl.CostEstimate(flops=flops, bytes_accessed=size, transcendentals=0),
        compiler_params=pltpu.CompilerParams(vmem_limit_bytes=40 * 1024 * 1024),
    )(*args)


def out(shape, dtype):
    return jax.ShapeDtypeStruct(shape, dtype)


def request_ends(meta):
    ends = [meta[0]]
    for r in range(1, REQS):
        ends.append(ends[-1] + meta[r])
    return ends


def seg_of(pos, ends):
    total = jnp.where(pos >= ends[0], 1, 0)
    for r in range(1, REQS):
        total = total + jnp.where(pos >= ends[r], 1, 0)
    return total


def start_of(pos, ends):
    begin = jnp.where(pos >= ends[0], ends[0], 0)
    for r in range(1, REQS):
        begin = jnp.maximum(begin, jnp.where(pos >= ends[r], ends[r], 0))
    return begin


def iota(shape, dim):
    return lax.broadcasted_iota(jnp.int32, shape, dim)


def prep_kernel(
    meta, x_ref, halo_ref, taps_ref, beta_ref,
    map_ref, uw_ref, local_ref, link_ref, kb_ref, ks_ref, edge_ref,
):
    rows = x_ref.shape[1]
    heads = x_ref.shape[2] // DK
    half = rows // 2
    ends = request_ends(meta)
    first = meta[4]
    pos = first + iota((rows, 1), 0)
    pos_r = first + iota((1, rows), 1)
    seg = seg_of(pos, ends)
    seg_r = seg_of(pos_r, ends)
    begin = start_of(pos, ends)
    coupled = jnp.where(begin < first, 1.0, 0.0).astype(F32)
    last = first + rows - 1
    last_seg = seg_of(last, ends)
    last_link = start_of(last, ends) < first
    in_last = jnp.where(seg == last_seg, 1.0, 0.0).astype(F32)

    edge_id = iota((EDGE_ROWS, 1), 0)
    wanted = jnp.full((EDGE_ROWS, 1), -1, jnp.int32)
    for r in range(REQS):
        end = ends[r]
        begin_r = end - meta[r]
        owned = (end - 1 >= first) & (end - 1 <= last)
        for i in range(CONV - 1):
            spot = end - (CONV - 1) + i
            good = owned & (spot >= begin_r)
            wanted = jnp.where(edge_id == r * (CONV - 1) + i, jnp.where(good, spot, -1), wanted)
    ext_pos = first - HALO + iota((EDGE_ROWS, rows + HALO), 1)
    select = jnp.where((ext_pos == wanted) & (ext_pos >= 0), 1.0, 0.0).astype(BF16)

    planes = []
    for c in range(3):
        ext = jnp.concatenate([halo_ref[c], x_ref[c]], axis=0)
        picked = dot(select, ext).astype(BF16)
        for b in range(heads):
            edge_ref[c * heads + b] = picked[:, b * DK : (b + 1) * DK]
        wide = ext.astype(F32)
        taps = taps_ref[c]
        pre = wide[HALO:] * taps[CONV - 1 : CONV]
        for back in range(1, CONV):
            moved = pltpu.roll(wide, back, 0)[HALO:]
            ok = jnp.where(pos - back >= begin, 1.0, 0.0).astype(F32)
            pre = pre + moved * taps[CONV - 1 - back : CONV - back] * ok
        planes.append((pre / (1.0 + jnp.exp(-pre))).astype(BF16))

    row_id = iota((rows, rows), 0)
    col_id = iota((rows, rows), 1)
    same = seg == seg_r
    strict = same & (row_id > col_id)
    causal = same & (row_id >= col_id)
    diag = row_id == col_id
    row_h = iota((half, half), 0)
    col_h = iota((half, half), 1)
    eye_h = jnp.where(row_h == col_h, 1.0, 0.0).astype(F32)

    def as_row(column):
        return jnp.sum(jnp.where(diag, column, 0.0), axis=0, keepdims=True)

    def as_column(row):
        return jnp.sum(jnp.where(diag, row, 0.0), axis=1, keepdims=True)

    state = []
    for h in range(heads):
        lanes = slice(h * DK, (h + 1) * DK)
        qb, kb, vb = (planes[c][:, lanes] for c in range(3))
        q32, k32, v32 = (t.astype(F32) for t in (qb, kb, vb))
        qs = lax.rsqrt(jnp.sum(q32 * q32, axis=1, keepdims=True) + 1e-06)
        ks = lax.rsqrt(jnp.sum(k32 * k32, axis=1, keepdims=True) + 1e-06)
        ks_row = as_row(ks)
        beta = as_column(1.0 / (1.0 + jnp.exp(-beta_ref[h : h + 1, :])))
        system = jnp.where(strict, dot(kb, kb, NT) * (beta * ks) * ks_row, 0.0)
        scores = jnp.where(causal, dot(qb, kb, NT) * qs * ks_row, 0.0)
        targets = jnp.concatenate([beta * v32, (beta * coupled * ks) * k32], axis=1)
        state.append((q32 * qs, kb, ks, system, scores, targets))

    blocks = []
    for h in range(heads):
        system = state[h][3]
        for d in range(2):
            blocks.append(system[d * half : (d + 1) * half, d * half : (d + 1) * half])
    inverses = []
    low = ((row_h ^ col_h) == 1) & (row_h > col_h)
    for a in blocks:
        inverses.append(eye_h - jnp.where(low, a, 0.0))
    level = 1
    while (2 << level) <= half:
        low = (((row_h >> level) ^ (col_h >> level)) == 1) & (row_h > col_h)
        parts = [split(x) for x in inverses]
        inner = [dot_split(split(jnp.where(low, a, 0.0)), p) for a, p in zip(blocks, parts)]
        inverses = [x - dot_split(p, split(t)) for x, p, t in zip(inverses, parts, inner)]
        level += 1

    for h in range(heads):
        q32, kb, ks, system, scores, targets = state[h]
        top = dot32(inverses[2 * h], targets[:half])
        rest = targets[half:] - dot32(system[half:, :half], top)
        uw = jnp.concatenate([top, dot32(inverses[2 * h + 1], rest)], axis=0)
        uw_ref[h] = uw
        mixed = dot32(scores, uw)
        local_ref[h] = mixed[:, :DK]
        link_ref[h] = coupled * q32 - mixed[:, DK:]
        kb_ref[h] = kb
        ks_ref[h] = ks
        scaled = jnp.concatenate([uw[:, DK:] * ks, uw[:, :DK] * (ks * in_last)], axis=1)
        high, less = split(scaled)
        fold = dot(kb, high, TN) + dot(kb, less, TN)
        eye_k = jnp.where(iota((DK, DK), 0) == iota((DK, DK), 1), 1.0, 0.0).astype(F32)
        map_ref[h, :, :DK] = jnp.where(last_link, fold[:, :DK], eye_k).astype(BF16)
        map_ref[h, :, DK:] = fold[:, DK:].astype(BF16)


def window_kernel(m1_ref, m2_ref, m3_ref, m4_ref, wide_ref, send_ref, tail_ref):
    for h in range(m1_ref.shape[0]):
        pairs = []
        for newer, older in ((m1_ref, m2_ref), (m3_ref, m4_ref)):
            a, b = newer[h], older[h]
            pairs.append(a.astype(F32) + b.astype(F32) - dot(a[:, :DK], b))
        joined = pairs[0] + pairs[1] - dot32(pairs[0][:, :DK], pairs[1])
        wide_ref[h] = joined
        send_ref[h] = joined.astype(BF16)
        tail_ref[h] = joined[:, DK:].astype(BF16)


def attend_kernel(
    meta, e0_ref, e4_ref, e8_ref, e12_ref, uw_ref, local_ref, link_ref, kb_ref, ks_ref,
    edge_ref, gain_ref, w_ref, own_ref, other_ref, pay_ref, heads_ref,
):
    heads, rows, _ = local_ref.shape
    wins, cores, piece, _ = heads_ref.shape
    ends = request_ends(meta)
    first, win, core = meta[4], meta[5], meta[6]
    last = first + rows - 1
    seg = seg_of(first + iota((rows, 1), 0), ends)
    gain = gain_ref[...]
    for h in range(heads):
        e0, e4, e8 = e0_ref[h], e4_ref[h], e8_ref[h]
        near = e0 + e4.astype(F32) - dot32(e0[:, :DK], e4.astype(F32))
        far = (
            e8[:, DK:].astype(F32) + e12_ref[h].astype(F32) - dot(e8[:, :DK], e12_ref[h])
        )
        enter = near[:, DK:] + far - dot32(near[:, :DK], far)
        parts = split(enter)
        attended = local_ref[h] + dot_split(split(link_ref[h]), parts)
        scale = lax.rsqrt(jnp.mean(attended * attended, axis=1, keepdims=True) + 1e-05)
        normed = attended * scale * gain
        lanes = slice(h * DK, (h + 1) * DK)
        for p in range(wins * cores):
            heads_ref[p // cores, p % cores, :, lanes] = normed[p * piece : (p + 1) * piece].astype(
                BF16
            )
        uw = uw_ref[h]
        corrected = (uw[:, :DK] - dot_split(split(uw[:, DK:]), parts)) * ks_ref[h]
        for r in range(REQS):
            owned = (ends[r] - 1 >= first) & (ends[r] - 1 <= last)
            carried = owned & (ends[r] - meta[r] < first)
            member = (seg == r) & owned
            high, less = split(jnp.where(member, corrected, 0.0))
            final = dot(kb_ref[h], high, TN) + dot(kb_ref[h], less, TN)
            final = final + jnp.where(carried, enter, 0.0)
            spot = (r * heads + h) * DK
            pay_ref[spot : spot + DK, :] = final.astype(BF16)
    base = REQS * heads * DK
    for b in range(edge_ref.shape[0]):
        pay_ref[base + b * EDGE_ROWS : base + (b + 1) * EDGE_ROWS, :] = edge_ref[b]
    order = [lax.rem(win + k, wins) for k in range(wins)]
    w = w_ref[...]
    mine = jnp.concatenate([heads_ref[o, core] for o in order], axis=0)
    own_ref[...] = dot(mine, w)
    theirs = jnp.concatenate([heads_ref[o, cores - 1 - core] for o in order], axis=0)
    other_ref[...] = dot(theirs, w).astype(BF16)


def pair_kernel(own_ref, got_ref, keep_ref, *send_refs):
    piece = keep_ref.shape[0]
    keep_ref[...] = own_ref[:piece] + got_ref[:piece].astype(F32)
    for k, ref in enumerate(send_refs):
        part = slice((k + 1) * piece, (k + 2) * piece)
        ref[...] = (own_ref[part] + got_ref[part].astype(F32)).astype(BF16)


def norm_kernel(meta, hidden_ref, gain_ref, keep_ref, *refs):
    wins = refs[-1].shape[0]
    got, (stream_ref, *piece_refs), cols_ref = refs[: wins - 1], refs[wins - 1 : -1], refs[-1]
    total = keep_ref[...]
    for ref in got:
        total = total + ref[...].astype(F32)
    total = hidden_ref[...].astype(F32) + total
    stream_ref[...] = total.astype(BF16)
    scale = lax.rsqrt(jnp.mean(total * total, axis=1, keepdims=True) + 1e-05)
    normed = (total * scale * gain_ref[...]).astype(BF16)
    width = normed.shape[1] // wins
    for k in range(wins):
        cols_ref[k] = normed[:, k * width : (k + 1) * width]
    for k, ref in enumerate(piece_refs):
        ref[...] = cols_ref[lax.rem(meta[5] + k, wins)]


def body(qkv_in, conv_w, beta_logits, lengths, out_gain, w_out, hidden_in, norm_gain, w_qkv):
    rows = qkv_in.shape[0]
    width = qkv_in.shape[2]
    heads = width // DK
    model = w_out.shape[1]
    n_seq, wins, cores = (lax.axis_size(a) for a in ("seq", "win", "wout"))
    piece = rows // (wins * cores)
    seq, win, core = (lax.axis_index(a).astype(jnp.int32) for a in ("seq", "win", "wout"))
    meta = jnp.concatenate([lengths, jnp.stack([seq * rows, win, core, core])])
    x = qkv_in.transpose(1, 0, 2)
    halo = shift(x[:, rows - HALO :], "seq", 1)
    maps, uw, local, link, kb, ks, edges = call(
        prep_kernel,
        [
            out((heads, DK, 2 * DK), BF16),
            out((heads, rows, 2 * DK), F32),
            out((heads, rows, DK), F32),
            out((heads, rows, DK), F32),
            out((heads, rows, DK), BF16),
            out((heads, rows, 1), F32),
            out((3 * heads, EDGE_ROWS, DK), BF16),
        ],
        "prep",
        2 * 10**9,
        meta, x, halo, conv_w, beta_logits,
    )

    def sent(value, steps):
        return shift(value, "seq", steps) if steps < n_seq else jnp.zeros_like(value)

    near = [sent(maps, k) for k in range(1, 5)]
    wide, send, tail = call(
        window_kernel,
        [
            out((heads, DK, 2 * DK), F32),
            out((heads, DK, 2 * DK), BF16),
            out((heads, DK, DK), BF16),
        ],
        "window",
        10**8,
        *near,
        smem=0,
    )
    far = [sent(send, 4), sent(send, 8), sent(tail, 12)]
    state_rows = REQS * heads * DK
    pay_rows = state_rows + 3 * heads * EDGE_ROWS
    own, other, payload = call(
        attend_kernel,
        [
            out((wins * piece, model), F32),
            out((wins * piece, model), BF16),
            out((pay_rows, DK), BF16),
        ],
        "attend",
        10**9,
        meta, wide, *far, uw, local, link, kb, ks, edges, out_gain.reshape(1, DK), w_out,
        scratch=[pltpu.VMEM((wins, cores, piece, width), BF16)],
    )
    got = rotate(other, "wout", 1)
    sums = call(
        pair_kernel,
        [out((piece, model), F32)] + [out((piece, model), BF16)] * (wins - 1),
        "pair",
        10**6,
        own, got,
        smem=0,
    )
    reduced = [rotate(sums[k], "win", k) for k in range(1, wins)]
    stream_out, *cols = call(
        norm_kernel,
        [out((piece, model), BF16)] + [out((piece, model // wins), BF16)] * wins,
        "norm",
        10**6,
        meta, hidden_in, norm_gain.reshape(1, model), sums[0], *reduced,
        scratch=[pltpu.VMEM((wins, piece, model // wins), BF16)],
    )
    blocks = [cols[0]] + [rotate(cols[k], "win", k) for k in range(1, wins)]
    peers = rotate(jnp.concatenate(blocks, axis=0), "wout", 1)

    def partial(k):
        j = (wins - k) % wins
        mine, theirs = blocks[j], peers[j * piece : (j + 1) * piece]
        lower = jnp.where(core == 0, mine, theirs)
        upper = jnp.where(core == 0, theirs, mine)
        return jnp.dot(
            jnp.concatenate([lower, upper], axis=0), w_qkv, preferred_element_type=F32
        )

    arrived = [rotate(partial(k).astype(BF16), "win", k) for k in range(1, wins)]
    total = partial(0)
    for part in arrived:
        total = total + part.astype(F32)
    projected = total.astype(BF16)

    bit = 1
    while bit < n_seq:
        payload = payload + exchange(payload, "seq", bit)
        bit *= 2
    final_states = payload[:state_rows].astype(F32).reshape(REQS, heads, DK, DK)
    edges = payload[state_rows:].reshape(3 * heads, EDGE_ROWS, DK)[:, : REQS * (CONV - 1)]
    conv_edges = edges.transpose(1, 0, 2).reshape(REQS, CONV - 1, 3, width)
    return (projected, stream_out, final_states, conv_edges)


def solution(mesh):
    return jax.shard_map(
        body,
        mesh=mesh,
        in_specs=(
            P("seq", None, ("win", "wout")),
            P(None, None, ("win", "wout")),
            P(("win", "wout"), "seq"),
            P(),
            P(),
            P(("win", "wout"), None),
            P(("seq", "win", "wout"), None),
            P(),
            P("win", "wout"),
        ),
        out_specs=(
            P(("seq", "win"), "wout"),
            P(("seq", "win", "wout"), None),
            P(None, ("win", "wout"), None, None),
            P(None, None, None, ("win", "wout")),
        ),
        check_vma=False,
    )
```

time: 701 us -> 128 us (0.18)
  waiting for transfers between devices: 191 us -> 43.4 us
  blocking collectives: 143 us -> 0 us
  starting transfers between devices: 190 us -> 60 us
  matrix products: 73.4 us -> 3.54 us
  other arithmetic: 63.6 us -> 3.69 us
  local copies, waits for them, and re-layouts: 22.1 us -> 5.33 us
  between operations: 15.5 us -> 0.91 us
  Pallas kernels: 0 us -> 9.96 us
    psum x1 -> x0, blocking collectives: 143 us -> none  [body(): lax.psum(edge_vals.astype(jnp.bfloat16), 'seq').astype(jnp.float32)]
    ppermute x32 -> x24, starting transfers between devices: 189 us -> 60 us  [the longest x8 36.4 us: shift(): lax.ppermute(value, axis, [(s, s + steps) for s in range(count - steps)])]
    reduce_scatter x2 -> x0, waiting for transfers between devices: 80.9 us -> none  [the longest x1 80.9 us: body(): lax.psum_scatter(jnp.dot(normed_heads, w_out, preferred_element_type=jnp....]
    dot_general x56 -> x4, matrix products: 71.6 us -> 3.54 us  [partial(): jnp.dot(jnp.concatenate([lower, upper], axis=0), w_qkv, preferred_element...]
    ppermute x32 -> x24, waiting for transfers between devices: 92 us -> 43.4 us  [the longest x5 28.9 us: exchange(): lax.ppermute(value, axis, [(s, s ^ bit) for s in range(lax.axis_size(axis...]
    another operation x5 -> x0, other arithmetic: 42.8 us -> none  [the longest x4 42 us: body(): lax.linalg.triangular_solve(system, targets, left_side=True, lower=True,...]
    all_gather x1 -> x0, waiting for transfers between devices: 17.6 us -> none  [body(): lax.all_gather(normed_stream, ('win', 'wout'), axis=0, tiled=True)]
    pallas_call x0 -> x5, Pallas kernels: none -> 9.96 us  [call(): pl.pallas_call(kernel, out_shape=outs, in_specs=[SMEM] * smem + [VMEM] *...]
  transfers between devices with their start and end apart: 36 -> 24, of which waited for: 33 -> 14; matrix products, arithmetic and copies ran while one was open for 4% -> 6% of each run, Pallas kernels for 0% -> 1%
where the time goes in v1:
time: 128 us; the launch traced here: 127 us
  starting transfers between devices  60 us (47%)
  waiting for transfers between devices  43.4 us (34%)
  Pallas kernels  9.96 us (8%)
  local copies, waits for them, and re-layouts  5.33 us (4%)
  other arithmetic  3.69 us (3%)
  matrix products  3.54 us (3%)
    ppermute x8, starting transfers between devices, shift(): lax.ppermute(value, axis, [(s, s + steps) for s in range(count - steps)])  36.4 us
    ppermute x5, waiting for transfers between devices, exchange(): lax.ppermute(value, axis, [(s, s ^ bit) for s in range(lax.axis_size(axis...  28.9 us
    ppermute x5, starting transfers between devices, exchange(): lax.ppermute(value, axis, [(s, s ^ bit) for s in range(lax.axis_size(axis...  13.9 us
    pallas_call x5, Pallas kernels, call(): pl.pallas_call(kernel, out_shape=outs, in_specs=[SMEM] * smem + [VMEM] *...  9.96 us
    ppermute x11, starting transfers between devices, rotate(): lax.ppermute(value, axis, [(s, (s + steps) % count) for s in range(count)])  9.66 us
    ppermute x11, waiting for transfers between devices, rotate(): lax.ppermute(value, axis, [(s, (s + steps) % count) for s in range(count)])  9.38 us
    ppermute x8, waiting for transfers between devices, shift(): lax.ppermute(value, axis, [(s, s + steps) for s in range(count - steps)])  5.13 us
    unnamed x20, local copies, waits for them, and re-layouts  3.65 us
  transfers between devices with their start and end apart: 24, of which 14 were waited for; matrix products, arithmetic and copies ran while one was open for 6% of the time, Pallas kernels for 1%

profile of v1, /device:TPU:24, one launch (start us, length us, event | category | flops | bytes accessed | tf_op | source)
XLA Modules:
  0.0 126.8 jit_solution(12222666266127258060)
XLA Ops:
  0.6 0.9 slice.32
  1.5 3.5 %collective-permute-start = (bf16[3,16,256]{2,1,0:T(8,128)(2,1)S(1)}, bf16[3,16,256]{2,1,0:T(8,128)(2,1)S(1)}, u32[]{:S(2)}, u32[]{:S(2)}) collective-permute-start(bf16[3,16,256]{2,1,0:T(8,128)(2,1)S(1)} %slice.32), channel_id=1, source_target_pairs={{0,8},{8,16},{16,24},{24,32},{32,40},{40,48},{48,56},{56,64},{64,7... | collective-permute-start | bytes 73736 | tf_op jit(solution)/shard_map/ppermute | solution.py:27
  5.1 0.7 concatenate.18.meta
  5.8 0.8 collective-permute-done.halo_ref
  6.6 1.0 copy-done.3
  7.6 0.7 copy-done.5
  8.3 0.7 copy-done.6
  9.0 5.5 %prep.1 = (bf16[2,128,256]{2,1,0:T(8,128)(2,1)S(1)}, f32[2,256,256]{2,1,0:T(8,128)S(1)}, f32[2,256,128]{2,1,0:T(8,128)S(1)}, f32[2,256,128]{2,1,0:T(8,128)S(1)},...) custom-call(s32[8]{0:T(128)S(1)} %concatenate.18.meta, ...), custom_call_target="tpu_custom_call" | custom-call | flops 2000000000 | bytes 1769504 | tf_op jit(solution)/shard_map/prep/pallas_call | solution.py:62
  14.4 6.7 %collective-permute-start.4 = (bf16[2,128,256]{2,1,0:T(8,128)(2,1)S(1)}, bf16[2,128,256]{2,1,0:T(8,128)(2,1)S(1)}, u32[]{:S(2)}, u32[]{:S(2)}) collective-permute-start(bf16[2,128,256]{2,1,0:T(8,128)(2,1)S(1)} %get-tuple-element.26), channel_id=1, source_target_pairs={{0,32},{8,40},{16,48},{24,56},{32,64},{40,72},{48,80},{56,88},{64,... | collective-permute-start | bytes 393224 | tf_op jit(solution)/shard_map/ppermute | solution.py:27
  21.2 2.6 %collective-permute-start.3 = (bf16[2,128,256]{2,1,0:T(8,128)(2,1)S(1)}, bf16[2,128,256]{2,1,0:T(8,128)(2,1)S(1)}, u32[]{:S(2)}, u32[]{:S(2)}) collective-permute-start(bf16[2,128,256]{2,1,0:T(8,128)(2,1)S(1)} %get-tuple-element.26), channel_id=1, source_target_pairs={{0,24},{8,32},{16,40},{24,48},{32,56},{40,64},{48,72},{56,80},{64,... | collective-permute-start | bytes 393224 | tf_op jit(solution)/shard_map/ppermute | solution.py:27
  23.8 4.1 %collective-permute-start.2 = (bf16[2,128,256]{2,1,0:T(8,128)(2,1)S(1)}, bf16[2,128,256]{2,1,0:T(8,128)(2,1)S(1)}, u32[]{:S(2)}, u32[]{:S(2)}) collective-permute-start(bf16[2,128,256]{2,1,0:T(8,128)(2,1)S(1)} %get-tuple-element.26), channel_id=1, source_target_pairs={{0,16},{8,24},{16,32},{24,40},{32,48},{40,56},{48,64},{56,72},{64,... | collective-permute-start | bytes 393224 | tf_op jit(solution)/shard_map/ppermute | solution.py:27
  27.8 2.8 %collective-permute-start.1 = (bf16[2,128,256]{2,1,0:T(8,128)(2,1)S(1)}, bf16[2,128,256]{2,1,0:T(8,128)(2,1)S(1)}, u32[]{:S(2)}, u32[]{:S(2)}) collective-permute-start(bf16[2,128,256]{2,1,0:T(8,128)(2,1)S(1)} %get-tuple-element.26), channel_id=1, source_target_pairs={{0,8},{8,16},{16,24},{24,32},{32,40},{40,48},{48,56},{56,64},{64,7... | collective-permute-start | bytes 393224 | tf_op jit(solution)/shard_map/ppermute | solution.py:27
  30.7 0.7 collective-permute-done.2.m2_ref
  31.4 1.8 %collective-permute-done.1.m1_ref = bf16[2,128,256]{2,1,0:T(8,128)(2,1)S(1)} collective-permute-done((bf16[2,128,256]{2,1,0:T(8,128)(2,1)S(1)}, bf16[2,128,256]{2,1,0:T(8,128)(2,1)S(1)}, u32[]{:S(2)}, u32[]{:S(2)}) %collective-permute-start.1) | collective-permute-done | bytes 131104 | tf_op jit(solution)/shard_map/ppermute | solution.py:27
  33.6 11.4 %collective-permute-start.6 = (bf16[2,128,256]{2,1,0:T(8,128)(2,1)S(1)}, bf16[2,128,256]{2,1,0:T(8,128)(2,1)S(1)}, u32[]{:S(2)}, u32[]{:S(2)}) collective-permute-start(bf16[2,128,256]{2,1,0:T(8,128)(2,1)S(1)} %get-tuple-element.28), channel_id=1, source_target_pairs={{0,64},{8,72},{16,80},{24,88},{32,96},{40,104},{48,112},{56,120},{... | collective-permute-start | bytes 393224 | tf_op jit(solution)/shard_map/ppermute | solution.py:27
  45.1 2.2 %collective-permute-start.5 = (bf16[2,128,256]{2,1,0:T(8,128)(2,1)S(1)}, bf16[2,128,256]{2,1,0:T(8,128)(2,1)S(1)}, u32[]{:S(2)}, u32[]{:S(2)}) collective-permute-start(bf16[2,128,256]{2,1,0:T(8,128)(2,1)S(1)} %get-tuple-element.28), channel_id=1, source_target_pairs={{0,32},{8,40},{16,48},{24,56},{32,64},{40,72},{48,80},{56,88},{64,... | collective-permute-start | bytes 393224 | tf_op jit(solution)/shard_map/ppermute | solution.py:27
  47.2 3.1 %collective-permute-start.7 = (bf16[2,128,128]{2,1,0:T(8,128)(2,1)S(1)}, bf16[2,128,128]{2,1,0:T(8,128)(2,1)S(1)}, u32[]{:S(2)}, u32[]{:S(2)}) collective-permute-start(bf16[2,128,128]{2,1,0:T(8,128)(2,1)S(1)} %get-tuple-element.29), channel_id=1, source_target_pairs={{0,96},{8,104},{16,112},{24,120},{32,128},{40,136},{48,144},{56,15... | collective-permute-start | bytes 196616 | tf_op jit(solution)/shard_map/ppermute | solution.py:27
  50.4 1.9 %collective-permute-done.7.e12_ref = bf16[2,128,128]{2,1,0:T(8,128)(2,1)S(1)} collective-permute-done((bf16[2,128,128]{2,1,0:T(8,128)(2,1)S(1)}, bf16[2,128,128]{2,1,0:T(8,128)(2,1)S(1)}, u32[]{:S(2)}, u32[]{:S(2)}) %collective-permute-start.7) | collective-permute-done | bytes 65568 | tf_op jit(solution)/shard_map/ppermute | solution.py:27
  52.3 2.6 %attend.1 = (f32[128,2048]{1,0:T(8,128)S(1)}, bf16[128,2048]{1,0:T(8,128)(2,1)S(1)}, bf16[1120,128]{1,0:T(8,128)(2,1)S(1)}) custom-call(s32[8]{0:T(128)S(1)} %concatenate.18.meta, f32[2,128,256]{2,1,0:T(8,128)S(1)} %get-tuple-element.27.e0_ref, bf16[2,128,256]{2,1,0:T(8,128)(2,1)S(1)} %collective-permute-done.5.e4_ref, ...), custom_call_target="tpu_custom_call" | custom-call | flops 1000000000 | bytes 4704800 | tf_op jit(solution)/shard_map/attend/pallas_call | solution.py:62
  55.1 1.8 %collective-permute-done.8.got_ref = bf16[128,2048]{1,0:T(8,128)(2,1)S(1)} collective-permute-done((bf16[128,2048]{1,0:T(8,128)(2,1)S(1)}, bf16[128,2048]{1,0:T(8,128)(2,1)S(1)}, u32[]{:S(2)}, u32[]{:S(2)}) %collective-permute-start.8) | collective-permute-done | bytes 524320 | tf_op jit(solution)/shard_map/ppermute | solution.py:32
  57.3 2.6 %collective-permute-start.10 = (bf16[32,2048]{1,0:T(8,128)(2,1)S(1)}, bf16[32,2048]{1,0:T(8,128)(2,1)S(1)}, u32[]{:S(2)}, u32[]{:S(2)}) collective-permute-start(bf16[32,2048]{1,0:T(8,128)(2,1)S(1)} %get-tuple-element.40), channel_id=1, source_target_pairs={{0,4},{2,6},{4,0},{6,2},{1,5},{3,7},{5,1},{7,3},{8,12},{10,14},{12... | collective-permute-start | bytes 393224 | tf_op jit(solution)/shard_map/ppermute | solution.py:32
  59.9 4.3 %collective-permute-done.19 = bf16[1120,128]{1,0:T(8,128)(2,1)S(1)} collective-permute-done((bf16[1120,128]{1,0:T(8,128)(2,1)S(1)}, bf16[1120,128]{1,0:T(8,128)(2,1)S(1)}, u32[]{:S(2)}, u32[]{:S(2)}) %collective-permute-start.19) | collective-permute-done | bytes 286752 | tf_op jit(solution)/shard_map/ppermute | solution.py:36
  64.5 0.6 collective-permute-done.10.refs_1_
  65.0 2.0 %collective-permute-done.11.refs_2_ = bf16[32,2048]{1,0:T(8,128)(2,1)S(1)} collective-permute-done((bf16[32,2048]{1,0:T(8,128)(2,1)S(1)}, bf16[32,2048]{1,0:T(8,128)(2,1)S(1)}, u32[]{:S(2)}, u32[]{:S(2)}) %collective-permute-start.11) | collective-permute-done | bytes 131104 | tf_op jit(solution)/shard_map/ppermute | solution.py:32
  67.0 1.3 %norm.1 = (bf16[32,2048]{1,0:T(8,128)(2,1)}, bf16[32,512]{1,0:T(8,128)(2,1)S(1)}, bf16[32,512]{1,0:T(8,128)(2,1)S(1)}, bf16[32,512]{1,0:T(8,128)(2,1)S(1)}, bf16[32,512]{1,0:T(8,128)(2,1)S(1)}) custom-call(s32[8]{0:T(128)S(1)} %concatenate.18.meta, bf16[32,2048]{1,0:T(8,128)(2,1)S(1)} %copy-done.1, f32[1,2048]{1,0:T(1,128)S(1)} %bitcast.17, ...), custom_call_target="tpu_custom_call" | custom-call | flops 1000000 | bytes 1056800 | tf_op jit(solution)/shard_map/norm/pallas_call | solution.py:62
  68.3 1.1 collective-permute-start.12
  69.4 2.0 %collective-permute-start.13 = (bf16[32,512]{1,0:T(8,128)(2,1)S(1)}, bf16[32,512]{1,0:T(8,128)(2,1)S(1)}, u32[]{:S(2)}, u32[]{:S(2)}) collective-permute-start(bf16[32,512]{1,0:T(8,128)(2,1)S(1)} %get-tuple-element.44), channel_id=1, source_target_pairs={{0,4},{2,6},{4,0},{6,2},{1,5},{3,7},{5,1},{7,3},{8,12},{10,14},{12... | collective-permute-start | bytes 98312 | tf_op jit(solution)/shard_map/ppermute | solution.py:32
  71.5 0.7 collective-permute-done.12
  72.3 2.6 %collective-permute-done.13 = bf16[32,512]{1,0:T(8,128)(2,1)S(1)} collective-permute-done((bf16[32,512]{1,0:T(8,128)(2,1)S(1)}, bf16[32,512]{1,0:T(8,128)(2,1)S(1)}, u32[]{:S(2)}, u32[]{:S(2)}) %collective-permute-start.13) | collective-permute-done | bytes 32800 | tf_op jit(solution)/shard_map/ppermute | solution.py:32
  74.8 1.7 %collective-permute-done.14 = bf16[32,512]{1,0:T(8,128)(2,1)S(1)} collective-permute-done((bf16[32,512]{1,0:T(8,128)(2,1)S(1)}, bf16[32,512]{1,0:T(8,128)(2,1)S(1)}, u32[]{:S(2)}, u32[]{:S(2)}) %collective-permute-start.14) | collective-permute-done | bytes 32800 | tf_op jit(solution)/shard_map/ppermute | solution.py:32
  76.5 0.6 copy-done.8
  77.1 0.7 pad_maximum_fusion
  77.8 1.0 add.28
  78.8 2.9 %collective-permute-start.21 = (bf16[1120,128]{1,0:T(8,128)(2,1)S(1)}, bf16[1120,128]{1,0:T(8,128)(2,1)S(1)}, u32[]{:S(2)}, u32[]{:S(2)}) collective-permute-start(bf16[1120,128]{1,0:T(8,128)(2,1)S(1)} %add.28), channel_id=1, source_target_pairs={{0,32},{8,40},{16,48},{24,56},{32,0},{40,8},{48,16},{56,24},{64,96... | collective-permute-start | bytes 860168 | tf_op jit(solution)/shard_map/ppermute | solution.py:36
  81.7 0.8 broadcast_select_fusion.7
  82.6 0.7 convolution_convert_fusion
  83.3 0.7 convolution_convert_fusion.1
  84.0 2.0 %collective-permute-start.17 = (bf16[64,3072]{1,0:T(8,128)(2,1)S(1)}, bf16[64,3072]{1,0:T(8,128)(2,1)S(1)}, u32[]{:S(2)}, u32[]{:S(2)}) collective-permute-start(bf16[64,3072]{1,0:T(8,128)(2,1)S(1)} %convolution_convert_fusion.1), channel_id=1, source_target_pairs={{0,4},{2,6},{4,0},{6,2},{1,5},{3,7},{5,1},{7,3},{8,12},{10,14},{12... | collective-permute-start | bytes 1179656 | tf_op jit(solution)/shard_map/ppermute | solution.py:32
  86.0 0.7 convolution_convert_fusion.2
  86.7 1.4 %collective-permute-start.16 = (bf16[64,3072]{1,0:T(8,128)(2,1)S(1)}, bf16[64,3072]{1,0:T(8,128)(2,1)S(1)}, u32[]{:S(2)}, u32[]{:S(2)}) collective-permute-start(bf16[64,3072]{1,0:T(8,128)(2,1)S(1)} %convolution_convert_fusion.2), channel_id=1, source_target_pairs={{0,2},{2,4},{4,6},{6,0},{1,3},{3,5},{5,7},{7,1},{8,10},{10,12},{12... | collective-permute-start | bytes 1179656 | tf_op jit(solution)/shard_map/ppermute | solution.py:32
  88.1 1.1 collective-permute-done.21
  89.3 4.1 %collective-permute-start.22 = (bf16[1120,128]{1,0:T(8,128)(2,1)S(1)}, bf16[1120,128]{1,0:T(8,128)(2,1)S(1)}, u32[]{:S(2)}, u32[]{:S(2)}) collective-permute-start(bf16[1120,128]{1,0:T(8,128)(2,1)S(1)} %add.29), channel_id=1, source_target_pairs={{0,64},{8,72},{16,80},{24,88},{32,96},{40,104},{48,112},{56,120},{... | collective-permute-start | bytes 860168 | tf_op jit(solution)/shard_map/ppermute | solution.py:36
  93.5 12.9 %collective-permute-done.22 = bf16[1120,128]{1,0:T(8,128)(2,1)S(1)} collective-permute-done((bf16[1120,128]{1,0:T(8,128)(2,1)S(1)}, bf16[1120,128]{1,0:T(8,128)(2,1)S(1)}, u32[]{:S(2)}, u32[]{:S(2)}) %collective-permute-start.22) | collective-permute-done | bytes 286752 | tf_op jit(solution)/shard_map/ppermute | solution.py:36
  106.4 6.7 %collective-permute-start.23 = (bf16[1120,128]{1,0:T(8,128)(2,1)S(1)}, bf16[1120,128]{1,0:T(8,128)(2,1)S(1)}, u32[]{:S(2)}, u32[]{:S(2)}) collective-permute-start(bf16[1120,128]{1,0:T(8,128)(2,1)S(1)} %add.30), channel_id=1, source_target_pairs={{0,128},{8,136},{16,144},{24,152},{32,160},{40,168},{48,176},{56,1... | collective-permute-start | bytes 860168 | tf_op jit(solution)/shard_map/ppermute | solution.py:36
  113.1 1.6 %fusion.2 = bf16[64,3072]{1,0:T(8,128)(2,1)} fusion(bf16[512,3072]{1,0:T(8,128)(2,1)S(1)} %copy-done, bf16[64,3072]{1,0:T(8,128)(2,1)S(1)} %collective-permute-done.18, bf16[64,3072]{1,0:T(8,128)(2,1)S(1)} %collective-permute-done.17, bf16[64,3072]{1,0:T(8,128)(2,1)S(1)} %collective-permute-done.16, bf16[32,512]{1,0:T(8,128)(2,1)S(1)} %get-tuple-element.53, ...), kind=kOutput, calls=%fused_computation.3 | convolution fusion | flops 202833920 | bytes 4784128 | tf_op jit(solution)/shard_map/dot_general | solution.py:388
  114.6 10.5 %collective-permute-done.23 = bf16[1120,128]{1,0:T(8,128)(2,1)S(1)} collective-permute-done((bf16[1120,128]{1,0:T(8,128)(2,1)S(1)}, bf16[1120,128]{1,0:T(8,128)(2,1)S(1)}, u32[]{:S(2)}, u32[]{:S(2)}) %collective-permute-start.23) | collective-permute-done | bytes 286752 | tf_op jit(solution)/shard_map/ppermute | solution.py:36
  125.3 0.6 copy.14
  125.9 0.8 convert.1
  (42 shorter events, 1.9 us)
Async XLA Ops:
  0.6 81.9 %copy-start = (bf16[512,3072]{1,0:T(8,128)(2,1)S(1)}, bf16[512,3072]{1,0:T(8,128)(2,1)}, u32[]{:S(2)}) copy-start(bf16[512,3072]{1,0:T(8,128)(2,1)} %param.17) | copy-start | bytes 9437188
  1.5 5.0 %collective-permute-start = (bf16[3,16,256]{2,1,0:T(8,128)(2,1)S(1)}, bf16[3,16,256]{2,1,0:T(8,128)(2,1)S(1)}, u32[]{:S(2)}, u32[]{:S(2)}) collective-permute-start(bf16[3,16,256]{2,1,0:T(8,128)(2,1)S(1)} %slice.32), channel_id=1, source_target_pairs={{0,8},{8,16},{16,24},{24,32},{32,40},{40,48},{48,56},{56,64},{64,7... | collective-permute-start | bytes 73736 | tf_op jit(solution)/shard_map/ppermute | solution.py:27
  6.6 1.0 copy-start.3
  7.6 0.7 copy-start.5
  8.3 0.7 copy-start.6
  9.0 43.3 %copy-start.4 = (bf16[256,2048]{1,0:T(8,128)(2,1)S(1)}, bf16[256,2048]{1,0:T(8,128)(2,1)}, u32[]{:S(2)}) copy-start(bf16[256,2048]{1,0:T(8,128)(2,1)} %w_ref.1) | copy-start | bytes 3145732
  9.0 43.3 %copy-start.7 = (f32[128]{0:T(128)S(1)}, f32[128]{0:T(128)}, u32[]{:S(2)}) copy-start(f32[128]{0:T(128)} %param.13) | copy-start | bytes 1540
  14.4 16.2 %collective-permute-start.4 = (bf16[2,128,256]{2,1,0:T(8,128)(2,1)S(1)}, bf16[2,128,256]{2,1,0:T(8,128)(2,1)S(1)}, u32[]{:S(2)}, u32[]{:S(2)}) collective-permute-start(bf16[2,128,256]{2,1,0:T(8,128)(2,1)S(1)} %get-tuple-element.26), channel_id=1, source_target_pairs={{0,32},{8,40},{16,48},{24,56},{32,64},{40,72},{48,80},{56,88},{64,... | collective-permute-start | bytes 393224 | tf_op jit(solution)/shard_map/ppermute | solution.py:27
  21.2 9.5 %collective-permute-start.3 = (bf16[2,128,256]{2,1,0:T(8,128)(2,1)S(1)}, bf16[2,128,256]{2,1,0:T(8,128)(2,1)S(1)}, u32[]{:S(2)}, u32[]{:S(2)}) collective-permute-start(bf16[2,128,256]{2,1,0:T(8,128)(2,1)S(1)} %get-tuple-element.26), channel_id=1, source_target_pairs={{0,24},{8,32},{16,40},{24,48},{32,56},{40,64},{48,72},{56,80},{64,... | collective-permute-start | bytes 393224 | tf_op jit(solution)/shard_map/ppermute | solution.py:27
  23.8 7.6 %collective-permute-start.2 = (bf16[2,128,256]{2,1,0:T(8,128)(2,1)S(1)}, bf16[2,128,256]{2,1,0:T(8,128)(2,1)S(1)}, u32[]{:S(2)}, u32[]{:S(2)}) collective-permute-start(bf16[2,128,256]{2,1,0:T(8,128)(2,1)S(1)} %get-tuple-element.26), channel_id=1, source_target_pairs={{0,16},{8,24},{16,32},{24,40},{32,48},{40,56},{48,64},{56,72},{64,... | collective-permute-start | bytes 393224 | tf_op jit(solution)/shard_map/ppermute | solution.py:27
  27.8 5.3 %collective-permute-start.1 = (bf16[2,128,256]{2,1,0:T(8,128)(2,1)S(1)}, bf16[2,128,256]{2,1,0:T(8,128)(2,1)S(1)}, u32[]{:S(2)}, u32[]{:S(2)}) collective-permute-start(bf16[2,128,256]{2,1,0:T(8,128)(2,1)S(1)} %get-tuple-element.26), channel_id=1, source_target_pairs={{0,8},{8,16},{16,24},{24,32},{32,40},{40,48},{48,56},{56,64},{64,7... | collective-permute-start | bytes 393224 | tf_op jit(solution)/shard_map/ppermute | solution.py:27
  33.6 33.4 %copy-start.1 = (bf16[32,2048]{1,0:T(8,128)(2,1)S(1)}, bf16[32,2048]{1,0:T(8,128)(2,1)}, u32[]{:S(2)}) copy-start(bf16[32,2048]{1,0:T(8,128)(2,1)} %hidden_ref.1) | copy-start | bytes 393220
  33.6 33.4 %copy-start.2 = (f32[2048]{0:T(1024)S(1)}, f32[2048]{0:T(1024)}, u32[]{:S(2)}) copy-start(f32[2048]{0:T(1024)} %param.16) | copy-start | bytes 24580
  33.6 18.6 %collective-permute-start.6 = (bf16[2,128,256]{2,1,0:T(8,128)(2,1)S(1)}, bf16[2,128,256]{2,1,0:T(8,128)(2,1)S(1)}, u32[]{:S(2)}, u32[]{:S(2)}) collective-permute-start(bf16[2,128,256]{2,1,0:T(8,128)(2,1)S(1)} %get-tuple-element.28), channel_id=1, source_target_pairs={{0,64},{8,72},{16,80},{24,88},{32,96},{40,104},{48,112},{56,120},{... | collective-permute-start | bytes 393224 | tf_op jit(solution)/shard_map/ppermute | solution.py:27
  45.1 7.2 %collective-permute-start.5 = (bf16[2,128,256]{2,1,0:T(8,128)(2,1)S(1)}, bf16[2,128,256]{2,1,0:T(8,128)(2,1)S(1)}, u32[]{:S(2)}, u32[]{:S(2)}) collective-permute-start(bf16[2,128,256]{2,1,0:T(8,128)(2,1)S(1)} %get-tuple-element.28), channel_id=1, source_target_pairs={{0,32},{8,40},{16,48},{24,56},{32,64},{40,72},{48,80},{56,88},{64,... | collective-permute-start | bytes 393224 | tf_op jit(solution)/shard_map/ppermute | solution.py:27
  47.2 5.0 %collective-permute-start.7 = (bf16[2,128,128]{2,1,0:T(8,128)(2,1)S(1)}, bf16[2,128,128]{2,1,0:T(8,128)(2,1)S(1)}, u32[]{:S(2)}, u32[]{:S(2)}) collective-permute-start(bf16[2,128,128]{2,1,0:T(8,128)(2,1)S(1)} %get-tuple-element.29), channel_id=1, source_target_pairs={{0,96},{8,104},{16,112},{24,120},{32,128},{40,136},{48,144},{56,15... | collective-permute-start | bytes 196616 | tf_op jit(solution)/shard_map/ppermute | solution.py:27
  54.9 2.0 %collective-permute-start.8 = (bf16[128,2048]{1,0:T(8,128)(2,1)S(1)}, bf16[128,2048]{1,0:T(8,128)(2,1)S(1)}, u32[]{:S(2)}, u32[]{:S(2)}) collective-permute-start(bf16[128,2048]{1,0:T(8,128)(2,1)S(1)} %get-tuple-element.37), channel_id=1, source_target_pairs={{0,1},{1,0},{2,3},{3,2},{4,5},{5,4},{6,7},{7,6},{8,9},{9,8},{10,11... | collective-permute-start | bytes 1572872 | tf_op jit(solution)/shard_map/ppermute | solution.py:32
  55.0 9.3 %collective-permute-start.19 = (bf16[1120,128]{1,0:T(8,128)(2,1)S(1)}, bf16[1120,128]{1,0:T(8,128)(2,1)S(1)}, u32[]{:S(2)}, u32[]{:S(2)}) collective-permute-start(bf16[1120,128]{1,0:T(8,128)(2,1)S(1)} %get-tuple-element.47), channel_id=1, source_target_pairs={{0,8},{8,0},{16,24},{24,16},{32,40},{40,32},{48,56},{56,48},{64,72... | collective-permute-start | bytes 860168 | tf_op jit(solution)/shard_map/ppermute | solution.py:36
  57.0 7.5 %collective-permute-start.9 = (bf16[32,2048]{1,0:T(8,128)(2,1)S(1)}, bf16[32,2048]{1,0:T(8,128)(2,1)S(1)}, u32[]{:S(2)}, u32[]{:S(2)}) collective-permute-start(bf16[32,2048]{1,0:T(8,128)(2,1)S(1)} %get-tuple-element.39), channel_id=1, source_target_pairs={{0,2},{2,4},{4,6},{6,0},{1,3},{3,5},{5,7},{7,1},{8,10},{10,12},{12... | collective-permute-start | bytes 393224 | tf_op jit(solution)/shard_map/ppermute | solution.py:32
  57.3 7.8 %collective-permute-start.10 = (bf16[32,2048]{1,0:T(8,128)(2,1)S(1)}, bf16[32,2048]{1,0:T(8,128)(2,1)S(1)}, u32[]{:S(2)}, u32[]{:S(2)}) collective-permute-start(bf16[32,2048]{1,0:T(8,128)(2,1)S(1)} %get-tuple-element.40), channel_id=1, source_target_pairs={{0,4},{2,6},{4,0},{6,2},{1,5},{3,7},{5,1},{7,3},{8,12},{10,14},{12... | collective-permute-start | bytes 393224 | tf_op jit(solution)/shard_map/ppermute | solution.py:32
  59.9 7.1 %collective-permute-start.11 = (bf16[32,2048]{1,0:T(8,128)(2,1)S(1)}, bf16[32,2048]{1,0:T(8,128)(2,1)S(1)}, u32[]{:S(2)}, u32[]{:S(2)}) collective-permute-start(bf16[32,2048]{1,0:T(8,128)(2,1)S(1)} %get-tuple-element.41), channel_id=1, source_target_pairs={{0,6},{2,0},{4,2},{6,4},{1,7},{3,1},{5,3},{7,5},{8,14},{10,8},{12,... | collective-permute-start | bytes 393224 | tf_op jit(solution)/shard_map/ppermute | solution.py:32
  64.3 13.5 %collective-permute-start.20 = (bf16[1120,128]{1,0:T(8,128)(2,1)S(1)}, bf16[1120,128]{1,0:T(8,128)(2,1)}, u32[]{:S(2)}, u32[]{:S(2)}) collective-permute-start(bf16[1120,128]{1,0:T(8,128)(2,1)S(1)} %add.27), channel_id=1, source_target_pairs={{0,16},{8,24},{16,0},{24,8},{32,48},{40,56},{48,32},{56,40},{64,80... | collective-permute-start | bytes 860168 | tf_op jit(solution)/shard_map/ppermute | solution.py:36
  68.3 3.9 %collective-permute-start.12 = (bf16[32,512]{1,0:T(8,128)(2,1)S(1)}, bf16[32,512]{1,0:T(8,128)(2,1)S(1)}, u32[]{:S(2)}, u32[]{:S(2)}) collective-permute-start(bf16[32,512]{1,0:T(8,128)(2,1)S(1)} %get-tuple-element.43), channel_id=1, source_target_pairs={{0,2},{2,4},{4,6},{6,0},{1,3},{3,5},{5,7},{7,1},{8,10},{10,12},{12... | collective-permute-start | bytes 98312 | tf_op jit(solution)/shard_map/ppermute | solution.py:32
  69.4 5.4 %collective-permute-start.13 = (bf16[32,512]{1,0:T(8,128)(2,1)S(1)}, bf16[32,512]{1,0:T(8,128)(2,1)S(1)}, u32[]{:S(2)}, u32[]{:S(2)}) collective-permute-start(bf16[32,512]{1,0:T(8,128)(2,1)S(1)} %get-tuple-element.44), channel_id=1, source_target_pairs={{0,4},{2,6},{4,0},{6,2},{1,5},{3,7},{5,1},{7,3},{8,12},{10,14},{12... | collective-permute-start | bytes 98312 | tf_op jit(solution)/shard_map/ppermute | solution.py:32
  71.4 5.1 %collective-permute-start.14 = (bf16[32,512]{1,0:T(8,128)(2,1)S(1)}, bf16[32,512]{1,0:T(8,128)(2,1)S(1)}, u32[]{:S(2)}, u32[]{:S(2)}) collective-permute-start(bf16[32,512]{1,0:T(8,128)(2,1)S(1)} %get-tuple-element.45), channel_id=1, source_target_pairs={{0,6},{2,0},{4,2},{6,4},{1,7},{3,1},{5,3},{7,5},{8,14},{10,8},{12,... | collective-permute-start | bytes 98312 | tf_op jit(solution)/shard_map/ppermute | solution.py:32
  76.5 0.6 copy-start.8
  77.8 3.9 %collective-permute-start.15 = (bf16[128,512]{1,0:T(8,128)(2,1)}, bf16[128,512]{1,0:T(8,128)(2,1)}, u32[]{:S(2)}, u32[]{:S(2)}) collective-permute-start(bf16[128,512]{1,0:T(8,128)(2,1)} %pad_maximum_fusion), channel_id=1, source_target_pairs={{0,1},{1,0},{2,3},{3,2},{4,5},{5,4},{6,7},{7,6},{8,9},{9,8},{10,11... | collective-permute-start | bytes 393224 | tf_op jit(solution)/shard_map/ppermute | solution.py:32
  78.8 10.4 %collective-permute-start.21 = (bf16[1120,128]{1,0:T(8,128)(2,1)S(1)}, bf16[1120,128]{1,0:T(8,128)(2,1)S(1)}, u32[]{:S(2)}, u32[]{:S(2)}) collective-permute-start(bf16[1120,128]{1,0:T(8,128)(2,1)S(1)} %add.28), channel_id=1, source_target_pairs={{0,32},{8,40},{16,48},{24,56},{32,0},{40,8},{48,16},{56,24},{64,96... | collective-permute-start | bytes 860168 | tf_op jit(solution)/shard_map/ppermute | solution.py:36
  83.3 29.8 %collective-permute-start.18 = (bf16[64,3072]{1,0:T(8,128)(2,1)S(1)}, bf16[64,3072]{1,0:T(8,128)(2,1)S(1)}, u32[]{:S(2)}, u32[]{:S(2)}) collective-permute-start(bf16[64,3072]{1,0:T(8,128)(2,1)S(1)} %convolution_convert_fusion), channel_id=1, source_target_pairs={{0,6},{2,0},{4,2},{6,4},{1,7},{3,1},{5,3},{7,5},{8,14},{10,8},{12,... | collective-permute-start | bytes 1179656 | tf_op jit(solution)/shard_map/ppermute | solution.py:32
  84.0 29.1 %collective-permute-start.17 = (bf16[64,3072]{1,0:T(8,128)(2,1)S(1)}, bf16[64,3072]{1,0:T(8,128)(2,1)S(1)}, u32[]{:S(2)}, u32[]{:S(2)}) collective-permute-start(bf16[64,3072]{1,0:T(8,128)(2,1)S(1)} %convolution_convert_fusion.1), channel_id=1, source_target_pairs={{0,4},{2,6},{4,0},{6,2},{1,5},{3,7},{5,1},{7,3},{8,12},{10,14},{12... | collective-permute-start | bytes 1179656 | tf_op jit(solution)/shard_map/ppermute | solution.py:32
  86.7 26.4 %collective-permute-start.16 = (bf16[64,3072]{1,0:T(8,128)(2,1)S(1)}, bf16[64,3072]{1,0:T(8,128)(2,1)S(1)}, u32[]{:S(2)}, u32[]{:S(2)}) collective-permute-start(bf16[64,3072]{1,0:T(8,128)(2,1)S(1)} %convolution_convert_fusion.2), channel_id=1, source_target_pairs={{0,2},{2,4},{4,6},{6,0},{1,3},{3,5},{5,7},{7,1},{8,10},{10,12},{12... | collective-permute-start | bytes 1179656 | tf_op jit(solution)/shard_map/ppermute | solution.py:32
  89.3 17.0 %collective-permute-start.22 = (bf16[1120,128]{1,0:T(8,128)(2,1)S(1)}, bf16[1120,128]{1,0:T(8,128)(2,1)S(1)}, u32[]{:S(2)}, u32[]{:S(2)}) collective-permute-start(bf16[1120,128]{1,0:T(8,128)(2,1)S(1)} %add.29), channel_id=1, source_target_pairs={{0,64},{8,72},{16,80},{24,88},{32,96},{40,104},{48,112},{56,120},{... | collective-permute-start | bytes 860168 | tf_op jit(solution)/shard_map/ppermute | solution.py:36
  106.4 18.7 %collective-permute-start.23 = (bf16[1120,128]{1,0:T(8,128)(2,1)S(1)}, bf16[1120,128]{1,0:T(8,128)(2,1)S(1)}, u32[]{:S(2)}, u32[]{:S(2)}) collective-permute-start(bf16[1120,128]{1,0:T(8,128)(2,1)S(1)} %add.30), channel_id=1, source_target_pairs={{0,128},{8,136},{16,144},{24,152},{32,160},{40,168},{48,176},{56,1... | collective-permute-start | bytes 860168 | tf_op jit(solution)/shard_map/ppermute | solution.py:36

commit v2 on v1

--- a/solution.py
+++ b/solution.py
@@ -20,6 +20,7 @@
 TN = ((0,), (0,))
 VMEM = pl.BlockSpec(memory_space=pltpu.VMEM)
 SMEM = pl.BlockSpec(memory_space=pltpu.SMEM)
+HBM = pl.BlockSpec(memory_space=pltpu.HBM)
 
 
 def shift(value, axis, steps):
@@ -55,14 +56,14 @@
     return dot_split(split(left), split(right), dims)
 
 
-def call(kernel, outs, name, flops, *args, scratch=(), smem=1):
+def call(kernel, outs, name, flops, *args, scratch=(), smem=1, hbm=0):
     size = sum(a.size * a.dtype.itemsize for a in args) + sum(
         o.size * o.dtype.itemsize for o in outs
     )
     return pl.pallas_call(
         kernel,
         out_shape=outs,
-        in_specs=[SMEM] * smem + [VMEM] * (len(args) - smem),
+        in_specs=[SMEM] * smem + [HBM] * hbm + [VMEM] * (len(args) - smem - hbm),
         out_specs=[VMEM] * len(outs),
         scratch_shapes=list(scratch),
         name=name,
@@ -72,6 +73,10 @@
     )(*args)
 
 
+def in_hbm(value):
+    return value if INTERPRET else pltpu.with_memory_space_constraint(value, pltpu.HBM)
+
+
 def out(shape, dtype):
     return jax.ShapeDtypeStruct(shape, dtype)
 
@@ -101,12 +106,64 @@
     return lax.broadcasted_iota(jnp.int32, shape, dim)
 
 
+def conv_rows(ext, taps, pos, begin):
+    pre = ext[HALO:] * taps[CONV - 1 : CONV]
+    for back in range(1, CONV):
+        moved = pltpu.roll(ext, back, 0)[HALO:]
+        ok = jnp.where(pos - back >= begin, 1.0, 0.0).astype(F32)
+        pre = pre + moved * taps[CONV - 1 - back : CONV - back] * ok
+    return (pre / (1.0 + jnp.exp(-pre))).astype(BF16)
+
+
+def edge_select(meta, ends, first, last, ext_pos):
+    edge_id = iota((EDGE_ROWS, 1), 0)
+    wanted = jnp.full((EDGE_ROWS, 1), -1, jnp.int32)
+    for r in range(REQS):
+        begin = ends[r] - meta[r]
+        owned = (ends[r] - 1 >= first) & (ends[r] - 1 <= last)
+        for i in range(CONV - 1):
+            spot = ends[r] - (CONV - 1) + i
+            good = owned & (spot >= begin)
+            wanted = jnp.where(edge_id == r * (CONV - 1) + i, jnp.where(good, spot, -1), wanted)
+    return jnp.where((ext_pos == wanted) & (ext_pos >= 0), 1.0, 0.0).astype(BF16)
+
+
+def conv_kernel(
+    meta, x_hbm, taps_hbm, beta_hbm,
+    act_ref, head_ref, edge_ref, taps_ref, beta_ref, x_ref, sems,
+):
+    copies = [
+        pltpu.make_async_copy(x_hbm, x_ref, sems.at[0]),
+        pltpu.make_async_copy(taps_hbm, taps_ref, sems.at[1]),
+        pltpu.make_async_copy(beta_hbm, beta_ref, sems.at[2]),
+    ]
+    for copy in copies:
+        copy.start()
+    for copy in copies:
+        copy.wait()
+    rows = x_ref.shape[1]
+    ends = request_ends(meta)
+    first = meta[4]
+    pos = first + iota((rows, 1), 0)
+    begin = start_of(pos, ends)
+    select = edge_select(
+        meta, ends, first, first + rows - 1, first + iota((EDGE_ROWS, rows), 1)
+    )
+    for c in range(3):
+        x = x_ref[c]
+        edge_ref[c] = dot(select, x).astype(BF16)
+        head_ref[c] = x[:HALO]
+        wide = x.astype(F32)
+        act_ref[c, HALO:] = conv_rows(wide, taps_ref[c], pos[HALO:], begin[HALO:])
+        act_ref[c, :HALO] = jnp.zeros((HALO, x.shape[1]), BF16)
+
+
 def prep_kernel(
-    meta, x_ref, halo_ref, taps_ref, beta_ref,
+    meta, act_ref, head_ref, part_ref, taps_ref, beta_ref, halo_ref,
     map_ref, uw_ref, local_ref, link_ref, kb_ref, ks_ref, edge_ref,
 ):
-    rows = x_ref.shape[1]
-    heads = x_ref.shape[2] // DK
+    rows = act_ref.shape[1]
+    heads = act_ref.shape[2] // DK
     half = rows // 2
     ends = request_ends(meta)
     first = meta[4]
@@ -120,34 +177,17 @@
     last_seg = seg_of(last, ends)
     last_link = start_of(last, ends) < first
     in_last = jnp.where(seg == last_seg, 1.0, 0.0).astype(F32)
-
-    edge_id = iota((EDGE_ROWS, 1), 0)
-    wanted = jnp.full((EDGE_ROWS, 1), -1, jnp.int32)
-    for r in range(REQS):
-        end = ends[r]
-        begin_r = end - meta[r]
-        owned = (end - 1 >= first) & (end - 1 <= last)
-        for i in range(CONV - 1):
-            spot = end - (CONV - 1) + i
-            good = owned & (spot >= begin_r)
-            wanted = jnp.where(edge_id == r * (CONV - 1) + i, jnp.where(good, spot, -1), wanted)
-    ext_pos = first - HALO + iota((EDGE_ROWS, rows + HALO), 1)
-    select = jnp.where((ext_pos == wanted) & (ext_pos >= 0), 1.0, 0.0).astype(BF16)
+    select = edge_select(meta, ends, first, last, first - HALO + iota((EDGE_ROWS, HALO), 1))
 
     planes = []
     for c in range(3):
-        ext = jnp.concatenate([halo_ref[c], x_ref[c]], axis=0)
-        picked = dot(select, ext).astype(BF16)
+        halo = halo_ref[c]
+        picked = part_ref[c] + dot(select, halo).astype(BF16)
         for b in range(heads):
             edge_ref[c * heads + b] = picked[:, b * DK : (b + 1) * DK]
-        wide = ext.astype(F32)
-        taps = taps_ref[c]
-        pre = wide[HALO:] * taps[CONV - 1 : CONV]
-        for back in range(1, CONV):
-            moved = pltpu.roll(wide, back, 0)[HALO:]
-            ok = jnp.where(pos - back >= begin, 1.0, 0.0).astype(F32)
-            pre = pre + moved * taps[CONV - 1 - back : CONV - back] * ok
-        planes.append((pre / (1.0 + jnp.exp(-pre))).astype(BF16))
+        ext = jnp.concatenate([halo, head_ref[c]], axis=0).astype(F32)
+        lead = conv_rows(ext, taps_ref[c], pos[:HALO], begin[:HALO])
+        planes.append(jnp.concatenate([lead, act_ref[c, HALO:]], axis=0))
 
     row_id = iota((rows, rows), 0)
     col_id = iota((rows, rows), 1)
@@ -284,19 +324,27 @@
         ref[...] = (own_ref[part] + got_ref[part].astype(F32)).astype(BF16)
 
 
-def norm_kernel(meta, hidden_ref, gain_ref, keep_ref, *refs):
-    wins = refs[-1].shape[0]
-    got, (stream_ref, *piece_refs), cols_ref = refs[: wins - 1], refs[wins - 1 : -1], refs[-1]
+def norm_kernel(hidden_ref, gain_ref, pay_ref, came_ref, keep_ref, *refs):
+    *got, stream_ref, normed_ref, sum_ref = refs
     total = keep_ref[...]
     for ref in got:
         total = total + ref[...].astype(F32)
     total = hidden_ref[...].astype(F32) + total
     stream_ref[...] = total.astype(BF16)
     scale = lax.rsqrt(jnp.mean(total * total, axis=1, keepdims=True) + 1e-05)
-    normed = (total * scale * gain_ref[...]).astype(BF16)
-    width = normed.shape[1] // wins
+    normed_ref[...] = (total * scale * gain_ref[...]).astype(BF16)
+    sum_ref[...] = pay_ref[...] + came_ref[...]
+
+
+def columns_kernel(meta, mine_ref, peer_ref, *refs):
+    *piece_refs, cols_ref = refs
+    wins, rows, width = cols_ref.shape
+    mine, peer = mine_ref[...], peer_ref[...]
+    lower = jnp.where(meta[6] == 0, mine, peer)
+    upper = jnp.where(meta[6] == 0, peer, mine)
     for k in range(wins):
-        cols_ref[k] = normed[:, k * width : (k + 1) * width]
+        cols_ref[k, : rows // 2] = lower[:, k * width : (k + 1) * width]
+        cols_ref[k, rows // 2 :] = upper[:, k * width : (k + 1) * width]
     for k, ref in enumerate(piece_refs):
         ref[...] = cols_ref[lax.rem(meta[5] + k, wins)]
 
@@ -312,6 +360,21 @@
     meta = jnp.concatenate([lengths, jnp.stack([seq * rows, win, core, core])])
     x = qkv_in.transpose(1, 0, 2)
     halo = shift(x[:, rows - HALO :], "seq", 1)
+    act, lead, parts, taps, beta = call(
+        conv_kernel,
+        [
+            out((3, rows, width), BF16),
+            out((3, HALO, width), BF16),
+            out((3, EDGE_ROWS, width), BF16),
+            out((3, CONV, width), F32),
+            out((heads, rows), F32),
+        ],
+        "conv",
+        10**8,
+        meta, *(in_hbm(a) for a in (x, conv_w, beta_logits)),
+        scratch=[pltpu.VMEM((3, rows, width), BF16), pltpu.SemaphoreType.DMA((3,))],
+        hbm=3,
+    )
     maps, uw, local, link, kb, ks, edges = call(
         prep_kernel,
         [
@@ -325,7 +388,7 @@
         ],
         "prep",
         2 * 10**9,
-        meta, x, halo, conv_w, beta_logits,
+        meta, act, lead, parts, taps, beta, halo,
     )
 
     def sent(value, steps):
@@ -360,6 +423,8 @@
         scratch=[pltpu.VMEM((wins, cores, piece, width), BF16)],
     )
     got = rotate(other, "wout", 1)
+    bits = [1 << b for b in reversed(range((n_seq - 1).bit_length()))]
+    came = exchange(payload, "seq", bits[0])
     sums = call(
         pair_kernel,
         [out((piece, model), F32)] + [out((piece, model), BF16)] * (wins - 1),
@@ -369,25 +434,29 @@
         smem=0,
     )
     reduced = [rotate(sums[k], "win", k) for k in range(1, wins)]
-    stream_out, *cols = call(
+    stream_out, normed, payload = call(
         norm_kernel,
-        [out((piece, model), BF16)] + [out((piece, model // wins), BF16)] * wins,
+        [out((piece, model), BF16), out((piece, model), BF16), out((pay_rows, DK), BF16)],
         "norm",
         10**6,
-        meta, hidden_in, norm_gain.reshape(1, model), sums[0], *reduced,
-        scratch=[pltpu.VMEM((wins, piece, model // wins), BF16)],
+        hidden_in, norm_gain.reshape(1, model), payload, came, sums[0], *reduced,
+        smem=0,
+    )
+    peer = rotate(normed, "wout", 1)
+    came = exchange(payload, "seq", bits[1])
+    cols = call(
+        columns_kernel,
+        [out((2 * piece, model // wins), BF16)] * wins,
+        "columns",
+        10**6,
+        meta, normed, peer,
+        scratch=[pltpu.VMEM((wins, 2 * piece, model // wins), BF16)],
     )
     blocks = [cols[0]] + [rotate(cols[k], "win", k) for k in range(1, wins)]
-    peers = rotate(jnp.concatenate(blocks, axis=0), "wout", 1)
+    *blocks, payload = lax.optimization_barrier((*blocks, payload + came))
 
     def partial(k):
-        j = (wins - k) % wins
-        mine, theirs = blocks[j], peers[j * piece : (j + 1) * piece]
-        lower = jnp.where(core == 0, mine, theirs)
-        upper = jnp.where(core == 0, theirs, mine)
-        return jnp.dot(
-            jnp.concatenate([lower, upper], axis=0), w_qkv, preferred_element_type=F32
-        )
+        return jnp.dot(blocks[(wins - k) % wins], w_qkv, preferred_element_type=F32)
 
     arrived = [rotate(partial(k).astype(BF16), "win", k) for k in range(1, wins)]
     total = partial(0)
@@ -395,10 +464,8 @@
         total = total + part.astype(F32)
     projected = total.astype(BF16)
 
-    bit = 1
-    while bit < n_seq:
+    for bit in bits[2:]:
         payload = payload + exchange(payload, "seq", bit)
-        bit *= 2
     final_states = payload[:state_rows].astype(F32).reshape(REQS, heads, DK, DK)
     edges = payload[state_rows:].reshape(3 * heads, EDGE_ROWS, DK)[:, : REQS * (CONV - 1)]
     conv_edges = edges.transpose(1, 0, 2).reshape(REQS, CONV - 1, 3, width)

time: 128 us -> 120 us (0.938)
  the two profiles are of different devices: /device:TPU:24 before, /device:TPU:1 now
where the time goes in v2:
time: 120 us
  starting transfers between devices  64.3 us (54%)
  waiting for transfers between devices  36 us (30%)
  Pallas kernels  11.8 us (10%)
  matrix products  3.57 us (3%)
  local copies, waits for them, and re-layouts  2.34 us (2%)
    ppermute x8, starting transfers between devices, shift(): lax.ppermute(value, axis, [(s, s + steps) for s in range(count - steps)])  33.6 us
    ppermute x5, waiting for transfers between devices, exchange(): lax.ppermute(value, axis, [(s, s ^ bit) for s in range(lax.axis_size(axis...  18 us
    ppermute x11, starting transfers between devices, rotate(): lax.ppermute(value, axis, [(s, (s + steps) % count) for s in range(count)])  17.5 us
    ppermute x5, starting transfers between devices, exchange(): lax.ppermute(value, axis, [(s, s ^ bit) for s in range(lax.axis_size(axis...  13.1 us
    ppermute x11, waiting for transfers between devices, rotate(): lax.ppermute(value, axis, [(s, (s + steps) % count) for s in range(count)])  12.8 us
    pallas_call x7, Pallas kernels, call(): pl.pallas_call(kernel, out_shape=outs, in_specs=[SMEM] * smem + [HBM] * h...  11.8 us
    ppermute x8, waiting for transfers between devices, shift(): lax.ppermute(value, axis, [(s, s + steps) for s in range(count - steps)])  5.23 us
    dot_general x4, matrix products, partial(): return jnp.dot(blocks[(wins - k) % wins], w_qkv, preferred_element_type=F32)  3.57 us
  transfers between devices with their start and end apart: 24, of which 10 were waited for; matrix products, arithmetic and copies ran while one was open for 4% of the time, Pallas kernels for 3%

profile of v2, /device:TPU:1, one launch (start us, length us, event | category | flops | bytes accessed | tf_op | source)
XLA Modules:
  0.0 120.1 jit_solution(2387522694153885069)
XLA Ops:
  0.6 0.9 slice.16
  1.5 4.1 %collective-permute-start = (bf16[3,16,256]{2,1,0:T(8,128)(2,1)S(1)}, bf16[3,16,256]{2,1,0:T(8,128)(2,1)S(1)}, u32[]{:S(2)}, u32[]{:S(2)}) collective-permute-start(bf16[3,16,256]{2,1,0:T(8,128)(2,1)S(1)} %slice.16), channel_id=1, source_target_pairs={{0,8},{8,16},{16,24},{24,32},{32,40},{40,48},{48,56},{56,64},{64,7... | collective-permute-start | bytes 73736 | tf_op jit(solution)/shard_map/ppermute | solution.py:28
  5.6 0.7 concatenate.3.meta
  6.4 2.4 %conv.1 = (bf16[3,256,256]{2,1,0:T(8,128)(2,1)S(1)}, bf16[3,16,256]{2,1,0:T(8,128)(2,1)S(1)}, bf16[3,16,256]{2,1,0:T(8,128)(2,1)S(1)}, f32[3,4,256]{2,1,0:T(4,128)S(1)}, f32[2,256]{1,0:T(2,128)S(1)}) custom-call(s32[8]{0:T(128)S(1)} %concatenate.3.meta, bf16[3,256,256]{2,1,0:T(8,128)(2,1)} %bitcast.25, f32[3,4,256]{2,1,0:T(4,128)} %taps_hbm.1, f32[2,256]{1,0:T(2,128)} %beta_hbm.1), custom_call_target="tpu_custom_call" | custom-call | flops 100000000 | bytes 864288 | tf_op jit(solution)/shard_map/conv/pallas_call | solution.py:63
  8.8 4.9 %prep.1 = (bf16[2,128,256]{2,1,0:T(8,128)(2,1)S(1)}, f32[2,256,256]{2,1,0:T(8,128)S(1)}, f32[2,256,128]{2,1,0:T(8,128)S(1)}, f32[2,256,128]{2,1,0:T(8,128)S(1)},...) custom-call(s32[8]{0:T(128)S(1)} %concatenate.3.meta, ...), custom_call_target="tpu_custom_call" | custom-call | flops 2000000000 | bytes 1818656 | tf_op jit(solution)/shard_map/prep/pallas_call | solution.py:63
  13.7 4.0 %collective-permute-start.4 = (bf16[2,128,256]{2,1,0:T(8,128)(2,1)S(1)}, bf16[2,128,256]{2,1,0:T(8,128)(2,1)S(1)}, u32[]{:S(2)}, u32[]{:S(2)}) collective-permute-start(bf16[2,128,256]{2,1,0:T(8,128)(2,1)S(1)} %get-tuple-element.43), channel_id=1, source_target_pairs={{0,32},{8,40},{16,48},{24,56},{32,64},{40,72},{48,80},{56,88},{64,... | collective-permute-start | bytes 393224 | tf_op jit(solution)/shard_map/ppermute | solution.py:28
  17.7 4.4 %collective-permute-start.3 = (bf16[2,128,256]{2,1,0:T(8,128)(2,1)S(1)}, bf16[2,128,256]{2,1,0:T(8,128)(2,1)S(1)}, u32[]{:S(2)}, u32[]{:S(2)}) collective-permute-start(bf16[2,128,256]{2,1,0:T(8,128)(2,1)S(1)} %get-tuple-element.43), channel_id=1, source_target_pairs={{0,24},{8,32},{16,40},{24,48},{32,56},{40,64},{48,72},{56,80},{64,... | collective-permute-start | bytes 393224 | tf_op jit(solution)/shard_map/ppermute | solution.py:28
  22.2 3.4 %collective-permute-start.2 = (bf16[2,128,256]{2,1,0:T(8,128)(2,1)S(1)}, bf16[2,128,256]{2,1,0:T(8,128)(2,1)S(1)}, u32[]{:S(2)}, u32[]{:S(2)}) collective-permute-start(bf16[2,128,256]{2,1,0:T(8,128)(2,1)S(1)} %get-tuple-element.43), channel_id=1, source_target_pairs={{0,16},{8,24},{16,32},{24,40},{32,48},{40,56},{48,64},{56,72},{64,... | collective-permute-start | bytes 393224 | tf_op jit(solution)/shard_map/ppermute | solution.py:28
  25.6 2.2 %collective-permute-start.1 = (bf16[2,128,256]{2,1,0:T(8,128)(2,1)S(1)}, bf16[2,128,256]{2,1,0:T(8,128)(2,1)S(1)}, u32[]{:S(2)}, u32[]{:S(2)}) collective-permute-start(bf16[2,128,256]{2,1,0:T(8,128)(2,1)S(1)} %get-tuple-element.43), channel_id=1, source_target_pairs={{0,8},{8,16},{16,24},{24,32},{32,40},{40,48},{48,56},{56,64},{64,7... | collective-permute-start | bytes 393224 | tf_op jit(solution)/shard_map/ppermute | solution.py:28
  27.9 3.3 %collective-permute-done.1.m1_ref = bf16[2,128,256]{2,1,0:T(8,128)(2,1)S(1)} collective-permute-done((bf16[2,128,256]{2,1,0:T(8,128)(2,1)S(1)}, bf16[2,128,256]{2,1,0:T(8,128)(2,1)S(1)}, u32[]{:S(2)}, u32[]{:S(2)}) %collective-permute-start.1) | collective-permute-done | bytes 131104 | tf_op jit(solution)/shard_map/ppermute | solution.py:28
  31.1 0.5 window.1
  31.6 9.2 %collective-permute-start.6 = (bf16[2,128,256]{2,1,0:T(8,128)(2,1)S(1)}, bf16[2,128,256]{2,1,0:T(8,128)(2,1)S(1)}, u32[]{:S(2)}, u32[]{:S(2)}) collective-permute-start(bf16[2,128,256]{2,1,0:T(8,128)(2,1)S(1)} %get-tuple-element.45), channel_id=1, source_target_pairs={{0,64},{8,72},{16,80},{24,88},{32,96},{40,104},{48,112},{56,120},{... | collective-permute-start | bytes 393224 | tf_op jit(solution)/shard_map/ppermute | solution.py:28
  40.8 3.3 %collective-permute-start.5 = (bf16[2,128,256]{2,1,0:T(8,128)(2,1)S(1)}, bf16[2,128,256]{2,1,0:T(8,128)(2,1)S(1)}, u32[]{:S(2)}, u32[]{:S(2)}) collective-permute-start(bf16[2,128,256]{2,1,0:T(8,128)(2,1)S(1)} %get-tuple-element.45), channel_id=1, source_target_pairs={{0,32},{8,40},{16,48},{24,56},{32,64},{40,72},{48,80},{56,88},{64,... | collective-permute-start | bytes 393224 | tf_op jit(solution)/shard_map/ppermute | solution.py:28
  44.1 2.9 %collective-permute-start.7 = (bf16[2,128,128]{2,1,0:T(8,128)(2,1)S(1)}, bf16[2,128,128]{2,1,0:T(8,128)(2,1)S(1)}, u32[]{:S(2)}, u32[]{:S(2)}) collective-permute-start(bf16[2,128,128]{2,1,0:T(8,128)(2,1)S(1)} %get-tuple-element.46), channel_id=1, source_target_pairs={{0,96},{8,104},{16,112},{24,120},{32,128},{40,136},{48,144},{56,15... | collective-permute-start | bytes 196616 | tf_op jit(solution)/shard_map/ppermute | solution.py:28
  47.1 2.0 %collective-permute-done.7.e12_ref = bf16[2,128,128]{2,1,0:T(8,128)(2,1)S(1)} collective-permute-done((bf16[2,128,128]{2,1,0:T(8,128)(2,1)S(1)}, bf16[2,128,128]{2,1,0:T(8,128)(2,1)S(1)}, u32[]{:S(2)}, u32[]{:S(2)}) %collective-permute-start.7) | collective-permute-done | bytes 65568 | tf_op jit(solution)/shard_map/ppermute | solution.py:28
  49.1 2.6 %attend.1 = (f32[128,2048]{1,0:T(8,128)S(1)}, bf16[128,2048]{1,0:T(8,128)(2,1)S(1)}, bf16[1120,128]{1,0:T(8,128)(2,1)S(1)}) custom-call(s32[8]{0:T(128)S(1)} %concatenate.3.meta, f32[2,128,256]{2,1,0:T(8,128)S(1)} %get-tuple-element.44.e0_ref, bf16[2,128,256]{2,1,0:T(8,128)(2,1)S(1)} %collective-permute-done.5.e4_ref, ...), custom_call_target="tpu_custom_call" | custom-call | flops 1000000000 | bytes 4704800 | tf_op jit(solution)/shard_map/attend/pallas_call | solution.py:63
  51.7 2.7 %collective-permute-start.9 = (bf16[128,2048]{1,0:T(8,128)(2,1)S(1)}, bf16[128,2048]{1,0:T(8,128)(2,1)S(1)}, u32[]{:S(2)}, u32[]{:S(2)}) collective-permute-start(bf16[128,2048]{1,0:T(8,128)(2,1)S(1)} %get-tuple-element.55), channel_id=1, source_target_pairs={{0,1},{1,0},{2,3},{3,2},{4,5},{5,4},{6,7},{7,6},{8,9},{9,8},{10,11... | collective-permute-start | bytes 1572872 | tf_op jit(solution)/shard_map/ppermute | solution.py:33
  54.3 7.5 %collective-permute-start.8 = (bf16[1120,128]{1,0:T(8,128)(2,1)S(1)}, bf16[1120,128]{1,0:T(8,128)(2,1)S(1)}, u32[]{:S(2)}, u32[]{:S(2)}) collective-permute-start(bf16[1120,128]{1,0:T(8,128)(2,1)S(1)} %get-tuple-element.53.pay_ref), channel_id=1, source_target_pairs={{0,128},{8,136},{16,144},{24,152},{32,160},{40,168},{48,176},{56,1... | collective-permute-start | bytes 860168 | tf_op jit(solution)/shard_map/ppermute | solution.py:37
  61.9 1.4 %collective-permute-start.10 = (bf16[32,2048]{1,0:T(8,128)(2,1)S(1)}, bf16[32,2048]{1,0:T(8,128)(2,1)S(1)}, u32[]{:S(2)}, u32[]{:S(2)}) collective-permute-start(bf16[32,2048]{1,0:T(8,128)(2,1)S(1)} %get-tuple-element.57), channel_id=1, source_target_pairs={{0,2},{2,4},{4,6},{6,0},{1,3},{3,5},{5,7},{7,1},{8,10},{10,12},{12... | collective-permute-start | bytes 393224 | tf_op jit(solution)/shard_map/ppermute | solution.py:33
  63.3 2.6 %collective-permute-start.11 = (bf16[32,2048]{1,0:T(8,128)(2,1)S(1)}, bf16[32,2048]{1,0:T(8,128)(2,1)S(1)}, u32[]{:S(2)}, u32[]{:S(2)}) collective-permute-start(bf16[32,2048]{1,0:T(8,128)(2,1)S(1)} %get-tuple-element.58), channel_id=1, source_target_pairs={{0,4},{2,6},{4,0},{6,2},{1,5},{3,7},{5,1},{7,3},{8,12},{10,14},{12... | collective-permute-start | bytes 393224 | tf_op jit(solution)/shard_map/ppermute | solution.py:33
  65.9 1.1 collective-permute-start.12
  67.0 3.7 %collective-permute-done.8.came_ref = bf16[1120,128]{1,0:T(8,128)(2,1)S(1)} collective-permute-done((bf16[1120,128]{1,0:T(8,128)(2,1)S(1)}, bf16[1120,128]{1,0:T(8,128)(2,1)S(1)}, u32[]{:S(2)}, u32[]{:S(2)}) %collective-permute-start.8) | collective-permute-done | bytes 286752 | tf_op jit(solution)/shard_map/ppermute | solution.py:37
  70.7 1.3 %collective-permute-done.11.refs_1_ = bf16[32,2048]{1,0:T(8,128)(2,1)S(1)} collective-permute-done((bf16[32,2048]{1,0:T(8,128)(2,1)S(1)}, bf16[32,2048]{1,0:T(8,128)(2,1)S(1)}, u32[]{:S(2)}, u32[]{:S(2)}) %collective-permute-start.11) | collective-permute-done | bytes 131104 | tf_op jit(solution)/shard_map/ppermute | solution.py:33
  72.0 0.8 norm.1
  72.7 5.4 %collective-permute-start.17 = (bf16[1120,128]{1,0:T(8,128)(2,1)S(1)}, bf16[1120,128]{1,0:T(8,128)(2,1)S(1)}, u32[]{:S(2)}, u32[]{:S(2)}) collective-permute-start(bf16[1120,128]{1,0:T(8,128)(2,1)S(1)} %get-tuple-element.65), channel_id=1, source_target_pairs={{0,64},{8,72},{16,80},{24,88},{32,96},{40,104},{48,112},{56,120},{... | collective-permute-start | bytes 860168 | tf_op jit(solution)/shard_map/ppermute | solution.py:37
  78.1 0.9 collective-permute-start.13
  79.0 1.0 collective-permute-done.13.peer_ref
  80.0 0.6 columns.1
  80.6 1.4 %collective-permute-start.14 = (bf16[64,512]{1,0:T(8,128)(2,1)S(1)}, bf16[64,512]{1,0:T(8,128)(2,1)S(1)}, u32[]{:S(2)}, u32[]{:S(2)}) collective-permute-start(bf16[64,512]{1,0:T(8,128)(2,1)S(1)} %get-tuple-element.62), channel_id=1, source_target_pairs={{0,2},{2,4},{4,6},{6,0},{1,3},{3,5},{5,7},{7,1},{8,10},{10,12},{12... | collective-permute-start | bytes 196616 | tf_op jit(solution)/shard_map/ppermute | solution.py:33
  82.0 2.6 %collective-permute-start.15 = (bf16[64,512]{1,0:T(8,128)(2,1)S(1)}, bf16[64,512]{1,0:T(8,128)(2,1)S(1)}, u32[]{:S(2)}, u32[]{:S(2)}) collective-permute-start(bf16[64,512]{1,0:T(8,128)(2,1)S(1)} %get-tuple-element.63), channel_id=1, source_target_pairs={{0,4},{2,6},{4,0},{6,2},{1,5},{3,7},{5,1},{7,3},{8,12},{10,14},{12... | collective-permute-start | bytes 196616 | tf_op jit(solution)/shard_map/ppermute | solution.py:33
  84.6 1.1 collective-permute-start.16
  85.7 5.3 %collective-permute-done.17 = bf16[1120,128]{1,0:T(8,128)(2,1)S(1)} collective-permute-done((bf16[1120,128]{1,0:T(8,128)(2,1)S(1)}, bf16[1120,128]{1,0:T(8,128)(2,1)S(1)}, u32[]{:S(2)}, u32[]{:S(2)}) %collective-permute-start.17) | collective-permute-done | bytes 286752 | tf_op jit(solution)/shard_map/ppermute | solution.py:37
  91.0 0.1 collective-permute-start.21
  91.1 0.7 convolution_convert_fusion.2
  91.8 0.7 convolution_convert_fusion.1
  92.5 0.7 convolution_convert_fusion
  93.2 2.8 %collective-permute-start.20 = (bf16[64,3072]{1,0:T(8,128)(2,1)S(1)}, bf16[64,3072]{1,0:T(8,128)(2,1)S(1)}, u32[]{:S(2)}, u32[]{:S(2)}) collective-permute-start(bf16[64,3072]{1,0:T(8,128)(2,1)S(1)} %convolution_convert_fusion), channel_id=1, source_target_pairs={{0,6},{2,0},{4,2},{6,4},{1,7},{3,1},{5,3},{7,5},{8,14},{10,8},{12,... | collective-permute-start | bytes 1179656 | tf_op jit(solution)/shard_map/ppermute | solution.py:33
  96.0 0.3 collective-permute-start.19
  96.4 0.7 collective-permute-start.18
  97.0 1.3 %collective-permute-done.21 = bf16[1120,128]{1,0:T(8,128)(2,1)S(1)} collective-permute-done((bf16[1120,128]{1,0:T(8,128)(2,1)S(1)}, bf16[1120,128]{1,0:T(8,128)(2,1)S(1)}, u32[]{:S(2)}, u32[]{:S(2)}) %collective-permute-start.21) | collective-permute-done | bytes 286752 | tf_op jit(solution)/shard_map/ppermute | solution.py:37
  98.4 0.1 collective-permute-start.22
  98.5 7.7 %collective-permute-done.22 = bf16[1120,128]{1,0:T(8,128)(2,1)S(1)} collective-permute-done((bf16[1120,128]{1,0:T(8,128)(2,1)S(1)}, bf16[1120,128]{1,0:T(8,128)(2,1)S(1)}, u32[]{:S(2)}, u32[]{:S(2)}) %collective-permute-start.22) | collective-permute-done | bytes 286752 | tf_op jit(solution)/shard_map/ppermute | solution.py:37
  106.3 0.1 collective-permute-start.23
  106.4 0.3 collective-permute-done.19
  106.7 10.3 %collective-permute-done.18 = bf16[64,3072]{1,0:T(8,128)(2,1)S(1)} collective-permute-done((bf16[64,3072]{1,0:T(8,128)(2,1)S(1)}, bf16[64,3072]{1,0:T(8,128)(2,1)S(1)}, u32[]{:S(2)}, u32[]{:S(2)}) %collective-permute-start.18) | collective-permute-done | bytes 393248 | tf_op jit(solution)/shard_map/ppermute | solution.py:33
  117.0 1.6 %fusion.2 = bf16[64,3072]{1,0:T(8,128)(2,1)} fusion(bf16[64,512]{1,0:T(8,128)(2,1)S(1)} %get-tuple-element.66, bf16[512,3072]{1,0:T(8,128)(2,1)S(1)} %copy-done, bf16[64,3072]{1,0:T(8,128)(2,1)S(1)} %collective-permute-done.20, bf16[64,3072]{1,0:T(8,128)(2,1)S(1)} %collective-permute-done.19, bf16[64,3072]{1,0:T(8,128)(2,1)S(1)} %collective-permute-done.18), kind=kOutput, calls=%fused_computation.3 | convolution fusion | flops 202702848 | bytes 4784128 | tf_op jit(solution)/shard_map/dot_general | solution.py:459
  118.7 0.6 copy.14
  119.3 0.8 convert.1
  (33 shorter events, 0.5 us)
Async XLA Ops:
  0.6 90.5 %copy-start = (bf16[512,3072]{1,0:T(8,128)(2,1)S(1)}, bf16[512,3072]{1,0:T(8,128)(2,1)}, u32[]{:S(2)}) copy-start(bf16[512,3072]{1,0:T(8,128)(2,1)} %param.17) | copy-start | bytes 9437188
  1.5 7.3 %collective-permute-start = (bf16[3,16,256]{2,1,0:T(8,128)(2,1)S(1)}, bf16[3,16,256]{2,1,0:T(8,128)(2,1)S(1)}, u32[]{:S(2)}, u32[]{:S(2)}) collective-permute-start(bf16[3,16,256]{2,1,0:T(8,128)(2,1)S(1)} %slice.16), channel_id=1, source_target_pairs={{0,8},{8,16},{16,24},{24,32},{32,40},{40,48},{48,56},{56,64},{64,7... | collective-permute-start | bytes 73736 | tf_op jit(solution)/shard_map/ppermute | solution.py:28
  8.8 40.2 %copy-start.3 = (bf16[256,2048]{1,0:T(8,128)(2,1)S(1)}, bf16[256,2048]{1,0:T(8,128)(2,1)}, u32[]{:S(2)}) copy-start(bf16[256,2048]{1,0:T(8,128)(2,1)} %w_ref.1) | copy-start | bytes 3145732
  8.8 40.2 %copy-start.4 = (f32[128]{0:T(128)S(1)}, f32[128]{0:T(128)}, u32[]{:S(2)}) copy-start(f32[128]{0:T(128)} %param.13) | copy-start | bytes 1540
  13.7 58.2 %copy-start.1 = (bf16[32,2048]{1,0:T(8,128)(2,1)S(1)}, bf16[32,2048]{1,0:T(8,128)(2,1)}, u32[]{:S(2)}) copy-start(bf16[32,2048]{1,0:T(8,128)(2,1)} %hidden_ref.1) | copy-start | bytes 393220
  13.7 58.2 %copy-start.2 = (f32[2048]{0:T(1024)S(1)}, f32[2048]{0:T(1024)}, u32[]{:S(2)}) copy-start(f32[2048]{0:T(1024)} %param.16) | copy-start | bytes 24580
  13.7 14.1 %collective-permute-start.4 = (bf16[2,128,256]{2,1,0:T(8,128)(2,1)S(1)}, bf16[2,128,256]{2,1,0:T(8,128)(2,1)S(1)}, u32[]{:S(2)}, u32[]{:S(2)}) collective-permute-start(bf16[2,128,256]{2,1,0:T(8,128)(2,1)S(1)} %get-tuple-element.43), channel_id=1, source_target_pairs={{0,32},{8,40},{16,48},{24,56},{32,64},{40,72},{48,80},{56,88},{64,... | collective-permute-start | bytes 393224 | tf_op jit(solution)/shard_map/ppermute | solution.py:28
  17.7 10.1 %collective-permute-start.3 = (bf16[2,128,256]{2,1,0:T(8,128)(2,1)S(1)}, bf16[2,128,256]{2,1,0:T(8,128)(2,1)S(1)}, u32[]{:S(2)}, u32[]{:S(2)}) collective-permute-start(bf16[2,128,256]{2,1,0:T(8,128)(2,1)S(1)} %get-tuple-element.43), channel_id=1, source_target_pairs={{0,24},{8,32},{16,40},{24,48},{32,56},{40,64},{48,72},{56,80},{64,... | collective-permute-start | bytes 393224 | tf_op jit(solution)/shard_map/ppermute | solution.py:28
  22.2 5.7 %collective-permute-start.2 = (bf16[2,128,256]{2,1,0:T(8,128)(2,1)S(1)}, bf16[2,128,256]{2,1,0:T(8,128)(2,1)S(1)}, u32[]{:S(2)}, u32[]{:S(2)}) collective-permute-start(bf16[2,128,256]{2,1,0:T(8,128)(2,1)S(1)} %get-tuple-element.43), channel_id=1, source_target_pairs={{0,16},{8,24},{16,32},{24,40},{32,48},{40,56},{48,64},{56,72},{64,... | collective-permute-start | bytes 393224 | tf_op jit(solution)/shard_map/ppermute | solution.py:28
  25.6 5.5 %collective-permute-start.1 = (bf16[2,128,256]{2,1,0:T(8,128)(2,1)S(1)}, bf16[2,128,256]{2,1,0:T(8,128)(2,1)S(1)}, u32[]{:S(2)}, u32[]{:S(2)}) collective-permute-start(bf16[2,128,256]{2,1,0:T(8,128)(2,1)S(1)} %get-tuple-element.43), channel_id=1, source_target_pairs={{0,8},{8,16},{16,24},{24,32},{32,40},{40,48},{48,56},{56,64},{64,7... | collective-permute-start | bytes 393224 | tf_op jit(solution)/shard_map/ppermute | solution.py:28
  31.6 17.5 %collective-permute-start.6 = (bf16[2,128,256]{2,1,0:T(8,128)(2,1)S(1)}, bf16[2,128,256]{2,1,0:T(8,128)(2,1)S(1)}, u32[]{:S(2)}, u32[]{:S(2)}) collective-permute-start(bf16[2,128,256]{2,1,0:T(8,128)(2,1)S(1)} %get-tuple-element.45), channel_id=1, source_target_pairs={{0,64},{8,72},{16,80},{24,88},{32,96},{40,104},{48,112},{56,120},{... | collective-permute-start | bytes 393224 | tf_op jit(solution)/shard_map/ppermute | solution.py:28
  40.8 8.2 %collective-permute-start.5 = (bf16[2,128,256]{2,1,0:T(8,128)(2,1)S(1)}, bf16[2,128,256]{2,1,0:T(8,128)(2,1)S(1)}, u32[]{:S(2)}, u32[]{:S(2)}) collective-permute-start(bf16[2,128,256]{2,1,0:T(8,128)(2,1)S(1)} %get-tuple-element.45), channel_id=1, source_target_pairs={{0,32},{8,40},{16,48},{24,56},{32,64},{40,72},{48,80},{56,88},{64,... | collective-permute-start | bytes 393224 | tf_op jit(solution)/shard_map/ppermute | solution.py:28
  44.1 4.9 %collective-permute-start.7 = (bf16[2,128,128]{2,1,0:T(8,128)(2,1)S(1)}, bf16[2,128,128]{2,1,0:T(8,128)(2,1)S(1)}, u32[]{:S(2)}, u32[]{:S(2)}) collective-permute-start(bf16[2,128,128]{2,1,0:T(8,128)(2,1)S(1)} %get-tuple-element.46), channel_id=1, source_target_pairs={{0,96},{8,104},{16,112},{24,120},{32,128},{40,136},{48,144},{56,15... | collective-permute-start | bytes 196616 | tf_op jit(solution)/shard_map/ppermute | solution.py:28
  51.7 10.1 %collective-permute-start.9 = (bf16[128,2048]{1,0:T(8,128)(2,1)S(1)}, bf16[128,2048]{1,0:T(8,128)(2,1)S(1)}, u32[]{:S(2)}, u32[]{:S(2)}) collective-permute-start(bf16[128,2048]{1,0:T(8,128)(2,1)S(1)} %get-tuple-element.55), channel_id=1, source_target_pairs={{0,1},{1,0},{2,3},{3,2},{4,5},{5,4},{6,7},{7,6},{8,9},{9,8},{10,11... | collective-permute-start | bytes 1572872 | tf_op jit(solution)/shard_map/ppermute | solution.py:33
  54.3 16.3 %collective-permute-start.8 = (bf16[1120,128]{1,0:T(8,128)(2,1)S(1)}, bf16[1120,128]{1,0:T(8,128)(2,1)S(1)}, u32[]{:S(2)}, u32[]{:S(2)}) collective-permute-start(bf16[1120,128]{1,0:T(8,128)(2,1)S(1)} %get-tuple-element.53.pay_ref), channel_id=1, source_target_pairs={{0,128},{8,136},{16,144},{24,152},{32,160},{40,168},{48,176},{56,1... | collective-permute-start | bytes 860168 | tf_op jit(solution)/shard_map/ppermute | solution.py:37
  61.9 8.8 %collective-permute-start.10 = (bf16[32,2048]{1,0:T(8,128)(2,1)S(1)}, bf16[32,2048]{1,0:T(8,128)(2,1)S(1)}, u32[]{:S(2)}, u32[]{:S(2)}) collective-permute-start(bf16[32,2048]{1,0:T(8,128)(2,1)S(1)} %get-tuple-element.57), channel_id=1, source_target_pairs={{0,2},{2,4},{4,6},{6,0},{1,3},{3,5},{5,7},{7,1},{8,10},{10,12},{12... | collective-permute-start | bytes 393224 | tf_op jit(solution)/shard_map/ppermute | solution.py:33
  63.3 8.7 %collective-permute-start.11 = (bf16[32,2048]{1,0:T(8,128)(2,1)S(1)}, bf16[32,2048]{1,0:T(8,128)(2,1)S(1)}, u32[]{:S(2)}, u32[]{:S(2)}) collective-permute-start(bf16[32,2048]{1,0:T(8,128)(2,1)S(1)} %get-tuple-element.58), channel_id=1, source_target_pairs={{0,4},{2,6},{4,0},{6,2},{1,5},{3,7},{5,1},{7,3},{8,12},{10,14},{12... | collective-permute-start | bytes 393224 | tf_op jit(solution)/shard_map/ppermute | solution.py:33
  65.9 6.1 %collective-permute-start.12 = (bf16[32,2048]{1,0:T(8,128)(2,1)S(1)}, bf16[32,2048]{1,0:T(8,128)(2,1)S(1)}, u32[]{:S(2)}, u32[]{:S(2)}) collective-permute-start(bf16[32,2048]{1,0:T(8,128)(2,1)S(1)} %get-tuple-element.59), channel_id=1, source_target_pairs={{0,6},{2,0},{4,2},{6,4},{1,7},{3,1},{5,3},{7,5},{8,14},{10,8},{12,... | collective-permute-start | bytes 393224 | tf_op jit(solution)/shard_map/ppermute | solution.py:33
  72.7 18.2 %collective-permute-start.17 = (bf16[1120,128]{1,0:T(8,128)(2,1)S(1)}, bf16[1120,128]{1,0:T(8,128)(2,1)S(1)}, u32[]{:S(2)}, u32[]{:S(2)}) collective-permute-start(bf16[1120,128]{1,0:T(8,128)(2,1)S(1)} %get-tuple-element.65), channel_id=1, source_target_pairs={{0,64},{8,72},{16,80},{24,88},{32,96},{40,104},{48,112},{56,120},{... | collective-permute-start | bytes 860168 | tf_op jit(solution)/shard_map/ppermute | solution.py:37
  78.1 1.9 %collective-permute-start.13 = (bf16[32,2048]{1,0:T(8,128)(2,1)S(1)}, bf16[32,2048]{1,0:T(8,128)(2,1)S(1)}, u32[]{:S(2)}, u32[]{:S(2)}) collective-permute-start(bf16[32,2048]{1,0:T(8,128)(2,1)S(1)} %get-tuple-element.60.mine_ref), channel_id=1, source_target_pairs={{0,1},{1,0},{2,3},{3,2},{4,5},{5,4},{6,7},{7,6},{8,9},{9,8},{10,11... | collective-permute-start | bytes 393224 | tf_op jit(solution)/shard_map/ppermute | solution.py:33
  80.6 10.4 %collective-permute-start.14 = (bf16[64,512]{1,0:T(8,128)(2,1)S(1)}, bf16[64,512]{1,0:T(8,128)(2,1)S(1)}, u32[]{:S(2)}, u32[]{:S(2)}) collective-permute-start(bf16[64,512]{1,0:T(8,128)(2,1)S(1)} %get-tuple-element.62), channel_id=1, source_target_pairs={{0,2},{2,4},{4,6},{6,0},{1,3},{3,5},{5,7},{7,1},{8,10},{10,12},{12... | collective-permute-start | bytes 196616 | tf_op jit(solution)/shard_map/ppermute | solution.py:33
  82.0 9.0 %collective-permute-start.15 = (bf16[64,512]{1,0:T(8,128)(2,1)S(1)}, bf16[64,512]{1,0:T(8,128)(2,1)S(1)}, u32[]{:S(2)}, u32[]{:S(2)}) collective-permute-start(bf16[64,512]{1,0:T(8,128)(2,1)S(1)} %get-tuple-element.63), channel_id=1, source_target_pairs={{0,4},{2,6},{4,0},{6,2},{1,5},{3,7},{5,1},{7,3},{8,12},{10,14},{12... | collective-permute-start | bytes 196616 | tf_op jit(solution)/shard_map/ppermute | solution.py:33
  84.6 6.4 %collective-permute-start.16 = (bf16[64,512]{1,0:T(8,128)(2,1)S(1)}, bf16[64,512]{1,0:T(8,128)(2,1)S(1)}, u32[]{:S(2)}, u32[]{:S(2)}) collective-permute-start(bf16[64,512]{1,0:T(8,128)(2,1)S(1)} %get-tuple-element.64), channel_id=1, source_target_pairs={{0,6},{2,0},{4,2},{6,4},{1,7},{3,1},{5,3},{7,5},{8,14},{10,8},{12,... | collective-permute-start | bytes 196616 | tf_op jit(solution)/shard_map/ppermute | solution.py:33
  91.0 7.3 %collective-permute-start.21 = (bf16[1120,128]{1,0:T(8,128)(2,1)S(1)}, bf16[1120,128]{1,0:T(8,128)(2,1)S(1)}, u32[]{:S(2)}, u32[]{:S(2)}) collective-permute-start(bf16[1120,128]{1,0:T(8,128)(2,1)S(1)} %add.21), channel_id=1, source_target_pairs={{0,32},{8,40},{16,48},{24,56},{32,0},{40,8},{48,16},{56,24},{64,96... | collective-permute-start | bytes 860168 | tf_op jit(solution)/shard_map/ppermute | solution.py:37
  93.2 13.2 %collective-permute-start.20 = (bf16[64,3072]{1,0:T(8,128)(2,1)S(1)}, bf16[64,3072]{1,0:T(8,128)(2,1)S(1)}, u32[]{:S(2)}, u32[]{:S(2)}) collective-permute-start(bf16[64,3072]{1,0:T(8,128)(2,1)S(1)} %convolution_convert_fusion), channel_id=1, source_target_pairs={{0,6},{2,0},{4,2},{6,4},{1,7},{3,1},{5,3},{7,5},{8,14},{10,8},{12,... | collective-permute-start | bytes 1179656 | tf_op jit(solution)/shard_map/ppermute | solution.py:33
  96.0 10.7 %collective-permute-start.19 = (bf16[64,3072]{1,0:T(8,128)(2,1)S(1)}, bf16[64,3072]{1,0:T(8,128)(2,1)S(1)}, u32[]{:S(2)}, u32[]{:S(2)}) collective-permute-start(bf16[64,3072]{1,0:T(8,128)(2,1)S(1)} %convolution_convert_fusion.1), channel_id=1, source_target_pairs={{0,4},{2,6},{4,0},{6,2},{1,5},{3,7},{5,1},{7,3},{8,12},{10,14},{12... | collective-permute-start | bytes 1179656 | tf_op jit(solution)/shard_map/ppermute | solution.py:33
  96.4 20.6 %collective-permute-start.18 = (bf16[64,3072]{1,0:T(8,128)(2,1)S(1)}, bf16[64,3072]{1,0:T(8,128)(2,1)S(1)}, u32[]{:S(2)}, u32[]{:S(2)}) collective-permute-start(bf16[64,3072]{1,0:T(8,128)(2,1)S(1)} %convolution_convert_fusion.2), channel_id=1, source_target_pairs={{0,2},{2,4},{4,6},{6,0},{1,3},{3,5},{5,7},{7,1},{8,10},{10,12},{12... | collective-permute-start | bytes 1179656 | tf_op jit(solution)/shard_map/ppermute | solution.py:33
  98.4 7.8 %collective-permute-start.22 = (bf16[1120,128]{1,0:T(8,128)(2,1)S(1)}, bf16[1120,128]{1,0:T(8,128)(2,1)S(1)}, u32[]{:S(2)}, u32[]{:S(2)}) collective-permute-start(bf16[1120,128]{1,0:T(8,128)(2,1)S(1)} %add.25), channel_id=1, source_target_pairs={{0,16},{8,24},{16,0},{24,8},{32,48},{40,56},{48,32},{56,40},{64,80... | collective-permute-start | bytes 860168 | tf_op jit(solution)/shard_map/ppermute | solution.py:37
  106.3 12.2 %collective-permute-start.23 = (bf16[1120,128]{1,0:T(8,128)(2,1)S(1)}, bf16[1120,128]{1,0:T(8,128)(2,1)S(1)}, u32[]{:S(2)}, u32[]{:S(2)}) collective-permute-start(bf16[1120,128]{1,0:T(8,128)(2,1)S(1)} %add.26), channel_id=1, source_target_pairs={{0,8},{8,0},{16,24},{24,16},{32,40},{40,32},{48,56},{56,48},{64,72... | collective-permute-start | bytes 860168 | tf_op jit(solution)/shard_map/ppermute | solution.py:37

commit v3 on v2

--- a/solution.py
+++ b/solution.py
@@ -11,6 +11,7 @@
 CONV = 4
 REQS = 4
 HALO = 16
+ROW = 4
 EDGE_ROWS = 16
 INTERPRET = False
 F32 = jnp.float32
@@ -25,12 +26,18 @@
 
 def shift(value, axis, steps):
     count = lax.axis_size(axis)
-    return lax.ppermute(value, axis, [(s, s + steps) for s in range(count - steps)])
+    return lax.ppermute(value, axis, [(s, s + steps) for s in range(max(0, count - steps))])
 
 
 def rotate(value, axis, steps):
     count = lax.axis_size(axis)
     return lax.ppermute(value, axis, [(s, (s + steps) % count) for s in range(count)])
+
+
+def row_rotate(value, steps):
+    count = lax.axis_size("seq")
+    pairs = [(s, s // ROW * ROW + (s + steps) % ROW) for s in range(count)]
+    return lax.ppermute(value, "seq", pairs)
 
 
 def exchange(value, axis, bit):
@@ -124,7 +131,7 @@
         for i in range(CONV - 1):
             spot = ends[r] - (CONV - 1) + i
             good = owned & (spot >= begin)
-            wanted = jnp.where(edge_id == r * (CONV - 1) + i, jnp.where(good, spot, -1), wanted)
+            wanted = jnp.where(edge_id == i * REQS + r, jnp.where(good, spot, -1), wanted)
     return jnp.where((ext_pos == wanted) & (ext_pos >= 0), 1.0, 0.0).astype(BF16)
 
 
@@ -255,20 +262,37 @@
         map_ref[h, :, DK:] = fold[:, DK:].astype(BF16)
 
 
-def window_kernel(m1_ref, m2_ref, m3_ref, m4_ref, wide_ref, send_ref, tail_ref):
-    for h in range(m1_ref.shape[0]):
-        pairs = []
-        for newer, older in ((m1_ref, m2_ref), (m3_ref, m4_ref)):
-            a, b = newer[h], older[h]
-            pairs.append(a.astype(F32) + b.astype(F32) - dot(a[:, :DK], b))
-        joined = pairs[0] + pairs[1] - dot32(pairs[0][:, :DK], pairs[1])
-        wide_ref[h] = joined
-        send_ref[h] = joined.astype(BF16)
-        tail_ref[h] = joined[:, DK:].astype(BF16)
+def joined(newer, older):
+    return newer + older - dot32(newer[:, :DK], older)
+
+
+def row_kernel(meta, own_ref, *refs):
+    *came, prefix_ref, send_ref, maps_ref = refs
+    here = meta[7]
+    maps_ref[here] = own_ref[...]
+    for k, ref in enumerate(came):
+        maps_ref[lax.rem(here + ROW - 1 - k, ROW)] = ref[...]
+    for h in range(own_ref.shape[0]):
+        maps = [maps_ref[i, h] for i in range(ROW)]
+        wide = [m.astype(F32) for m in maps]
+        first = wide[1] + wide[0] - dot(maps[1][:, :DK], maps[0])
+        second = wide[3] + wide[2] - dot(maps[3][:, :DK], maps[2])
+        send_ref[h] = joined(second, first).astype(BF16)
+        third = joined(wide[2], first)
+        prefix = jnp.where(here == 1, wide[0], jnp.where(here == 2, first, third))
+        prefix_ref[h] = jnp.where(here == 0, 0.0, prefix)
+
+
+def join_kernel(near_ref, far_ref, wide_ref, tail_ref):
+    for h in range(near_ref.shape[0]):
+        near, far = near_ref[h], far_ref[h]
+        both = near.astype(F32) + far.astype(F32) - dot(near[:, :DK], far)
+        wide_ref[h] = both
+        tail_ref[h] = both[:, DK:].astype(BF16)
 
 
 def attend_kernel(
-    meta, e0_ref, e4_ref, e8_ref, e12_ref, uw_ref, local_ref, link_ref, kb_ref, ks_ref,
+    meta, prefix_ref, wide_ref, tail_ref, uw_ref, local_ref, link_ref, kb_ref, ks_ref,
     edge_ref, gain_ref, w_ref, own_ref, other_ref, pay_ref, heads_ref,
 ):
     heads, rows, _ = local_ref.shape
@@ -279,12 +303,9 @@
     seg = seg_of(first + iota((rows, 1), 0), ends)
     gain = gain_ref[...]
     for h in range(heads):
-        e0, e4, e8 = e0_ref[h], e4_ref[h], e8_ref[h]
-        near = e0 + e4.astype(F32) - dot32(e0[:, :DK], e4.astype(F32))
-        far = (
-            e8[:, DK:].astype(F32) + e12_ref[h].astype(F32) - dot(e8[:, :DK], e12_ref[h])
-        )
-        enter = near[:, DK:] + far - dot32(near[:, :DK], far)
+        wide, prefix, tail = wide_ref[h], prefix_ref[h], tail_ref[h].astype(F32)
+        ahead = wide[:, DK:] + tail - dot32(wide[:, :DK], tail)
+        enter = prefix[:, DK:] + ahead - dot32(prefix[:, :DK], ahead)
         parts = split(enter)
         attended = local_ref[h] + dot_split(split(link_ref[h]), parts)
         scale = lax.rsqrt(jnp.mean(attended * attended, axis=1, keepdims=True) + 1e-05)
@@ -349,6 +370,18 @@
         ref[...] = cols_ref[lax.rem(meta[5] + k, wins)]
 
 
+def finish_kernel(pay_ref, came_ref, state_ref, edge_ref):
+    rows = state_ref.shape[0]
+    state_ref[...] = (pay_ref[:rows] + came_ref[:rows]).astype(F32)
+    heads = edge_ref.shape[3] // DK
+    for b in range(3 * heads):
+        part = slice(rows + b * EDGE_ROWS, rows + (b + 1) * EDGE_ROWS)
+        edges = pay_ref[part].astype(F32) + came_ref[part].astype(F32)
+        lanes = slice(b % heads * DK, (b % heads + 1) * DK)
+        for i in range(CONV - 1):
+            edge_ref[i, b // heads, :, lanes] = edges[i * REQS : (i + 1) * REQS].astype(BF16)
+
+
 def body(qkv_in, conv_w, beta_logits, lengths, out_gain, w_out, hidden_in, norm_gain, w_qkv):
     rows = qkv_in.shape[0]
     width = qkv_in.shape[2]
@@ -357,7 +390,7 @@
     n_seq, wins, cores = (lax.axis_size(a) for a in ("seq", "win", "wout"))
     piece = rows // (wins * cores)
     seq, win, core = (lax.axis_index(a).astype(jnp.int32) for a in ("seq", "win", "wout"))
-    meta = jnp.concatenate([lengths, jnp.stack([seq * rows, win, core, core])])
+    meta = jnp.concatenate([lengths, jnp.stack([seq * rows, win, core, seq % ROW])])
     x = qkv_in.transpose(1, 0, 2)
     halo = shift(x[:, rows - HALO :], "seq", 1)
     act, lead, parts, taps, beta = call(
@@ -391,23 +424,24 @@
         meta, act, lead, parts, taps, beta, halo,
     )
 
-    def sent(value, steps):
-        return shift(value, "seq", steps) if steps < n_seq else jnp.zeros_like(value)
-
-    near = [sent(maps, k) for k in range(1, 5)]
-    wide, send, tail = call(
-        window_kernel,
-        [
-            out((heads, DK, 2 * DK), F32),
-            out((heads, DK, 2 * DK), BF16),
-            out((heads, DK, DK), BF16),
-        ],
-        "window",
+    came = [row_rotate(maps, k) for k in range(1, ROW)]
+    prefix, total = call(
+        row_kernel,
+        [out((heads, DK, 2 * DK), F32), out((heads, DK, 2 * DK), BF16)],
+        "row",
         10**8,
-        *near,
+        meta, maps, *came,
+        scratch=[pltpu.VMEM((ROW, heads, DK, 2 * DK), BF16)],
+    )
+    wide, tail = call(
+        join_kernel,
+        [out((heads, DK, 2 * DK), F32), out((heads, DK, DK), BF16)],
+        "join",
+        10**8,
+        shift(total, "seq", ROW), shift(total, "seq", 2 * ROW),
         smem=0,
     )
-    far = [sent(send, 4), sent(send, 8), sent(tail, 12)]
+    tail = shift(tail, "seq", 2 * ROW)
     state_rows = REQS * heads * DK
     pay_rows = state_rows + 3 * heads * EDGE_ROWS
     own, other, payload = call(
@@ -419,7 +453,7 @@
         ],
         "attend",
         10**9,
-        meta, wide, *far, uw, local, link, kb, ks, edges, out_gain.reshape(1, DK), w_out,
+        meta, prefix, wide, tail, uw, local, link, kb, ks, edges, out_gain.reshape(1, DK), w_out,
         scratch=[pltpu.VMEM((wins, cores, piece, width), BF16)],
     )
     got = rotate(other, "wout", 1)
@@ -464,11 +498,18 @@
         total = total + part.astype(F32)
     projected = total.astype(BF16)
 
-    for bit in bits[2:]:
+    for bit in bits[2:-1]:
         payload = payload + exchange(payload, "seq", bit)
-    final_states = payload[:state_rows].astype(F32).reshape(REQS, heads, DK, DK)
-    edges = payload[state_rows:].reshape(3 * heads, EDGE_ROWS, DK)[:, : REQS * (CONV - 1)]
-    conv_edges = edges.transpose(1, 0, 2).reshape(REQS, CONV - 1, 3, width)
+    final_states, conv_edges = call(
+        finish_kernel,
+        [out((state_rows, DK), F32), out((CONV - 1, 3, REQS, width), BF16)],
+        "finish",
+        10**6,
+        payload, exchange(payload, "seq", bits[-1]),
+        smem=0,
+    )
+    final_states = final_states.reshape(REQS, heads, DK, DK)
+    conv_edges = conv_edges.transpose(2, 0, 1, 3)
     return (projected, stream_out, final_states, conv_edges)
 
 

time: 120 us -> 117 us (0.975)
  starting transfers between devices: 64.3 us -> 49.9 us
  waiting for transfers between devices: 36 us -> 47 us
  Pallas kernels: 11.8 us -> 13.5 us
    ppermute x8 -> x7, starting transfers between devices: 33.6 us -> 24.1 us  [the longest x4 20.5 us: shift(): lax.ppermute(value, axis, [(s, s + steps) for s in range(max(0, count - s...]
    ppermute x5, waiting for transfers between devices: 18 us -> 25.3 us  [exchange(): lax.ppermute(value, axis, [(s, s ^ bit) for s in range(lax.axis_size(axis...]
    ppermute x8 -> x7, waiting for transfers between devices: 5.23 us -> 11.7 us  [the longest x3 8.45 us: row_rotate(): return lax.ppermute(value, 'seq', pairs)]
    ppermute x5, starting transfers between devices: 13.1 us -> 9.07 us  [exchange(): lax.ppermute(value, axis, [(s, s ^ bit) for s in range(lax.axis_size(axis...]
    ppermute x11, waiting for transfers between devices: 12.8 us -> 10 us  [rotate(): lax.ppermute(value, axis, [(s, (s + steps) % count) for s in range(count)])]
    pallas_call x7 -> x9, Pallas kernels: 11.8 us -> 13.5 us  [call(): pl.pallas_call(kernel, out_shape=outs, in_specs=[SMEM] * smem + [HBM] * h...]
  transfers between devices with their start and end apart: 24 -> 23, of which waited for: 10 -> 12; matrix products, arithmetic and copies ran while one was open for 4% -> 4% of each run, Pallas kernels for 3% -> 3%
where the time goes in v3:
time: 117 us
  starting transfers between devices  49.9 us (43%)
  waiting for transfers between devices  47 us (40%)
  Pallas kernels  13.5 us (12%)
  matrix products  3.5 us (3%)
  local copies, waits for them, and re-layouts  1.67 us (1%)
    ppermute x5, waiting for transfers between devices, exchange(): lax.ppermute(value, axis, [(s, s ^ bit) for s in range(lax.axis_size(axis...  25.3 us
    ppermute x4, starting transfers between devices, shift(): lax.ppermute(value, axis, [(s, s + steps) for s in range(max(0, count - s...  20.5 us
    ppermute x11, starting transfers between devices, rotate(): lax.ppermute(value, axis, [(s, (s + steps) % count) for s in range(count)])  16.7 us
    pallas_call x9, Pallas kernels, call(): pl.pallas_call(kernel, out_shape=outs, in_specs=[SMEM] * smem + [HBM] * h...  13.5 us
    ppermute x11, waiting for transfers between devices, rotate(): lax.ppermute(value, axis, [(s, (s + steps) % count) for s in range(count)])  10 us
    ppermute x5, starting transfers between devices, exchange(): lax.ppermute(value, axis, [(s, s ^ bit) for s in range(lax.axis_size(axis...  9.07 us
    ppermute x3, waiting for transfers between devices, row_rotate(): return lax.ppermute(value, 'seq', pairs)  8.45 us
    ppermute x3, starting transfers between devices, row_rotate(): return lax.ppermute(value, 'seq', pairs)  3.58 us
  transfers between devices with their start and end apart: 23, of which 12 were waited for; matrix products, arithmetic and copies ran while one was open for 4% of the time, Pallas kernels for 3%

profile of v3, /device:TPU:1, one launch (start us, length us, event | category | flops | bytes accessed | tf_op | source)
XLA Modules:
  0.0 116.7 jit_solution(9663031246474628775)
XLA Ops:
  0.6 0.9 slice.4
  1.5 4.1 %collective-permute-start = (bf16[3,16,256]{2,1,0:T(8,128)(2,1)S(1)}, bf16[3,16,256]{2,1,0:T(8,128)(2,1)S(1)}, u32[]{:S(2)}, u32[]{:S(2)}) collective-permute-start(bf16[3,16,256]{2,1,0:T(8,128)(2,1)S(1)} %slice.4), channel_id=1, source_target_pairs={{0,8},{8,16},{16,24},{24,32},{32,40},{40,48},{48,56},{56,64},{64,7... | collective-permute-start | bytes 73736 | tf_op jit(solution)/shard_map/ppermute | solution.py:29
  5.6 0.7 concatenate.3.meta
  6.4 2.4 %conv.1 = (bf16[3,256,256]{2,1,0:T(8,128)(2,1)S(1)}, bf16[3,16,256]{2,1,0:T(8,128)(2,1)S(1)}, bf16[3,16,256]{2,1,0:T(8,128)(2,1)S(1)}, f32[3,4,256]{2,1,0:T(4,128)S(1)}, f32[2,256]{1,0:T(2,128)S(1)}) custom-call(s32[8]{0:T(128)S(1)} %concatenate.3.meta, bf16[3,256,256]{2,1,0:T(8,128)(2,1)} %bitcast.20, f32[3,4,256]{2,1,0:T(4,128)} %taps_hbm.1, f32[2,256]{1,0:T(2,128)} %beta_hbm.1), custom_call_target="tpu_custom_call" | custom-call | flops 100000000 | bytes 864288 | tf_op jit(solution)/shard_map/conv/pallas_call | solution.py:70
  8.9 4.9 %prep.1 = (bf16[2,128,256]{2,1,0:T(8,128)(2,1)S(1)}, f32[2,256,256]{2,1,0:T(8,128)S(1)}, f32[2,256,128]{2,1,0:T(8,128)S(1)}, f32[2,256,128]{2,1,0:T(8,128)S(1)},...) custom-call(s32[8]{0:T(128)S(1)} %concatenate.3.meta, ...), custom_call_target="tpu_custom_call" | custom-call | flops 2000000000 | bytes 1818656 | tf_op jit(solution)/shard_map/prep/pallas_call | solution.py:70
  13.7 2.9 %collective-permute-start.3 = (bf16[2,128,256]{2,1,0:T(8,128)(2,1)S(1)}, bf16[2,128,256]{2,1,0:T(8,128)(2,1)S(1)}, u32[]{:S(2)}, u32[]{:S(2)}) collective-permute-start(bf16[2,128,256]{2,1,0:T(8,128)(2,1)S(1)} %get-tuple-element.46.own_ref), channel_id=1, source_target_pairs={{0,24},{8,0},{16,8},{24,16},{32,56},{40,32},{48,40},{56,48},{64,88... | collective-permute-start | bytes 393224 | tf_op jit(solution)/shard_map/ppermute | solution.py:40
  16.6 0.2 collective-permute-start.2
  16.8 0.5 collective-permute-start.1
  17.3 4.4 %collective-permute-done.3.refs_2_ = bf16[2,128,256]{2,1,0:T(8,128)(2,1)S(1)} collective-permute-done((bf16[2,128,256]{2,1,0:T(8,128)(2,1)S(1)}, bf16[2,128,256]{2,1,0:T(8,128)(2,1)S(1)}, u32[]{:S(2)}, u32[]{:S(2)}) %collective-permute-start.3) | collective-permute-done | bytes 131104 | tf_op jit(solution)/shard_map/ppermute | solution.py:40
  21.7 0.4 collective-permute-done.2.refs_1_
  22.1 3.7 %collective-permute-done.1.refs_0_ = bf16[2,128,256]{2,1,0:T(8,128)(2,1)S(1)} collective-permute-done((bf16[2,128,256]{2,1,0:T(8,128)(2,1)S(1)}, bf16[2,128,256]{2,1,0:T(8,128)(2,1)S(1)}, u32[]{:S(2)}, u32[]{:S(2)}) %collective-permute-start.1) | collective-permute-done | bytes 131104 | tf_op jit(solution)/shard_map/ppermute | solution.py:40
  25.8 1.3 %row.1 = (f32[2,128,256]{2,1,0:T(8,128)S(1)}, bf16[2,128,256]{2,1,0:T(8,128)(2,1)S(1)}) custom-call(s32[8]{0:T(128)S(1)} %concatenate.3.meta, bf16[2,128,256]{2,1,0:T(8,128)(2,1)S(1)} %get-tuple-element.46.own_ref, bf16[2,128,256]{2,1,0:T(8,128)(2,1)S(1)} %collective-permute-done.1.refs_0_, bf16[2,128,256]{2,1,0:T(8,128)(2,1)S(1)} %collective-permute-done.2.refs_1_, ...), custom_call_target="tpu_custom_call" | custom-call | flops 100000000 | bytes 917536 | tf_op jit(solution)/shard_map/row/pallas_call | solution.py:70
  27.0 4.9 %collective-permute-start.5 = (bf16[2,128,256]{2,1,0:T(8,128)(2,1)S(1)}, bf16[2,128,256]{2,1,0:T(8,128)(2,1)S(1)}, u32[]{:S(2)}, u32[]{:S(2)}) collective-permute-start(bf16[2,128,256]{2,1,0:T(8,128)(2,1)S(1)} %get-tuple-element.48), channel_id=1, source_target_pairs={{0,64},{8,72},{16,80},{24,88},{32,96},{40,104},{48,112},{56,120},{... | collective-permute-start | bytes 393224 | tf_op jit(solution)/shard_map/ppermute | solution.py:29
  31.9 4.7 %collective-permute-start.4 = (bf16[2,128,256]{2,1,0:T(8,128)(2,1)S(1)}, bf16[2,128,256]{2,1,0:T(8,128)(2,1)S(1)}, u32[]{:S(2)}, u32[]{:S(2)}) collective-permute-start(bf16[2,128,256]{2,1,0:T(8,128)(2,1)S(1)} %get-tuple-element.48), channel_id=1, source_target_pairs={{0,32},{8,40},{16,48},{24,56},{32,64},{40,72},{48,80},{56,88},{64,... | collective-permute-start | bytes 393224 | tf_op jit(solution)/shard_map/ppermute | solution.py:29
  36.7 1.9 %collective-permute-done.4.near_ref = bf16[2,128,256]{2,1,0:T(8,128)(2,1)S(1)} collective-permute-done((bf16[2,128,256]{2,1,0:T(8,128)(2,1)S(1)}, bf16[2,128,256]{2,1,0:T(8,128)(2,1)S(1)}, u32[]{:S(2)}, u32[]{:S(2)}) %collective-permute-start.4) | collective-permute-done | bytes 131104 | tf_op jit(solution)/shard_map/ppermute | solution.py:29
  38.6 0.2 join.1
  38.8 6.8 %collective-permute-start.6 = (bf16[2,128,128]{2,1,0:T(8,128)(2,1)S(1)}, bf16[2,128,128]{2,1,0:T(8,128)(2,1)S(1)}, u32[]{:S(2)}, u32[]{:S(2)}) collective-permute-start(bf16[2,128,128]{2,1,0:T(8,128)(2,1)S(1)} %get-tuple-element.50), channel_id=1, source_target_pairs={{0,64},{8,72},{16,80},{24,88},{32,96},{40,104},{48,112},{56,120},{... | collective-permute-start | bytes 196616 | tf_op jit(solution)/shard_map/ppermute | solution.py:29
  45.6 1.3 %collective-permute-done.6.tail_ref = bf16[2,128,128]{2,1,0:T(8,128)(2,1)S(1)} collective-permute-done((bf16[2,128,128]{2,1,0:T(8,128)(2,1)S(1)}, bf16[2,128,128]{2,1,0:T(8,128)(2,1)S(1)}, u32[]{:S(2)}, u32[]{:S(2)}) %collective-permute-start.6) | collective-permute-done | bytes 65568 | tf_op jit(solution)/shard_map/ppermute | solution.py:29
  46.9 2.5 %attend.1 = (f32[128,2048]{1,0:T(8,128)S(1)}, bf16[128,2048]{1,0:T(8,128)(2,1)S(1)}, bf16[1120,128]{1,0:T(8,128)(2,1)S(1)}) custom-call(s32[8]{0:T(128)S(1)} %concatenate.3.meta, f32[2,128,256]{2,1,0:T(8,128)S(1)} %get-tuple-element.47.prefix_ref, f32[2,128,256]{2,1,0:T(8,128)S(1)} %get-tuple-element.49.wide_ref, ...), custom_call_target="tpu_custom_call" | custom-call | flops 1000000000 | bytes 4704800 | tf_op jit(solution)/shard_map/attend/pallas_call | solution.py:70
  49.4 2.0 %collective-permute-start.8 = (bf16[128,2048]{1,0:T(8,128)(2,1)S(1)}, bf16[128,2048]{1,0:T(8,128)(2,1)S(1)}, u32[]{:S(2)}, u32[]{:S(2)}) collective-permute-start(bf16[128,2048]{1,0:T(8,128)(2,1)S(1)} %get-tuple-element.59), channel_id=1, source_target_pairs={{0,1},{1,0},{2,3},{3,2},{4,5},{5,4},{6,7},{7,6},{8,9},{9,8},{10,11... | collective-permute-start | bytes 1572872 | tf_op jit(solution)/shard_map/ppermute | solution.py:34
  51.5 7.7 %collective-permute-start.7 = (bf16[1120,128]{1,0:T(8,128)(2,1)S(1)}, bf16[1120,128]{1,0:T(8,128)(2,1)S(1)}, u32[]{:S(2)}, u32[]{:S(2)}) collective-permute-start(bf16[1120,128]{1,0:T(8,128)(2,1)S(1)} %get-tuple-element.57.pay_ref), channel_id=1, source_target_pairs={{0,128},{8,136},{16,144},{24,152},{32,160},{40,168},{48,176},{56,1... | collective-permute-start | bytes 860168 | tf_op jit(solution)/shard_map/ppermute | solution.py:44
  59.3 1.4 %collective-permute-start.9 = (bf16[32,2048]{1,0:T(8,128)(2,1)S(1)}, bf16[32,2048]{1,0:T(8,128)(2,1)S(1)}, u32[]{:S(2)}, u32[]{:S(2)}) collective-permute-start(bf16[32,2048]{1,0:T(8,128)(2,1)S(1)} %get-tuple-element.61), channel_id=1, source_target_pairs={{0,2},{2,4},{4,6},{6,0},{1,3},{3,5},{5,7},{7,1},{8,10},{10,12},{12... | collective-permute-start | bytes 393224 | tf_op jit(solution)/shard_map/ppermute | solution.py:34
  60.7 2.6 %collective-permute-start.10 = (bf16[32,2048]{1,0:T(8,128)(2,1)S(1)}, bf16[32,2048]{1,0:T(8,128)(2,1)S(1)}, u32[]{:S(2)}, u32[]{:S(2)}) collective-permute-start(bf16[32,2048]{1,0:T(8,128)(2,1)S(1)} %get-tuple-element.62), channel_id=1, source_target_pairs={{0,4},{2,6},{4,0},{6,2},{1,5},{3,7},{5,1},{7,3},{8,12},{10,14},{12... | collective-permute-start | bytes 393224 | tf_op jit(solution)/shard_map/ppermute | solution.py:34
  63.3 1.1 collective-permute-start.11
  64.3 8.1 %collective-permute-done.7.came_ref = bf16[1120,128]{1,0:T(8,128)(2,1)S(1)} collective-permute-done((bf16[1120,128]{1,0:T(8,128)(2,1)S(1)}, bf16[1120,128]{1,0:T(8,128)(2,1)S(1)}, u32[]{:S(2)}, u32[]{:S(2)}) %collective-permute-start.7) | collective-permute-done | bytes 286752 | tf_op jit(solution)/shard_map/ppermute | solution.py:44
  72.5 0.8 norm.1
  73.2 0.7 collective-permute-start.12
  74.0 1.0 collective-permute-done.12.peer_ref
  75.0 0.6 columns.1
  75.6 1.4 %collective-permute-start.13 = (bf16[64,512]{1,0:T(8,128)(2,1)S(1)}, bf16[64,512]{1,0:T(8,128)(2,1)S(1)}, u32[]{:S(2)}, u32[]{:S(2)}) collective-permute-start(bf16[64,512]{1,0:T(8,128)(2,1)S(1)} %get-tuple-element.66), channel_id=1, source_target_pairs={{0,2},{2,4},{4,6},{6,0},{1,3},{3,5},{5,7},{7,1},{8,10},{10,12},{12... | collective-permute-start | bytes 196616 | tf_op jit(solution)/shard_map/ppermute | solution.py:34
  76.9 2.6 %collective-permute-start.14 = (bf16[64,512]{1,0:T(8,128)(2,1)S(1)}, bf16[64,512]{1,0:T(8,128)(2,1)S(1)}, u32[]{:S(2)}, u32[]{:S(2)}) collective-permute-start(bf16[64,512]{1,0:T(8,128)(2,1)S(1)} %get-tuple-element.67), channel_id=1, source_target_pairs={{0,4},{2,6},{4,0},{6,2},{1,5},{3,7},{5,1},{7,3},{8,12},{10,14},{12... | collective-permute-start | bytes 196616 | tf_op jit(solution)/shard_map/ppermute | solution.py:34
  79.6 1.1 collective-permute-start.15
  80.6 7.7 %collective-permute-done.16 = bf16[1120,128]{1,0:T(8,128)(2,1)S(1)} collective-permute-done((bf16[1120,128]{1,0:T(8,128)(2,1)S(1)}, bf16[1120,128]{1,0:T(8,128)(2,1)S(1)}, u32[]{:S(2)}, u32[]{:S(2)}) %collective-permute-start.16) | collective-permute-done | bytes 286752 | tf_op jit(solution)/shard_map/ppermute | solution.py:44
  88.4 0.1 collective-permute-start.20
  88.5 0.7 convolution_convert_fusion.2
  89.2 0.7 convolution_convert_fusion.1
  89.9 0.7 convolution_convert_fusion
  90.5 2.8 %collective-permute-start.19 = (bf16[64,3072]{1,0:T(8,128)(2,1)S(1)}, bf16[64,3072]{1,0:T(8,128)(2,1)S(1)}, u32[]{:S(2)}, u32[]{:S(2)}) collective-permute-start(bf16[64,3072]{1,0:T(8,128)(2,1)S(1)} %convolution_convert_fusion), channel_id=1, source_target_pairs={{0,6},{2,0},{4,2},{6,4},{1,7},{3,1},{5,3},{7,5},{8,14},{10,8},{12,... | collective-permute-start | bytes 1179656 | tf_op jit(solution)/shard_map/ppermute | solution.py:34
  93.3 0.4 collective-permute-start.18
  93.7 0.7 collective-permute-start.17
  94.4 2.0 %collective-permute-done.20 = bf16[1120,128]{1,0:T(8,128)(2,1)S(1)} collective-permute-done((bf16[1120,128]{1,0:T(8,128)(2,1)S(1)}, bf16[1120,128]{1,0:T(8,128)(2,1)S(1)}, u32[]{:S(2)}, u32[]{:S(2)}) %collective-permute-start.20) | collective-permute-done | bytes 286752 | tf_op jit(solution)/shard_map/ppermute | solution.py:44
  96.5 1.1 collective-permute-start.21
  97.7 7.4 %collective-permute-done.21 = bf16[1120,128]{1,0:T(8,128)(2,1)S(1)} collective-permute-done((bf16[1120,128]{1,0:T(8,128)(2,1)S(1)}, bf16[1120,128]{1,0:T(8,128)(2,1)S(1)}, u32[]{:S(2)}, u32[]{:S(2)}) %collective-permute-start.21) | collective-permute-done | bytes 286752 | tf_op jit(solution)/shard_map/ppermute | solution.py:44
  105.2 0.1 collective-permute-start.22
  105.3 4.3 %collective-permute-done.19 = bf16[64,3072]{1,0:T(8,128)(2,1)S(1)} collective-permute-done((bf16[64,3072]{1,0:T(8,128)(2,1)S(1)}, bf16[64,3072]{1,0:T(8,128)(2,1)S(1)}, u32[]{:S(2)}, u32[]{:S(2)}) %collective-permute-start.19) | collective-permute-done | bytes 393248 | tf_op jit(solution)/shard_map/ppermute | solution.py:34
  109.6 4.7 %collective-permute-done.17 = bf16[64,3072]{1,0:T(8,128)(2,1)S(1)} collective-permute-done((bf16[64,3072]{1,0:T(8,128)(2,1)S(1)}, bf16[64,3072]{1,0:T(8,128)(2,1)S(1)}, u32[]{:S(2)}, u32[]{:S(2)}) %collective-permute-start.17) | collective-permute-done | bytes 393248 | tf_op jit(solution)/shard_map/ppermute | solution.py:34
  114.3 1.5 %fusion.2 = bf16[64,3072]{1,0:T(8,128)(2,1)} fusion(bf16[64,512]{1,0:T(8,128)(2,1)S(1)} %get-tuple-element.70, bf16[512,3072]{1,0:T(8,128)(2,1)S(1)} %copy-done, bf16[64,3072]{1,0:T(8,128)(2,1)S(1)} %collective-permute-done.19, bf16[64,3072]{1,0:T(8,128)(2,1)S(1)} %collective-permute-done.18, bf16[64,3072]{1,0:T(8,128)(2,1)S(1)} %collective-permute-done.17), kind=kOutput, calls=%fused_computation.3 | convolution fusion | flops 202702848 | bytes 4784128 | tf_op jit(solution)/shard_map/dot_general | solution.py:493
  115.8 0.9 finish.1
  (26 shorter events, 0.4 us)
Async XLA Ops:
  0.6 87.9 %copy-start = (bf16[512,3072]{1,0:T(8,128)(2,1)S(1)}, bf16[512,3072]{1,0:T(8,128)(2,1)}, u32[]{:S(2)}) copy-start(bf16[512,3072]{1,0:T(8,128)(2,1)} %param.17) | copy-start | bytes 9437188
  1.5 7.3 %collective-permute-start = (bf16[3,16,256]{2,1,0:T(8,128)(2,1)S(1)}, bf16[3,16,256]{2,1,0:T(8,128)(2,1)S(1)}, u32[]{:S(2)}, u32[]{:S(2)}) collective-permute-start(bf16[3,16,256]{2,1,0:T(8,128)(2,1)S(1)} %slice.4), channel_id=1, source_target_pairs={{0,8},{8,16},{16,24},{24,32},{32,40},{40,48},{48,56},{56,64},{64,7... | collective-permute-start | bytes 73736 | tf_op jit(solution)/shard_map/ppermute | solution.py:29
  8.8 38.1 %copy-start.3 = (bf16[256,2048]{1,0:T(8,128)(2,1)S(1)}, bf16[256,2048]{1,0:T(8,128)(2,1)}, u32[]{:S(2)}) copy-start(bf16[256,2048]{1,0:T(8,128)(2,1)} %w_ref.1) | copy-start | bytes 3145732
  8.8 38.1 %copy-start.4 = (f32[128]{0:T(128)S(1)}, f32[128]{0:T(128)}, u32[]{:S(2)}) copy-start(f32[128]{0:T(128)} %param.13) | copy-start | bytes 1540
  13.7 58.7 %copy-start.1 = (bf16[32,2048]{1,0:T(8,128)(2,1)S(1)}, bf16[32,2048]{1,0:T(8,128)(2,1)}, u32[]{:S(2)}) copy-start(bf16[32,2048]{1,0:T(8,128)(2,1)} %hidden_ref.1) | copy-start | bytes 393220
  13.7 58.7 %copy-start.2 = (f32[2048]{0:T(1024)S(1)}, f32[2048]{0:T(1024)}, u32[]{:S(2)}) copy-start(f32[2048]{0:T(1024)} %param.16) | copy-start | bytes 24580
  13.7 8.0 %collective-permute-start.3 = (bf16[2,128,256]{2,1,0:T(8,128)(2,1)S(1)}, bf16[2,128,256]{2,1,0:T(8,128)(2,1)S(1)}, u32[]{:S(2)}, u32[]{:S(2)}) collective-permute-start(bf16[2,128,256]{2,1,0:T(8,128)(2,1)S(1)} %get-tuple-element.46.own_ref), channel_id=1, source_target_pairs={{0,24},{8,0},{16,8},{24,16},{32,56},{40,32},{48,40},{56,48},{64,88... | collective-permute-start | bytes 393224 | tf_op jit(solution)/shard_map/ppermute | solution.py:40
  16.6 5.4 %collective-permute-start.2 = (bf16[2,128,256]{2,1,0:T(8,128)(2,1)S(1)}, bf16[2,128,256]{2,1,0:T(8,128)(2,1)S(1)}, u32[]{:S(2)}, u32[]{:S(2)}) collective-permute-start(bf16[2,128,256]{2,1,0:T(8,128)(2,1)S(1)} %get-tuple-element.46.own_ref), channel_id=1, source_target_pairs={{0,16},{8,24},{16,0},{24,8},{32,48},{40,56},{48,32},{56,40},{64,80... | collective-permute-start | bytes 393224 | tf_op jit(solution)/shard_map/ppermute | solution.py:40
  16.8 8.9 %collective-permute-start.1 = (bf16[2,128,256]{2,1,0:T(8,128)(2,1)S(1)}, bf16[2,128,256]{2,1,0:T(8,128)(2,1)S(1)}, u32[]{:S(2)}, u32[]{:S(2)}) collective-permute-start(bf16[2,128,256]{2,1,0:T(8,128)(2,1)S(1)} %get-tuple-element.46.own_ref), channel_id=1, source_target_pairs={{0,8},{8,16},{16,24},{24,0},{32,40},{40,48},{48,56},{56,32},{64,72... | collective-permute-start | bytes 393224 | tf_op jit(solution)/shard_map/ppermute | solution.py:40
  27.0 9.6 %collective-permute-start.5 = (bf16[2,128,256]{2,1,0:T(8,128)(2,1)S(1)}, bf16[2,128,256]{2,1,0:T(8,128)(2,1)S(1)}, u32[]{:S(2)}, u32[]{:S(2)}) collective-permute-start(bf16[2,128,256]{2,1,0:T(8,128)(2,1)S(1)} %get-tuple-element.48), channel_id=1, source_target_pairs={{0,64},{8,72},{16,80},{24,88},{32,96},{40,104},{48,112},{56,120},{... | collective-permute-start | bytes 393224 | tf_op jit(solution)/shard_map/ppermute | solution.py:29
  31.9 6.7 %collective-permute-start.4 = (bf16[2,128,256]{2,1,0:T(8,128)(2,1)S(1)}, bf16[2,128,256]{2,1,0:T(8,128)(2,1)S(1)}, u32[]{:S(2)}, u32[]{:S(2)}) collective-permute-start(bf16[2,128,256]{2,1,0:T(8,128)(2,1)S(1)} %get-tuple-element.48), channel_id=1, source_target_pairs={{0,32},{8,40},{16,48},{24,56},{32,64},{40,72},{48,80},{56,88},{64,... | collective-permute-start | bytes 393224 | tf_op jit(solution)/shard_map/ppermute | solution.py:29
  38.8 8.1 %collective-permute-start.6 = (bf16[2,128,128]{2,1,0:T(8,128)(2,1)S(1)}, bf16[2,128,128]{2,1,0:T(8,128)(2,1)S(1)}, u32[]{:S(2)}, u32[]{:S(2)}) collective-permute-start(bf16[2,128,128]{2,1,0:T(8,128)(2,1)S(1)} %get-tuple-element.50), channel_id=1, source_target_pairs={{0,64},{8,72},{16,80},{24,88},{32,96},{40,104},{48,112},{56,120},{... | collective-permute-start | bytes 196616 | tf_op jit(solution)/shard_map/ppermute | solution.py:29
  49.4 9.8 %collective-permute-start.8 = (bf16[128,2048]{1,0:T(8,128)(2,1)S(1)}, bf16[128,2048]{1,0:T(8,128)(2,1)S(1)}, u32[]{:S(2)}, u32[]{:S(2)}) collective-permute-start(bf16[128,2048]{1,0:T(8,128)(2,1)S(1)} %get-tuple-element.59), channel_id=1, source_target_pairs={{0,1},{1,0},{2,3},{3,2},{4,5},{5,4},{6,7},{7,6},{8,9},{9,8},{10,11... | collective-permute-start | bytes 1572872 | tf_op jit(solution)/shard_map/ppermute | solution.py:34
  51.5 21.0 %collective-permute-start.7 = (bf16[1120,128]{1,0:T(8,128)(2,1)S(1)}, bf16[1120,128]{1,0:T(8,128)(2,1)S(1)}, u32[]{:S(2)}, u32[]{:S(2)}) collective-permute-start(bf16[1120,128]{1,0:T(8,128)(2,1)S(1)} %get-tuple-element.57.pay_ref), channel_id=1, source_target_pairs={{0,128},{8,136},{16,144},{24,152},{32,160},{40,168},{48,176},{56,1... | collective-permute-start | bytes 860168 | tf_op jit(solution)/shard_map/ppermute | solution.py:44
  59.3 13.2 %collective-permute-start.9 = (bf16[32,2048]{1,0:T(8,128)(2,1)S(1)}, bf16[32,2048]{1,0:T(8,128)(2,1)S(1)}, u32[]{:S(2)}, u32[]{:S(2)}) collective-permute-start(bf16[32,2048]{1,0:T(8,128)(2,1)S(1)} %get-tuple-element.61), channel_id=1, source_target_pairs={{0,2},{2,4},{4,6},{6,0},{1,3},{3,5},{5,7},{7,1},{8,10},{10,12},{12... | collective-permute-start | bytes 393224 | tf_op jit(solution)/shard_map/ppermute | solution.py:34
  60.7 11.8 %collective-permute-start.10 = (bf16[32,2048]{1,0:T(8,128)(2,1)S(1)}, bf16[32,2048]{1,0:T(8,128)(2,1)S(1)}, u32[]{:S(2)}, u32[]{:S(2)}) collective-permute-start(bf16[32,2048]{1,0:T(8,128)(2,1)S(1)} %get-tuple-element.62), channel_id=1, source_target_pairs={{0,4},{2,6},{4,0},{6,2},{1,5},{3,7},{5,1},{7,3},{8,12},{10,14},{12... | collective-permute-start | bytes 393224 | tf_op jit(solution)/shard_map/ppermute | solution.py:34
  63.3 9.2 %collective-permute-start.11 = (bf16[32,2048]{1,0:T(8,128)(2,1)S(1)}, bf16[32,2048]{1,0:T(8,128)(2,1)S(1)}, u32[]{:S(2)}, u32[]{:S(2)}) collective-permute-start(bf16[32,2048]{1,0:T(8,128)(2,1)S(1)} %get-tuple-element.63), channel_id=1, source_target_pairs={{0,6},{2,0},{4,2},{6,4},{1,7},{3,1},{5,3},{7,5},{8,14},{10,8},{12,... | collective-permute-start | bytes 393224 | tf_op jit(solution)/shard_map/ppermute | solution.py:34
  73.2 15.1 %collective-permute-start.16 = (bf16[1120,128]{1,0:T(8,128)(2,1)S(1)}, bf16[1120,128]{1,0:T(8,128)(2,1)S(1)}, u32[]{:S(2)}, u32[]{:S(2)}) collective-permute-start(bf16[1120,128]{1,0:T(8,128)(2,1)S(1)} %get-tuple-element.69), channel_id=1, source_target_pairs={{0,64},{8,72},{16,80},{24,88},{32,96},{40,104},{48,112},{56,120},{... | collective-permute-start | bytes 860168 | tf_op jit(solution)/shard_map/ppermute | solution.py:44
  73.2 1.7 %collective-permute-start.12 = (bf16[32,2048]{1,0:T(8,128)(2,1)S(1)}, bf16[32,2048]{1,0:T(8,128)(2,1)S(1)}, u32[]{:S(2)}, u32[]{:S(2)}) collective-permute-start(bf16[32,2048]{1,0:T(8,128)(2,1)S(1)} %get-tuple-element.64.mine_ref), channel_id=1, source_target_pairs={{0,1},{1,0},{2,3},{3,2},{4,5},{5,4},{6,7},{7,6},{8,9},{9,8},{10,11... | collective-permute-start | bytes 393224 | tf_op jit(solution)/shard_map/ppermute | solution.py:34
  75.6 12.8 %collective-permute-start.13 = (bf16[64,512]{1,0:T(8,128)(2,1)S(1)}, bf16[64,512]{1,0:T(8,128)(2,1)S(1)}, u32[]{:S(2)}, u32[]{:S(2)}) collective-permute-start(bf16[64,512]{1,0:T(8,128)(2,1)S(1)} %get-tuple-element.66), channel_id=1, source_target_pairs={{0,2},{2,4},{4,6},{6,0},{1,3},{3,5},{5,7},{7,1},{8,10},{10,12},{12... | collective-permute-start | bytes 196616 | tf_op jit(solution)/shard_map/ppermute | solution.py:34
  76.9 11.5 %collective-permute-start.14 = (bf16[64,512]{1,0:T(8,128)(2,1)S(1)}, bf16[64,512]{1,0:T(8,128)(2,1)S(1)}, u32[]{:S(2)}, u32[]{:S(2)}) collective-permute-start(bf16[64,512]{1,0:T(8,128)(2,1)S(1)} %get-tuple-element.67), channel_id=1, source_target_pairs={{0,4},{2,6},{4,0},{6,2},{1,5},{3,7},{5,1},{7,3},{8,12},{10,14},{12... | collective-permute-start | bytes 196616 | tf_op jit(solution)/shard_map/ppermute | solution.py:34
  79.6 8.9 %collective-permute-start.15 = (bf16[64,512]{1,0:T(8,128)(2,1)S(1)}, bf16[64,512]{1,0:T(8,128)(2,1)S(1)}, u32[]{:S(2)}, u32[]{:S(2)}) collective-permute-start(bf16[64,512]{1,0:T(8,128)(2,1)S(1)} %get-tuple-element.68), channel_id=1, source_target_pairs={{0,6},{2,0},{4,2},{6,4},{1,7},{3,1},{5,3},{7,5},{8,14},{10,8},{12,... | collective-permute-start | bytes 196616 | tf_op jit(solution)/shard_map/ppermute | solution.py:34
  88.4 8.0 %collective-permute-start.20 = (bf16[1120,128]{1,0:T(8,128)(2,1)S(1)}, bf16[1120,128]{1,0:T(8,128)(2,1)S(1)}, u32[]{:S(2)}, u32[]{:S(2)}) collective-permute-start(bf16[1120,128]{1,0:T(8,128)(2,1)S(1)} %add.23), channel_id=1, source_target_pairs={{0,32},{8,40},{16,48},{24,56},{32,0},{40,8},{48,16},{56,24},{64,96... | collective-permute-start | bytes 860168 | tf_op jit(solution)/shard_map/ppermute | solution.py:44
  90.5 19.1 %collective-permute-start.19 = (bf16[64,3072]{1,0:T(8,128)(2,1)S(1)}, bf16[64,3072]{1,0:T(8,128)(2,1)S(1)}, u32[]{:S(2)}, u32[]{:S(2)}) collective-permute-start(bf16[64,3072]{1,0:T(8,128)(2,1)S(1)} %convolution_convert_fusion), channel_id=1, source_target_pairs={{0,6},{2,0},{4,2},{6,4},{1,7},{3,1},{5,3},{7,5},{8,14},{10,8},{12,... | collective-permute-start | bytes 1179656 | tf_op jit(solution)/shard_map/ppermute | solution.py:34
  93.3 16.3 %collective-permute-start.18 = (bf16[64,3072]{1,0:T(8,128)(2,1)S(1)}, bf16[64,3072]{1,0:T(8,128)(2,1)S(1)}, u32[]{:S(2)}, u32[]{:S(2)}) collective-permute-start(bf16[64,3072]{1,0:T(8,128)(2,1)S(1)} %convolution_convert_fusion.1), channel_id=1, source_target_pairs={{0,4},{2,6},{4,0},{6,2},{1,5},{3,7},{5,1},{7,3},{8,12},{10,14},{12... | collective-permute-start | bytes 1179656 | tf_op jit(solution)/shard_map/ppermute | solution.py:34
  93.7 20.6 %collective-permute-start.17 = (bf16[64,3072]{1,0:T(8,128)(2,1)S(1)}, bf16[64,3072]{1,0:T(8,128)(2,1)S(1)}, u32[]{:S(2)}, u32[]{:S(2)}) collective-permute-start(bf16[64,3072]{1,0:T(8,128)(2,1)S(1)} %convolution_convert_fusion.2), channel_id=1, source_target_pairs={{0,2},{2,4},{4,6},{6,0},{1,3},{3,5},{5,7},{7,1},{8,10},{10,12},{12... | collective-permute-start | bytes 1179656 | tf_op jit(solution)/shard_map/ppermute | solution.py:34
  96.5 8.6 %collective-permute-start.21 = (bf16[1120,128]{1,0:T(8,128)(2,1)S(1)}, bf16[1120,128]{1,0:T(8,128)(2,1)S(1)}, u32[]{:S(2)}, u32[]{:S(2)}) collective-permute-start(bf16[1120,128]{1,0:T(8,128)(2,1)S(1)} %add.27), channel_id=1, source_target_pairs={{0,16},{8,24},{16,0},{24,8},{32,48},{40,56},{48,32},{56,40},{64,80... | collective-permute-start | bytes 860168 | tf_op jit(solution)/shard_map/ppermute | solution.py:44
  105.2 10.7 %collective-permute-start.22 = (bf16[1120,128]{1,0:T(8,128)(2,1)S(1)}, bf16[1120,128]{1,0:T(8,128)(2,1)S(1)}, u32[]{:S(2)}, u32[]{:S(2)}) collective-permute-start(bf16[1120,128]{1,0:T(8,128)(2,1)S(1)} %add.28.pay_ref), channel_id=1, source_target_pairs={{0,8},{8,0},{16,24},{24,16},{32,40},{40,32},{48,56},{56,48},{64,72... | collective-permute-start | bytes 860168 | tf_op jit(solution)/shard_map/ppermute | solution.py:44

commit v4 on v3

--- a/solution.py
+++ b/solution.py
@@ -32,12 +32,6 @@
 def rotate(value, axis, steps):
     count = lax.axis_size(axis)
     return lax.ppermute(value, axis, [(s, (s + steps) % count) for s in range(count)])
-
-
-def row_rotate(value, steps):
-    count = lax.axis_size("seq")
-    pairs = [(s, s // ROW * ROW + (s + steps) % ROW) for s in range(count)]
-    return lax.ppermute(value, "seq", pairs)
 
 
 def exchange(value, axis, bit):
@@ -263,37 +257,44 @@
 
 
 def joined(newer, older):
-    return newer + older - dot32(newer[:, :DK], older)
-
-
-def row_kernel(meta, own_ref, *refs):
-    *came, prefix_ref, send_ref, maps_ref = refs
+    return newer.astype(F32) + older.astype(F32) - dot(newer[:, :DK], older)
+
+
+def twin_kernel(meta, own_ref, came_ref, twin_ref):
+    odd = lax.rem(meta[7], 2) == 1
+    for h in range(own_ref.shape[0]):
+        own, came = own_ref[h], came_ref[h]
+        newer = jnp.where(odd, own, came)
+        older = jnp.where(odd, came, own)
+        twin_ref[h] = joined(newer, older).astype(BF16)
+
+
+def row_kernel(meta, own_ref, came_ref, twin_ref, other_ref, prefix_ref, total_ref):
     here = meta[7]
-    maps_ref[here] = own_ref[...]
-    for k, ref in enumerate(came):
-        maps_ref[lax.rem(here + ROW - 1 - k, ROW)] = ref[...]
+    late = here >= ROW // 2
+    odd = lax.rem(here, 2) == 1
     for h in range(own_ref.shape[0]):
-        maps = [maps_ref[i, h] for i in range(ROW)]
-        wide = [m.astype(F32) for m in maps]
-        first = wide[1] + wide[0] - dot(maps[1][:, :DK], maps[0])
-        second = wide[3] + wide[2] - dot(maps[3][:, :DK], maps[2])
-        send_ref[h] = joined(second, first).astype(BF16)
-        third = joined(wide[2], first)
-        prefix = jnp.where(here == 1, wide[0], jnp.where(here == 2, first, third))
-        prefix_ref[h] = jnp.where(here == 0, 0.0, prefix)
-
-
-def join_kernel(near_ref, far_ref, wide_ref, tail_ref):
-    for h in range(near_ref.shape[0]):
-        near, far = near_ref[h], far_ref[h]
-        both = near.astype(F32) + far.astype(F32) - dot(near[:, :DK], far)
-        wide_ref[h] = both
-        tail_ref[h] = both[:, DK:].astype(BF16)
+        twin, other = twin_ref[h], other_ref[h]
+        older = jnp.where(late, other, twin)
+        total_ref[h] = joined(jnp.where(late, twin, other), older).astype(BF16)
+        step = jnp.where(odd, came_ref[h], jnp.zeros_like(twin))
+        prefix_ref[h] = joined(step, jnp.where(late, other, jnp.zeros_like(twin)))
+
+
+def join_kernel(total_ref, near_ref, both_ref, tail_ref):
+    for h in range(total_ref.shape[0]):
+        both = joined(total_ref[h], near_ref[h]).astype(BF16)
+        both_ref[h] = both
+        tail_ref[h] = both[:, DK:]
+
+
+def quarter_of(here):
+    return lax.rem((here + 1) // 2, 2) * 2 + here // 2
 
 
 def attend_kernel(
     meta, prefix_ref, wide_ref, tail_ref, uw_ref, local_ref, link_ref, kb_ref, ks_ref,
-    edge_ref, gain_ref, w_ref, own_ref, other_ref, pay_ref, heads_ref,
+    edge_ref, gain_ref, w_ref, own_ref, other_ref, keep_ref, give_ref, heads_ref, pay_ref,
 ):
     heads, rows, _ = local_ref.shape
     wins, cores, piece, _ = heads_ref.shape
@@ -303,8 +304,8 @@
     seg = seg_of(first + iota((rows, 1), 0), ends)
     gain = gain_ref[...]
     for h in range(heads):
-        wide, prefix, tail = wide_ref[h], prefix_ref[h], tail_ref[h].astype(F32)
-        ahead = wide[:, DK:] + tail - dot32(wide[:, :DK], tail)
+        wide, prefix, tail = wide_ref[h], prefix_ref[h], tail_ref[h]
+        ahead = wide[:, DK:].astype(F32) + tail.astype(F32) - dot(wide[:, :DK], tail)
         enter = prefix[:, DK:] + ahead - dot32(prefix[:, :DK], ahead)
         parts = split(enter)
         attended = local_ref[h] + dot_split(split(link_ref[h]), parts)
@@ -329,6 +330,15 @@
     base = REQS * heads * DK
     for b in range(edge_ref.shape[0]):
         pay_ref[base + b * EDGE_ROWS : base + (b + 1) * EDGE_ROWS, :] = edge_ref[b]
+    used = base + edge_ref.shape[0] * EDGE_ROWS
+    pay_ref[used:, :] = jnp.zeros((pay_ref.shape[0] - used, DK), BF16)
+    quarter = keep_ref.shape[0] // 2
+    mine = quarter_of(meta[7])
+    twin = quarter_of(meta[7] + 1 - 2 * lax.rem(meta[7], 2))
+    for ref, spot in ((keep_ref, mine), (give_ref, twin)):
+        for part, which in enumerate((spot, spot + 1 - 2 * lax.rem(spot, 2))):
+            start = pl.multiple_of(which * quarter, EDGE_ROWS)
+            ref[part * quarter : (part + 1) * quarter] = pay_ref[pl.ds(start, quarter), :]
     order = [lax.rem(win + k, wins) for k in range(wins)]
     w = w_ref[...]
     mine = jnp.concatenate([heads_ref[o, core] for o in order], axis=0)
@@ -337,12 +347,16 @@
     other_ref[...] = dot(theirs, w).astype(BF16)
 
 
-def pair_kernel(own_ref, got_ref, keep_ref, *send_refs):
+def pair_kernel(own_ref, got_ref, pay_ref, came_ref, keep_ref, *refs):
+    *send_refs, quarter_ref, give_ref = refs
     piece = keep_ref.shape[0]
     keep_ref[...] = own_ref[:piece] + got_ref[:piece].astype(F32)
     for k, ref in enumerate(send_refs):
         part = slice((k + 1) * piece, (k + 2) * piece)
         ref[...] = (own_ref[part] + got_ref[part].astype(F32)).astype(BF16)
+    quarter = quarter_ref.shape[0]
+    quarter_ref[...] = pay_ref[:quarter] + came_ref[:quarter]
+    give_ref[...] = pay_ref[quarter:] + came_ref[quarter:]
 
 
 def norm_kernel(hidden_ref, gain_ref, pay_ref, came_ref, keep_ref, *refs):
@@ -370,13 +384,23 @@
         ref[...] = cols_ref[lax.rem(meta[5] + k, wins)]
 
 
-def finish_kernel(pay_ref, came_ref, state_ref, edge_ref):
+def finish_kernel(meta, q0_ref, q1_ref, q3_ref, q2_ref, state_ref, edge_ref, pay_ref):
+    here = meta[7]
+    quarter = q0_ref.shape[0]
+    flip = 1 - 2 * lax.rem(here, 2)
+    for ref, place in (
+        (q0_ref, here),
+        (q1_ref, here + flip),
+        (q3_ref, ROW - 1 - here),
+        (q2_ref, ROW - 1 - here - flip),
+    ):
+        start = pl.multiple_of(quarter_of(place) * quarter, EDGE_ROWS)
+        pay_ref[pl.ds(start, quarter), :] = ref[...]
     rows = state_ref.shape[0]
-    state_ref[...] = (pay_ref[:rows] + came_ref[:rows]).astype(F32)
+    state_ref[...] = pay_ref[:rows].astype(F32)
     heads = edge_ref.shape[3] // DK
     for b in range(3 * heads):
-        part = slice(rows + b * EDGE_ROWS, rows + (b + 1) * EDGE_ROWS)
-        edges = pay_ref[part].astype(F32) + came_ref[part].astype(F32)
+        edges = pay_ref[rows + b * EDGE_ROWS : rows + (b + 1) * EDGE_ROWS].astype(F32)
         lanes = slice(b % heads * DK, (b % heads + 1) * DK)
         for i in range(CONV - 1):
             edge_ref[i, b // heads, :, lanes] = edges[i * REQS : (i + 1) * REQS].astype(BF16)
@@ -424,60 +448,68 @@
         meta, act, lead, parts, taps, beta, halo,
     )
 
-    came = [row_rotate(maps, k) for k in range(1, ROW)]
+    maps_out = out((heads, DK, 2 * DK), BF16)
+    came = exchange(maps, "seq", 1)
+    (twin,) = call(twin_kernel, [maps_out], "twin", 10**8, meta, maps, came)
     prefix, total = call(
         row_kernel,
-        [out((heads, DK, 2 * DK), F32), out((heads, DK, 2 * DK), BF16)],
+        [out((heads, DK, 2 * DK), F32), maps_out],
         "row",
         10**8,
-        meta, maps, *came,
-        scratch=[pltpu.VMEM((ROW, heads, DK, 2 * DK), BF16)],
-    )
-    wide, tail = call(
+        meta, maps, came, twin, exchange(twin, "seq", ROW - 1),
+    )
+    both, tail = call(
         join_kernel,
-        [out((heads, DK, 2 * DK), F32), out((heads, DK, DK), BF16)],
+        [maps_out, out((heads, DK, DK), BF16)],
         "join",
         10**8,
-        shift(total, "seq", ROW), shift(total, "seq", 2 * ROW),
+        total, shift(total, "seq", ROW),
         smem=0,
     )
-    tail = shift(tail, "seq", 2 * ROW)
+    tail = shift(tail, "seq", 3 * ROW)
+    wide = shift(both, "seq", ROW)
     state_rows = REQS * heads * DK
-    pay_rows = state_rows + 3 * heads * EDGE_ROWS
-    own, other, payload = call(
+    grain = ROW * EDGE_ROWS
+    pay_rows = -(-(state_rows + 3 * heads * EDGE_ROWS) // grain) * grain
+    half, quarter = out((pay_rows // 2, DK), BF16), out((pay_rows // 4, DK), BF16)
+    own, other, keep, give = call(
         attend_kernel,
         [
             out((wins * piece, model), F32),
             out((wins * piece, model), BF16),
-            out((pay_rows, DK), BF16),
+            half,
+            half,
         ],
         "attend",
         10**9,
         meta, prefix, wide, tail, uw, local, link, kb, ks, edges, out_gain.reshape(1, DK), w_out,
-        scratch=[pltpu.VMEM((wins, cores, piece, width), BF16)],
+        scratch=[
+            pltpu.VMEM((wins, cores, piece, width), BF16),
+            pltpu.VMEM((pay_rows, DK), BF16),
+        ],
     )
     got = rotate(other, "wout", 1)
-    bits = [1 << b for b in reversed(range((n_seq - 1).bit_length()))]
-    came = exchange(payload, "seq", bits[0])
-    sums = call(
+    *sums, payload, give = call(
         pair_kernel,
-        [out((piece, model), F32)] + [out((piece, model), BF16)] * (wins - 1),
+        [out((piece, model), F32)] + [out((piece, model), BF16)] * (wins - 1) + [quarter] * 2,
         "pair",
         10**6,
-        own, got,
+        own, got, keep, exchange(give, "seq", 1),
         smem=0,
     )
+    came = exchange(give, "seq", ROW - 1)
     reduced = [rotate(sums[k], "win", k) for k in range(1, wins)]
     stream_out, normed, payload = call(
         norm_kernel,
-        [out((piece, model), BF16), out((piece, model), BF16), out((pay_rows, DK), BF16)],
+        [out((piece, model), BF16), out((piece, model), BF16), quarter],
         "norm",
         10**6,
         hidden_in, norm_gain.reshape(1, model), payload, came, sums[0], *reduced,
         smem=0,
     )
     peer = rotate(normed, "wout", 1)
-    came = exchange(payload, "seq", bits[1])
+    bits = [ROW << b for b in reversed(range((n_seq // ROW - 1).bit_length()))]
+    came = exchange(payload, "seq", bits[0])
     cols = call(
         columns_kernel,
         [out((2 * piece, model // wins), BF16)] * wins,
@@ -498,15 +530,16 @@
         total = total + part.astype(F32)
     projected = total.astype(BF16)
 
-    for bit in bits[2:-1]:
+    for bit in bits[1:]:
         payload = payload + exchange(payload, "seq", bit)
+    across = exchange(payload, "seq", ROW - 1)
     final_states, conv_edges = call(
         finish_kernel,
         [out((state_rows, DK), F32), out((CONV - 1, 3, REQS, width), BF16)],
         "finish",
         10**6,
-        payload, exchange(payload, "seq", bits[-1]),
-        smem=0,
+        meta, payload, exchange(payload, "seq", 1), across, exchange(across, "seq", 1),
+        scratch=[pltpu.VMEM((pay_rows, DK), BF16)],
     )
     final_states = final_states.reshape(REQS, heads, DK, DK)
     conv_edges = conv_edges.transpose(2, 0, 1, 3)

time: 117 us -> 114 us (0.974)
  the two profiles are of different devices: /device:TPU:1 before, /device:TPU:24 now
where the time goes in v4:
time: 114 us; the launch traced here: 113 us
  waiting for transfers between devices  46.5 us (41%)
  starting transfers between devices  45.5 us (40%)
  Pallas kernels  14.3 us (13%)
  matrix products  3.59 us (3%)
  local copies, waits for them, and re-layouts  1.67 us (1%)
    ppermute x10, waiting for transfers between devices, exchange(): lax.ppermute(value, axis, [(s, s ^ bit) for s in range(lax.axis_size(axis...  35.7 us
    ppermute x4, starting transfers between devices, shift(): lax.ppermute(value, axis, [(s, s + steps) for s in range(max(0, count - s...  23.1 us
    pallas_call x10, Pallas kernels, call(): pl.pallas_call(kernel, out_shape=outs, in_specs=[SMEM] * smem + [HBM] * h...  14.3 us
    ppermute x10, starting transfers between devices, exchange(): lax.ppermute(value, axis, [(s, s ^ bit) for s in range(lax.axis_size(axis...  11.9 us
    ppermute x11, starting transfers between devices, rotate(): lax.ppermute(value, axis, [(s, (s + steps) % count) for s in range(count)])  10.5 us
    ppermute x11, waiting for transfers between devices, rotate(): lax.ppermute(value, axis, [(s, (s + steps) % count) for s in range(count)])  6.42 us
    ppermute x4, waiting for transfers between devices, shift(): lax.ppermute(value, axis, [(s, s + steps) for s in range(max(0, count - s...  4.39 us
    dot_general x4, matrix products, partial(): return jnp.dot(blocks[(wins - k) % wins], w_qkv, preferred_element_type=F32)  3.59 us
  transfers between devices with their start and end apart: 25, of which 15 were waited for; matrix products, arithmetic and copies ran while one was open for 1% of the time, Pallas kernels for 4%

profile of v4, /device:TPU:24, one launch (start us, length us, event | category | flops | bytes accessed | tf_op | source)
XLA Modules:
  0.0 112.5 jit_solution(8975965051939834772)
XLA Ops:
  0.6 0.9 slice.4
  1.5 3.5 %collective-permute-start = (bf16[3,16,256]{2,1,0:T(8,128)(2,1)S(1)}, bf16[3,16,256]{2,1,0:T(8,128)(2,1)S(1)}, u32[]{:S(2)}, u32[]{:S(2)}) collective-permute-start(bf16[3,16,256]{2,1,0:T(8,128)(2,1)S(1)} %slice.4), channel_id=1, source_target_pairs={{0,8},{8,16},{16,24},{24,32},{32,40},{40,48},{48,56},{56,64},{64,7... | collective-permute-start | bytes 73736 | tf_op jit(solution)/shard_map/ppermute | solution.py:29
  5.1 0.7 concatenate.3.meta
  5.8 2.4 %conv.1 = (bf16[3,256,256]{2,1,0:T(8,128)(2,1)S(1)}, bf16[3,16,256]{2,1,0:T(8,128)(2,1)S(1)}, bf16[3,16,256]{2,1,0:T(8,128)(2,1)S(1)}, f32[3,4,256]{2,1,0:T(4,128)S(1)}, f32[2,256]{1,0:T(2,128)S(1)}) custom-call(s32[8]{0:T(128)S(1)} %concatenate.3.meta, bf16[3,256,256]{2,1,0:T(8,128)(2,1)} %bitcast.20, f32[3,4,256]{2,1,0:T(4,128)} %taps_hbm.1, f32[2,256]{1,0:T(2,128)} %beta_hbm.1), custom_call_target="tpu_custom_call" | custom-call | flops 100000000 | bytes 864288 | tf_op jit(solution)/shard_map/conv/pallas_call | solution.py:64
  8.3 4.9 %prep.1 = (bf16[2,128,256]{2,1,0:T(8,128)(2,1)S(1)}, f32[2,256,256]{2,1,0:T(8,128)S(1)}, f32[2,256,128]{2,1,0:T(8,128)S(1)}, f32[2,256,128]{2,1,0:T(8,128)S(1)},...) custom-call(s32[8]{0:T(128)S(1)} %concatenate.3.meta, ...), custom_call_target="tpu_custom_call" | custom-call | flops 2000000000 | bytes 1818656 | tf_op jit(solution)/shard_map/prep/pallas_call | solution.py:64
  13.2 1.6 %collective-permute-start.1 = (bf16[2,128,256]{2,1,0:T(8,128)(2,1)S(1)}, bf16[2,128,256]{2,1,0:T(8,128)(2,1)S(1)}, u32[]{:S(2)}, u32[]{:S(2)}) collective-permute-start(bf16[2,128,256]{2,1,0:T(8,128)(2,1)S(1)} %get-tuple-element.49.own_ref), channel_id=1, source_target_pairs={{0,8},{8,0},{16,24},{24,16},{32,40},{40,32},{48,56},{56,48},{64,72... | collective-permute-start | bytes 393224 | tf_op jit(solution)/shard_map/ppermute | solution.py:38
  14.8 3.5 %collective-permute-done.1.came_ref = bf16[2,128,256]{2,1,0:T(8,128)(2,1)S(1)} collective-permute-done((bf16[2,128,256]{2,1,0:T(8,128)(2,1)S(1)}, bf16[2,128,256]{2,1,0:T(8,128)(2,1)S(1)}, u32[]{:S(2)}, u32[]{:S(2)}) %collective-permute-start.1) | collective-permute-done | bytes 131104 | tf_op jit(solution)/shard_map/ppermute | solution.py:38
  18.2 0.7 twin.1.twin_ref
  19.0 3.2 %collective-permute-start.2 = (bf16[2,128,256]{2,1,0:T(8,128)(2,1)S(1)}, bf16[2,128,256]{2,1,0:T(8,128)(2,1)S(1)}, u32[]{:S(2)}, u32[]{:S(2)}) collective-permute-start(bf16[2,128,256]{2,1,0:T(8,128)(2,1)S(1)} %twin.1.twin_ref), channel_id=1, source_target_pairs={{0,24},{8,16},{16,8},{24,0},{32,56},{40,48},{48,40},{56,32},{64,88... | collective-permute-start | bytes 393224 | tf_op jit(solution)/shard_map/ppermute | solution.py:38
  22.2 3.1 %collective-permute-done.2.other_ref = bf16[2,128,256]{2,1,0:T(8,128)(2,1)S(1)} collective-permute-done((bf16[2,128,256]{2,1,0:T(8,128)(2,1)S(1)}, bf16[2,128,256]{2,1,0:T(8,128)(2,1)S(1)}, u32[]{:S(2)}, u32[]{:S(2)}) %collective-permute-start.2) | collective-permute-done | bytes 131104 | tf_op jit(solution)/shard_map/ppermute | solution.py:38
  25.2 0.8 row.1
  26.0 5.0 %collective-permute-start.3 = (bf16[2,128,256]{2,1,0:T(8,128)(2,1)S(1)}, bf16[2,128,256]{2,1,0:T(8,128)(2,1)S(1)}, u32[]{:S(2)}, u32[]{:S(2)}) collective-permute-start(bf16[2,128,256]{2,1,0:T(8,128)(2,1)S(1)} %get-tuple-element.51.total_ref), channel_id=1, source_target_pairs={{0,32},{8,40},{16,48},{24,56},{32,64},{40,72},{48,80},{56,88},{64,... | collective-permute-start | bytes 393224 | tf_op jit(solution)/shard_map/ppermute | solution.py:29
  31.0 2.5 %collective-permute-done.3.near_ref = bf16[2,128,256]{2,1,0:T(8,128)(2,1)S(1)} collective-permute-done((bf16[2,128,256]{2,1,0:T(8,128)(2,1)S(1)}, bf16[2,128,256]{2,1,0:T(8,128)(2,1)S(1)}, u32[]{:S(2)}, u32[]{:S(2)}) %collective-permute-start.3) | collective-permute-done | bytes 131104 | tf_op jit(solution)/shard_map/ppermute | solution.py:29
  33.5 0.2 join.1
  33.7 4.4 %collective-permute-start.4 = (bf16[2,128,256]{2,1,0:T(8,128)(2,1)S(1)}, bf16[2,128,256]{2,1,0:T(8,128)(2,1)S(1)}, u32[]{:S(2)}, u32[]{:S(2)}) collective-permute-start(bf16[2,128,256]{2,1,0:T(8,128)(2,1)S(1)} %get-tuple-element.52), channel_id=1, source_target_pairs={{0,32},{8,40},{16,48},{24,56},{32,64},{40,72},{48,80},{56,88},{64,... | collective-permute-start | bytes 393224 | tf_op jit(solution)/shard_map/ppermute | solution.py:29
  38.1 10.1 %collective-permute-start.5 = (bf16[2,128,128]{2,1,0:T(8,128)(2,1)S(1)}, bf16[2,128,128]{2,1,0:T(8,128)(2,1)S(1)}, u32[]{:S(2)}, u32[]{:S(2)}) collective-permute-start(bf16[2,128,128]{2,1,0:T(8,128)(2,1)S(1)} %get-tuple-element.53), channel_id=1, source_target_pairs={{0,96},{8,104},{16,112},{24,120},{32,128},{40,136},{48,144},{56,15... | collective-permute-start | bytes 196616 | tf_op jit(solution)/shard_map/ppermute | solution.py:29
  48.3 1.9 %collective-permute-done.5.tail_ref = bf16[2,128,128]{2,1,0:T(8,128)(2,1)S(1)} collective-permute-done((bf16[2,128,128]{2,1,0:T(8,128)(2,1)S(1)}, bf16[2,128,128]{2,1,0:T(8,128)(2,1)S(1)}, u32[]{:S(2)}, u32[]{:S(2)}) %collective-permute-start.5) | collective-permute-done | bytes 65568 | tf_op jit(solution)/shard_map/ppermute | solution.py:29
  50.1 2.5 %attend.1 = (f32[128,2048]{1,0:T(8,128)S(1)}, bf16[128,2048]{1,0:T(8,128)(2,1)S(1)}, bf16[576,128]{1,0:T(8,128)(2,1)S(1)}, bf16[576,128]{1,0:T(8,128)(2,1)S(1)}) custom-call(s32[8]{0:T(128)S(1)} %concatenate.3.meta, f32[2,128,256]{2,1,0:T(8,128)S(1)} %get-tuple-element.50.prefix_ref, bf16[2,128,256]{2,1,0:T(8,128)(2,1)S(1)} %collective-permute-done.4.wide_ref, ...), custom_call_target="tpu_custom_call" | custom-call | flops 1000000000 | bytes 4581920 | tf_op jit(solution)/shard_map/attend/pallas_call | solution.py:64
  52.8 6.2 %collective-permute-done.7.came_ref = bf16[576,128]{1,0:T(8,128)(2,1)S(1)} collective-permute-done((bf16[576,128]{1,0:T(8,128)(2,1)S(1)}, bf16[576,128]{1,0:T(8,128)(2,1)S(1)}, u32[]{:S(2)}, u32[]{:S(2)}) %collective-permute-start.7) | collective-permute-done | bytes 147488 | tf_op jit(solution)/shard_map/ppermute | solution.py:38
  59.0 0.1 pair.1
  59.1 0.3 collective-permute-start.9
  59.4 2.6 %collective-permute-start.10 = (bf16[32,2048]{1,0:T(8,128)(2,1)S(1)}, bf16[32,2048]{1,0:T(8,128)(2,1)S(1)}, u32[]{:S(2)}, u32[]{:S(2)}) collective-permute-start(bf16[32,2048]{1,0:T(8,128)(2,1)S(1)} %get-tuple-element.68), channel_id=1, source_target_pairs={{0,4},{2,6},{4,0},{6,2},{1,5},{3,7},{5,1},{7,3},{8,12},{10,14},{12... | collective-permute-start | bytes 393224 | tf_op jit(solution)/shard_map/ppermute | solution.py:34
  62.0 5.6 %collective-permute-done.8.came_ref = bf16[288,128]{1,0:T(8,128)(2,1)S(1)} collective-permute-done((bf16[288,128]{1,0:T(8,128)(2,1)S(1)}, bf16[288,128]{1,0:T(8,128)(2,1)S(1)}, u32[]{:S(2)}, u32[]{:S(2)}) %collective-permute-start.8) | collective-permute-done | bytes 73760 | tf_op jit(solution)/shard_map/ppermute | solution.py:38
  67.6 1.1 collective-permute-done.11.refs_2_
  68.7 0.8 norm.1
  69.5 4.8 %collective-permute-start.16 = (bf16[288,128]{1,0:T(8,128)(2,1)S(1)}, bf16[288,128]{1,0:T(8,128)(2,1)S(1)}, u32[]{:S(2)}, u32[]{:S(2)}) collective-permute-start(bf16[288,128]{1,0:T(8,128)(2,1)S(1)} %get-tuple-element.75), channel_id=1, source_target_pairs={{0,128},{8,136},{16,144},{24,152},{32,160},{40,168},{48,176},{56,1... | collective-permute-start | bytes 221192 | tf_op jit(solution)/shard_map/ppermute | solution.py:38
  74.3 0.6 columns.1
  74.9 2.2 %collective-permute-start.13 = (bf16[64,512]{1,0:T(8,128)(2,1)S(1)}, bf16[64,512]{1,0:T(8,128)(2,1)S(1)}, u32[]{:S(2)}, u32[]{:S(2)}) collective-permute-start(bf16[64,512]{1,0:T(8,128)(2,1)S(1)} %get-tuple-element.72), channel_id=1, source_target_pairs={{0,2},{2,4},{4,6},{6,0},{1,3},{3,5},{5,7},{7,1},{8,10},{10,12},{12... | collective-permute-start | bytes 196616 | tf_op jit(solution)/shard_map/ppermute | solution.py:34
  77.1 0.9 collective-permute-start.14
  78.0 0.7 collective-permute-start.15
  78.7 1.6 %collective-permute-done.13 = bf16[64,512]{1,0:T(8,128)(2,1)S(1)} collective-permute-done((bf16[64,512]{1,0:T(8,128)(2,1)S(1)}, bf16[64,512]{1,0:T(8,128)(2,1)S(1)}, u32[]{:S(2)}, u32[]{:S(2)}) %collective-permute-start.13) | collective-permute-done | bytes 65568 | tf_op jit(solution)/shard_map/ppermute | solution.py:34
  80.3 3.0 %collective-permute-done.14 = bf16[64,512]{1,0:T(8,128)(2,1)S(1)} collective-permute-done((bf16[64,512]{1,0:T(8,128)(2,1)S(1)}, bf16[64,512]{1,0:T(8,128)(2,1)S(1)}, u32[]{:S(2)}, u32[]{:S(2)}) %collective-permute-start.14) | collective-permute-done | bytes 65568 | tf_op jit(solution)/shard_map/ppermute | solution.py:34
  83.3 0.7 collective-permute-done.15
  84.0 0.7 convolution_convert_fusion.2
  84.6 0.7 convolution_convert_fusion.1
  85.3 0.7 convolution_convert_fusion
  86.1 2.0 %collective-permute-start.18 = (bf16[64,3072]{1,0:T(8,128)(2,1)S(1)}, bf16[64,3072]{1,0:T(8,128)(2,1)S(1)}, u32[]{:S(2)}, u32[]{:S(2)}) collective-permute-start(bf16[64,3072]{1,0:T(8,128)(2,1)S(1)} %convolution_convert_fusion.1), channel_id=1, source_target_pairs={{0,4},{2,6},{4,0},{6,2},{1,5},{3,7},{5,1},{7,3},{8,12},{10,14},{12... | collective-permute-start | bytes 1179656 | tf_op jit(solution)/shard_map/ppermute | solution.py:34
  88.1 1.6 %collective-permute-start.17 = (bf16[64,3072]{1,0:T(8,128)(2,1)S(1)}, bf16[64,3072]{1,0:T(8,128)(2,1)S(1)}, u32[]{:S(2)}, u32[]{:S(2)}) collective-permute-start(bf16[64,3072]{1,0:T(8,128)(2,1)S(1)} %convolution_convert_fusion.2), channel_id=1, source_target_pairs={{0,2},{2,4},{4,6},{6,0},{1,3},{3,5},{5,7},{7,1},{8,10},{10,12},{12... | collective-permute-start | bytes 1179656 | tf_op jit(solution)/shard_map/ppermute | solution.py:34
  89.8 1.2 %collective-permute-start.20 = (bf16[288,128]{1,0:T(8,128)(2,1)S(1)}, bf16[288,128]{1,0:T(8,128)(2,1)S(1)}, u32[]{:S(2)}, u32[]{:S(2)}) collective-permute-start(bf16[288,128]{1,0:T(8,128)(2,1)S(1)} %add.23), channel_id=1, source_target_pairs={{0,64},{8,72},{16,80},{24,88},{32,96},{40,104},{48,112},{56,120},{... | collective-permute-start | bytes 221192 | tf_op jit(solution)/shard_map/ppermute | solution.py:38
  91.0 4.0 %collective-permute-done.20 = bf16[288,128]{1,0:T(8,128)(2,1)S(1)} collective-permute-done((bf16[288,128]{1,0:T(8,128)(2,1)S(1)}, bf16[288,128]{1,0:T(8,128)(2,1)S(1)}, u32[]{:S(2)}, u32[]{:S(2)}) %collective-permute-start.20) | collective-permute-done | bytes 73760 | tf_op jit(solution)/shard_map/ppermute | solution.py:38
  95.1 0.1 collective-permute-start.21
  95.2 4.3 %collective-permute-done.21 = bf16[288,128]{1,0:T(8,128)(2,1)S(1)} collective-permute-done((bf16[288,128]{1,0:T(8,128)(2,1)S(1)}, bf16[288,128]{1,0:T(8,128)(2,1)S(1)}, u32[]{:S(2)}, u32[]{:S(2)}) %collective-permute-start.21) | collective-permute-done | bytes 73760 | tf_op jit(solution)/shard_map/ppermute | solution.py:38
  99.5 0.9 collective-permute-start.23
  100.4 4.8 %collective-permute-done.23.q3_ref = bf16[288,128]{1,0:T(8,128)(2,1)S(1)} collective-permute-done((bf16[288,128]{1,0:T(8,128)(2,1)S(1)}, bf16[288,128]{1,0:T(8,128)(2,1)S(1)}, u32[]{:S(2)}, u32[]{:S(2)}) %collective-permute-start.23) | collective-permute-done | bytes 73760 | tf_op jit(solution)/shard_map/ppermute | solution.py:38
  105.2 0.2 collective-permute-done.22.q1_ref
  105.4 4.1 %collective-permute-done.24.q2_ref = bf16[288,128]{1,0:T(8,128)(2,1)S(1)} collective-permute-done((bf16[288,128]{1,0:T(8,128)(2,1)S(1)}, bf16[288,128]{1,0:T(8,128)(2,1)S(1)}, u32[]{:S(2)}, u32[]{:S(2)}) %collective-permute-start.24) | collective-permute-done | bytes 73760 | tf_op jit(solution)/shard_map/ppermute | solution.py:38
  109.5 1.4 %finish.1 = (f32[1024,128]{1,0:T(8,128)}, bf16[3,3,4,256]{3,2,1,0:T(4,128)(2,1)}) custom-call(s32[8]{0:T(128)S(1)} %concatenate.3.meta, bf16[288,128]{1,0:T(8,128)(2,1)S(1)} %add.28.q0_ref, bf16[288,128]{1,0:T(8,128)(2,1)S(1)} %collective-permute-done.22.q1_ref, bf16[288,128]{1,0:T(8,128)(2,1)S(1)} %collective-permute-done.23.q3_ref, ...), custom_call_target="tpu_custom_call" | custom-call | flops 1000000 | bytes 837664 | tf_op jit(solution)/shard_map/finish/pallas_call | solution.py:64
  111.0 1.6 %fusion.2 = bf16[64,3072]{1,0:T(8,128)(2,1)} fusion(bf16[64,512]{1,0:T(8,128)(2,1)S(1)} %get-tuple-element.76, bf16[512,3072]{1,0:T(8,128)(2,1)S(1)} %copy-done, bf16[64,3072]{1,0:T(8,128)(2,1)S(1)} %collective-permute-done.19, bf16[64,3072]{1,0:T(8,128)(2,1)S(1)} %collective-permute-done.18, bf16[64,3072]{1,0:T(8,128)(2,1)S(1)} %collective-permute-done.17), kind=kOutput, calls=%fused_computation.3 | convolution fusion | flops 202702848 | bytes 4784128 | tf_op jit(solution)/shard_map/dot_general | solution.py:525
  (31 shorter events, 0.4 us)
Async XLA Ops:
  0.6 83.3 %copy-start = (bf16[512,3072]{1,0:T(8,128)(2,1)S(1)}, bf16[512,3072]{1,0:T(8,128)(2,1)}, u32[]{:S(2)}) copy-start(bf16[512,3072]{1,0:T(8,128)(2,1)} %param.17) | copy-start | bytes 9437188
  1.5 6.7 %collective-permute-start = (bf16[3,16,256]{2,1,0:T(8,128)(2,1)S(1)}, bf16[3,16,256]{2,1,0:T(8,128)(2,1)S(1)}, u32[]{:S(2)}, u32[]{:S(2)}) collective-permute-start(bf16[3,16,256]{2,1,0:T(8,128)(2,1)S(1)} %slice.4), channel_id=1, source_target_pairs={{0,8},{8,16},{16,24},{24,32},{32,40},{40,48},{48,56},{56,64},{64,7... | collective-permute-start | bytes 73736 | tf_op jit(solution)/shard_map/ppermute | solution.py:29
  8.3 41.9 %copy-start.3 = (bf16[256,2048]{1,0:T(8,128)(2,1)S(1)}, bf16[256,2048]{1,0:T(8,128)(2,1)}, u32[]{:S(2)}) copy-start(bf16[256,2048]{1,0:T(8,128)(2,1)} %w_ref.1) | copy-start | bytes 3145732
  8.3 41.9 %copy-start.4 = (f32[128]{0:T(128)S(1)}, f32[128]{0:T(128)}, u32[]{:S(2)}) copy-start(f32[128]{0:T(128)} %param.13) | copy-start | bytes 1540
  13.2 5.1 %collective-permute-start.1 = (bf16[2,128,256]{2,1,0:T(8,128)(2,1)S(1)}, bf16[2,128,256]{2,1,0:T(8,128)(2,1)S(1)}, u32[]{:S(2)}, u32[]{:S(2)}) collective-permute-start(bf16[2,128,256]{2,1,0:T(8,128)(2,1)S(1)} %get-tuple-element.49.own_ref), channel_id=1, source_target_pairs={{0,8},{8,0},{16,24},{24,16},{32,40},{40,32},{48,56},{56,48},{64,72... | collective-permute-start | bytes 393224 | tf_op jit(solution)/shard_map/ppermute | solution.py:38
  19.0 49.7 %copy-start.1 = (bf16[32,2048]{1,0:T(8,128)(2,1)S(1)}, bf16[32,2048]{1,0:T(8,128)(2,1)}, u32[]{:S(2)}) copy-start(bf16[32,2048]{1,0:T(8,128)(2,1)} %hidden_ref.1) | copy-start | bytes 393220
  19.0 49.7 %copy-start.2 = (f32[2048]{0:T(1024)S(1)}, f32[2048]{0:T(1024)}, u32[]{:S(2)}) copy-start(f32[2048]{0:T(1024)} %param.16) | copy-start | bytes 24580
  19.0 6.3 %collective-permute-start.2 = (bf16[2,128,256]{2,1,0:T(8,128)(2,1)S(1)}, bf16[2,128,256]{2,1,0:T(8,128)(2,1)S(1)}, u32[]{:S(2)}, u32[]{:S(2)}) collective-permute-start(bf16[2,128,256]{2,1,0:T(8,128)(2,1)S(1)} %twin.1.twin_ref), channel_id=1, source_target_pairs={{0,24},{8,16},{16,8},{24,0},{32,56},{40,48},{48,40},{56,32},{64,88... | collective-permute-start | bytes 393224 | tf_op jit(solution)/shard_map/ppermute | solution.py:38
  26.0 7.5 %collective-permute-start.3 = (bf16[2,128,256]{2,1,0:T(8,128)(2,1)S(1)}, bf16[2,128,256]{2,1,0:T(8,128)(2,1)S(1)}, u32[]{:S(2)}, u32[]{:S(2)}) collective-permute-start(bf16[2,128,256]{2,1,0:T(8,128)(2,1)S(1)} %get-tuple-element.51.total_ref), channel_id=1, source_target_pairs={{0,32},{8,40},{16,48},{24,56},{32,64},{40,72},{48,80},{56,88},{64,... | collective-permute-start | bytes 393224 | tf_op jit(solution)/shard_map/ppermute | solution.py:29
  33.7 16.4 %collective-permute-start.4 = (bf16[2,128,256]{2,1,0:T(8,128)(2,1)S(1)}, bf16[2,128,256]{2,1,0:T(8,128)(2,1)S(1)}, u32[]{:S(2)}, u32[]{:S(2)}) collective-permute-start(bf16[2,128,256]{2,1,0:T(8,128)(2,1)S(1)} %get-tuple-element.52), channel_id=1, source_target_pairs={{0,32},{8,40},{16,48},{24,56},{32,64},{40,72},{48,80},{56,88},{64,... | collective-permute-start | bytes 393224 | tf_op jit(solution)/shard_map/ppermute | solution.py:29
  38.1 12.0 %collective-permute-start.5 = (bf16[2,128,128]{2,1,0:T(8,128)(2,1)S(1)}, bf16[2,128,128]{2,1,0:T(8,128)(2,1)S(1)}, u32[]{:S(2)}, u32[]{:S(2)}) collective-permute-start(bf16[2,128,128]{2,1,0:T(8,128)(2,1)S(1)} %get-tuple-element.53), channel_id=1, source_target_pairs={{0,96},{8,104},{16,112},{24,120},{32,128},{40,136},{48,144},{56,15... | collective-permute-start | bytes 196616 | tf_op jit(solution)/shard_map/ppermute | solution.py:29
  52.6 6.4 %collective-permute-start.6 = (bf16[128,2048]{1,0:T(8,128)(2,1)S(1)}, bf16[128,2048]{1,0:T(8,128)(2,1)S(1)}, u32[]{:S(2)}, u32[]{:S(2)}) collective-permute-start(bf16[128,2048]{1,0:T(8,128)(2,1)S(1)} %get-tuple-element.61), channel_id=1, source_target_pairs={{0,1},{1,0},{2,3},{3,2},{4,5},{5,4},{6,7},{7,6},{8,9},{9,8},{10,11... | collective-permute-start | bytes 1572872 | tf_op jit(solution)/shard_map/ppermute | solution.py:34
  52.7 6.3 %collective-permute-start.7 = (bf16[576,128]{1,0:T(8,128)(2,1)S(1)}, bf16[576,128]{1,0:T(8,128)(2,1)S(1)}, u32[]{:S(2)}, u32[]{:S(2)}) collective-permute-start(bf16[576,128]{1,0:T(8,128)(2,1)S(1)} %get-tuple-element.63), channel_id=1, source_target_pairs={{0,8},{8,0},{16,24},{24,16},{32,40},{40,32},{48,56},{56,48},{64,72... | collective-permute-start | bytes 442376 | tf_op jit(solution)/shard_map/ppermute | solution.py:38
  59.1 8.5 %collective-permute-start.9 = (bf16[32,2048]{1,0:T(8,128)(2,1)S(1)}, bf16[32,2048]{1,0:T(8,128)(2,1)S(1)}, u32[]{:S(2)}, u32[]{:S(2)}) collective-permute-start(bf16[32,2048]{1,0:T(8,128)(2,1)S(1)} %get-tuple-element.67), channel_id=1, source_target_pairs={{0,2},{2,4},{4,6},{6,0},{1,3},{3,5},{5,7},{7,1},{8,10},{10,12},{12... | collective-permute-start | bytes 393224 | tf_op jit(solution)/shard_map/ppermute | solution.py:34
  59.4 8.2 %collective-permute-start.10 = (bf16[32,2048]{1,0:T(8,128)(2,1)S(1)}, bf16[32,2048]{1,0:T(8,128)(2,1)S(1)}, u32[]{:S(2)}, u32[]{:S(2)}) collective-permute-start(bf16[32,2048]{1,0:T(8,128)(2,1)S(1)} %get-tuple-element.68), channel_id=1, source_target_pairs={{0,4},{2,6},{4,0},{6,2},{1,5},{3,7},{5,1},{7,3},{8,12},{10,14},{12... | collective-permute-start | bytes 393224 | tf_op jit(solution)/shard_map/ppermute | solution.py:34
  62.0 6.7 %collective-permute-start.11 = (bf16[32,2048]{1,0:T(8,128)(2,1)S(1)}, bf16[32,2048]{1,0:T(8,128)(2,1)S(1)}, u32[]{:S(2)}, u32[]{:S(2)}) collective-permute-start(bf16[32,2048]{1,0:T(8,128)(2,1)S(1)} %get-tuple-element.69), channel_id=1, source_target_pairs={{0,6},{2,0},{4,2},{6,4},{1,7},{3,1},{5,3},{7,5},{8,14},{10,8},{12,... | collective-permute-start | bytes 393224 | tf_op jit(solution)/shard_map/ppermute | solution.py:34
  62.0 5.6 %collective-permute-start.8 = (bf16[288,128]{1,0:T(8,128)(2,1)S(1)}, bf16[288,128]{1,0:T(8,128)(2,1)S(1)}, u32[]{:S(2)}, u32[]{:S(2)}) collective-permute-start(bf16[288,128]{1,0:T(8,128)(2,1)S(1)} %get-tuple-element.65), channel_id=1, source_target_pairs={{0,24},{8,16},{16,8},{24,0},{32,56},{40,48},{48,40},{56,32},{64,88... | collective-permute-start | bytes 221192 | tf_op jit(solution)/shard_map/ppermute | solution.py:38
  69.4 4.8 %collective-permute-start.12 = (bf16[32,2048]{1,0:T(8,128)(2,1)S(1)}, bf16[32,2048]{1,0:T(8,128)(2,1)S(1)}, u32[]{:S(2)}, u32[]{:S(2)}) collective-permute-start(bf16[32,2048]{1,0:T(8,128)(2,1)S(1)} %get-tuple-element.70.mine_ref), channel_id=1, source_target_pairs={{0,1},{1,0},{2,3},{3,2},{4,5},{5,4},{6,7},{7,6},{8,9},{9,8},{10,11... | collective-permute-start | bytes 393224 | tf_op jit(solution)/shard_map/ppermute | solution.py:34
  69.5 9.2 %collective-permute-start.16 = (bf16[288,128]{1,0:T(8,128)(2,1)S(1)}, bf16[288,128]{1,0:T(8,128)(2,1)S(1)}, u32[]{:S(2)}, u32[]{:S(2)}) collective-permute-start(bf16[288,128]{1,0:T(8,128)(2,1)S(1)} %get-tuple-element.75), channel_id=1, source_target_pairs={{0,128},{8,136},{16,144},{24,152},{32,160},{40,168},{48,176},{56,1... | collective-permute-start | bytes 221192 | tf_op jit(solution)/shard_map/ppermute | solution.py:38
  74.9 5.4 %collective-permute-start.13 = (bf16[64,512]{1,0:T(8,128)(2,1)S(1)}, bf16[64,512]{1,0:T(8,128)(2,1)S(1)}, u32[]{:S(2)}, u32[]{:S(2)}) collective-permute-start(bf16[64,512]{1,0:T(8,128)(2,1)S(1)} %get-tuple-element.72), channel_id=1, source_target_pairs={{0,2},{2,4},{4,6},{6,0},{1,3},{3,5},{5,7},{7,1},{8,10},{10,12},{12... | collective-permute-start | bytes 196616 | tf_op jit(solution)/shard_map/ppermute | solution.py:34
  77.1 6.2 %collective-permute-start.14 = (bf16[64,512]{1,0:T(8,128)(2,1)S(1)}, bf16[64,512]{1,0:T(8,128)(2,1)S(1)}, u32[]{:S(2)}, u32[]{:S(2)}) collective-permute-start(bf16[64,512]{1,0:T(8,128)(2,1)S(1)} %get-tuple-element.73), channel_id=1, source_target_pairs={{0,4},{2,6},{4,0},{6,2},{1,5},{3,7},{5,1},{7,3},{8,12},{10,14},{12... | collective-permute-start | bytes 196616 | tf_op jit(solution)/shard_map/ppermute | solution.py:34
  78.0 6.0 %collective-permute-start.15 = (bf16[64,512]{1,0:T(8,128)(2,1)S(1)}, bf16[64,512]{1,0:T(8,128)(2,1)S(1)}, u32[]{:S(2)}, u32[]{:S(2)}) collective-permute-start(bf16[64,512]{1,0:T(8,128)(2,1)S(1)} %get-tuple-element.74), channel_id=1, source_target_pairs={{0,6},{2,0},{4,2},{6,4},{1,7},{3,1},{5,3},{7,5},{8,14},{10,8},{12,... | collective-permute-start | bytes 196616 | tf_op jit(solution)/shard_map/ppermute | solution.py:34
  86.0 24.9 %collective-permute-start.19 = (bf16[64,3072]{1,0:T(8,128)(2,1)S(1)}, bf16[64,3072]{1,0:T(8,128)(2,1)S(1)}, u32[]{:S(2)}, u32[]{:S(2)}) collective-permute-start(bf16[64,3072]{1,0:T(8,128)(2,1)S(1)} %convolution_convert_fusion), channel_id=1, source_target_pairs={{0,6},{2,0},{4,2},{6,4},{1,7},{3,1},{5,3},{7,5},{8,14},{10,8},{12,... | collective-permute-start | bytes 1179656 | tf_op jit(solution)/shard_map/ppermute | solution.py:34
  86.1 24.9 %collective-permute-start.18 = (bf16[64,3072]{1,0:T(8,128)(2,1)S(1)}, bf16[64,3072]{1,0:T(8,128)(2,1)S(1)}, u32[]{:S(2)}, u32[]{:S(2)}) collective-permute-start(bf16[64,3072]{1,0:T(8,128)(2,1)S(1)} %convolution_convert_fusion.1), channel_id=1, source_target_pairs={{0,4},{2,6},{4,0},{6,2},{1,5},{3,7},{5,1},{7,3},{8,12},{10,14},{12... | collective-permute-start | bytes 1179656 | tf_op jit(solution)/shard_map/ppermute | solution.py:34
  88.1 22.8 %collective-permute-start.17 = (bf16[64,3072]{1,0:T(8,128)(2,1)S(1)}, bf16[64,3072]{1,0:T(8,128)(2,1)S(1)}, u32[]{:S(2)}, u32[]{:S(2)}) collective-permute-start(bf16[64,3072]{1,0:T(8,128)(2,1)S(1)} %convolution_convert_fusion.2), channel_id=1, source_target_pairs={{0,2},{2,4},{4,6},{6,0},{1,3},{3,5},{5,7},{7,1},{8,10},{10,12},{12... | collective-permute-start | bytes 1179656 | tf_op jit(solution)/shard_map/ppermute | solution.py:34
  89.8 5.3 %collective-permute-start.20 = (bf16[288,128]{1,0:T(8,128)(2,1)S(1)}, bf16[288,128]{1,0:T(8,128)(2,1)S(1)}, u32[]{:S(2)}, u32[]{:S(2)}) collective-permute-start(bf16[288,128]{1,0:T(8,128)(2,1)S(1)} %add.23), channel_id=1, source_target_pairs={{0,64},{8,72},{16,80},{24,88},{32,96},{40,104},{48,112},{56,120},{... | collective-permute-start | bytes 221192 | tf_op jit(solution)/shard_map/ppermute | solution.py:38
  95.1 4.4 %collective-permute-start.21 = (bf16[288,128]{1,0:T(8,128)(2,1)S(1)}, bf16[288,128]{1,0:T(8,128)(2,1)S(1)}, u32[]{:S(2)}, u32[]{:S(2)}) collective-permute-start(bf16[288,128]{1,0:T(8,128)(2,1)S(1)} %add.27), channel_id=1, source_target_pairs={{0,32},{8,40},{16,48},{24,56},{32,0},{40,8},{48,16},{56,24},{64,96... | collective-permute-start | bytes 221192 | tf_op jit(solution)/shard_map/ppermute | solution.py:38
  99.5 5.7 %collective-permute-start.23 = (bf16[288,128]{1,0:T(8,128)(2,1)S(1)}, bf16[288,128]{1,0:T(8,128)(2,1)S(1)}, u32[]{:S(2)}, u32[]{:S(2)}) collective-permute-start(bf16[288,128]{1,0:T(8,128)(2,1)S(1)} %add.28.q0_ref), channel_id=1, source_target_pairs={{0,24},{8,16},{16,8},{24,0},{32,56},{40,48},{48,40},{56,32},{64,88... | collective-permute-start | bytes 221192 | tf_op jit(solution)/shard_map/ppermute | solution.py:38
  100.4 5.0 %collective-permute-start.22 = (bf16[288,128]{1,0:T(8,128)(2,1)S(1)}, bf16[288,128]{1,0:T(8,128)(2,1)S(1)}, u32[]{:S(2)}, u32[]{:S(2)}) collective-permute-start(bf16[288,128]{1,0:T(8,128)(2,1)S(1)} %add.28.q0_ref), channel_id=1, source_target_pairs={{0,8},{8,0},{16,24},{24,16},{32,40},{40,32},{48,56},{56,48},{64,72... | collective-permute-start | bytes 221192 | tf_op jit(solution)/shard_map/ppermute | solution.py:38
  105.2 4.4 %collective-permute-start.24 = (bf16[288,128]{1,0:T(8,128)(2,1)S(1)}, bf16[288,128]{1,0:T(8,128)(2,1)S(1)}, u32[]{:S(2)}, u32[]{:S(2)}) collective-permute-start(bf16[288,128]{1,0:T(8,128)(2,1)S(1)} %collective-permute-done.23.q3_ref), channel_id=1, source_target_pairs={{0,8},{8,0},{16,24},{24,16},{32,40},{40,32},{48,56},{56,48},{64,72... | collective-permute-start | bytes 221192 | tf_op jit(solution)/shard_map/ppermute | solution.py:38

commit v5 on v4

--- a/solution.py
+++ b/solution.py
@@ -32,6 +32,12 @@
 def rotate(value, axis, steps):
     count = lax.axis_size(axis)
     return lax.ppermute(value, axis, [(s, (s + steps) % count) for s in range(count)])
+
+
+def row_rotate(value, steps):
+    count = lax.axis_size("seq")
+    pairs = [(s, s // ROW * ROW + (s + steps) % ROW) for s in range(count)]
+    return lax.ppermute(value, "seq", pairs)
 
 
 def exchange(value, axis, bit):
@@ -372,11 +378,13 @@
 
 
 def columns_kernel(meta, mine_ref, peer_ref, *refs):
-    *piece_refs, cols_ref = refs
+    full_ref, *piece_refs, cols_ref = refs
     wins, rows, width = cols_ref.shape
     mine, peer = mine_ref[...], peer_ref[...]
     lower = jnp.where(meta[6] == 0, mine, peer)
     upper = jnp.where(meta[6] == 0, peer, mine)
+    full_ref[: rows // 2] = lower
+    full_ref[rows // 2 :] = upper
     for k in range(wins):
         cols_ref[k, : rows // 2] = lower[:, k * width : (k + 1) * width]
         cols_ref[k, rows // 2 :] = upper[:, k * width : (k + 1) * width]
@@ -384,16 +392,21 @@
         ref[...] = cols_ref[lax.rem(meta[5] + k, wins)]
 
 
-def finish_kernel(meta, q0_ref, q1_ref, q3_ref, q2_ref, state_ref, edge_ref, pay_ref):
-    here = meta[7]
-    quarter = q0_ref.shape[0]
-    flip = 1 - 2 * lax.rem(here, 2)
-    for ref, place in (
-        (q0_ref, here),
-        (q1_ref, here + flip),
-        (q3_ref, ROW - 1 - here),
-        (q2_ref, ROW - 1 - here - flip),
-    ):
+def last_kernel(done_ref, own_ref, *refs):
+    *came, all_ref = refs
+    direct = done_ref.shape[1]
+    all_ref[:, :direct] = done_ref[...]
+    total = own_ref[...]
+    for ref in came:
+        total = total + ref[...].astype(F32)
+    all_ref[:, direct:] = total.astype(BF16)
+
+
+def finish_kernel(meta, *refs):
+    *quarters, state_ref, edge_ref, pay_ref = refs
+    for k, ref in enumerate(quarters):
+        quarter = ref.shape[0]
+        place = lax.rem(meta[7] + ROW - k, ROW)
         start = pl.multiple_of(quarter_of(place) * quarter, EDGE_ROWS)
         pay_ref[pl.ds(start, quarter), :] = ref[...]
     rows = state_ref.shape[0]
@@ -415,6 +428,8 @@
     piece = rows // (wins * cores)
     seq, win, core = (lax.axis_index(a).astype(jnp.int32) for a in ("seq", "win", "wout"))
     meta = jnp.concatenate([lengths, jnp.stack([seq * rows, win, core, seq % ROW])])
+    direct = w_qkv.shape[1] // 3
+    gathered = lax.all_gather(w_qkv[:, :direct], "win", axis=0, tiled=True)
     x = qkv_in.transpose(1, 0, 2)
     halo = shift(x[:, rows - HALO :], "seq", 1)
     act, lead, parts, taps, beta = call(
@@ -508,37 +523,51 @@
         smem=0,
     )
     peer = rotate(normed, "wout", 1)
-    bits = [ROW << b for b in reversed(range((n_seq // ROW - 1).bit_length()))]
-    came = exchange(payload, "seq", bits[0])
-    cols = call(
+    lines = n_seq // ROW
+    bits = [b for b in (4, 2, 1) if 2 * b <= lines]
+    came = exchange(payload, "seq", bits[0] * ROW)
+    full, *cols = call(
         columns_kernel,
-        [out((2 * piece, model // wins), BF16)] * wins,
+        [out((2 * piece, model), BF16)] + [out((2 * piece, model // wins), BF16)] * wins,
         "columns",
         10**6,
         meta, normed, peer,
         scratch=[pltpu.VMEM((wins, 2 * piece, model // wins), BF16)],
     )
     blocks = [cols[0]] + [rotate(cols[k], "win", k) for k in range(1, wins)]
+    finished = jnp.dot(full, gathered, preferred_element_type=F32).astype(BF16)
+    finished, came = lax.optimization_barrier((finished, came))
     *blocks, payload = lax.optimization_barrier((*blocks, payload + came))
 
     def partial(k):
-        return jnp.dot(blocks[(wins - k) % wins], w_qkv, preferred_element_type=F32)
-
-    arrived = [rotate(partial(k).astype(BF16), "win", k) for k in range(1, wins)]
-    total = partial(0)
-    for part in arrived:
-        total = total + part.astype(F32)
-    projected = total.astype(BF16)
-
-    for bit in bits[1:]:
-        payload = payload + exchange(payload, "seq", bit)
-    across = exchange(payload, "seq", ROW - 1)
+        return jnp.dot(blocks[(wins - k) % wins], w_qkv[:, direct:], preferred_element_type=F32)
+
+    parts = [partial(k).astype(BF16) for k in range(1, wins)]
+    *parts, payload = lax.optimization_barrier((*parts, payload))
+    arrived = [rotate(part, "win", k + 1) for k, part in enumerate(parts)]
+    (projected,) = call(
+        last_kernel,
+        [out((2 * piece, w_qkv.shape[1]), BF16)],
+        "last",
+        10**10,
+        finished, partial(0), *arrived,
+        smem=0,
+    )
+
+    if lines == 8:
+        turns = [rotate(payload, "seq", steps * ROW) for steps in (1, 7, 2)]
+        payload = payload + (turns[0] + turns[1]) + turns[2]
+    else:
+        for bit in bits[1:]:
+            payload = payload + exchange(payload, "seq", bit * ROW)
+    quarters = [payload] + [row_rotate(payload, k) for k in range(1, ROW)]
+    projected, *quarters = lax.optimization_barrier((projected, *quarters))
     final_states, conv_edges = call(
         finish_kernel,
         [out((state_rows, DK), F32), out((CONV - 1, 3, REQS, width), BF16)],
         "finish",
         10**6,
-        meta, payload, exchange(payload, "seq", 1), across, exchange(across, "seq", 1),
+        meta, *quarters,
         scratch=[pltpu.VMEM((pay_rows, DK), BF16)],
     )
     final_states = final_states.reshape(REQS, heads, DK, DK)

time: 114 us -> 121 us (1.061); the launches traced: 113 us -> 121 us
  between operations: 0.88 us -> 14.3 us
  waiting for transfers between devices: 46.5 us -> 34.3 us
  starting transfers between devices: 45.5 us -> 48.5 us
  matrix products: 3.59 us -> 5.16 us
  local copies, waits for them, and re-layouts: 1.67 us -> 3.15 us
    ppermute x10 -> x5, waiting for transfers between devices: 35.7 us -> 18.3 us  [exchange(): lax.ppermute(value, axis, [(s, s ^ bit) for s in range(lax.axis_size(axis...]
    ppermute x11 -> x14, waiting for transfers between devices: 6.42 us -> 11.7 us  [rotate(): lax.ppermute(value, axis, [(s, (s + steps) % count) for s in range(count)])]
    ppermute x0 -> x3, starting transfers between devices: none -> 2.45 us  [row_rotate(): return lax.ppermute(value, 'seq', pairs)]
    slice x0 -> x1, local copies, waits for them, and re-layouts: none -> 2.29 us  [body(): gathered = lax.all_gather(w_qkv[:, :direct], 'win', axis=0, tiled=True)]
    ppermute x11 -> x14, starting transfers between devices: 10.5 us -> 12.8 us  [rotate(): lax.ppermute(value, axis, [(s, (s + steps) % count) for s in range(count)])]
    ppermute x10 -> x5, starting transfers between devices: 11.9 us -> 9.7 us  [exchange(): lax.ppermute(value, axis, [(s, s ^ bit) for s in range(lax.axis_size(axis...]
    dot_general x4 -> x5, matrix products: 3.59 us -> 5.16 us  [the longest x1 3.19 us: body(): finished = jnp.dot(full, gathered, preferred_element_type=F32).astype(BF16)]
    pallas_call x10 -> x11, Pallas kernels: 14.3 us -> 15.3 us  [call(): pl.pallas_call(kernel, out_shape=outs, in_specs=[SMEM] * smem + [HBM] * h...]
  transfers between devices with their start and end apart: 25 -> 27, of which waited for: 15 -> 13; matrix products, arithmetic and copies ran while one was open for 1% -> 4% of each run, Pallas kernels for 4% -> 11%
where the time goes in v5:
time: 121 us
  starting transfers between devices  48.5 us (40%)
  waiting for transfers between devices  34.3 us (28%)
  Pallas kernels  15.3 us (13%)
  between operations  14.3 us (12%)
  matrix products  5.16 us (4%)
  local copies, waits for them, and re-layouts  3.15 us (3%)
    ppermute x4, starting transfers between devices, shift(): lax.ppermute(value, axis, [(s, s + steps) for s in range(max(0, count - s...  23.6 us
    ppermute x5, waiting for transfers between devices, exchange(): lax.ppermute(value, axis, [(s, s ^ bit) for s in range(lax.axis_size(axis...  18.3 us
    pallas_call x11, Pallas kernels, call(): pl.pallas_call(kernel, out_shape=outs, in_specs=[SMEM] * smem + [HBM] * h...  15.3 us
    ppermute x14, starting transfers between devices, rotate(): lax.ppermute(value, axis, [(s, (s + steps) % count) for s in range(count)])  12.8 us
    ppermute x14, waiting for transfers between devices, rotate(): lax.ppermute(value, axis, [(s, (s + steps) % count) for s in range(count)])  11.7 us
    ppermute x5, starting transfers between devices, exchange(): lax.ppermute(value, axis, [(s, s ^ bit) for s in range(lax.axis_size(axis...  9.7 us
    ppermute x4, waiting for transfers between devices, shift(): lax.ppermute(value, axis, [(s, s + steps) for s in range(max(0, count - s...  4.39 us
    dot_general x1, matrix products, body(): finished = jnp.dot(full, gathered, preferred_element_type=F32).astype(BF16)  3.19 us
  transfers between devices with their start and end apart: 27, of which 13 were waited for; matrix products, arithmetic and copies ran while one was open for 4% of the time, Pallas kernels for 11%

profile of v5, /device:TPU:24, one launch (start us, length us, event | category | flops | bytes accessed | tf_op | source)
XLA Modules:
  0.0 120.8 jit_solution(17893079441598663256)
XLA Ops:
  7.2 2.3 %slice.13 = bf16[512,1024]{1,0:T(8,128)(2,1)} slice(bf16[512,3072]{1,0:T(8,128)(2,1)} %param.17), slice={[0:512], [0:1024]} | slice | bytes 2097152 | tf_op jit(solution)/shard_map/slice | solution.py:432
  9.5 0.7 slice.15
  10.3 3.4 %collective-permute-start = (bf16[3,16,256]{2,1,0:T(8,128)(2,1)S(1)}, bf16[3,16,256]{2,1,0:T(8,128)(2,1)S(1)}, u32[]{:S(2)}, u32[]{:S(2)}) collective-permute-start(bf16[3,16,256]{2,1,0:T(8,128)(2,1)S(1)} %slice.15), channel_id=1, source_target_pairs={{0,8},{8,16},{16,24},{24,32},{32,40},{40,48},{48,56},{56,64},{64,7... | collective-permute-start | bytes 73736 | tf_op jit(solution)/shard_map/ppermute | solution.py:29
  13.8 2.4 %conv.1 = (bf16[3,256,256]{2,1,0:T(8,128)(2,1)S(1)}, bf16[3,16,256]{2,1,0:T(8,128)(2,1)S(1)}, bf16[3,16,256]{2,1,0:T(8,128)(2,1)S(1)}, f32[3,4,256]{2,1,0:T(4,128)S(1)}, f32[2,256]{1,0:T(2,128)S(1)}) custom-call(s32[8]{0:T(128)S(1)} %concatenate.3.meta, bf16[3,256,256]{2,1,0:T(8,128)(2,1)} %bitcast.18, f32[3,4,256]{2,1,0:T(4,128)} %taps_hbm.1, f32[2,256]{1,0:T(2,128)} %beta_hbm.1), custom_call_target="tpu_custom_call" | custom-call | flops 100000000 | bytes 864288 | tf_op jit(solution)/shard_map/conv/pallas_call | solution.py:70
  16.3 4.9 %prep.1 = (bf16[2,128,256]{2,1,0:T(8,128)(2,1)S(1)}, f32[2,256,256]{2,1,0:T(8,128)S(1)}, f32[2,256,128]{2,1,0:T(8,128)S(1)}, f32[2,256,128]{2,1,0:T(8,128)S(1)},...) custom-call(s32[8]{0:T(128)S(1)} %concatenate.3.meta, ...), custom_call_target="tpu_custom_call" | custom-call | flops 2000000000 | bytes 1818656 | tf_op jit(solution)/shard_map/prep/pallas_call | solution.py:70
  21.1 1.6 %collective-permute-start.1 = (bf16[2,128,256]{2,1,0:T(8,128)(2,1)S(1)}, bf16[2,128,256]{2,1,0:T(8,128)(2,1)S(1)}, u32[]{:S(2)}, u32[]{:S(2)}) collective-permute-start(bf16[2,128,256]{2,1,0:T(8,128)(2,1)S(1)} %get-tuple-element.61.own_ref), channel_id=1, source_target_pairs={{0,8},{8,0},{16,24},{24,16},{32,40},{40,32},{48,56},{56,48},{64,72... | collective-permute-start | bytes 393224 | tf_op jit(solution)/shard_map/ppermute | solution.py:44
  22.7 3.5 %collective-permute-done.1.came_ref = bf16[2,128,256]{2,1,0:T(8,128)(2,1)S(1)} collective-permute-done((bf16[2,128,256]{2,1,0:T(8,128)(2,1)S(1)}, bf16[2,128,256]{2,1,0:T(8,128)(2,1)S(1)}, u32[]{:S(2)}, u32[]{:S(2)}) %collective-permute-start.1) | collective-permute-done | bytes 131104 | tf_op jit(solution)/shard_map/ppermute | solution.py:44
  26.2 0.7 twin.1.twin_ref
  26.9 3.2 %collective-permute-start.2 = (bf16[2,128,256]{2,1,0:T(8,128)(2,1)S(1)}, bf16[2,128,256]{2,1,0:T(8,128)(2,1)S(1)}, u32[]{:S(2)}, u32[]{:S(2)}) collective-permute-start(bf16[2,128,256]{2,1,0:T(8,128)(2,1)S(1)} %twin.1.twin_ref), channel_id=1, source_target_pairs={{0,24},{8,16},{16,8},{24,0},{32,56},{40,48},{48,40},{56,32},{64,88... | collective-permute-start | bytes 393224 | tf_op jit(solution)/shard_map/ppermute | solution.py:44
  30.1 3.1 %collective-permute-done.2.other_ref = bf16[2,128,256]{2,1,0:T(8,128)(2,1)S(1)} collective-permute-done((bf16[2,128,256]{2,1,0:T(8,128)(2,1)S(1)}, bf16[2,128,256]{2,1,0:T(8,128)(2,1)S(1)}, u32[]{:S(2)}, u32[]{:S(2)}) %collective-permute-start.2) | collective-permute-done | bytes 131104 | tf_op jit(solution)/shard_map/ppermute | solution.py:44
  33.2 0.8 row.1
  34.0 5.7 %collective-permute-start.3 = (bf16[2,128,256]{2,1,0:T(8,128)(2,1)S(1)}, bf16[2,128,256]{2,1,0:T(8,128)(2,1)S(1)}, u32[]{:S(2)}, u32[]{:S(2)}) collective-permute-start(bf16[2,128,256]{2,1,0:T(8,128)(2,1)S(1)} %get-tuple-element.63.total_ref), channel_id=1, source_target_pairs={{0,32},{8,40},{16,48},{24,56},{32,64},{40,72},{48,80},{56,88},{64,... | collective-permute-start | bytes 393224 | tf_op jit(solution)/shard_map/ppermute | solution.py:29
  39.7 2.5 %collective-permute-done.3.near_ref = bf16[2,128,256]{2,1,0:T(8,128)(2,1)S(1)} collective-permute-done((bf16[2,128,256]{2,1,0:T(8,128)(2,1)S(1)}, bf16[2,128,256]{2,1,0:T(8,128)(2,1)S(1)}, u32[]{:S(2)}, u32[]{:S(2)}) %collective-permute-start.3) | collective-permute-done | bytes 131104 | tf_op jit(solution)/shard_map/ppermute | solution.py:29
  42.1 0.2 join.1
  42.3 4.4 %collective-permute-start.4 = (bf16[2,128,256]{2,1,0:T(8,128)(2,1)S(1)}, bf16[2,128,256]{2,1,0:T(8,128)(2,1)S(1)}, u32[]{:S(2)}, u32[]{:S(2)}) collective-permute-start(bf16[2,128,256]{2,1,0:T(8,128)(2,1)S(1)} %get-tuple-element.64), channel_id=1, source_target_pairs={{0,32},{8,40},{16,48},{24,56},{32,64},{40,72},{48,80},{56,88},{64,... | collective-permute-start | bytes 393224 | tf_op jit(solution)/shard_map/ppermute | solution.py:29
  46.7 10.2 %collective-permute-start.5 = (bf16[2,128,128]{2,1,0:T(8,128)(2,1)S(1)}, bf16[2,128,128]{2,1,0:T(8,128)(2,1)S(1)}, u32[]{:S(2)}, u32[]{:S(2)}) collective-permute-start(bf16[2,128,128]{2,1,0:T(8,128)(2,1)S(1)} %get-tuple-element.65), channel_id=1, source_target_pairs={{0,96},{8,104},{16,112},{24,120},{32,128},{40,136},{48,144},{56,15... | collective-permute-start | bytes 196616 | tf_op jit(solution)/shard_map/ppermute | solution.py:29
  56.9 1.9 %collective-permute-done.5.tail_ref = bf16[2,128,128]{2,1,0:T(8,128)(2,1)S(1)} collective-permute-done((bf16[2,128,128]{2,1,0:T(8,128)(2,1)S(1)}, bf16[2,128,128]{2,1,0:T(8,128)(2,1)S(1)}, u32[]{:S(2)}, u32[]{:S(2)}) %collective-permute-start.5) | collective-permute-done | bytes 65568 | tf_op jit(solution)/shard_map/ppermute | solution.py:29
  58.8 2.5 %attend.1 = (f32[128,2048]{1,0:T(8,128)S(1)}, bf16[128,2048]{1,0:T(8,128)(2,1)S(1)}, bf16[576,128]{1,0:T(8,128)(2,1)S(1)}, bf16[576,128]{1,0:T(8,128)(2,1)S(1)}) custom-call(s32[8]{0:T(128)S(1)} %concatenate.3.meta, f32[2,128,256]{2,1,0:T(8,128)S(1)} %get-tuple-element.62.prefix_ref, bf16[2,128,256]{2,1,0:T(8,128)(2,1)S(1)} %collective-permute-done.4.wide_ref, ...), custom_call_target="tpu_custom_call" | custom-call | flops 1000000000 | bytes 4581920 | tf_op jit(solution)/shard_map/attend/pallas_call | solution.py:70
  61.4 6.2 %collective-permute-done.7.came_ref = bf16[576,128]{1,0:T(8,128)(2,1)S(1)} collective-permute-done((bf16[576,128]{1,0:T(8,128)(2,1)S(1)}, bf16[576,128]{1,0:T(8,128)(2,1)S(1)}, u32[]{:S(2)}, u32[]{:S(2)}) %collective-permute-start.7) | collective-permute-done | bytes 147488 | tf_op jit(solution)/shard_map/ppermute | solution.py:44
  67.8 1.3 %collective-permute-start.10 = (bf16[32,2048]{1,0:T(8,128)(2,1)S(1)}, bf16[32,2048]{1,0:T(8,128)(2,1)S(1)}, u32[]{:S(2)}, u32[]{:S(2)}) collective-permute-start(bf16[32,2048]{1,0:T(8,128)(2,1)S(1)} %get-tuple-element.80), channel_id=1, source_target_pairs={{0,4},{2,6},{4,0},{6,2},{1,5},{3,7},{5,1},{7,3},{8,12},{10,14},{12... | collective-permute-start | bytes 393224 | tf_op jit(solution)/shard_map/ppermute | solution.py:34
  69.1 3.2 %collective-permute-start.9 = (bf16[32,2048]{1,0:T(8,128)(2,1)S(1)}, bf16[32,2048]{1,0:T(8,128)(2,1)S(1)}, u32[]{:S(2)}, u32[]{:S(2)}) collective-permute-start(bf16[32,2048]{1,0:T(8,128)(2,1)S(1)} %get-tuple-element.79), channel_id=1, source_target_pairs={{0,2},{2,4},{4,6},{6,0},{1,3},{3,5},{5,7},{7,1},{8,10},{10,12},{12... | collective-permute-start | bytes 393224 | tf_op jit(solution)/shard_map/ppermute | solution.py:34
  72.3 5.6 %collective-permute-done.8.came_ref = bf16[288,128]{1,0:T(8,128)(2,1)S(1)} collective-permute-done((bf16[288,128]{1,0:T(8,128)(2,1)S(1)}, bf16[288,128]{1,0:T(8,128)(2,1)S(1)}, u32[]{:S(2)}, u32[]{:S(2)}) %collective-permute-start.8) | collective-permute-done | bytes 73760 | tf_op jit(solution)/shard_map/ppermute | solution.py:44
  77.9 0.8 norm.1
  78.7 4.8 %collective-permute-start.13 = (bf16[288,128]{1,0:T(8,128)(2,1)S(1)}, bf16[288,128]{1,0:T(8,128)(2,1)S(1)}, u32[]{:S(2)}, u32[]{:S(2)}) collective-permute-start(bf16[288,128]{1,0:T(8,128)(2,1)S(1)} %get-tuple-element.84), channel_id=1, source_target_pairs={{0,128},{8,136},{16,144},{24,152},{32,160},{40,168},{48,176},{56,1... | collective-permute-start | bytes 221192 | tf_op jit(solution)/shard_map/ppermute | solution.py:44
  83.5 0.6 columns.1
  84.1 1.0 collective-permute-start.14
  85.2 1.1 collective-permute-start.15
  86.3 0.4 collective-permute-start.16
  86.7 3.2 %convolution_convert_fusion.3.done_ref = bf16[64,1024]{1,0:T(8,128)(2,1)S(1)} fusion(bf16[64,2048]{1,0:T(8,128)(2,1)S(1)} %get-tuple-element.83, bf16[2048,1024]{1,0:T(8,128)(2,1)} %all-gather.2.cloned.1.call-done), kind=kOutput, calls=%fused_computation.8 | convolution fusion | flops 268500992 | bytes 4587520 | tf_op jit(solution)/shard_map/dot_general | solution.py:538
  90.0 1.4 %collective-permute-done.15 = bf16[64,512]{1,0:T(8,128)(2,1)S(1)} collective-permute-done((bf16[64,512]{1,0:T(8,128)(2,1)S(1)}, bf16[64,512]{1,0:T(8,128)(2,1)S(1)}, u32[]{:S(2)}, u32[]{:S(2)}) %collective-permute-start.15) | collective-permute-done | bytes 65568 | tf_op jit(solution)/shard_map/ppermute | solution.py:34
  91.4 0.7 collective-permute-done.16
  92.0 0.5 convolution_convert_fusion
  92.5 0.5 convolution_convert_fusion.1
  93.0 0.5 convolution_convert_fusion.2
  93.6 3.2 %collective-permute-start.21 = (bf16[288,128]{1,0:T(8,128)(2,1)S(1)}, bf16[288,128]{1,0:T(8,128)(2,1)S(1)}, u32[]{:S(2)}, u32[]{:S(2)}) collective-permute-start(bf16[288,128]{1,0:T(8,128)(2,1)S(1)} %add.17), channel_id=1, source_target_pairs={{0,224},{8,232},{16,240},{24,248},{32,0},{40,8},{48,16},{56,24},{6... | collective-permute-start | bytes 221192 | tf_op jit(solution)/shard_map/ppermute | solution.py:34
  96.8 1.1 collective-permute-start.17
  98.0 0.9 collective-permute-start.18
  98.9 0.8 collective-permute-done.20
  99.9 0.5 fusion.3.own_ref
  100.4 3.2 %collective-permute-done.22 = bf16[288,128]{1,0:T(8,128)(2,1)S(1)} collective-permute-done((bf16[288,128]{1,0:T(8,128)(2,1)S(1)}, bf16[288,128]{1,0:T(8,128)(2,1)S(1)}, u32[]{:S(2)}, u32[]{:S(2)}) %collective-permute-start.22) | collective-permute-done | bytes 73760 | tf_op jit(solution)/shard_map/ppermute | solution.py:34
  103.7 0.3 collective-permute-start.23
  104.0 1.3 %collective-permute-start.24 = (bf16[288,128]{1,0:T(8,128)(2,1)S(1)}, bf16[288,128]{1,0:T(8,128)(2,1)S(1)}, u32[]{:S(2)}, u32[]{:S(2)}) collective-permute-start(bf16[288,128]{1,0:T(8,128)(2,1)S(1)} %add_add_fusion.refs_0_), channel_id=1, source_target_pairs={{0,16},{8,24},{16,0},{24,8},{32,48},{40,56},{48,32},{56,40},{64,80... | collective-permute-start | bytes 221192 | tf_op jit(solution)/shard_map/ppermute | solution.py:40
  105.2 0.9 collective-permute-done.17.refs_0_
  106.1 0.9 collective-permute-start.25
  107.0 1.8 %collective-permute-done.18.refs_1_ = bf16[64,2048]{1,0:T(8,128)(2,1)S(1)} collective-permute-done((bf16[64,2048]{1,0:T(8,128)(2,1)S(1)}, bf16[64,2048]{1,0:T(8,128)(2,1)S(1)}, u32[]{:S(2)}, u32[]{:S(2)}) %collective-permute-start.18) | collective-permute-done | bytes 262176 | tf_op jit(solution)/shard_map/ppermute | solution.py:34
  108.8 2.9 %collective-permute-done.19.refs_2_ = bf16[64,2048]{1,0:T(8,128)(2,1)S(1)} collective-permute-done((bf16[64,2048]{1,0:T(8,128)(2,1)S(1)}, bf16[64,2048]{1,0:T(8,128)(2,1)S(1)}, u32[]{:S(2)}, u32[]{:S(2)}) %collective-permute-start.19) | collective-permute-done | bytes 262176 | tf_op jit(solution)/shard_map/ppermute | solution.py:34
  111.6 0.9 last.1
  112.5 1.4 %finish.1 = (f32[1024,128]{1,0:T(8,128)}, bf16[3,3,4,256]{3,2,1,0:T(4,128)(2,1)}) custom-call(s32[8]{0:T(128)S(1)} %concatenate.3.meta, bf16[288,128]{1,0:T(8,128)(2,1)S(1)} %add_add_fusion.refs_0_, bf16[288,128]{1,0:T(8,128)(2,1)S(1)} %collective-permute-done.23.refs_1_, bf16[288,128]{1,0:T(8,128)(2,1)S(1)} %collective-permute-done.24.refs_2_, ...), custom_call_target="tpu_custom_call" | custom-call | flops 1000000 | bytes 837664 | tf_op jit(solution)/shard_map/finish/pallas_call | solution.py:70
  (40 shorter events, 0.8 us)
Async XLA Ops:
  7.2 6.5 %copy-start.5 = (s32[4]{0:T(128)S(1)}, s32[4]{0:T(128)}, u32[]{:S(2)}) copy-start(s32[4]{0:T(128)} %param.12) | copy-start | bytes 52
  7.2 79.5 %all-gather.2.cloned.1.call-start = ((), (), s32[]{:S(2)}) async-start(), calls=%async_computation | async-start | bytes 5242880 | tf_op jit(solution)/shard_map/all_gather | solution.py:432
  10.3 6.0 %collective-permute-start = (bf16[3,16,256]{2,1,0:T(8,128)(2,1)S(1)}, bf16[3,16,256]{2,1,0:T(8,128)(2,1)S(1)}, u32[]{:S(2)}, u32[]{:S(2)}) collective-permute-start(bf16[3,16,256]{2,1,0:T(8,128)(2,1)S(1)} %slice.15), channel_id=1, source_target_pairs={{0,8},{8,16},{16,24},{24,32},{32,40},{40,48},{48,56},{56,64},{64,7... | collective-permute-start | bytes 73736 | tf_op jit(solution)/shard_map/ppermute | solution.py:29
  16.2 42.5 %copy-start.2 = (bf16[256,2048]{1,0:T(8,128)(2,1)S(1)}, bf16[256,2048]{1,0:T(8,128)(2,1)}, u32[]{:S(2)}) copy-start(bf16[256,2048]{1,0:T(8,128)(2,1)} %w_ref.1) | copy-start | bytes 3145732
  16.3 42.5 %copy-start.3 = (f32[128]{0:T(128)S(1)}, f32[128]{0:T(128)}, u32[]{:S(2)}) copy-start(f32[128]{0:T(128)} %param.13) | copy-start | bytes 1540
  21.1 5.1 %collective-permute-start.1 = (bf16[2,128,256]{2,1,0:T(8,128)(2,1)S(1)}, bf16[2,128,256]{2,1,0:T(8,128)(2,1)S(1)}, u32[]{:S(2)}, u32[]{:S(2)}) collective-permute-start(bf16[2,128,256]{2,1,0:T(8,128)(2,1)S(1)} %get-tuple-element.61.own_ref), channel_id=1, source_target_pairs={{0,8},{8,0},{16,24},{24,16},{32,40},{40,32},{48,56},{56,48},{64,72... | collective-permute-start | bytes 393224 | tf_op jit(solution)/shard_map/ppermute | solution.py:44
  26.9 51.0 %copy-start = (bf16[32,2048]{1,0:T(8,128)(2,1)S(1)}, bf16[32,2048]{1,0:T(8,128)(2,1)}, u32[]{:S(2)}) copy-start(bf16[32,2048]{1,0:T(8,128)(2,1)} %hidden_ref.1) | copy-start | bytes 393220
  26.9 51.0 %copy-start.1 = (f32[2048]{0:T(1024)S(1)}, f32[2048]{0:T(1024)}, u32[]{:S(2)}) copy-start(f32[2048]{0:T(1024)} %param.16) | copy-start | bytes 24580
  26.9 6.3 %collective-permute-start.2 = (bf16[2,128,256]{2,1,0:T(8,128)(2,1)S(1)}, bf16[2,128,256]{2,1,0:T(8,128)(2,1)S(1)}, u32[]{:S(2)}, u32[]{:S(2)}) collective-permute-start(bf16[2,128,256]{2,1,0:T(8,128)(2,1)S(1)} %twin.1.twin_ref), channel_id=1, source_target_pairs={{0,24},{8,16},{16,8},{24,0},{32,56},{40,48},{48,40},{56,32},{64,88... | collective-permute-start | bytes 393224 | tf_op jit(solution)/shard_map/ppermute | solution.py:44
  34.0 8.2 %collective-permute-start.3 = (bf16[2,128,256]{2,1,0:T(8,128)(2,1)S(1)}, bf16[2,128,256]{2,1,0:T(8,128)(2,1)S(1)}, u32[]{:S(2)}, u32[]{:S(2)}) collective-permute-start(bf16[2,128,256]{2,1,0:T(8,128)(2,1)S(1)} %get-tuple-element.63.total_ref), channel_id=1, source_target_pairs={{0,32},{8,40},{16,48},{24,56},{32,64},{40,72},{48,80},{56,88},{64,... | collective-permute-start | bytes 393224 | tf_op jit(solution)/shard_map/ppermute | solution.py:29
  42.3 16.4 %collective-permute-start.4 = (bf16[2,128,256]{2,1,0:T(8,128)(2,1)S(1)}, bf16[2,128,256]{2,1,0:T(8,128)(2,1)S(1)}, u32[]{:S(2)}, u32[]{:S(2)}) collective-permute-start(bf16[2,128,256]{2,1,0:T(8,128)(2,1)S(1)} %get-tuple-element.64), channel_id=1, source_target_pairs={{0,32},{8,40},{16,48},{24,56},{32,64},{40,72},{48,80},{56,88},{64,... | collective-permute-start | bytes 393224 | tf_op jit(solution)/shard_map/ppermute | solution.py:29
  46.7 12.0 %collective-permute-start.5 = (bf16[2,128,128]{2,1,0:T(8,128)(2,1)S(1)}, bf16[2,128,128]{2,1,0:T(8,128)(2,1)S(1)}, u32[]{:S(2)}, u32[]{:S(2)}) collective-permute-start(bf16[2,128,128]{2,1,0:T(8,128)(2,1)S(1)} %get-tuple-element.65), channel_id=1, source_target_pairs={{0,96},{8,104},{16,112},{24,120},{32,128},{40,136},{48,144},{56,15... | collective-permute-start | bytes 196616 | tf_op jit(solution)/shard_map/ppermute | solution.py:29
  61.2 6.4 %collective-permute-start.6 = (bf16[128,2048]{1,0:T(8,128)(2,1)S(1)}, bf16[128,2048]{1,0:T(8,128)(2,1)S(1)}, u32[]{:S(2)}, u32[]{:S(2)}) collective-permute-start(bf16[128,2048]{1,0:T(8,128)(2,1)S(1)} %get-tuple-element.73), channel_id=1, source_target_pairs={{0,1},{1,0},{2,3},{3,2},{4,5},{5,4},{6,7},{7,6},{8,9},{9,8},{10,11... | collective-permute-start | bytes 1572872 | tf_op jit(solution)/shard_map/ppermute | solution.py:34
  61.3 6.3 %collective-permute-start.7 = (bf16[576,128]{1,0:T(8,128)(2,1)S(1)}, bf16[576,128]{1,0:T(8,128)(2,1)S(1)}, u32[]{:S(2)}, u32[]{:S(2)}) collective-permute-start(bf16[576,128]{1,0:T(8,128)(2,1)S(1)} %get-tuple-element.75), channel_id=1, source_target_pairs={{0,8},{8,0},{16,24},{24,16},{32,40},{40,32},{48,56},{56,48},{64,72... | collective-permute-start | bytes 442376 | tf_op jit(solution)/shard_map/ppermute | solution.py:44
  67.8 10.1 %collective-permute-start.10 = (bf16[32,2048]{1,0:T(8,128)(2,1)S(1)}, bf16[32,2048]{1,0:T(8,128)(2,1)S(1)}, u32[]{:S(2)}, u32[]{:S(2)}) collective-permute-start(bf16[32,2048]{1,0:T(8,128)(2,1)S(1)} %get-tuple-element.80), channel_id=1, source_target_pairs={{0,4},{2,6},{4,0},{6,2},{1,5},{3,7},{5,1},{7,3},{8,12},{10,14},{12... | collective-permute-start | bytes 393224 | tf_op jit(solution)/shard_map/ppermute | solution.py:34
  69.1 8.8 %collective-permute-start.11 = (bf16[32,2048]{1,0:T(8,128)(2,1)S(1)}, bf16[32,2048]{1,0:T(8,128)(2,1)S(1)}, u32[]{:S(2)}, u32[]{:S(2)}) collective-permute-start(bf16[32,2048]{1,0:T(8,128)(2,1)S(1)} %get-tuple-element.81), channel_id=1, source_target_pairs={{0,6},{2,0},{4,2},{6,4},{1,7},{3,1},{5,3},{7,5},{8,14},{10,8},{12,... | collective-permute-start | bytes 393224 | tf_op jit(solution)/shard_map/ppermute | solution.py:34
  69.1 8.8 %collective-permute-start.9 = (bf16[32,2048]{1,0:T(8,128)(2,1)S(1)}, bf16[32,2048]{1,0:T(8,128)(2,1)S(1)}, u32[]{:S(2)}, u32[]{:S(2)}) collective-permute-start(bf16[32,2048]{1,0:T(8,128)(2,1)S(1)} %get-tuple-element.79), channel_id=1, source_target_pairs={{0,2},{2,4},{4,6},{6,0},{1,3},{3,5},{5,7},{7,1},{8,10},{10,12},{12... | collective-permute-start | bytes 393224 | tf_op jit(solution)/shard_map/ppermute | solution.py:34
  72.3 5.6 %collective-permute-start.8 = (bf16[288,128]{1,0:T(8,128)(2,1)S(1)}, bf16[288,128]{1,0:T(8,128)(2,1)S(1)}, u32[]{:S(2)}, u32[]{:S(2)}) collective-permute-start(bf16[288,128]{1,0:T(8,128)(2,1)S(1)} %get-tuple-element.77), channel_id=1, source_target_pairs={{0,24},{8,16},{16,8},{24,0},{32,56},{40,48},{48,40},{56,32},{64,88... | collective-permute-start | bytes 221192 | tf_op jit(solution)/shard_map/ppermute | solution.py:44
  78.7 4.8 %collective-permute-start.12 = (bf16[32,2048]{1,0:T(8,128)(2,1)S(1)}, bf16[32,2048]{1,0:T(8,128)(2,1)S(1)}, u32[]{:S(2)}, u32[]{:S(2)}) collective-permute-start(bf16[32,2048]{1,0:T(8,128)(2,1)S(1)} %get-tuple-element.82.mine_ref), channel_id=1, source_target_pairs={{0,1},{1,0},{2,3},{3,2},{4,5},{5,4},{6,7},{7,6},{8,9},{9,8},{10,11... | collective-permute-start | bytes 393224 | tf_op jit(solution)/shard_map/ppermute | solution.py:34
  78.7 11.2 %collective-permute-start.13 = (bf16[288,128]{1,0:T(8,128)(2,1)S(1)}, bf16[288,128]{1,0:T(8,128)(2,1)S(1)}, u32[]{:S(2)}, u32[]{:S(2)}) collective-permute-start(bf16[288,128]{1,0:T(8,128)(2,1)S(1)} %get-tuple-element.84), channel_id=1, source_target_pairs={{0,128},{8,136},{16,144},{24,152},{32,160},{40,168},{48,176},{56,1... | collective-permute-start | bytes 221192 | tf_op jit(solution)/shard_map/ppermute | solution.py:44
  84.1 5.8 %collective-permute-start.14 = (bf16[64,512]{1,0:T(8,128)(2,1)S(1)}, bf16[64,512]{1,0:T(8,128)(2,1)S(1)}, u32[]{:S(2)}, u32[]{:S(2)}) collective-permute-start(bf16[64,512]{1,0:T(8,128)(2,1)S(1)} %get-tuple-element.87), channel_id=1, source_target_pairs={{0,2},{2,4},{4,6},{6,0},{1,3},{3,5},{5,7},{7,1},{8,10},{10,12},{12... | collective-permute-start | bytes 196616 | tf_op jit(solution)/shard_map/ppermute | solution.py:34
  85.2 6.2 %collective-permute-start.15 = (bf16[64,512]{1,0:T(8,128)(2,1)S(1)}, bf16[64,512]{1,0:T(8,128)(2,1)S(1)}, u32[]{:S(2)}, u32[]{:S(2)}) collective-permute-start(bf16[64,512]{1,0:T(8,128)(2,1)S(1)} %get-tuple-element.88), channel_id=1, source_target_pairs={{0,4},{2,6},{4,0},{6,2},{1,5},{3,7},{5,1},{7,3},{8,12},{10,14},{12... | collective-permute-start | bytes 196616 | tf_op jit(solution)/shard_map/ppermute | solution.py:34
  86.3 5.7 %collective-permute-start.16 = (bf16[64,512]{1,0:T(8,128)(2,1)S(1)}, bf16[64,512]{1,0:T(8,128)(2,1)S(1)}, u32[]{:S(2)}, u32[]{:S(2)}) collective-permute-start(bf16[64,512]{1,0:T(8,128)(2,1)S(1)} %get-tuple-element.89), channel_id=1, source_target_pairs={{0,6},{2,0},{4,2},{6,4},{1,7},{3,1},{5,3},{7,5},{8,14},{10,8},{12,... | collective-permute-start | bytes 196616 | tf_op jit(solution)/shard_map/ppermute | solution.py:34
  86.7 5.3 %copy-start.4 = (bf16[512,3072]{1,0:T(8,128)(2,1)S(1)}, bf16[512,3072]{1,0:T(8,128)(2,1)}, u32[]{:S(2)}) copy-start(bf16[512,3072]{1,0:T(8,128)(2,1)} %param.17) | copy-start | bytes 9437188
  93.5 6.2 %collective-permute-start.20 = (bf16[288,128]{1,0:T(8,128)(2,1)S(1)}, bf16[288,128]{1,0:T(8,128)(2,1)S(1)}, u32[]{:S(2)}, u32[]{:S(2)}) collective-permute-start(bf16[288,128]{1,0:T(8,128)(2,1)S(1)} %add.17), channel_id=1, source_target_pairs={{0,32},{8,40},{16,48},{24,56},{32,64},{40,72},{48,80},{56,88},{64,... | collective-permute-start | bytes 221192 | tf_op jit(solution)/shard_map/ppermute | solution.py:34
  93.6 6.8 %collective-permute-start.21 = (bf16[288,128]{1,0:T(8,128)(2,1)S(1)}, bf16[288,128]{1,0:T(8,128)(2,1)S(1)}, u32[]{:S(2)}, u32[]{:S(2)}) collective-permute-start(bf16[288,128]{1,0:T(8,128)(2,1)S(1)} %add.17), channel_id=1, source_target_pairs={{0,224},{8,232},{16,240},{24,248},{32,0},{40,8},{48,16},{56,24},{6... | collective-permute-start | bytes 221192 | tf_op jit(solution)/shard_map/ppermute | solution.py:34
  96.8 6.8 %collective-permute-start.22 = (bf16[288,128]{1,0:T(8,128)(2,1)S(1)}, bf16[288,128]{1,0:T(8,128)(2,1)S(1)}, u32[]{:S(2)}, u32[]{:S(2)}) collective-permute-start(bf16[288,128]{1,0:T(8,128)(2,1)S(1)} %add.17), channel_id=1, source_target_pairs={{0,64},{8,72},{16,80},{24,88},{32,96},{40,104},{48,112},{56,120},{... | collective-permute-start | bytes 221192 | tf_op jit(solution)/shard_map/ppermute | solution.py:34
  96.8 9.2 %collective-permute-start.17 = (bf16[64,2048]{1,0:T(8,128)(2,1)S(1)}, bf16[64,2048]{1,0:T(8,128)(2,1)S(1)}, u32[]{:S(2)}, u32[]{:S(2)}) collective-permute-start(bf16[64,2048]{1,0:T(8,128)(2,1)S(1)} %convolution_convert_fusion.2), channel_id=1, source_target_pairs={{0,2},{2,4},{4,6},{6,0},{1,3},{3,5},{5,7},{7,1},{8,10},{10,12},{12... | collective-permute-start | bytes 786440 | tf_op jit(solution)/shard_map/ppermute | solution.py:34
  98.0 10.8 %collective-permute-start.18 = (bf16[64,2048]{1,0:T(8,128)(2,1)S(1)}, bf16[64,2048]{1,0:T(8,128)(2,1)S(1)}, u32[]{:S(2)}, u32[]{:S(2)}) collective-permute-start(bf16[64,2048]{1,0:T(8,128)(2,1)S(1)} %convolution_convert_fusion.1), channel_id=1, source_target_pairs={{0,4},{2,6},{4,0},{6,2},{1,5},{3,7},{5,1},{7,3},{8,12},{10,14},{12... | collective-permute-start | bytes 786440 | tf_op jit(solution)/shard_map/ppermute | solution.py:34
  99.7 11.9 %collective-permute-start.19 = (bf16[64,2048]{1,0:T(8,128)(2,1)S(1)}, bf16[64,2048]{1,0:T(8,128)(2,1)S(1)}, u32[]{:S(2)}, u32[]{:S(2)}) collective-permute-start(bf16[64,2048]{1,0:T(8,128)(2,1)S(1)} %convolution_convert_fusion), channel_id=1, source_target_pairs={{0,6},{2,0},{4,2},{6,4},{1,7},{3,1},{5,3},{7,5},{8,14},{10,8},{12,... | collective-permute-start | bytes 786440 | tf_op jit(solution)/shard_map/ppermute | solution.py:34
  103.7 8.8 %collective-permute-start.23 = (bf16[288,128]{1,0:T(8,128)(2,1)S(1)}, bf16[288,128]{1,0:T(8,128)(2,1)S(1)}, u32[]{:S(2)}, u32[]{:S(2)}) collective-permute-start(bf16[288,128]{1,0:T(8,128)(2,1)S(1)} %add_add_fusion.refs_0_), channel_id=1, source_target_pairs={{0,8},{8,16},{16,24},{24,0},{32,40},{40,48},{48,56},{56,32},{64,72... | collective-permute-start | bytes 221192 | tf_op jit(solution)/shard_map/ppermute | solution.py:40
  104.0 8.6 %collective-permute-start.24 = (bf16[288,128]{1,0:T(8,128)(2,1)S(1)}, bf16[288,128]{1,0:T(8,128)(2,1)S(1)}, u32[]{:S(2)}, u32[]{:S(2)}) collective-permute-start(bf16[288,128]{1,0:T(8,128)(2,1)S(1)} %add_add_fusion.refs_0_), channel_id=1, source_target_pairs={{0,16},{8,24},{16,0},{24,8},{32,48},{40,56},{48,32},{56,40},{64,80... | collective-permute-start | bytes 221192 | tf_op jit(solution)/shard_map/ppermute | solution.py:40
  106.1 6.4 %collective-permute-start.25 = (bf16[288,128]{1,0:T(8,128)(2,1)S(1)}, bf16[288,128]{1,0:T(8,128)(2,1)S(1)}, u32[]{:S(2)}, u32[]{:S(2)}) collective-permute-start(bf16[288,128]{1,0:T(8,128)(2,1)S(1)} %add_add_fusion.refs_0_), channel_id=1, source_target_pairs={{0,24},{8,0},{16,8},{24,16},{32,56},{40,32},{48,40},{56,48},{64,88... | collective-permute-start | bytes 221192 | tf_op jit(solution)/shard_map/ppermute | solution.py:40
Sparse Core Ops, SparseCore 0:
  9.8 51.7 all-gather.1

commit v6 on v5

--- a/solution.py
+++ b/solution.py
@@ -275,23 +275,25 @@
         twin_ref[h] = joined(newer, older).astype(BF16)
 
 
-def row_kernel(meta, own_ref, came_ref, twin_ref, other_ref, prefix_ref, total_ref):
+def row_kernel(
+    meta, own_ref, came_ref, twin_ref, other_ref, below_ref, cross_ref,
+    prefix_ref, both_ref, tail_ref,
+):
     here = meta[7]
     late = here >= ROW // 2
     odd = lax.rem(here, 2) == 1
     for h in range(own_ref.shape[0]):
-        twin, other = twin_ref[h], other_ref[h]
-        older = jnp.where(late, other, twin)
-        total_ref[h] = joined(jnp.where(late, twin, other), older).astype(BF16)
-        step = jnp.where(odd, came_ref[h], jnp.zeros_like(twin))
-        prefix_ref[h] = joined(step, jnp.where(late, other, jnp.zeros_like(twin)))
-
-
-def join_kernel(total_ref, near_ref, both_ref, tail_ref):
-    for h in range(total_ref.shape[0]):
-        both = joined(total_ref[h], near_ref[h]).astype(BF16)
+        totals = []
+        for same_ref, far_ref in ((twin_ref, other_ref), (below_ref, cross_ref)):
+            same, far = same_ref[h], far_ref[h]
+            newer = jnp.where(late, same, far)
+            totals.append(joined(newer, jnp.where(late, far, same)).astype(BF16))
+        both = joined(*totals).astype(BF16)
         both_ref[h] = both
         tail_ref[h] = both[:, DK:]
+        other = other_ref[h]
+        step = jnp.where(odd, came_ref[h], jnp.zeros_like(other))
+        prefix_ref[h] = joined(step, jnp.where(late, other, jnp.zeros_like(other)))
 
 
 def quarter_of(here):
@@ -353,20 +355,22 @@
     other_ref[...] = dot(theirs, w).astype(BF16)
 
 
-def pair_kernel(own_ref, got_ref, pay_ref, came_ref, keep_ref, *refs):
-    *send_refs, quarter_ref, give_ref = refs
+def pair_kernel(own_ref, got_ref, keep_ref, *send_refs):
     piece = keep_ref.shape[0]
     keep_ref[...] = own_ref[:piece] + got_ref[:piece].astype(F32)
     for k, ref in enumerate(send_refs):
         part = slice((k + 1) * piece, (k + 2) * piece)
         ref[...] = (own_ref[part] + got_ref[part].astype(F32)).astype(BF16)
+
+
+def halve_kernel(pay_ref, came_ref, quarter_ref, give_ref):
     quarter = quarter_ref.shape[0]
     quarter_ref[...] = pay_ref[:quarter] + came_ref[:quarter]
     give_ref[...] = pay_ref[quarter:] + came_ref[quarter:]
 
 
-def norm_kernel(hidden_ref, gain_ref, pay_ref, came_ref, keep_ref, *refs):
-    *got, stream_ref, normed_ref, sum_ref = refs
+def norm_kernel(hidden_ref, gain_ref, keep_ref, *refs):
+    *got, stream_ref, normed_ref = refs
     total = keep_ref[...]
     for ref in got:
         total = total + ref[...].astype(F32)
@@ -374,32 +378,28 @@
     stream_ref[...] = total.astype(BF16)
     scale = lax.rsqrt(jnp.mean(total * total, axis=1, keepdims=True) + 1e-05)
     normed_ref[...] = (total * scale * gain_ref[...]).astype(BF16)
-    sum_ref[...] = pay_ref[...] + came_ref[...]
-
-
-def columns_kernel(meta, mine_ref, peer_ref, *refs):
-    full_ref, *piece_refs, cols_ref = refs
+
+
+def columns_kernel(meta, mine_ref, peer_ref, pay_ref, came_ref, sum_ref, *refs):
+    *piece_refs, cols_ref = refs
     wins, rows, width = cols_ref.shape
     mine, peer = mine_ref[...], peer_ref[...]
     lower = jnp.where(meta[6] == 0, mine, peer)
     upper = jnp.where(meta[6] == 0, peer, mine)
-    full_ref[: rows // 2] = lower
-    full_ref[rows // 2 :] = upper
     for k in range(wins):
         cols_ref[k, : rows // 2] = lower[:, k * width : (k + 1) * width]
         cols_ref[k, rows // 2 :] = upper[:, k * width : (k + 1) * width]
     for k, ref in enumerate(piece_refs):
         ref[...] = cols_ref[lax.rem(meta[5] + k, wins)]
-
-
-def last_kernel(done_ref, own_ref, *refs):
+    sum_ref[...] = pay_ref[...] + came_ref[...]
+
+
+def last_kernel(own_ref, *refs):
     *came, all_ref = refs
-    direct = done_ref.shape[1]
-    all_ref[:, :direct] = done_ref[...]
     total = own_ref[...]
     for ref in came:
         total = total + ref[...].astype(F32)
-    all_ref[:, direct:] = total.astype(BF16)
+    all_ref[...] = total.astype(BF16)
 
 
 def finish_kernel(meta, *refs):
@@ -428,8 +428,6 @@
     piece = rows // (wins * cores)
     seq, win, core = (lax.axis_index(a).astype(jnp.int32) for a in ("seq", "win", "wout"))
     meta = jnp.concatenate([lengths, jnp.stack([seq * rows, win, core, seq % ROW])])
-    direct = w_qkv.shape[1] // 3
-    gathered = lax.all_gather(w_qkv[:, :direct], "win", axis=0, tiled=True)
     x = qkv_in.transpose(1, 0, 2)
     halo = shift(x[:, rows - HALO :], "seq", 1)
     act, lead, parts, taps, beta = call(
@@ -466,20 +464,15 @@
     maps_out = out((heads, DK, 2 * DK), BF16)
     came = exchange(maps, "seq", 1)
     (twin,) = call(twin_kernel, [maps_out], "twin", 10**8, meta, maps, came)
-    prefix, total = call(
+    cross = lax.ppermute(
+        twin, "seq", [(s, (s ^ (ROW - 1)) + ROW) for s in range(n_seq - ROW)]
+    )
+    prefix, both, tail = call(
         row_kernel,
-        [out((heads, DK, 2 * DK), F32), maps_out],
+        [out((heads, DK, 2 * DK), F32), maps_out, out((heads, DK, DK), BF16)],
         "row",
         10**8,
-        meta, maps, came, twin, exchange(twin, "seq", ROW - 1),
-    )
-    both, tail = call(
-        join_kernel,
-        [maps_out, out((heads, DK, DK), BF16)],
-        "join",
-        10**8,
-        total, shift(total, "seq", ROW),
-        smem=0,
+        meta, maps, came, twin, exchange(twin, "seq", ROW - 1), shift(twin, "seq", ROW), cross,
     )
     tail = shift(tail, "seq", 3 * ROW)
     wide = shift(both, "seq", ROW)
@@ -504,43 +497,49 @@
         ],
     )
     got = rotate(other, "wout", 1)
-    *sums, payload, give = call(
+    sums = call(
         pair_kernel,
-        [out((piece, model), F32)] + [out((piece, model), BF16)] * (wins - 1) + [quarter] * 2,
+        [out((piece, model), F32)] + [out((piece, model), BF16)] * (wins - 1),
         "pair",
         10**6,
-        own, got, keep, exchange(give, "seq", 1),
+        own, got,
         smem=0,
     )
-    came = exchange(give, "seq", ROW - 1)
+    came = exchange(give, "seq", 1)
     reduced = [rotate(sums[k], "win", k) for k in range(1, wins)]
-    stream_out, normed, payload = call(
+    payload, give = call(
+        halve_kernel,
+        [quarter] * 2,
+        "halve",
+        10**6,
+        keep, came,
+        smem=0,
+    )
+    stream_out, normed = call(
         norm_kernel,
-        [out((piece, model), BF16), out((piece, model), BF16), quarter],
+        [out((piece, model), BF16)] * 2,
         "norm",
         10**6,
-        hidden_in, norm_gain.reshape(1, model), payload, came, sums[0], *reduced,
+        hidden_in, norm_gain.reshape(1, model), sums[0], *reduced,
         smem=0,
     )
     peer = rotate(normed, "wout", 1)
+    payload, *cols = call(
+        columns_kernel,
+        [quarter] + [out((2 * piece, model // wins), BF16)] * wins,
+        "columns",
+        10**6,
+        meta, normed, peer, payload, exchange(give, "seq", ROW - 1),
+        scratch=[pltpu.VMEM((wins, 2 * piece, model // wins), BF16)],
+    )
     lines = n_seq // ROW
     bits = [b for b in (4, 2, 1) if 2 * b <= lines]
     came = exchange(payload, "seq", bits[0] * ROW)
-    full, *cols = call(
-        columns_kernel,
-        [out((2 * piece, model), BF16)] + [out((2 * piece, model // wins), BF16)] * wins,
-        "columns",
-        10**6,
-        meta, normed, peer,
-        scratch=[pltpu.VMEM((wins, 2 * piece, model // wins), BF16)],
-    )
     blocks = [cols[0]] + [rotate(cols[k], "win", k) for k in range(1, wins)]
-    finished = jnp.dot(full, gathered, preferred_element_type=F32).astype(BF16)
-    finished, came = lax.optimization_barrier((finished, came))
     *blocks, payload = lax.optimization_barrier((*blocks, payload + came))
 
     def partial(k):
-        return jnp.dot(blocks[(wins - k) % wins], w_qkv[:, direct:], preferred_element_type=F32)
+        return jnp.dot(blocks[(wins - k) % wins], w_qkv, preferred_element_type=F32)
 
     parts = [partial(k).astype(BF16) for k in range(1, wins)]
     *parts, payload = lax.optimization_barrier((*parts, payload))
@@ -550,7 +549,7 @@
         [out((2 * piece, w_qkv.shape[1]), BF16)],
         "last",
         10**10,
-        finished, partial(0), *arrived,
+        partial(0), *arrived,
         smem=0,
     )
 

time: 121 us -> 111 us (0.917)
  between operations: 14.3 us -> 0.86 us
  waiting for transfers between devices: 34.3 us -> 42.8 us
  matrix products: 5.16 us -> 2.71 us
  starting transfers between devices: 48.5 us -> 46.7 us
  local copies, waits for them, and re-layouts: 3.15 us -> 1.67 us
    ppermute x14, waiting for transfers between devices: 11.7 us -> 28.7 us  [rotate(): lax.ppermute(value, axis, [(s, (s + steps) % count) for s in range(count)])]
    ppermute x4, starting transfers between devices: 23.6 us -> 16.4 us  [shift(): lax.ppermute(value, axis, [(s, s + steps) for s in range(max(0, count - s...]
    ppermute x5, waiting for transfers between devices: 18.3 us -> 11.1 us  [exchange(): lax.ppermute(value, axis, [(s, s ^ bit) for s in range(lax.axis_size(axis...]
    ppermute x0 -> x1, starting transfers between devices: none -> 6.51 us  [body(): lax.ppermute(twin, 'seq', [(s, (s ^ ROW - 1) + ROW) for s in range(n_seq...]
    dot_general x5 -> x4, matrix products: 5.16 us -> 2.71 us  [partial(): return jnp.dot(blocks[(wins - k) % wins], w_qkv, preferred_element_type=F32)]
    slice x1 -> x0, local copies, waits for them, and re-layouts: 2.29 us -> none  [body(): gathered = lax.all_gather(w_qkv[:, :direct], 'win', axis=0, tiled=True)]
    ppermute x14, starting transfers between devices: 12.8 us -> 10.5 us  [rotate(): lax.ppermute(value, axis, [(s, (s + steps) % count) for s in range(count)])]
    ppermute x4, waiting for transfers between devices: 4.39 us -> 2.98 us  [shift(): lax.ppermute(value, axis, [(s, s + steps) for s in range(max(0, count - s...]
  transfers between devices with their start and end apart: 27 -> 27, of which waited for: 13 -> 17; matrix products, arithmetic and copies ran while one was open for 4% -> 1% of each run, Pallas kernels for 11% -> 4%
where the time goes in v6:
time: 111 us; the launch traced here: 110 us
  starting transfers between devices  46.7 us (42%)
  waiting for transfers between devices  42.8 us (39%)
  Pallas kernels  15.4 us (14%)
  matrix products  2.71 us (2%)
  local copies, waits for them, and re-layouts  1.67 us (2%)
    ppermute x14, waiting for transfers between devices, rotate(): lax.ppermute(value, axis, [(s, (s + steps) % count) for s in range(count)])  28.7 us
    ppermute x4, starting transfers between devices, shift(): lax.ppermute(value, axis, [(s, s + steps) for s in range(max(0, count - s...  16.4 us
    pallas_call x11, Pallas kernels, call(): pl.pallas_call(kernel, out_shape=outs, in_specs=[SMEM] * smem + [HBM] * h...  15.4 us
    ppermute x5, waiting for transfers between devices, exchange(): lax.ppermute(value, axis, [(s, s ^ bit) for s in range(lax.axis_size(axis...  11.1 us
    ppermute x5, starting transfers between devices, exchange(): lax.ppermute(value, axis, [(s, s ^ bit) for s in range(lax.axis_size(axis...  10.9 us
    ppermute x14, starting transfers between devices, rotate(): lax.ppermute(value, axis, [(s, (s + steps) % count) for s in range(count)])  10.5 us
    ppermute x1, starting transfers between devices, body(): lax.ppermute(twin, 'seq', [(s, (s ^ ROW - 1) + ROW) for s in range(n_seq...  6.51 us
    ppermute x4, waiting for transfers between devices, shift(): lax.ppermute(value, axis, [(s, s + steps) for s in range(max(0, count - s...  2.98 us
  transfers between devices with their start and end apart: 27, of which 17 were waited for; matrix products, arithmetic and copies ran while one was open for 1% of the time, Pallas kernels for 4%

profile of v6, /device:TPU:24, one launch (start us, length us, event | category | flops | bytes accessed | tf_op | source)
XLA Modules:
  0.0 110.2 jit_solution(12207440832272485369)
XLA Ops:
  0.6 0.9 slice.4
  1.5 3.5 %collective-permute-start = (bf16[3,16,256]{2,1,0:T(8,128)(2,1)S(1)}, bf16[3,16,256]{2,1,0:T(8,128)(2,1)S(1)}, u32[]{:S(2)}, u32[]{:S(2)}) collective-permute-start(bf16[3,16,256]{2,1,0:T(8,128)(2,1)S(1)} %slice.4), channel_id=1, source_target_pairs={{0,8},{8,16},{16,24},{24,32},{32,40},{40,48},{48,56},{56,64},{64,7... | collective-permute-start | bytes 73736 | tf_op jit(solution)/shard_map/ppermute | solution.py:29
  5.1 0.7 concatenate.3.meta
  5.8 2.4 %conv.1 = (bf16[3,256,256]{2,1,0:T(8,128)(2,1)S(1)}, bf16[3,16,256]{2,1,0:T(8,128)(2,1)S(1)}, bf16[3,16,256]{2,1,0:T(8,128)(2,1)S(1)}, f32[3,4,256]{2,1,0:T(4,128)S(1)}, f32[2,256]{1,0:T(2,128)S(1)}) custom-call(s32[8]{0:T(128)S(1)} %concatenate.3.meta, bf16[3,256,256]{2,1,0:T(8,128)(2,1)} %bitcast.20, f32[3,4,256]{2,1,0:T(4,128)} %taps_hbm.1, f32[2,256]{1,0:T(2,128)} %beta_hbm.1), custom_call_target="tpu_custom_call" | custom-call | flops 100000000 | bytes 864288 | tf_op jit(solution)/shard_map/conv/pallas_call | solution.py:70
  8.3 4.9 %prep.1 = (bf16[2,128,256]{2,1,0:T(8,128)(2,1)S(1)}, f32[2,256,256]{2,1,0:T(8,128)S(1)}, f32[2,256,128]{2,1,0:T(8,128)S(1)}, f32[2,256,128]{2,1,0:T(8,128)S(1)},...) custom-call(s32[8]{0:T(128)S(1)} %concatenate.3.meta, ...), custom_call_target="tpu_custom_call" | custom-call | flops 2000000000 | bytes 1818656 | tf_op jit(solution)/shard_map/prep/pallas_call | solution.py:70
  13.2 1.6 %collective-permute-start.1 = (bf16[2,128,256]{2,1,0:T(8,128)(2,1)S(1)}, bf16[2,128,256]{2,1,0:T(8,128)(2,1)S(1)}, u32[]{:S(2)}, u32[]{:S(2)}) collective-permute-start(bf16[2,128,256]{2,1,0:T(8,128)(2,1)S(1)} %get-tuple-element.57.own_ref), channel_id=1, source_target_pairs={{0,8},{8,0},{16,24},{24,16},{32,40},{40,32},{48,56},{56,48},{64,72... | collective-permute-start | bytes 393224 | tf_op jit(solution)/shard_map/ppermute | solution.py:44
  14.8 3.5 %collective-permute-done.1.came_ref = bf16[2,128,256]{2,1,0:T(8,128)(2,1)S(1)} collective-permute-done((bf16[2,128,256]{2,1,0:T(8,128)(2,1)S(1)}, bf16[2,128,256]{2,1,0:T(8,128)(2,1)S(1)}, u32[]{:S(2)}, u32[]{:S(2)}) %collective-permute-start.1) | collective-permute-done | bytes 131104 | tf_op jit(solution)/shard_map/ppermute | solution.py:44
  18.2 0.7 twin.1.twin_ref
  19.0 6.5 %collective-permute-start.4 = (bf16[2,128,256]{2,1,0:T(8,128)(2,1)S(1)}, bf16[2,128,256]{2,1,0:T(8,128)(2,1)S(1)}, u32[]{:S(2)}, u32[]{:S(2)}) collective-permute-start(bf16[2,128,256]{2,1,0:T(8,128)(2,1)S(1)} %twin.1.twin_ref), channel_id=1, source_target_pairs={{0,56},{8,48},{16,40},{24,32},{32,88},{40,80},{48,72},{56,64},{64,... | collective-permute-start | bytes 393224 | tf_op jit(solution)/shard_map/ppermute | solution.py:467
  25.5 3.8 %collective-permute-start.3 = (bf16[2,128,256]{2,1,0:T(8,128)(2,1)S(1)}, bf16[2,128,256]{2,1,0:T(8,128)(2,1)S(1)}, u32[]{:S(2)}, u32[]{:S(2)}) collective-permute-start(bf16[2,128,256]{2,1,0:T(8,128)(2,1)S(1)} %twin.1.twin_ref), channel_id=1, source_target_pairs={{0,32},{8,40},{16,48},{24,56},{32,64},{40,72},{48,80},{56,88},{64,... | collective-permute-start | bytes 393224 | tf_op jit(solution)/shard_map/ppermute | solution.py:29
  29.3 1.4 %collective-permute-start.2 = (bf16[2,128,256]{2,1,0:T(8,128)(2,1)S(1)}, bf16[2,128,256]{2,1,0:T(8,128)(2,1)S(1)}, u32[]{:S(2)}, u32[]{:S(2)}) collective-permute-start(bf16[2,128,256]{2,1,0:T(8,128)(2,1)S(1)} %twin.1.twin_ref), channel_id=1, source_target_pairs={{0,24},{8,16},{16,8},{24,0},{32,56},{40,48},{48,40},{56,32},{64,88... | collective-permute-start | bytes 393224 | tf_op jit(solution)/shard_map/ppermute | solution.py:44
  30.7 1.1 collective-permute-done.3.below_ref
  31.8 3.8 %collective-permute-done.2.other_ref = bf16[2,128,256]{2,1,0:T(8,128)(2,1)S(1)} collective-permute-done((bf16[2,128,256]{2,1,0:T(8,128)(2,1)S(1)}, bf16[2,128,256]{2,1,0:T(8,128)(2,1)S(1)}, u32[]{:S(2)}, u32[]{:S(2)}) %collective-permute-start.2) | collective-permute-done | bytes 131104 | tf_op jit(solution)/shard_map/ppermute | solution.py:44
  35.6 1.0 row.1
  36.6 5.0 %collective-permute-start.5 = (bf16[2,128,256]{2,1,0:T(8,128)(2,1)S(1)}, bf16[2,128,256]{2,1,0:T(8,128)(2,1)S(1)}, u32[]{:S(2)}, u32[]{:S(2)}) collective-permute-start(bf16[2,128,256]{2,1,0:T(8,128)(2,1)S(1)} %get-tuple-element.59), channel_id=1, source_target_pairs={{0,32},{8,40},{16,48},{24,56},{32,64},{40,72},{48,80},{56,88},{64,... | collective-permute-start | bytes 393224 | tf_op jit(solution)/shard_map/ppermute | solution.py:29
  41.7 4.0 %collective-permute-start.6 = (bf16[2,128,128]{2,1,0:T(8,128)(2,1)S(1)}, bf16[2,128,128]{2,1,0:T(8,128)(2,1)S(1)}, u32[]{:S(2)}, u32[]{:S(2)}) collective-permute-start(bf16[2,128,128]{2,1,0:T(8,128)(2,1)S(1)} %get-tuple-element.60), channel_id=1, source_target_pairs={{0,96},{8,104},{16,112},{24,120},{32,128},{40,136},{48,144},{56,15... | collective-permute-start | bytes 196616 | tf_op jit(solution)/shard_map/ppermute | solution.py:29
  45.7 1.9 %collective-permute-done.6.tail_ref = bf16[2,128,128]{2,1,0:T(8,128)(2,1)S(1)} collective-permute-done((bf16[2,128,128]{2,1,0:T(8,128)(2,1)S(1)}, bf16[2,128,128]{2,1,0:T(8,128)(2,1)S(1)}, u32[]{:S(2)}, u32[]{:S(2)}) %collective-permute-start.6) | collective-permute-done | bytes 65568 | tf_op jit(solution)/shard_map/ppermute | solution.py:29
  47.6 2.5 %attend.1 = (f32[128,2048]{1,0:T(8,128)S(1)}, bf16[128,2048]{1,0:T(8,128)(2,1)S(1)}, bf16[576,128]{1,0:T(8,128)(2,1)S(1)}, bf16[576,128]{1,0:T(8,128)(2,1)S(1)}) custom-call(s32[8]{0:T(128)S(1)} %concatenate.3.meta, f32[2,128,256]{2,1,0:T(8,128)S(1)} %get-tuple-element.58.prefix_ref, bf16[2,128,256]{2,1,0:T(8,128)(2,1)S(1)} %collective-permute-done.5.wide_ref, ...), custom_call_target="tpu_custom_call" | custom-call | flops 1000000000 | bytes 4581920 | tf_op jit(solution)/shard_map/attend/pallas_call | solution.py:70
  50.2 1.9 %collective-permute-done.7.got_ref = bf16[128,2048]{1,0:T(8,128)(2,1)S(1)} collective-permute-done((bf16[128,2048]{1,0:T(8,128)(2,1)S(1)}, bf16[128,2048]{1,0:T(8,128)(2,1)S(1)}, u32[]{:S(2)}, u32[]{:S(2)}) %collective-permute-start.7) | collective-permute-done | bytes 524320 | tf_op jit(solution)/shard_map/ppermute | solution.py:34
  52.5 2.6 %collective-permute-start.9 = (bf16[32,2048]{1,0:T(8,128)(2,1)S(1)}, bf16[32,2048]{1,0:T(8,128)(2,1)S(1)}, u32[]{:S(2)}, u32[]{:S(2)}) collective-permute-start(bf16[32,2048]{1,0:T(8,128)(2,1)S(1)} %get-tuple-element.71), channel_id=1, source_target_pairs={{0,4},{2,6},{4,0},{6,2},{1,5},{3,7},{5,1},{7,3},{8,12},{10,14},{12... | collective-permute-start | bytes 393224 | tf_op jit(solution)/shard_map/ppermute | solution.py:34
  55.1 3.5 %collective-permute-done.8.refs_0_ = bf16[32,2048]{1,0:T(8,128)(2,1)S(1)} collective-permute-done((bf16[32,2048]{1,0:T(8,128)(2,1)S(1)}, bf16[32,2048]{1,0:T(8,128)(2,1)S(1)}, u32[]{:S(2)}, u32[]{:S(2)}) %collective-permute-start.8) | collective-permute-done | bytes 131104 | tf_op jit(solution)/shard_map/ppermute | solution.py:34
  58.6 1.6 %collective-permute-done.9.refs_1_ = bf16[32,2048]{1,0:T(8,128)(2,1)S(1)} collective-permute-done((bf16[32,2048]{1,0:T(8,128)(2,1)S(1)}, bf16[32,2048]{1,0:T(8,128)(2,1)S(1)}, u32[]{:S(2)}, u32[]{:S(2)}) %collective-permute-start.9) | collective-permute-done | bytes 131104 | tf_op jit(solution)/shard_map/ppermute | solution.py:34
  60.2 2.0 %collective-permute-done.10.refs_2_ = bf16[32,2048]{1,0:T(8,128)(2,1)S(1)} collective-permute-done((bf16[32,2048]{1,0:T(8,128)(2,1)S(1)}, bf16[32,2048]{1,0:T(8,128)(2,1)S(1)}, u32[]{:S(2)}, u32[]{:S(2)}) %collective-permute-start.10) | collective-permute-done | bytes 131104 | tf_op jit(solution)/shard_map/ppermute | solution.py:34
  62.2 0.8 norm.1
  63.0 2.3 %collective-permute-start.13 = (bf16[288,128]{1,0:T(8,128)(2,1)S(1)}, bf16[288,128]{1,0:T(8,128)(2,1)S(1)}, u32[]{:S(2)}, u32[]{:S(2)}) collective-permute-start(bf16[288,128]{1,0:T(8,128)(2,1)S(1)} %get-tuple-element.77), channel_id=1, source_target_pairs={{0,24},{8,16},{16,8},{24,0},{32,56},{40,48},{48,40},{56,32},{64,88... | collective-permute-start | bytes 221192 | tf_op jit(solution)/shard_map/ppermute | solution.py:44
  65.3 3.9 %collective-permute-done.13.came_ref = bf16[288,128]{1,0:T(8,128)(2,1)S(1)} collective-permute-done((bf16[288,128]{1,0:T(8,128)(2,1)S(1)}, bf16[288,128]{1,0:T(8,128)(2,1)S(1)}, u32[]{:S(2)}, u32[]{:S(2)}) %collective-permute-start.13) | collective-permute-done | bytes 73760 | tf_op jit(solution)/shard_map/ppermute | solution.py:44
  69.2 0.6 columns.1
  69.8 5.7 %collective-permute-start.17 = (bf16[288,128]{1,0:T(8,128)(2,1)S(1)}, bf16[288,128]{1,0:T(8,128)(2,1)S(1)}, u32[]{:S(2)}, u32[]{:S(2)}) collective-permute-start(bf16[288,128]{1,0:T(8,128)(2,1)S(1)} %get-tuple-element.82), channel_id=1, source_target_pairs={{0,128},{8,136},{16,144},{24,152},{32,160},{40,168},{48,176},{56,1... | collective-permute-start | bytes 221192 | tf_op jit(solution)/shard_map/ppermute | solution.py:44
  75.5 1.1 collective-permute-start.14
  76.5 2.0 %collective-permute-start.15 = (bf16[64,512]{1,0:T(8,128)(2,1)S(1)}, bf16[64,512]{1,0:T(8,128)(2,1)S(1)}, u32[]{:S(2)}, u32[]{:S(2)}) collective-permute-start(bf16[64,512]{1,0:T(8,128)(2,1)S(1)} %get-tuple-element.80), channel_id=1, source_target_pairs={{0,4},{2,6},{4,0},{6,2},{1,5},{3,7},{5,1},{7,3},{8,12},{10,14},{12... | collective-permute-start | bytes 196616 | tf_op jit(solution)/shard_map/ppermute | solution.py:34
  78.7 1.3 %collective-permute-done.14 = bf16[64,512]{1,0:T(8,128)(2,1)S(1)} collective-permute-done((bf16[64,512]{1,0:T(8,128)(2,1)S(1)}, bf16[64,512]{1,0:T(8,128)(2,1)S(1)}, u32[]{:S(2)}, u32[]{:S(2)}) %collective-permute-start.14) | collective-permute-done | bytes 65568 | tf_op jit(solution)/shard_map/ppermute | solution.py:34
  80.0 2.8 %collective-permute-done.15 = bf16[64,512]{1,0:T(8,128)(2,1)S(1)} collective-permute-done((bf16[64,512]{1,0:T(8,128)(2,1)S(1)}, bf16[64,512]{1,0:T(8,128)(2,1)S(1)}, u32[]{:S(2)}, u32[]{:S(2)}) %collective-permute-start.15) | collective-permute-done | bytes 65568 | tf_op jit(solution)/shard_map/ppermute | solution.py:34
  82.8 1.2 %collective-permute-done.16 = bf16[64,512]{1,0:T(8,128)(2,1)S(1)} collective-permute-done((bf16[64,512]{1,0:T(8,128)(2,1)S(1)}, bf16[64,512]{1,0:T(8,128)(2,1)S(1)}, u32[]{:S(2)}, u32[]{:S(2)}) %collective-permute-start.16) | collective-permute-done | bytes 65568 | tf_op jit(solution)/shard_map/ppermute | solution.py:34
  84.0 0.7 convolution_convert_fusion.2
  84.7 0.7 convolution_convert_fusion.1
  85.3 0.7 convolution_convert_fusion
  86.0 0.3 collective-permute-start.23
  86.3 2.5 %collective-permute-start.22 = (bf16[288,128]{1,0:T(8,128)(2,1)S(1)}, bf16[288,128]{1,0:T(8,128)(2,1)S(1)}, u32[]{:S(2)}, u32[]{:S(2)}) collective-permute-start(bf16[288,128]{1,0:T(8,128)(2,1)S(1)} %add.17), channel_id=1, source_target_pairs={{0,224},{8,232},{16,240},{24,248},{32,0},{40,8},{48,16},{56,24},{6... | collective-permute-start | bytes 221192 | tf_op jit(solution)/shard_map/ppermute | solution.py:34
  88.8 0.4 collective-permute-start.18
  89.3 1.1 %collective-permute-start.19 = (bf16[64,3072]{1,0:T(8,128)(2,1)S(1)}, bf16[64,3072]{1,0:T(8,128)(2,1)S(1)}, u32[]{:S(2)}, u32[]{:S(2)}) collective-permute-start(bf16[64,3072]{1,0:T(8,128)(2,1)S(1)} %convolution_convert_fusion.1), channel_id=1, source_target_pairs={{0,4},{2,6},{4,0},{6,2},{1,5},{3,7},{5,1},{7,3},{8,12},{10,14},{12... | collective-permute-start | bytes 1179656 | tf_op jit(solution)/shard_map/ppermute | solution.py:34
  90.4 3.1 %collective-permute-done.23 = bf16[288,128]{1,0:T(8,128)(2,1)S(1)} collective-permute-done((bf16[288,128]{1,0:T(8,128)(2,1)S(1)}, bf16[288,128]{1,0:T(8,128)(2,1)S(1)}, u32[]{:S(2)}, u32[]{:S(2)}) %collective-permute-start.23) | collective-permute-done | bytes 73760 | tf_op jit(solution)/shard_map/ppermute | solution.py:34
  93.5 0.7 fusion.own_ref
  94.4 2.4 %collective-permute-start.26 = (bf16[288,128]{1,0:T(8,128)(2,1)S(1)}, bf16[288,128]{1,0:T(8,128)(2,1)S(1)}, u32[]{:S(2)}, u32[]{:S(2)}) collective-permute-start(bf16[288,128]{1,0:T(8,128)(2,1)S(1)} %add_add_fusion.refs_0_), channel_id=1, source_target_pairs={{0,24},{8,0},{16,8},{24,16},{32,56},{40,32},{48,40},{56,48},{64,88... | collective-permute-start | bytes 221192 | tf_op jit(solution)/shard_map/ppermute | solution.py:40
  96.8 4.1 %collective-permute-done.18.refs_0_ = bf16[64,3072]{1,0:T(8,128)(2,1)S(1)} collective-permute-done((bf16[64,3072]{1,0:T(8,128)(2,1)S(1)}, bf16[64,3072]{1,0:T(8,128)(2,1)S(1)}, u32[]{:S(2)}, u32[]{:S(2)}) %collective-permute-start.18) | collective-permute-done | bytes 393248 | tf_op jit(solution)/shard_map/ppermute | solution.py:34
  100.9 1.9 %collective-permute-done.19.refs_1_ = bf16[64,3072]{1,0:T(8,128)(2,1)S(1)} collective-permute-done((bf16[64,3072]{1,0:T(8,128)(2,1)S(1)}, bf16[64,3072]{1,0:T(8,128)(2,1)S(1)}, u32[]{:S(2)}, u32[]{:S(2)}) %collective-permute-start.19) | collective-permute-done | bytes 393248 | tf_op jit(solution)/shard_map/ppermute | solution.py:34
  102.8 5.0 %collective-permute-done.20.refs_2_ = bf16[64,3072]{1,0:T(8,128)(2,1)S(1)} collective-permute-done((bf16[64,3072]{1,0:T(8,128)(2,1)S(1)}, bf16[64,3072]{1,0:T(8,128)(2,1)S(1)}, u32[]{:S(2)}, u32[]{:S(2)}) %collective-permute-start.20) | collective-permute-done | bytes 393248 | tf_op jit(solution)/shard_map/ppermute | solution.py:34
  107.8 1.0 last.1
  108.8 1.4 %finish.1 = (f32[1024,128]{1,0:T(8,128)}, bf16[3,3,4,256]{3,2,1,0:T(4,128)(2,1)}) custom-call(s32[8]{0:T(128)S(1)} %concatenate.3.meta, bf16[288,128]{1,0:T(8,128)(2,1)S(1)} %add_add_fusion.refs_0_, bf16[288,128]{1,0:T(8,128)(2,1)S(1)} %collective-permute-done.24.refs_1_, bf16[288,128]{1,0:T(8,128)(2,1)S(1)} %collective-permute-done.25.refs_2_, ...), custom_call_target="tpu_custom_call" | custom-call | flops 1000000 | bytes 837664 | tf_op jit(solution)/shard_map/finish/pallas_call | solution.py:70
  (35 shorter events, 1.0 us)
Async XLA Ops:
  0.6 83.4 %copy-start = (bf16[512,3072]{1,0:T(8,128)(2,1)S(1)}, bf16[512,3072]{1,0:T(8,128)(2,1)}, u32[]{:S(2)}) copy-start(bf16[512,3072]{1,0:T(8,128)(2,1)} %param.17) | copy-start | bytes 9437188
  1.5 6.7 %collective-permute-start = (bf16[3,16,256]{2,1,0:T(8,128)(2,1)S(1)}, bf16[3,16,256]{2,1,0:T(8,128)(2,1)S(1)}, u32[]{:S(2)}, u32[]{:S(2)}) collective-permute-start(bf16[3,16,256]{2,1,0:T(8,128)(2,1)S(1)} %slice.4), channel_id=1, source_target_pairs={{0,8},{8,16},{16,24},{24,32},{32,40},{40,48},{48,56},{56,64},{64,7... | collective-permute-start | bytes 73736 | tf_op jit(solution)/shard_map/ppermute | solution.py:29
  8.3 39.3 %copy-start.3 = (bf16[256,2048]{1,0:T(8,128)(2,1)S(1)}, bf16[256,2048]{1,0:T(8,128)(2,1)}, u32[]{:S(2)}) copy-start(bf16[256,2048]{1,0:T(8,128)(2,1)} %w_ref.1) | copy-start | bytes 3145732
  8.3 39.3 %copy-start.4 = (f32[128]{0:T(128)S(1)}, f32[128]{0:T(128)}, u32[]{:S(2)}) copy-start(f32[128]{0:T(128)} %param.13) | copy-start | bytes 1540
  13.2 5.1 %collective-permute-start.1 = (bf16[2,128,256]{2,1,0:T(8,128)(2,1)S(1)}, bf16[2,128,256]{2,1,0:T(8,128)(2,1)S(1)}, u32[]{:S(2)}, u32[]{:S(2)}) collective-permute-start(bf16[2,128,256]{2,1,0:T(8,128)(2,1)S(1)} %get-tuple-element.57.own_ref), channel_id=1, source_target_pairs={{0,8},{8,0},{16,24},{24,16},{32,40},{40,32},{48,56},{56,48},{64,72... | collective-permute-start | bytes 393224 | tf_op jit(solution)/shard_map/ppermute | solution.py:44
  19.0 43.3 %copy-start.1 = (bf16[32,2048]{1,0:T(8,128)(2,1)S(1)}, bf16[32,2048]{1,0:T(8,128)(2,1)}, u32[]{:S(2)}) copy-start(bf16[32,2048]{1,0:T(8,128)(2,1)} %hidden_ref.1) | copy-start | bytes 393220
  19.0 43.2 %copy-start.2 = (f32[2048]{0:T(1024)S(1)}, f32[2048]{0:T(1024)}, u32[]{:S(2)}) copy-start(f32[2048]{0:T(1024)} %param.16) | copy-start | bytes 24580
  19.0 11.8 %collective-permute-start.4 = (bf16[2,128,256]{2,1,0:T(8,128)(2,1)S(1)}, bf16[2,128,256]{2,1,0:T(8,128)(2,1)S(1)}, u32[]{:S(2)}, u32[]{:S(2)}) collective-permute-start(bf16[2,128,256]{2,1,0:T(8,128)(2,1)S(1)} %twin.1.twin_ref), channel_id=1, source_target_pairs={{0,56},{8,48},{16,40},{24,32},{32,88},{40,80},{48,72},{56,64},{64,... | collective-permute-start | bytes 393224 | tf_op jit(solution)/shard_map/ppermute | solution.py:467
  25.5 6.3 %collective-permute-start.3 = (bf16[2,128,256]{2,1,0:T(8,128)(2,1)S(1)}, bf16[2,128,256]{2,1,0:T(8,128)(2,1)S(1)}, u32[]{:S(2)}, u32[]{:S(2)}) collective-permute-start(bf16[2,128,256]{2,1,0:T(8,128)(2,1)S(1)} %twin.1.twin_ref), channel_id=1, source_target_pairs={{0,32},{8,40},{16,48},{24,56},{32,64},{40,72},{48,80},{56,88},{64,... | collective-permute-start | bytes 393224 | tf_op jit(solution)/shard_map/ppermute | solution.py:29
  29.3 6.3 %collective-permute-start.2 = (bf16[2,128,256]{2,1,0:T(8,128)(2,1)S(1)}, bf16[2,128,256]{2,1,0:T(8,128)(2,1)S(1)}, u32[]{:S(2)}, u32[]{:S(2)}) collective-permute-start(bf16[2,128,256]{2,1,0:T(8,128)(2,1)S(1)} %twin.1.twin_ref), channel_id=1, source_target_pairs={{0,24},{8,16},{16,8},{24,0},{32,56},{40,48},{48,40},{56,32},{64,88... | collective-permute-start | bytes 393224 | tf_op jit(solution)/shard_map/ppermute | solution.py:44
  36.6 11.0 %collective-permute-start.5 = (bf16[2,128,256]{2,1,0:T(8,128)(2,1)S(1)}, bf16[2,128,256]{2,1,0:T(8,128)(2,1)S(1)}, u32[]{:S(2)}, u32[]{:S(2)}) collective-permute-start(bf16[2,128,256]{2,1,0:T(8,128)(2,1)S(1)} %get-tuple-element.59), channel_id=1, source_target_pairs={{0,32},{8,40},{16,48},{24,56},{32,64},{40,72},{48,80},{56,88},{64,... | collective-permute-start | bytes 393224 | tf_op jit(solution)/shard_map/ppermute | solution.py:29
  41.7 5.9 %collective-permute-start.6 = (bf16[2,128,128]{2,1,0:T(8,128)(2,1)S(1)}, bf16[2,128,128]{2,1,0:T(8,128)(2,1)S(1)}, u32[]{:S(2)}, u32[]{:S(2)}) collective-permute-start(bf16[2,128,128]{2,1,0:T(8,128)(2,1)S(1)} %get-tuple-element.60), channel_id=1, source_target_pairs={{0,96},{8,104},{16,112},{24,120},{32,128},{40,136},{48,144},{56,15... | collective-permute-start | bytes 196616 | tf_op jit(solution)/shard_map/ppermute | solution.py:29
  50.1 2.0 %collective-permute-start.7 = (bf16[128,2048]{1,0:T(8,128)(2,1)S(1)}, bf16[128,2048]{1,0:T(8,128)(2,1)S(1)}, u32[]{:S(2)}, u32[]{:S(2)}) collective-permute-start(bf16[128,2048]{1,0:T(8,128)(2,1)S(1)} %get-tuple-element.68), channel_id=1, source_target_pairs={{0,1},{1,0},{2,3},{3,2},{4,5},{5,4},{6,7},{7,6},{8,9},{9,8},{10,11... | collective-permute-start | bytes 1572872 | tf_op jit(solution)/shard_map/ppermute | solution.py:34
  52.2 6.4 %collective-permute-start.8 = (bf16[32,2048]{1,0:T(8,128)(2,1)S(1)}, bf16[32,2048]{1,0:T(8,128)(2,1)S(1)}, u32[]{:S(2)}, u32[]{:S(2)}) collective-permute-start(bf16[32,2048]{1,0:T(8,128)(2,1)S(1)} %get-tuple-element.70), channel_id=1, source_target_pairs={{0,2},{2,4},{4,6},{6,0},{1,3},{3,5},{5,7},{7,1},{8,10},{10,12},{12... | collective-permute-start | bytes 393224 | tf_op jit(solution)/shard_map/ppermute | solution.py:34
  52.5 7.8 %collective-permute-start.9 = (bf16[32,2048]{1,0:T(8,128)(2,1)S(1)}, bf16[32,2048]{1,0:T(8,128)(2,1)S(1)}, u32[]{:S(2)}, u32[]{:S(2)}) collective-permute-start(bf16[32,2048]{1,0:T(8,128)(2,1)S(1)} %get-tuple-element.71), channel_id=1, source_target_pairs={{0,4},{2,6},{4,0},{6,2},{1,5},{3,7},{5,1},{7,3},{8,12},{10,14},{12... | collective-permute-start | bytes 393224 | tf_op jit(solution)/shard_map/ppermute | solution.py:34
  55.1 7.1 %collective-permute-start.10 = (bf16[32,2048]{1,0:T(8,128)(2,1)S(1)}, bf16[32,2048]{1,0:T(8,128)(2,1)S(1)}, u32[]{:S(2)}, u32[]{:S(2)}) collective-permute-start(bf16[32,2048]{1,0:T(8,128)(2,1)S(1)} %get-tuple-element.72), channel_id=1, source_target_pairs={{0,6},{2,0},{4,2},{6,4},{1,7},{3,1},{5,3},{7,5},{8,14},{10,8},{12,... | collective-permute-start | bytes 393224 | tf_op jit(solution)/shard_map/ppermute | solution.py:34
  55.1 7.9 %collective-permute-start.12 = (bf16[576,128]{1,0:T(8,128)(2,1)S(1)}, bf16[576,128]{1,0:T(8,128)(2,1)S(1)}, u32[]{:S(2)}, u32[]{:S(2)}) collective-permute-start(bf16[576,128]{1,0:T(8,128)(2,1)S(1)} %get-tuple-element.75), channel_id=1, source_target_pairs={{0,8},{8,0},{16,24},{24,16},{32,40},{40,32},{48,56},{56,48},{64,72... | collective-permute-start | bytes 442376 | tf_op jit(solution)/shard_map/ppermute | solution.py:44
  63.0 6.2 %collective-permute-start.11 = (bf16[32,2048]{1,0:T(8,128)(2,1)S(1)}, bf16[32,2048]{1,0:T(8,128)(2,1)S(1)}, u32[]{:S(2)}, u32[]{:S(2)}) collective-permute-start(bf16[32,2048]{1,0:T(8,128)(2,1)S(1)} %get-tuple-element.73.mine_ref), channel_id=1, source_target_pairs={{0,1},{1,0},{2,3},{3,2},{4,5},{5,4},{6,7},{7,6},{8,9},{9,8},{10,11... | collective-permute-start | bytes 393224 | tf_op jit(solution)/shard_map/ppermute | solution.py:34
  63.0 6.2 %collective-permute-start.13 = (bf16[288,128]{1,0:T(8,128)(2,1)S(1)}, bf16[288,128]{1,0:T(8,128)(2,1)S(1)}, u32[]{:S(2)}, u32[]{:S(2)}) collective-permute-start(bf16[288,128]{1,0:T(8,128)(2,1)S(1)} %get-tuple-element.77), channel_id=1, source_target_pairs={{0,24},{8,16},{16,8},{24,0},{32,56},{40,48},{48,40},{56,32},{64,88... | collective-permute-start | bytes 221192 | tf_op jit(solution)/shard_map/ppermute | solution.py:44
  69.8 8.8 %collective-permute-start.17 = (bf16[288,128]{1,0:T(8,128)(2,1)S(1)}, bf16[288,128]{1,0:T(8,128)(2,1)S(1)}, u32[]{:S(2)}, u32[]{:S(2)}) collective-permute-start(bf16[288,128]{1,0:T(8,128)(2,1)S(1)} %get-tuple-element.82), channel_id=1, source_target_pairs={{0,128},{8,136},{16,144},{24,152},{32,160},{40,168},{48,176},{56,1... | collective-permute-start | bytes 221192 | tf_op jit(solution)/shard_map/ppermute | solution.py:44
  75.5 4.5 %collective-permute-start.14 = (bf16[64,512]{1,0:T(8,128)(2,1)S(1)}, bf16[64,512]{1,0:T(8,128)(2,1)S(1)}, u32[]{:S(2)}, u32[]{:S(2)}) collective-permute-start(bf16[64,512]{1,0:T(8,128)(2,1)S(1)} %get-tuple-element.79), channel_id=1, source_target_pairs={{0,2},{2,4},{4,6},{6,0},{1,3},{3,5},{5,7},{7,1},{8,10},{10,12},{12... | collective-permute-start | bytes 196616 | tf_op jit(solution)/shard_map/ppermute | solution.py:34
  76.5 6.3 %collective-permute-start.15 = (bf16[64,512]{1,0:T(8,128)(2,1)S(1)}, bf16[64,512]{1,0:T(8,128)(2,1)S(1)}, u32[]{:S(2)}, u32[]{:S(2)}) collective-permute-start(bf16[64,512]{1,0:T(8,128)(2,1)S(1)} %get-tuple-element.80), channel_id=1, source_target_pairs={{0,4},{2,6},{4,0},{6,2},{1,5},{3,7},{5,1},{7,3},{8,12},{10,14},{12... | collective-permute-start | bytes 196616 | tf_op jit(solution)/shard_map/ppermute | solution.py:34
  78.5 5.5 %collective-permute-start.16 = (bf16[64,512]{1,0:T(8,128)(2,1)S(1)}, bf16[64,512]{1,0:T(8,128)(2,1)S(1)}, u32[]{:S(2)}, u32[]{:S(2)}) collective-permute-start(bf16[64,512]{1,0:T(8,128)(2,1)S(1)} %get-tuple-element.81), channel_id=1, source_target_pairs={{0,6},{2,0},{4,2},{6,4},{1,7},{3,1},{5,3},{7,5},{8,14},{10,8},{12,... | collective-permute-start | bytes 196616 | tf_op jit(solution)/shard_map/ppermute | solution.py:34
  86.0 7.4 %collective-permute-start.23 = (bf16[288,128]{1,0:T(8,128)(2,1)S(1)}, bf16[288,128]{1,0:T(8,128)(2,1)S(1)}, u32[]{:S(2)}, u32[]{:S(2)}) collective-permute-start(bf16[288,128]{1,0:T(8,128)(2,1)S(1)} %add.17), channel_id=1, source_target_pairs={{0,64},{8,72},{16,80},{24,88},{32,96},{40,104},{48,112},{56,120},{... | collective-permute-start | bytes 221192 | tf_op jit(solution)/shard_map/ppermute | solution.py:34
  86.3 7.8 %collective-permute-start.22 = (bf16[288,128]{1,0:T(8,128)(2,1)S(1)}, bf16[288,128]{1,0:T(8,128)(2,1)S(1)}, u32[]{:S(2)}, u32[]{:S(2)}) collective-permute-start(bf16[288,128]{1,0:T(8,128)(2,1)S(1)} %add.17), channel_id=1, source_target_pairs={{0,224},{8,232},{16,240},{24,248},{32,0},{40,8},{48,16},{56,24},{6... | collective-permute-start | bytes 221192 | tf_op jit(solution)/shard_map/ppermute | solution.py:34
  88.8 5.6 %collective-permute-start.21 = (bf16[288,128]{1,0:T(8,128)(2,1)S(1)}, bf16[288,128]{1,0:T(8,128)(2,1)S(1)}, u32[]{:S(2)}, u32[]{:S(2)}) collective-permute-start(bf16[288,128]{1,0:T(8,128)(2,1)S(1)} %add.17), channel_id=1, source_target_pairs={{0,32},{8,40},{16,48},{24,56},{32,64},{40,72},{48,80},{56,88},{64,... | collective-permute-start | bytes 221192 | tf_op jit(solution)/shard_map/ppermute | solution.py:34
  88.8 12.1 %collective-permute-start.18 = (bf16[64,3072]{1,0:T(8,128)(2,1)S(1)}, bf16[64,3072]{1,0:T(8,128)(2,1)S(1)}, u32[]{:S(2)}, u32[]{:S(2)}) collective-permute-start(bf16[64,3072]{1,0:T(8,128)(2,1)S(1)} %convolution_convert_fusion.2), channel_id=1, source_target_pairs={{0,2},{2,4},{4,6},{6,0},{1,3},{3,5},{5,7},{7,1},{8,10},{10,12},{12... | collective-permute-start | bytes 1179656 | tf_op jit(solution)/shard_map/ppermute | solution.py:34
  89.3 13.6 %collective-permute-start.19 = (bf16[64,3072]{1,0:T(8,128)(2,1)S(1)}, bf16[64,3072]{1,0:T(8,128)(2,1)S(1)}, u32[]{:S(2)}, u32[]{:S(2)}) collective-permute-start(bf16[64,3072]{1,0:T(8,128)(2,1)S(1)} %convolution_convert_fusion.1), channel_id=1, source_target_pairs={{0,4},{2,6},{4,0},{6,2},{1,5},{3,7},{5,1},{7,3},{8,12},{10,14},{12... | collective-permute-start | bytes 1179656 | tf_op jit(solution)/shard_map/ppermute | solution.py:34
  93.5 14.4 %collective-permute-start.20 = (bf16[64,3072]{1,0:T(8,128)(2,1)S(1)}, bf16[64,3072]{1,0:T(8,128)(2,1)S(1)}, u32[]{:S(2)}, u32[]{:S(2)}) collective-permute-start(bf16[64,3072]{1,0:T(8,128)(2,1)S(1)} %convolution_convert_fusion), channel_id=1, source_target_pairs={{0,6},{2,0},{4,2},{6,4},{1,7},{3,1},{5,3},{7,5},{8,14},{10,8},{12,... | collective-permute-start | bytes 1179656 | tf_op jit(solution)/shard_map/ppermute | solution.py:34
  94.4 14.4 %collective-permute-start.26 = (bf16[288,128]{1,0:T(8,128)(2,1)S(1)}, bf16[288,128]{1,0:T(8,128)(2,1)S(1)}, u32[]{:S(2)}, u32[]{:S(2)}) collective-permute-start(bf16[288,128]{1,0:T(8,128)(2,1)S(1)} %add_add_fusion.refs_0_), channel_id=1, source_target_pairs={{0,24},{8,0},{16,8},{24,16},{32,56},{40,32},{48,40},{56,48},{64,88... | collective-permute-start | bytes 221192 | tf_op jit(solution)/shard_map/ppermute | solution.py:40
  96.8 12.0 %collective-permute-start.25 = (bf16[288,128]{1,0:T(8,128)(2,1)S(1)}, bf16[288,128]{1,0:T(8,128)(2,1)S(1)}, u32[]{:S(2)}, u32[]{:S(2)}) collective-permute-start(bf16[288,128]{1,0:T(8,128)(2,1)S(1)} %add_add_fusion.refs_0_), channel_id=1, source_target_pairs={{0,16},{8,24},{16,0},{24,8},{32,48},{40,56},{48,32},{56,40},{64,80... | collective-permute-start | bytes 221192 | tf_op jit(solution)/shard_map/ppermute | solution.py:40
  100.9 7.9 %collective-permute-start.24 = (bf16[288,128]{1,0:T(8,128)(2,1)S(1)}, bf16[288,128]{1,0:T(8,128)(2,1)S(1)}, u32[]{:S(2)}, u32[]{:S(2)}) collective-permute-start(bf16[288,128]{1,0:T(8,128)(2,1)S(1)} %add_add_fusion.refs_0_), channel_id=1, source_target_pairs={{0,8},{8,16},{16,24},{24,0},{32,40},{40,48},{48,56},{56,32},{64,72... | collective-permute-start | bytes 221192 | tf_op jit(solution)/shard_map/ppermute | solution.py:40

commit v7 on v6

--- a/solution.py
+++ b/solution.py
@@ -131,7 +131,7 @@
         for i in range(CONV - 1):
             spot = ends[r] - (CONV - 1) + i
             good = owned & (spot >= begin)
-            wanted = jnp.where(edge_id == i * REQS + r, jnp.where(good, spot, -1), wanted)
+            wanted = jnp.where(edge_id == r * CONV + i, jnp.where(good, spot, -1), wanted)
     return jnp.where((ext_pos == wanted) & (ext_pos >= 0), 1.0, 0.0).astype(BF16)
 
 
@@ -185,13 +185,15 @@
     last_link = start_of(last, ends) < first
     in_last = jnp.where(seg == last_seg, 1.0, 0.0).astype(F32)
     select = edge_select(meta, ends, first, last, first - HALO + iota((EDGE_ROWS, HALO), 1))
+    edge_ref[...] = jnp.zeros_like(edge_ref)
 
     planes = []
     for c in range(3):
         halo = halo_ref[c]
         picked = part_ref[c] + dot(select, halo).astype(BF16)
-        for b in range(heads):
-            edge_ref[c * heads + b] = picked[:, b * DK : (b + 1) * DK]
+        picked = picked.astype(F32)
+        for r in range(REQS):
+            edge_ref[r, c * CONV : (c + 1) * CONV] = picked[r * CONV : (r + 1) * CONV]
         ext = jnp.concatenate([halo, head_ref[c]], axis=0).astype(F32)
         lead = conv_rows(ext, taps_ref[c], pos[:HALO], begin[:HALO])
         planes.append(jnp.concatenate([lead, act_ref[c, HALO:]], axis=0))
@@ -296,20 +298,65 @@
         prefix_ref[h] = joined(step, jnp.where(late, other, jnp.zeros_like(other)))
 
 
-def quarter_of(here):
-    return lax.rem((here + 1) // 2, 2) * 2 + here // 2
+def ends_kernel(meta, uw_ref, kb_ref, ks_ref, prefix_ref, edge_ref, *piece_refs):
+    heads, rows, _ = uw_ref.shape
+    ends = request_ends(meta)
+    first = meta[4]
+    pos = first + iota((rows, 1), 0)
+    seg = seg_of(pos, ends)
+    eye = jnp.where(iota((DK, DK), 0) == iota((DK, DK), 1), 1.0, 0.0).astype(F32)
+    for k, ref in enumerate(piece_refs):
+        r = lax.rem(meta[7] + k, REQS)
+        end = ends[0]
+        for i in range(1, REQS):
+            end = jnp.where(r == i, ends[i], end)
+        owned = (end - 1 >= first) & (end - 1 <= first + rows - 1)
+        carried = jnp.where(end - meta[r] < first, 1.0, 0.0)
+        ref[heads * DK :] = edge_ref[r].astype(BF16)
+
+        @pl.when(owned)
+        def _():
+            for h in range(heads):
+                scaled = jnp.where(seg == r, uw_ref[h] * ks_ref[h], 0.0)
+                high, less = split(scaled)
+                fold = dot(kb_ref[h], high, TN) + dot(kb_ref[h], less, TN)
+                link = carried * eye - fold[:, DK:]
+                prefix = prefix_ref[h]
+                both = dot32(link, prefix)
+                ref[h * DK : (h + 1) * DK, :DK] = (link - both[:, :DK]).astype(BF16)
+                ref[h * DK : (h + 1) * DK, DK:] = (both[:, DK:] + fold[:, :DK]).astype(BF16)
+
+        @pl.when(jnp.logical_not(owned))
+        def _():
+            ref[: heads * DK] = jnp.zeros((heads * DK, 2 * DK), BF16)
+
+
+def state_kernel(ahead_ref, *refs):
+    *piece_refs, pay_ref = refs
+    maps = piece_refs[0][...]
+    for ref in piece_refs[1:]:
+        maps = maps + ref[...]
+    heads = ahead_ref.shape[0]
+    for h in range(heads):
+        mine = maps[h * DK : (h + 1) * DK]
+        high, less = split(ahead_ref[h])
+        final = dot(mine[:, :DK], high) + dot(mine[:, :DK], less) + mine[:, DK:].astype(F32)
+        pay_ref[h * DK : (h + 1) * DK] = final.astype(BF16)
+        base = heads * DK + h * EDGE_ROWS
+        pay_ref[base : base + EDGE_ROWS] = maps[heads * DK :, h * DK : (h + 1) * DK]
+
+
+def sum_kernel(pay_ref, came_ref, sum_ref):
+    sum_ref[...] = pay_ref[...] + came_ref[...]
 
 
 def attend_kernel(
-    meta, prefix_ref, wide_ref, tail_ref, uw_ref, local_ref, link_ref, kb_ref, ks_ref,
-    edge_ref, gain_ref, w_ref, own_ref, other_ref, keep_ref, give_ref, heads_ref, pay_ref,
+    meta, prefix_ref, wide_ref, tail_ref, local_ref, link_ref, gain_ref, w_ref,
+    own_ref, other_ref, ahead_ref, heads_ref,
 ):
     heads, rows, _ = local_ref.shape
     wins, cores, piece, _ = heads_ref.shape
-    ends = request_ends(meta)
-    first, win, core = meta[4], meta[5], meta[6]
-    last = first + rows - 1
-    seg = seg_of(first + iota((rows, 1), 0), ends)
+    win, core = meta[5], meta[6]
     gain = gain_ref[...]
     for h in range(heads):
         wide, prefix, tail = wide_ref[h], prefix_ref[h], tail_ref[h]
@@ -324,29 +371,7 @@
             heads_ref[p // cores, p % cores, :, lanes] = normed[p * piece : (p + 1) * piece].astype(
                 BF16
             )
-        uw = uw_ref[h]
-        corrected = (uw[:, :DK] - dot_split(split(uw[:, DK:]), parts)) * ks_ref[h]
-        for r in range(REQS):
-            owned = (ends[r] - 1 >= first) & (ends[r] - 1 <= last)
-            carried = owned & (ends[r] - meta[r] < first)
-            member = (seg == r) & owned
-            high, less = split(jnp.where(member, corrected, 0.0))
-            final = dot(kb_ref[h], high, TN) + dot(kb_ref[h], less, TN)
-            final = final + jnp.where(carried, enter, 0.0)
-            spot = (r * heads + h) * DK
-            pay_ref[spot : spot + DK, :] = final.astype(BF16)
-    base = REQS * heads * DK
-    for b in range(edge_ref.shape[0]):
-        pay_ref[base + b * EDGE_ROWS : base + (b + 1) * EDGE_ROWS, :] = edge_ref[b]
-    used = base + edge_ref.shape[0] * EDGE_ROWS
-    pay_ref[used:, :] = jnp.zeros((pay_ref.shape[0] - used, DK), BF16)
-    quarter = keep_ref.shape[0] // 2
-    mine = quarter_of(meta[7])
-    twin = quarter_of(meta[7] + 1 - 2 * lax.rem(meta[7], 2))
-    for ref, spot in ((keep_ref, mine), (give_ref, twin)):
-        for part, which in enumerate((spot, spot + 1 - 2 * lax.rem(spot, 2))):
-            start = pl.multiple_of(which * quarter, EDGE_ROWS)
-            ref[part * quarter : (part + 1) * quarter] = pay_ref[pl.ds(start, quarter), :]
+        ahead_ref[h] = ahead
     order = [lax.rem(win + k, wins) for k in range(wins)]
     w = w_ref[...]
     mine = jnp.concatenate([heads_ref[o, core] for o in order], axis=0)
@@ -361,12 +386,6 @@
     for k, ref in enumerate(send_refs):
         part = slice((k + 1) * piece, (k + 2) * piece)
         ref[...] = (own_ref[part] + got_ref[part].astype(F32)).astype(BF16)
-
-
-def halve_kernel(pay_ref, came_ref, quarter_ref, give_ref):
-    quarter = quarter_ref.shape[0]
-    quarter_ref[...] = pay_ref[:quarter] + came_ref[:quarter]
-    give_ref[...] = pay_ref[quarter:] + came_ref[quarter:]
 
 
 def norm_kernel(hidden_ref, gain_ref, keep_ref, *refs):
@@ -380,7 +399,7 @@
     normed_ref[...] = (total * scale * gain_ref[...]).astype(BF16)
 
 
-def columns_kernel(meta, mine_ref, peer_ref, pay_ref, came_ref, sum_ref, *refs):
+def columns_kernel(meta, mine_ref, peer_ref, *refs):
     *piece_refs, cols_ref = refs
     wins, rows, width = cols_ref.shape
     mine, peer = mine_ref[...], peer_ref[...]
@@ -391,7 +410,6 @@
         cols_ref[k, rows // 2 :] = upper[:, k * width : (k + 1) * width]
     for k, ref in enumerate(piece_refs):
         ref[...] = cols_ref[lax.rem(meta[5] + k, wins)]
-    sum_ref[...] = pay_ref[...] + came_ref[...]
 
 
 def last_kernel(own_ref, *refs):
@@ -405,18 +423,19 @@
 def finish_kernel(meta, *refs):
     *quarters, state_ref, edge_ref, pay_ref = refs
     for k, ref in enumerate(quarters):
-        quarter = ref.shape[0]
-        place = lax.rem(meta[7] + ROW - k, ROW)
-        start = pl.multiple_of(quarter_of(place) * quarter, EDGE_ROWS)
-        pay_ref[pl.ds(start, quarter), :] = ref[...]
-    rows = state_ref.shape[0]
-    state_ref[...] = pay_ref[:rows].astype(F32)
-    heads = edge_ref.shape[3] // DK
-    for b in range(3 * heads):
-        edges = pay_ref[rows + b * EDGE_ROWS : rows + (b + 1) * EDGE_ROWS].astype(F32)
-        lanes = slice(b % heads * DK, (b % heads + 1) * DK)
-        for i in range(CONV - 1):
-            edge_ref[i, b // heads, :, lanes] = edges[i * REQS : (i + 1) * REQS].astype(BF16)
+        pay_ref[lax.rem(meta[7] + REQS - k, REQS)] = ref[...]
+    reqs, rows, _ = state_ref.shape
+    heads = rows // DK
+    for r in range(reqs):
+        state_ref[r] = pay_ref[r, :rows].astype(F32)
+    for h in range(heads):
+        base = rows + h * EDGE_ROWS
+        edges = [pay_ref[r, base : base + EDGE_ROWS].astype(F32) for r in range(reqs)]
+        for c in range(3):
+            for i in range(CONV - 1):
+                spot = c * CONV + i
+                lines = jnp.concatenate([e[spot : spot + 1] for e in edges], axis=0)
+                edge_ref[i, c, :, h * DK : (h + 1) * DK] = lines.astype(BF16)
 
 
 def body(qkv_in, conv_w, beta_logits, lengths, out_gain, w_out, hidden_in, norm_gain, w_qkv):
@@ -454,7 +473,7 @@
             out((heads, rows, DK), F32),
             out((heads, rows, DK), BF16),
             out((heads, rows, 1), F32),
-            out((3 * heads, EDGE_ROWS, DK), BF16),
+            out((REQS, EDGE_ROWS, width), F32),
         ],
         "prep",
         2 * 10**9,
@@ -476,27 +495,31 @@
     )
     tail = shift(tail, "seq", 3 * ROW)
     wide = shift(both, "seq", ROW)
-    state_rows = REQS * heads * DK
-    grain = ROW * EDGE_ROWS
-    pay_rows = -(-(state_rows + 3 * heads * EDGE_ROWS) // grain) * grain
-    half, quarter = out((pay_rows // 2, DK), BF16), out((pay_rows // 4, DK), BF16)
-    own, other, keep, give = call(
+    piece_rows = heads * DK + EDGE_ROWS
+    quarter = out((heads * (DK + EDGE_ROWS), DK), BF16)
+    pieces = call(
+        ends_kernel,
+        [out((piece_rows, 2 * DK), BF16)] * ROW,
+        "ends",
+        10**8,
+        meta, uw, kb, ks, prefix, edges,
+    )
+    pieces = [pieces[0]] + [row_rotate(pieces[k], k) for k in range(1, ROW)]
+    own, other, ahead = call(
         attend_kernel,
         [
             out((wins * piece, model), F32),
             out((wins * piece, model), BF16),
-            half,
-            half,
+            out((heads, DK, DK), F32),
         ],
         "attend",
         10**9,
-        meta, prefix, wide, tail, uw, local, link, kb, ks, edges, out_gain.reshape(1, DK), w_out,
-        scratch=[
-            pltpu.VMEM((wins, cores, piece, width), BF16),
-            pltpu.VMEM((pay_rows, DK), BF16),
-        ],
+        meta, prefix, wide, tail, local, link, out_gain.reshape(1, DK), w_out,
+        scratch=[pltpu.VMEM((wins, cores, piece, width), BF16)],
     )
     got = rotate(other, "wout", 1)
+    (payload,) = call(state_kernel, [quarter], "state", 10**10, ahead, *pieces, smem=0)
+    own, payload = lax.optimization_barrier((own, payload))
     sums = call(
         pair_kernel,
         [out((piece, model), F32)] + [out((piece, model), BF16)] * (wins - 1),
@@ -505,16 +528,10 @@
         own, got,
         smem=0,
     )
-    came = exchange(give, "seq", 1)
     reduced = [rotate(sums[k], "win", k) for k in range(1, wins)]
-    payload, give = call(
-        halve_kernel,
-        [quarter] * 2,
-        "halve",
-        10**6,
-        keep, came,
-        smem=0,
-    )
+    lines = n_seq // ROW
+    bits = [b for b in (4, 2, 1) if 2 * b <= lines]
+    came = exchange(payload, "seq", bits[0] * ROW)
     stream_out, normed = call(
         norm_kernel,
         [out((piece, model), BF16)] * 2,
@@ -524,25 +541,22 @@
         smem=0,
     )
     peer = rotate(normed, "wout", 1)
-    payload, *cols = call(
+    (payload,) = call(sum_kernel, [quarter], "sum", 10**10, payload, came, smem=0)
+    normed, payload = lax.optimization_barrier((normed, payload))
+    cols = call(
         columns_kernel,
-        [quarter] + [out((2 * piece, model // wins), BF16)] * wins,
+        [out((2 * piece, model // wins), BF16)] * wins,
         "columns",
         10**6,
-        meta, normed, peer, payload, exchange(give, "seq", ROW - 1),
+        meta, normed, peer,
         scratch=[pltpu.VMEM((wins, 2 * piece, model // wins), BF16)],
     )
-    lines = n_seq // ROW
-    bits = [b for b in (4, 2, 1) if 2 * b <= lines]
-    came = exchange(payload, "seq", bits[0] * ROW)
     blocks = [cols[0]] + [rotate(cols[k], "win", k) for k in range(1, wins)]
-    *blocks, payload = lax.optimization_barrier((*blocks, payload + came))
 
     def partial(k):
         return jnp.dot(blocks[(wins - k) % wins], w_qkv, preferred_element_type=F32)
 
     parts = [partial(k).astype(BF16) for k in range(1, wins)]
-    *parts, payload = lax.optimization_barrier((*parts, payload))
     arrived = [rotate(part, "win", k + 1) for k, part in enumerate(parts)]
     (projected,) = call(
         last_kernel,
@@ -563,11 +577,11 @@
     projected, *quarters = lax.optimization_barrier((projected, *quarters))
     final_states, conv_edges = call(
         finish_kernel,
-        [out((state_rows, DK), F32), out((CONV - 1, 3, REQS, width), BF16)],
+        [out((REQS, heads * DK, DK), F32), out((CONV - 1, 3, REQS, width), BF16)],
         "finish",
         10**6,
         meta, *quarters,
-        scratch=[pltpu.VMEM((pay_rows, DK), BF16)],
+        scratch=[pltpu.VMEM((REQS, *quarter.shape), BF16)],
     )
     final_states = final_states.reshape(REQS, heads, DK, DK)
     conv_edges = conv_edges.transpose(2, 0, 1, 3)

time: 111 us -> 105 us (0.946); the launches traced: 110 us -> 103 us
  waiting for transfers between devices: 42.8 us -> 30.7 us
  starting transfers between devices: 46.7 us -> 51.3 us
    ppermute x14, waiting for transfers between devices: 28.7 us -> 16.8 us  [rotate(): lax.ppermute(value, axis, [(s, (s + steps) % count) for s in range(count)])]
    ppermute x14, starting transfers between devices: 10.5 us -> 18 us  [rotate(): lax.ppermute(value, axis, [(s, (s + steps) % count) for s in range(count)])]
    ppermute x5 -> x3, starting transfers between devices: 10.9 us -> 4.3 us  [exchange(): lax.ppermute(value, axis, [(s, s ^ bit) for s in range(lax.axis_size(axis...]
    ppermute x3 -> x6, waiting for transfers between devices: 0.01 us -> 3.93 us  [row_rotate(): return lax.ppermute(value, 'seq', pairs)]
    ppermute x3 -> x6, starting transfers between devices: 2.36 us -> 6.25 us  [row_rotate(): return lax.ppermute(value, 'seq', pairs)]
    ppermute x5 -> x3, waiting for transfers between devices: 11.1 us -> 8.87 us  [exchange(): lax.ppermute(value, axis, [(s, s ^ bit) for s in range(lax.axis_size(axis...]
    ppermute x4, waiting for transfers between devices: 2.98 us -> 1.09 us  [shift(): lax.ppermute(value, axis, [(s, s + steps) for s in range(max(0, count - s...]
    pallas_call x11 -> x13, Pallas kernels: 15.4 us -> 15.5 us  [call(): pl.pallas_call(kernel, out_shape=outs, in_specs=[SMEM] * smem + [HBM] * h...]
  transfers between devices with their start and end apart: 27 -> 28, of which waited for: 17 -> 14; matrix products, arithmetic and copies ran while one was open for 1% -> 3% of each run, Pallas kernels for 4% -> 7%
where the time goes in v7:
time: 105 us; the launch traced here: 103 us
  starting transfers between devices  51.3 us (49%)
  waiting for transfers between devices  30.7 us (29%)
  Pallas kernels  15.5 us (15%)
  matrix products  2.64 us (3%)
  local copies, waits for them, and re-layouts  1.66 us (2%)
    ppermute x14, starting transfers between devices, rotate(): lax.ppermute(value, axis, [(s, (s + steps) % count) for s in range(count)])  18 us
    ppermute x14, waiting for transfers between devices, rotate(): lax.ppermute(value, axis, [(s, (s + steps) % count) for s in range(count)])  16.8 us
    ppermute x4, starting transfers between devices, shift(): lax.ppermute(value, axis, [(s, s + steps) for s in range(max(0, count - s...  16.4 us
    pallas_call x13, Pallas kernels, call(): pl.pallas_call(kernel, out_shape=outs, in_specs=[SMEM] * smem + [HBM] * h...  15.5 us
    ppermute x3, waiting for transfers between devices, exchange(): lax.ppermute(value, axis, [(s, s ^ bit) for s in range(lax.axis_size(axis...  8.87 us
    ppermute x1, starting transfers between devices, body(): lax.ppermute(twin, 'seq', [(s, (s ^ ROW - 1) + ROW) for s in range(n_seq...  6.36 us
    ppermute x6, starting transfers between devices, row_rotate(): return lax.ppermute(value, 'seq', pairs)  6.25 us
    ppermute x3, starting transfers between devices, exchange(): lax.ppermute(value, axis, [(s, s ^ bit) for s in range(lax.axis_size(axis...  4.3 us
  transfers between devices with their start and end apart: 28, of which 14 were waited for; matrix products, arithmetic and copies ran while one was open for 3% of the time, Pallas kernels for 7%

profile of v7, /device:TPU:24, one launch (start us, length us, event | category | flops | bytes accessed | tf_op | source)
XLA Modules:
  0.0 102.8 jit_solution(10026610469380627306)
XLA Ops:
  0.6 0.9 slice.4
  1.5 3.5 %collective-permute-start = (bf16[3,16,256]{2,1,0:T(8,128)(2,1)S(1)}, bf16[3,16,256]{2,1,0:T(8,128)(2,1)S(1)}, u32[]{:S(2)}, u32[]{:S(2)}) collective-permute-start(bf16[3,16,256]{2,1,0:T(8,128)(2,1)S(1)} %slice.4), channel_id=1, source_target_pairs={{0,8},{8,16},{16,24},{24,32},{32,40},{40,48},{48,56},{56,64},{64,7... | collective-permute-start | bytes 73736 | tf_op jit(solution)/shard_map/ppermute | solution.py:29
  5.1 0.7 concatenate.3.meta
  5.8 2.4 %conv.1 = (bf16[3,256,256]{2,1,0:T(8,128)(2,1)S(1)}, bf16[3,16,256]{2,1,0:T(8,128)(2,1)S(1)}, bf16[3,16,256]{2,1,0:T(8,128)(2,1)S(1)}, f32[3,4,256]{2,1,0:T(4,128)S(1)}, f32[2,256]{1,0:T(2,128)S(1)}) custom-call(s32[8]{0:T(128)S(1)} %concatenate.3.meta, bf16[3,256,256]{2,1,0:T(8,128)(2,1)} %bitcast.20, f32[3,4,256]{2,1,0:T(4,128)} %taps_hbm.1, f32[2,256]{1,0:T(2,128)} %beta_hbm.1), custom_call_target="tpu_custom_call" | custom-call | flops 100000000 | bytes 864288 | tf_op jit(solution)/shard_map/conv/pallas_call | solution.py:70
  8.3 4.9 %prep.1 = (bf16[2,128,256]{2,1,0:T(8,128)(2,1)S(1)}, f32[2,256,256]{2,1,0:T(8,128)S(1)}, f32[2,256,128]{2,1,0:T(8,128)S(1)}, f32[2,256,128]{2,1,0:T(8,128)S(1)},...) custom-call(s32[8]{0:T(128)S(1)} %concatenate.3.meta, ...), custom_call_target="tpu_custom_call" | custom-call | flops 2000000000 | bytes 1859616 | tf_op jit(solution)/shard_map/prep/pallas_call | solution.py:70
  13.2 1.6 %collective-permute-start.1 = (bf16[2,128,256]{2,1,0:T(8,128)(2,1)S(1)}, bf16[2,128,256]{2,1,0:T(8,128)(2,1)S(1)}, u32[]{:S(2)}, u32[]{:S(2)}) collective-permute-start(bf16[2,128,256]{2,1,0:T(8,128)(2,1)S(1)} %get-tuple-element.52.own_ref), channel_id=1, source_target_pairs={{0,8},{8,0},{16,24},{24,16},{32,40},{40,32},{48,56},{56,48},{64,72... | collective-permute-start | bytes 393224 | tf_op jit(solution)/shard_map/ppermute | solution.py:44
  14.7 3.5 %collective-permute-done.1.came_ref = bf16[2,128,256]{2,1,0:T(8,128)(2,1)S(1)} collective-permute-done((bf16[2,128,256]{2,1,0:T(8,128)(2,1)S(1)}, bf16[2,128,256]{2,1,0:T(8,128)(2,1)S(1)}, u32[]{:S(2)}, u32[]{:S(2)}) %collective-permute-start.1) | collective-permute-done | bytes 131104 | tf_op jit(solution)/shard_map/ppermute | solution.py:44
  18.2 0.7 twin.1.twin_ref
  18.9 6.4 %collective-permute-start.4 = (bf16[2,128,256]{2,1,0:T(8,128)(2,1)S(1)}, bf16[2,128,256]{2,1,0:T(8,128)(2,1)S(1)}, u32[]{:S(2)}, u32[]{:S(2)}) collective-permute-start(bf16[2,128,256]{2,1,0:T(8,128)(2,1)S(1)} %twin.1.twin_ref), channel_id=1, source_target_pairs={{0,56},{8,48},{16,40},{24,32},{32,88},{40,80},{48,72},{56,64},{64,... | collective-permute-start | bytes 393224 | tf_op jit(solution)/shard_map/ppermute | solution.py:486
  25.3 3.8 %collective-permute-start.3 = (bf16[2,128,256]{2,1,0:T(8,128)(2,1)S(1)}, bf16[2,128,256]{2,1,0:T(8,128)(2,1)S(1)}, u32[]{:S(2)}, u32[]{:S(2)}) collective-permute-start(bf16[2,128,256]{2,1,0:T(8,128)(2,1)S(1)} %twin.1.twin_ref), channel_id=1, source_target_pairs={{0,32},{8,40},{16,48},{24,56},{32,64},{40,72},{48,80},{56,88},{64,... | collective-permute-start | bytes 393224 | tf_op jit(solution)/shard_map/ppermute | solution.py:29
  29.1 1.4 %collective-permute-start.2 = (bf16[2,128,256]{2,1,0:T(8,128)(2,1)S(1)}, bf16[2,128,256]{2,1,0:T(8,128)(2,1)S(1)}, u32[]{:S(2)}, u32[]{:S(2)}) collective-permute-start(bf16[2,128,256]{2,1,0:T(8,128)(2,1)S(1)} %twin.1.twin_ref), channel_id=1, source_target_pairs={{0,24},{8,16},{16,8},{24,0},{32,56},{40,48},{48,40},{56,32},{64,88... | collective-permute-start | bytes 393224 | tf_op jit(solution)/shard_map/ppermute | solution.py:44
  30.6 1.1 %collective-permute-done.3.below_ref = bf16[2,128,256]{2,1,0:T(8,128)(2,1)S(1)} collective-permute-done((bf16[2,128,256]{2,1,0:T(8,128)(2,1)S(1)}, bf16[2,128,256]{2,1,0:T(8,128)(2,1)S(1)}, u32[]{:S(2)}, u32[]{:S(2)}) %collective-permute-start.3) | collective-permute-done | bytes 131104 | tf_op jit(solution)/shard_map/ppermute | solution.py:29
  31.6 3.8 %collective-permute-done.2.other_ref = bf16[2,128,256]{2,1,0:T(8,128)(2,1)S(1)} collective-permute-done((bf16[2,128,256]{2,1,0:T(8,128)(2,1)S(1)}, bf16[2,128,256]{2,1,0:T(8,128)(2,1)S(1)}, u32[]{:S(2)}, u32[]{:S(2)}) %collective-permute-start.2) | collective-permute-done | bytes 131104 | tf_op jit(solution)/shard_map/ppermute | solution.py:44
  35.4 1.0 %row.1 = (f32[2,128,256]{2,1,0:T(8,128)S(1)}, bf16[2,128,256]{2,1,0:T(8,128)(2,1)S(1)}, bf16[2,128,128]{2,1,0:T(8,128)(2,1)S(1)}) custom-call(s32[8]{0:T(128)S(1)} %concatenate.3.meta, bf16[2,128,256]{2,1,0:T(8,128)(2,1)S(1)} %get-tuple-element.52.own_ref, bf16[2,128,256]{2,1,0:T(8,128)(2,1)S(1)} %collective-permute-done.1.came_ref, ...), custom_call_target="tpu_custom_call" | custom-call | flops 100000000 | bytes 1245216 | tf_op jit(solution)/shard_map/row/pallas_call | solution.py:70
  36.4 5.0 %collective-permute-start.5 = (bf16[2,128,256]{2,1,0:T(8,128)(2,1)S(1)}, bf16[2,128,256]{2,1,0:T(8,128)(2,1)S(1)}, u32[]{:S(2)}, u32[]{:S(2)}) collective-permute-start(bf16[2,128,256]{2,1,0:T(8,128)(2,1)S(1)} %get-tuple-element.54), channel_id=1, source_target_pairs={{0,32},{8,40},{16,48},{24,56},{32,64},{40,72},{48,80},{56,88},{64,... | collective-permute-start | bytes 393224 | tf_op jit(solution)/shard_map/ppermute | solution.py:29
  41.5 4.1 %collective-permute-start.6 = (bf16[2,128,128]{2,1,0:T(8,128)(2,1)S(1)}, bf16[2,128,128]{2,1,0:T(8,128)(2,1)S(1)}, u32[]{:S(2)}, u32[]{:S(2)}) collective-permute-start(bf16[2,128,128]{2,1,0:T(8,128)(2,1)S(1)} %get-tuple-element.55), channel_id=1, source_target_pairs={{0,96},{8,104},{16,112},{24,120},{32,128},{40,136},{48,144},{56,15... | collective-permute-start | bytes 196616 | tf_op jit(solution)/shard_map/ppermute | solution.py:29
  45.5 0.7 ends.1
  46.3 3.5 %collective-permute-start.8 = (bf16[272,256]{1,0:T(8,128)(2,1)S(1)}, bf16[272,256]{1,0:T(8,128)(2,1)S(1)}, u32[]{:S(2)}, u32[]{:S(2)}) collective-permute-start(bf16[272,256]{1,0:T(8,128)(2,1)S(1)} %get-tuple-element.66), channel_id=1, source_target_pairs={{0,16},{8,24},{16,0},{24,8},{32,48},{40,56},{48,32},{56,40},{64,80... | collective-permute-start | bytes 417800 | tf_op jit(solution)/shard_map/ppermute | solution.py:40
  49.8 1.8 %attend.1 = (f32[128,2048]{1,0:T(8,128)S(1)}, bf16[128,2048]{1,0:T(8,128)(2,1)S(1)}, f32[2,128,128]{2,1,0:T(8,128)S(1)}) custom-call(s32[8]{0:T(128)S(1)} %concatenate.3.meta, f32[2,128,256]{2,1,0:T(8,128)S(1)} %get-tuple-element.53.prefix_ref, bf16[2,128,256]{2,1,0:T(8,128)(2,1)S(1)} %collective-permute-done.5.wide_ref, ...), custom_call_target="tpu_custom_call" | custom-call | flops 1000000000 | bytes 3736096 | tf_op jit(solution)/shard_map/attend/pallas_call | solution.py:70
  51.8 0.8 collective-permute-done.7.refs_1_
  52.6 1.7 %collective-permute-done.8.refs_2_ = bf16[272,256]{1,0:T(8,128)(2,1)S(1)} collective-permute-done((bf16[272,256]{1,0:T(8,128)(2,1)S(1)}, bf16[272,256]{1,0:T(8,128)(2,1)S(1)}, u32[]{:S(2)}, u32[]{:S(2)}) %collective-permute-start.8) | collective-permute-done | bytes 139296 | tf_op jit(solution)/shard_map/ppermute | solution.py:40
  54.3 0.7 collective-permute-done.9.refs_3_
  55.3 0.5 collective-permute-start.11
  55.8 2.6 %collective-permute-start.12 = (bf16[32,2048]{1,0:T(8,128)(2,1)S(1)}, bf16[32,2048]{1,0:T(8,128)(2,1)S(1)}, u32[]{:S(2)}, u32[]{:S(2)}) collective-permute-start(bf16[32,2048]{1,0:T(8,128)(2,1)S(1)} %get-tuple-element.72), channel_id=1, source_target_pairs={{0,4},{2,6},{4,0},{6,2},{1,5},{3,7},{5,1},{7,3},{8,12},{10,14},{12... | collective-permute-start | bytes 393224 | tf_op jit(solution)/shard_map/ppermute | solution.py:34
  58.4 1.3 %collective-permute-start.14 = (bf16[288,128]{1,0:T(8,128)(2,1)S(1)}, bf16[288,128]{1,0:T(8,128)(2,1)S(1)}, u32[]{:S(2)}, u32[]{:S(2)}) collective-permute-start(bf16[288,128]{1,0:T(8,128)(2,1)S(1)} %state.1.pay_ref), channel_id=1, source_target_pairs={{0,128},{8,136},{16,144},{24,152},{32,160},{40,168},{48,176},{56,1... | collective-permute-start | bytes 221192 | tf_op jit(solution)/shard_map/ppermute | solution.py:44
  59.7 1.3 %collective-permute-done.11.refs_0_ = bf16[32,2048]{1,0:T(8,128)(2,1)S(1)} collective-permute-done((bf16[32,2048]{1,0:T(8,128)(2,1)S(1)}, bf16[32,2048]{1,0:T(8,128)(2,1)S(1)}, u32[]{:S(2)}, u32[]{:S(2)}) %collective-permute-start.11) | collective-permute-done | bytes 131104 | tf_op jit(solution)/shard_map/ppermute | solution.py:34
  61.0 2.1 %collective-permute-done.12.refs_1_ = bf16[32,2048]{1,0:T(8,128)(2,1)S(1)} collective-permute-done((bf16[32,2048]{1,0:T(8,128)(2,1)S(1)}, bf16[32,2048]{1,0:T(8,128)(2,1)S(1)}, u32[]{:S(2)}, u32[]{:S(2)}) %collective-permute-start.12) | collective-permute-done | bytes 131104 | tf_op jit(solution)/shard_map/ppermute | solution.py:34
  63.2 1.4 %collective-permute-done.13.refs_2_ = bf16[32,2048]{1,0:T(8,128)(2,1)S(1)} collective-permute-done((bf16[32,2048]{1,0:T(8,128)(2,1)S(1)}, bf16[32,2048]{1,0:T(8,128)(2,1)S(1)}, u32[]{:S(2)}, u32[]{:S(2)}) %collective-permute-start.13) | collective-permute-done | bytes 131104 | tf_op jit(solution)/shard_map/ppermute | solution.py:34
  64.6 0.8 norm.1
  65.3 1.6 %collective-permute-done.14.came_ref = bf16[288,128]{1,0:T(8,128)(2,1)S(1)} collective-permute-done((bf16[288,128]{1,0:T(8,128)(2,1)S(1)}, bf16[288,128]{1,0:T(8,128)(2,1)S(1)}, u32[]{:S(2)}, u32[]{:S(2)}) %collective-permute-start.14) | collective-permute-done | bytes 73760 | tf_op jit(solution)/shard_map/ppermute | solution.py:44
  67.0 0.6 columns.1
  67.6 1.1 %collective-permute-start.16 = (bf16[64,512]{1,0:T(8,128)(2,1)S(1)}, bf16[64,512]{1,0:T(8,128)(2,1)S(1)}, u32[]{:S(2)}, u32[]{:S(2)}) collective-permute-start(bf16[64,512]{1,0:T(8,128)(2,1)S(1)} %get-tuple-element.78), channel_id=1, source_target_pairs={{0,6},{2,0},{4,2},{6,4},{1,7},{3,1},{5,3},{7,5},{8,14},{10,8},{12,... | collective-permute-start | bytes 196616 | tf_op jit(solution)/shard_map/ppermute | solution.py:34
  68.8 3.4 %collective-permute-start.23 = (bf16[288,128]{1,0:T(8,128)(2,1)S(1)}, bf16[288,128]{1,0:T(8,128)(2,1)S(1)}, u32[]{:S(2)}, u32[]{:S(2)}) collective-permute-start(bf16[288,128]{1,0:T(8,128)(2,1)S(1)} %sum.1), channel_id=1, source_target_pairs={{0,224},{8,232},{16,240},{24,248},{32,0},{40,8},{48,16},{56,24},{6... | collective-permute-start | bytes 221192 | tf_op jit(solution)/shard_map/ppermute | solution.py:34
  72.2 3.6 %collective-permute-start.18 = (bf16[64,512]{1,0:T(8,128)(2,1)S(1)}, bf16[64,512]{1,0:T(8,128)(2,1)S(1)}, u32[]{:S(2)}, u32[]{:S(2)}) collective-permute-start(bf16[64,512]{1,0:T(8,128)(2,1)S(1)} %get-tuple-element.79), channel_id=1, source_target_pairs={{0,4},{2,6},{4,0},{6,2},{1,5},{3,7},{5,1},{7,3},{8,12},{10,14},{12... | collective-permute-start | bytes 196616 | tf_op jit(solution)/shard_map/ppermute | solution.py:34
  75.9 1.3 %collective-permute-start.20 = (bf16[64,512]{1,0:T(8,128)(2,1)S(1)}, bf16[64,512]{1,0:T(8,128)(2,1)S(1)}, u32[]{:S(2)}, u32[]{:S(2)}) collective-permute-start(bf16[64,512]{1,0:T(8,128)(2,1)S(1)} %get-tuple-element.80), channel_id=1, source_target_pairs={{0,2},{2,4},{4,6},{6,0},{1,3},{3,5},{5,7},{7,1},{8,10},{10,12},{12... | collective-permute-start | bytes 196616 | tf_op jit(solution)/shard_map/ppermute | solution.py:34
  77.2 0.7 convolution_convert_fusion.2
  78.1 2.3 %collective-permute-start.17 = (bf16[64,3072]{1,0:T(8,128)(2,1)S(1)}, bf16[64,3072]{1,0:T(8,128)(2,1)S(1)}, u32[]{:S(2)}, u32[]{:S(2)}) collective-permute-start(bf16[64,3072]{1,0:T(8,128)(2,1)S(1)} %convolution_convert_fusion.2), channel_id=1, source_target_pairs={{0,2},{2,4},{4,6},{6,0},{1,3},{3,5},{5,7},{7,1},{8,10},{10,12},{12... | collective-permute-start | bytes 1179656 | tf_op jit(solution)/shard_map/ppermute | solution.py:34
  80.4 0.7 convolution_convert_fusion.1
  81.0 2.3 %collective-permute-start.19 = (bf16[64,3072]{1,0:T(8,128)(2,1)S(1)}, bf16[64,3072]{1,0:T(8,128)(2,1)S(1)}, u32[]{:S(2)}, u32[]{:S(2)}) collective-permute-start(bf16[64,3072]{1,0:T(8,128)(2,1)S(1)} %convolution_convert_fusion.1), channel_id=1, source_target_pairs={{0,4},{2,6},{4,0},{6,2},{1,5},{3,7},{5,1},{7,3},{8,12},{10,14},{12... | collective-permute-start | bytes 1179656 | tf_op jit(solution)/shard_map/ppermute | solution.py:34
  83.4 0.7 convolution_convert_fusion
  84.0 0.7 collective-permute-start.21
  84.8 2.6 %collective-permute-start.27 = (bf16[288,128]{1,0:T(8,128)(2,1)S(1)}, bf16[288,128]{1,0:T(8,128)(2,1)S(1)}, u32[]{:S(2)}, u32[]{:S(2)}) collective-permute-start(bf16[288,128]{1,0:T(8,128)(2,1)S(1)} %add_add_fusion.refs_0_), channel_id=1, source_target_pairs={{0,24},{8,0},{16,8},{24,16},{32,56},{40,32},{48,40},{56,48},{64,88... | collective-permute-start | bytes 221192 | tf_op jit(solution)/shard_map/ppermute | solution.py:40
  87.5 0.7 fusion.own_ref
  88.1 7.7 %collective-permute-done.17.refs_0_ = bf16[64,3072]{1,0:T(8,128)(2,1)S(1)} collective-permute-done((bf16[64,3072]{1,0:T(8,128)(2,1)S(1)}, bf16[64,3072]{1,0:T(8,128)(2,1)S(1)}, u32[]{:S(2)}, u32[]{:S(2)}) %collective-permute-start.17) | collective-permute-done | bytes 393248 | tf_op jit(solution)/shard_map/ppermute | solution.py:34
  95.8 3.9 %collective-permute-done.21.refs_2_ = bf16[64,3072]{1,0:T(8,128)(2,1)S(1)} collective-permute-done((bf16[64,3072]{1,0:T(8,128)(2,1)S(1)}, bf16[64,3072]{1,0:T(8,128)(2,1)S(1)}, u32[]{:S(2)}, u32[]{:S(2)}) %collective-permute-start.21) | collective-permute-done | bytes 393248 | tf_op jit(solution)/shard_map/ppermute | solution.py:34
  99.8 0.9 last.1
  100.7 0.7 collective-permute-done.25.refs_1_
  101.4 1.4 %finish.1 = (f32[4,256,128]{2,1,0:T(8,128)}, bf16[3,3,4,256]{3,2,1,0:T(4,128)(2,1)}) custom-call(s32[8]{0:T(128)S(1)} %concatenate.3.meta, bf16[288,128]{1,0:T(8,128)(2,1)S(1)} %add_add_fusion.refs_0_, bf16[288,128]{1,0:T(8,128)(2,1)S(1)} %collective-permute-done.25.refs_1_, bf16[288,128]{1,0:T(8,128)(2,1)S(1)} %collective-permute-done.26.refs_2_, ...), custom_call_target="tpu_custom_call" | custom-call | flops 1000000 | bytes 837664 | tf_op jit(solution)/shard_map/finish/pallas_call | solution.py:70
  (38 shorter events, 1.1 us)
Async XLA Ops:
  0.6 76.5 %copy-start = (bf16[512,3072]{1,0:T(8,128)(2,1)S(1)}, bf16[512,3072]{1,0:T(8,128)(2,1)}, u32[]{:S(2)}) copy-start(bf16[512,3072]{1,0:T(8,128)(2,1)} %param.17) | copy-start | bytes 9437188
  1.5 6.7 %collective-permute-start = (bf16[3,16,256]{2,1,0:T(8,128)(2,1)S(1)}, bf16[3,16,256]{2,1,0:T(8,128)(2,1)S(1)}, u32[]{:S(2)}, u32[]{:S(2)}) collective-permute-start(bf16[3,16,256]{2,1,0:T(8,128)(2,1)S(1)} %slice.4), channel_id=1, source_target_pairs={{0,8},{8,16},{16,24},{24,32},{32,40},{40,48},{48,56},{56,64},{64,7... | collective-permute-start | bytes 73736 | tf_op jit(solution)/shard_map/ppermute | solution.py:29
  8.3 41.5 %copy-start.3 = (bf16[256,2048]{1,0:T(8,128)(2,1)S(1)}, bf16[256,2048]{1,0:T(8,128)(2,1)}, u32[]{:S(2)}) copy-start(bf16[256,2048]{1,0:T(8,128)(2,1)} %w_ref.1) | copy-start | bytes 3145732
  8.3 41.5 %copy-start.4 = (f32[128]{0:T(128)S(1)}, f32[128]{0:T(128)}, u32[]{:S(2)}) copy-start(f32[128]{0:T(128)} %param.13) | copy-start | bytes 1540
  13.2 5.1 %collective-permute-start.1 = (bf16[2,128,256]{2,1,0:T(8,128)(2,1)S(1)}, bf16[2,128,256]{2,1,0:T(8,128)(2,1)S(1)}, u32[]{:S(2)}, u32[]{:S(2)}) collective-permute-start(bf16[2,128,256]{2,1,0:T(8,128)(2,1)S(1)} %get-tuple-element.52.own_ref), channel_id=1, source_target_pairs={{0,8},{8,0},{16,24},{24,16},{32,40},{40,32},{48,56},{56,48},{64,72... | collective-permute-start | bytes 393224 | tf_op jit(solution)/shard_map/ppermute | solution.py:44
  18.9 11.6 %collective-permute-start.4 = (bf16[2,128,256]{2,1,0:T(8,128)(2,1)S(1)}, bf16[2,128,256]{2,1,0:T(8,128)(2,1)S(1)}, u32[]{:S(2)}, u32[]{:S(2)}) collective-permute-start(bf16[2,128,256]{2,1,0:T(8,128)(2,1)S(1)} %twin.1.twin_ref), channel_id=1, source_target_pairs={{0,56},{8,48},{16,40},{24,32},{32,88},{40,80},{48,72},{56,64},{64,... | collective-permute-start | bytes 393224 | tf_op jit(solution)/shard_map/ppermute | solution.py:486
  25.3 6.3 %collective-permute-start.3 = (bf16[2,128,256]{2,1,0:T(8,128)(2,1)S(1)}, bf16[2,128,256]{2,1,0:T(8,128)(2,1)S(1)}, u32[]{:S(2)}, u32[]{:S(2)}) collective-permute-start(bf16[2,128,256]{2,1,0:T(8,128)(2,1)S(1)} %twin.1.twin_ref), channel_id=1, source_target_pairs={{0,32},{8,40},{16,48},{24,56},{32,64},{40,72},{48,80},{56,88},{64,... | collective-permute-start | bytes 393224 | tf_op jit(solution)/shard_map/ppermute | solution.py:29
  29.1 6.3 %collective-permute-start.2 = (bf16[2,128,256]{2,1,0:T(8,128)(2,1)S(1)}, bf16[2,128,256]{2,1,0:T(8,128)(2,1)S(1)}, u32[]{:S(2)}, u32[]{:S(2)}) collective-permute-start(bf16[2,128,256]{2,1,0:T(8,128)(2,1)S(1)} %twin.1.twin_ref), channel_id=1, source_target_pairs={{0,24},{8,16},{16,8},{24,0},{32,56},{40,48},{48,40},{56,32},{64,88... | collective-permute-start | bytes 393224 | tf_op jit(solution)/shard_map/ppermute | solution.py:44
  36.4 13.4 %collective-permute-start.5 = (bf16[2,128,256]{2,1,0:T(8,128)(2,1)S(1)}, bf16[2,128,256]{2,1,0:T(8,128)(2,1)S(1)}, u32[]{:S(2)}, u32[]{:S(2)}) collective-permute-start(bf16[2,128,256]{2,1,0:T(8,128)(2,1)S(1)} %get-tuple-element.54), channel_id=1, source_target_pairs={{0,32},{8,40},{16,48},{24,56},{32,64},{40,72},{48,80},{56,88},{64,... | collective-permute-start | bytes 393224 | tf_op jit(solution)/shard_map/ppermute | solution.py:29
  41.5 8.3 %collective-permute-start.6 = (bf16[2,128,128]{2,1,0:T(8,128)(2,1)S(1)}, bf16[2,128,128]{2,1,0:T(8,128)(2,1)S(1)}, u32[]{:S(2)}, u32[]{:S(2)}) collective-permute-start(bf16[2,128,128]{2,1,0:T(8,128)(2,1)S(1)} %get-tuple-element.55), channel_id=1, source_target_pairs={{0,96},{8,104},{16,112},{24,120},{32,128},{40,136},{48,144},{56,15... | collective-permute-start | bytes 196616 | tf_op jit(solution)/shard_map/ppermute | solution.py:29
  46.2 6.3 %collective-permute-start.7 = (bf16[272,256]{1,0:T(8,128)(2,1)S(1)}, bf16[272,256]{1,0:T(8,128)(2,1)S(1)}, u32[]{:S(2)}, u32[]{:S(2)}) collective-permute-start(bf16[272,256]{1,0:T(8,128)(2,1)S(1)} %get-tuple-element.65), channel_id=1, source_target_pairs={{0,8},{8,16},{16,24},{24,0},{32,40},{40,48},{48,56},{56,32},{64,72... | collective-permute-start | bytes 417800 | tf_op jit(solution)/shard_map/ppermute | solution.py:40
  46.3 8.0 %collective-permute-start.8 = (bf16[272,256]{1,0:T(8,128)(2,1)S(1)}, bf16[272,256]{1,0:T(8,128)(2,1)S(1)}, u32[]{:S(2)}, u32[]{:S(2)}) collective-permute-start(bf16[272,256]{1,0:T(8,128)(2,1)S(1)} %get-tuple-element.66), channel_id=1, source_target_pairs={{0,16},{8,24},{16,0},{24,8},{32,48},{40,56},{48,32},{56,40},{64,80... | collective-permute-start | bytes 417800 | tf_op jit(solution)/shard_map/ppermute | solution.py:40
  49.8 5.2 %collective-permute-start.9 = (bf16[272,256]{1,0:T(8,128)(2,1)S(1)}, bf16[272,256]{1,0:T(8,128)(2,1)S(1)}, u32[]{:S(2)}, u32[]{:S(2)}) collective-permute-start(bf16[272,256]{1,0:T(8,128)(2,1)S(1)} %get-tuple-element.67), channel_id=1, source_target_pairs={{0,24},{8,0},{16,8},{24,16},{32,56},{40,32},{48,40},{56,48},{64,88... | collective-permute-start | bytes 417800 | tf_op jit(solution)/shard_map/ppermute | solution.py:40
  51.7 3.5 %collective-permute-start.10 = (bf16[128,2048]{1,0:T(8,128)(2,1)S(1)}, bf16[128,2048]{1,0:T(8,128)(2,1)S(1)}, u32[]{:S(2)}, u32[]{:S(2)}) collective-permute-start(bf16[128,2048]{1,0:T(8,128)(2,1)S(1)} %get-tuple-element.69), channel_id=1, source_target_pairs={{0,1},{1,0},{2,3},{3,2},{4,5},{5,4},{6,7},{7,6},{8,9},{9,8},{10,11... | collective-permute-start | bytes 1572872 | tf_op jit(solution)/shard_map/ppermute | solution.py:34
  55.0 9.6 %copy-start.1 = (bf16[32,2048]{1,0:T(8,128)(2,1)S(1)}, bf16[32,2048]{1,0:T(8,128)(2,1)}, u32[]{:S(2)}) copy-start(bf16[32,2048]{1,0:T(8,128)(2,1)} %hidden_ref.1) | copy-start | bytes 393220
  55.0 9.6 %copy-start.2 = (f32[2048]{0:T(1024)S(1)}, f32[2048]{0:T(1024)}, u32[]{:S(2)}) copy-start(f32[2048]{0:T(1024)} %param.16) | copy-start | bytes 24580
  55.3 5.7 %collective-permute-start.11 = (bf16[32,2048]{1,0:T(8,128)(2,1)S(1)}, bf16[32,2048]{1,0:T(8,128)(2,1)S(1)}, u32[]{:S(2)}, u32[]{:S(2)}) collective-permute-start(bf16[32,2048]{1,0:T(8,128)(2,1)S(1)} %get-tuple-element.71), channel_id=1, source_target_pairs={{0,2},{2,4},{4,6},{6,0},{1,3},{3,5},{5,7},{7,1},{8,10},{10,12},{12... | collective-permute-start | bytes 393224 | tf_op jit(solution)/shard_map/ppermute | solution.py:34
  55.8 7.4 %collective-permute-start.12 = (bf16[32,2048]{1,0:T(8,128)(2,1)S(1)}, bf16[32,2048]{1,0:T(8,128)(2,1)S(1)}, u32[]{:S(2)}, u32[]{:S(2)}) collective-permute-start(bf16[32,2048]{1,0:T(8,128)(2,1)S(1)} %get-tuple-element.72), channel_id=1, source_target_pairs={{0,4},{2,6},{4,0},{6,2},{1,5},{3,7},{5,1},{7,3},{8,12},{10,14},{12... | collective-permute-start | bytes 393224 | tf_op jit(solution)/shard_map/ppermute | solution.py:34
  58.4 6.2 %collective-permute-start.13 = (bf16[32,2048]{1,0:T(8,128)(2,1)S(1)}, bf16[32,2048]{1,0:T(8,128)(2,1)S(1)}, u32[]{:S(2)}, u32[]{:S(2)}) collective-permute-start(bf16[32,2048]{1,0:T(8,128)(2,1)S(1)} %get-tuple-element.73), channel_id=1, source_target_pairs={{0,6},{2,0},{4,2},{6,4},{1,7},{3,1},{5,3},{7,5},{8,14},{10,8},{12,... | collective-permute-start | bytes 393224 | tf_op jit(solution)/shard_map/ppermute | solution.py:34
  58.4 8.6 %collective-permute-start.14 = (bf16[288,128]{1,0:T(8,128)(2,1)S(1)}, bf16[288,128]{1,0:T(8,128)(2,1)S(1)}, u32[]{:S(2)}, u32[]{:S(2)}) collective-permute-start(bf16[288,128]{1,0:T(8,128)(2,1)S(1)} %state.1.pay_ref), channel_id=1, source_target_pairs={{0,128},{8,136},{16,144},{24,152},{32,160},{40,168},{48,176},{56,1... | collective-permute-start | bytes 221192 | tf_op jit(solution)/shard_map/ppermute | solution.py:44
  65.3 1.6 %collective-permute-start.15 = (bf16[32,2048]{1,0:T(8,128)(2,1)S(1)}, bf16[32,2048]{1,0:T(8,128)(2,1)S(1)}, u32[]{:S(2)}, u32[]{:S(2)}) collective-permute-start(bf16[32,2048]{1,0:T(8,128)(2,1)S(1)} %get-tuple-element.76.mine_ref), channel_id=1, source_target_pairs={{0,1},{1,0},{2,3},{3,2},{4,5},{5,4},{6,7},{7,6},{8,9},{9,8},{10,11... | collective-permute-start | bytes 393224 | tf_op jit(solution)/shard_map/ppermute | solution.py:34
  67.6 8.3 %collective-permute-start.16 = (bf16[64,512]{1,0:T(8,128)(2,1)S(1)}, bf16[64,512]{1,0:T(8,128)(2,1)S(1)}, u32[]{:S(2)}, u32[]{:S(2)}) collective-permute-start(bf16[64,512]{1,0:T(8,128)(2,1)S(1)} %get-tuple-element.78), channel_id=1, source_target_pairs={{0,6},{2,0},{4,2},{6,4},{1,7},{3,1},{5,3},{7,5},{8,14},{10,8},{12,... | collective-permute-start | bytes 196616 | tf_op jit(solution)/shard_map/ppermute | solution.py:34
  68.7 15.4 %collective-permute-start.24 = (bf16[288,128]{1,0:T(8,128)(2,1)S(1)}, bf16[288,128]{1,0:T(8,128)(2,1)S(1)}, u32[]{:S(2)}, u32[]{:S(2)}) collective-permute-start(bf16[288,128]{1,0:T(8,128)(2,1)S(1)} %sum.1), channel_id=1, source_target_pairs={{0,64},{8,72},{16,80},{24,88},{32,96},{40,104},{48,112},{56,120},{... | collective-permute-start | bytes 221192 | tf_op jit(solution)/shard_map/ppermute | solution.py:34
  68.8 16.0 %collective-permute-start.23 = (bf16[288,128]{1,0:T(8,128)(2,1)S(1)}, bf16[288,128]{1,0:T(8,128)(2,1)S(1)}, u32[]{:S(2)}, u32[]{:S(2)}) collective-permute-start(bf16[288,128]{1,0:T(8,128)(2,1)S(1)} %sum.1), channel_id=1, source_target_pairs={{0,224},{8,232},{16,240},{24,248},{32,0},{40,8},{48,16},{56,24},{6... | collective-permute-start | bytes 221192 | tf_op jit(solution)/shard_map/ppermute | solution.py:34
  72.2 12.5 %collective-permute-start.22 = (bf16[288,128]{1,0:T(8,128)(2,1)S(1)}, bf16[288,128]{1,0:T(8,128)(2,1)S(1)}, u32[]{:S(2)}, u32[]{:S(2)}) collective-permute-start(bf16[288,128]{1,0:T(8,128)(2,1)S(1)} %sum.1), channel_id=1, source_target_pairs={{0,32},{8,40},{16,48},{24,56},{32,64},{40,72},{48,80},{56,88},{64,... | collective-permute-start | bytes 221192 | tf_op jit(solution)/shard_map/ppermute | solution.py:34
  72.2 5.9 %collective-permute-start.18 = (bf16[64,512]{1,0:T(8,128)(2,1)S(1)}, bf16[64,512]{1,0:T(8,128)(2,1)S(1)}, u32[]{:S(2)}, u32[]{:S(2)}) collective-permute-start(bf16[64,512]{1,0:T(8,128)(2,1)S(1)} %get-tuple-element.79), channel_id=1, source_target_pairs={{0,4},{2,6},{4,0},{6,2},{1,5},{3,7},{5,1},{7,3},{8,12},{10,14},{12... | collective-permute-start | bytes 196616 | tf_op jit(solution)/shard_map/ppermute | solution.py:34
  75.9 5.2 %collective-permute-start.20 = (bf16[64,512]{1,0:T(8,128)(2,1)S(1)}, bf16[64,512]{1,0:T(8,128)(2,1)S(1)}, u32[]{:S(2)}, u32[]{:S(2)}) collective-permute-start(bf16[64,512]{1,0:T(8,128)(2,1)S(1)} %get-tuple-element.80), channel_id=1, source_target_pairs={{0,2},{2,4},{4,6},{6,0},{1,3},{3,5},{5,7},{7,1},{8,10},{10,12},{12... | collective-permute-start | bytes 196616 | tf_op jit(solution)/shard_map/ppermute | solution.py:34
  78.1 17.7 %collective-permute-start.17 = (bf16[64,3072]{1,0:T(8,128)(2,1)S(1)}, bf16[64,3072]{1,0:T(8,128)(2,1)S(1)}, u32[]{:S(2)}, u32[]{:S(2)}) collective-permute-start(bf16[64,3072]{1,0:T(8,128)(2,1)S(1)} %convolution_convert_fusion.2), channel_id=1, source_target_pairs={{0,2},{2,4},{4,6},{6,0},{1,3},{3,5},{5,7},{7,1},{8,10},{10,12},{12... | collective-permute-start | bytes 1179656 | tf_op jit(solution)/shard_map/ppermute | solution.py:34
  81.0 14.8 %collective-permute-start.19 = (bf16[64,3072]{1,0:T(8,128)(2,1)S(1)}, bf16[64,3072]{1,0:T(8,128)(2,1)S(1)}, u32[]{:S(2)}, u32[]{:S(2)}) collective-permute-start(bf16[64,3072]{1,0:T(8,128)(2,1)S(1)} %convolution_convert_fusion.1), channel_id=1, source_target_pairs={{0,4},{2,6},{4,0},{6,2},{1,5},{3,7},{5,1},{7,3},{8,12},{10,14},{12... | collective-permute-start | bytes 1179656 | tf_op jit(solution)/shard_map/ppermute | solution.py:34
  84.0 15.7 %collective-permute-start.21 = (bf16[64,3072]{1,0:T(8,128)(2,1)S(1)}, bf16[64,3072]{1,0:T(8,128)(2,1)S(1)}, u32[]{:S(2)}, u32[]{:S(2)}) collective-permute-start(bf16[64,3072]{1,0:T(8,128)(2,1)S(1)} %convolution_convert_fusion), channel_id=1, source_target_pairs={{0,6},{2,0},{4,2},{6,4},{1,7},{3,1},{5,3},{7,5},{8,14},{10,8},{12,... | collective-permute-start | bytes 1179656 | tf_op jit(solution)/shard_map/ppermute | solution.py:34
  84.8 15.9 %collective-permute-start.27 = (bf16[288,128]{1,0:T(8,128)(2,1)S(1)}, bf16[288,128]{1,0:T(8,128)(2,1)S(1)}, u32[]{:S(2)}, u32[]{:S(2)}) collective-permute-start(bf16[288,128]{1,0:T(8,128)(2,1)S(1)} %add_add_fusion.refs_0_), channel_id=1, source_target_pairs={{0,24},{8,0},{16,8},{24,16},{32,56},{40,32},{48,40},{56,48},{64,88... | collective-permute-start | bytes 221192 | tf_op jit(solution)/shard_map/ppermute | solution.py:40
  87.4 13.3 %collective-permute-start.26 = (bf16[288,128]{1,0:T(8,128)(2,1)S(1)}, bf16[288,128]{1,0:T(8,128)(2,1)S(1)}, u32[]{:S(2)}, u32[]{:S(2)}) collective-permute-start(bf16[288,128]{1,0:T(8,128)(2,1)S(1)} %add_add_fusion.refs_0_), channel_id=1, source_target_pairs={{0,16},{8,24},{16,0},{24,8},{32,48},{40,56},{48,32},{56,40},{64,80... | collective-permute-start | bytes 221192 | tf_op jit(solution)/shard_map/ppermute | solution.py:40
  95.8 5.6 %collective-permute-start.25 = (bf16[288,128]{1,0:T(8,128)(2,1)S(1)}, bf16[288,128]{1,0:T(8,128)(2,1)S(1)}, u32[]{:S(2)}, u32[]{:S(2)}) collective-permute-start(bf16[288,128]{1,0:T(8,128)(2,1)S(1)} %add_add_fusion.refs_0_), channel_id=1, source_target_pairs={{0,8},{8,16},{16,24},{24,0},{32,40},{40,48},{48,56},{56,32},{64,72... | collective-permute-start | bytes 221192 | tf_op jit(solution)/shard_map/ppermute | solution.py:40

commit v8 on v7

--- a/solution.py
+++ b/solution.py
@@ -558,6 +558,15 @@
 
     parts = [partial(k).astype(BF16) for k in range(1, wins)]
     arrived = [rotate(part, "win", k + 1) for k, part in enumerate(parts)]
+    if lines == 8:
+        turns = [rotate(payload, "seq", steps * ROW) for steps in (1, 7, 2)]
+        payload = payload + (turns[0] + turns[1]) + turns[2]
+    else:
+        for bit in bits[1:]:
+            payload = payload + exchange(payload, "seq", bit * ROW)
+    quarters = [payload] + [row_rotate(payload, k) for k in range(1, ROW)]
+    *arrived, payload = lax.optimization_barrier((*arrived, quarters[1]))
+    quarters[1] = payload
     (projected,) = call(
         last_kernel,
         [out((2 * piece, w_qkv.shape[1]), BF16)],
@@ -567,14 +576,6 @@
         smem=0,
     )
 
-    if lines == 8:
-        turns = [rotate(payload, "seq", steps * ROW) for steps in (1, 7, 2)]
-        payload = payload + (turns[0] + turns[1]) + turns[2]
-    else:
-        for bit in bits[1:]:
-            payload = payload + exchange(payload, "seq", bit * ROW)
-    quarters = [payload] + [row_rotate(payload, k) for k in range(1, ROW)]
-    projected, *quarters = lax.optimization_barrier((projected, *quarters))
     final_states, conv_edges = call(
         finish_kernel,
         [out((REQS, heads * DK, DK), F32), out((CONV - 1, 3, REQS, width), BF16)],

time: 105 us -> 103 us (0.981); the launches traced: 103 us -> 102 us
    ppermute x14, waiting for transfers between devices: 16.8 us -> 12 us  [rotate(): lax.ppermute(value, axis, [(s, (s + steps) % count) for s in range(count)])]
    ppermute x6, waiting for transfers between devices: 3.93 us -> 8.13 us  [row_rotate(): return lax.ppermute(value, 'seq', pairs)]
where the time goes in v8:
time: 103 us; the launch traced here: 102 us
  starting transfers between devices  51.2 us (50%)
  waiting for transfers between devices  30.1 us (29%)
  Pallas kernels  15.6 us (15%)
  matrix products  2.64 us (3%)
  local copies, waits for them, and re-layouts  1.66 us (2%)
    ppermute x14, starting transfers between devices, rotate(): lax.ppermute(value, axis, [(s, (s + steps) % count) for s in range(count)])  18 us
    ppermute x4, starting transfers between devices, shift(): lax.ppermute(value, axis, [(s, s + steps) for s in range(max(0, count - s...  16.4 us
    pallas_call x13, Pallas kernels, call(): pl.pallas_call(kernel, out_shape=outs, in_specs=[SMEM] * smem + [HBM] * h...  15.6 us
    ppermute x14, waiting for transfers between devices, rotate(): lax.ppermute(value, axis, [(s, (s + steps) % count) for s in range(count)])  12 us
    ppermute x3, waiting for transfers between devices, exchange(): lax.ppermute(value, axis, [(s, s ^ bit) for s in range(lax.axis_size(axis...  8.87 us
    ppermute x6, waiting for transfers between devices, row_rotate(): return lax.ppermute(value, 'seq', pairs)  8.13 us
    ppermute x1, starting transfers between devices, body(): lax.ppermute(twin, 'seq', [(s, (s ^ ROW - 1) + ROW) for s in range(n_seq...  6.36 us
    ppermute x6, starting transfers between devices, row_rotate(): return lax.ppermute(value, 'seq', pairs)  6.16 us
  transfers between devices with their start and end apart: 28, of which 14 were waited for; matrix products, arithmetic and copies ran while one was open for 3% of the time, Pallas kernels for 7%

profile of v8, /device:TPU:24, one launch (start us, length us, event | category | flops | bytes accessed | tf_op | source)
XLA Modules:
  0.0 102.1 jit_solution(21547549245606934)
XLA Ops:
  0.6 0.9 slice.4
  1.5 3.5 %collective-permute-start = (bf16[3,16,256]{2,1,0:T(8,128)(2,1)S(1)}, bf16[3,16,256]{2,1,0:T(8,128)(2,1)S(1)}, u32[]{:S(2)}, u32[]{:S(2)}) collective-permute-start(bf16[3,16,256]{2,1,0:T(8,128)(2,1)S(1)} %slice.4), channel_id=1, source_target_pairs={{0,8},{8,16},{16,24},{24,32},{32,40},{40,48},{48,56},{56,64},{64,7... | collective-permute-start | bytes 73736 | tf_op jit(solution)/shard_map/ppermute | solution.py:29
  5.1 0.7 concatenate.3.meta
  5.8 2.4 %conv.1 = (bf16[3,256,256]{2,1,0:T(8,128)(2,1)S(1)}, bf16[3,16,256]{2,1,0:T(8,128)(2,1)S(1)}, bf16[3,16,256]{2,1,0:T(8,128)(2,1)S(1)}, f32[3,4,256]{2,1,0:T(4,128)S(1)}, f32[2,256]{1,0:T(2,128)S(1)}) custom-call(s32[8]{0:T(128)S(1)} %concatenate.3.meta, bf16[3,256,256]{2,1,0:T(8,128)(2,1)} %bitcast.20, f32[3,4,256]{2,1,0:T(4,128)} %taps_hbm.1, f32[2,256]{1,0:T(2,128)} %beta_hbm.1), custom_call_target="tpu_custom_call" | custom-call | flops 100000000 | bytes 864288 | tf_op jit(solution)/shard_map/conv/pallas_call | solution.py:70
  8.3 4.9 %prep.1 = (bf16[2,128,256]{2,1,0:T(8,128)(2,1)S(1)}, f32[2,256,256]{2,1,0:T(8,128)S(1)}, f32[2,256,128]{2,1,0:T(8,128)S(1)}, f32[2,256,128]{2,1,0:T(8,128)S(1)},...) custom-call(s32[8]{0:T(128)S(1)} %concatenate.3.meta, ...), custom_call_target="tpu_custom_call" | custom-call | flops 2000000000 | bytes 1859616 | tf_op jit(solution)/shard_map/prep/pallas_call | solution.py:70
  13.2 1.6 %collective-permute-start.1 = (bf16[2,128,256]{2,1,0:T(8,128)(2,1)S(1)}, bf16[2,128,256]{2,1,0:T(8,128)(2,1)S(1)}, u32[]{:S(2)}, u32[]{:S(2)}) collective-permute-start(bf16[2,128,256]{2,1,0:T(8,128)(2,1)S(1)} %get-tuple-element.51.own_ref), channel_id=1, source_target_pairs={{0,8},{8,0},{16,24},{24,16},{32,40},{40,32},{48,56},{56,48},{64,72... | collective-permute-start | bytes 393224 | tf_op jit(solution)/shard_map/ppermute | solution.py:44
  14.7 3.5 %collective-permute-done.1.came_ref = bf16[2,128,256]{2,1,0:T(8,128)(2,1)S(1)} collective-permute-done((bf16[2,128,256]{2,1,0:T(8,128)(2,1)S(1)}, bf16[2,128,256]{2,1,0:T(8,128)(2,1)S(1)}, u32[]{:S(2)}, u32[]{:S(2)}) %collective-permute-start.1) | collective-permute-done | bytes 131104 | tf_op jit(solution)/shard_map/ppermute | solution.py:44
  18.2 0.7 twin.1.twin_ref
  18.9 6.4 %collective-permute-start.4 = (bf16[2,128,256]{2,1,0:T(8,128)(2,1)S(1)}, bf16[2,128,256]{2,1,0:T(8,128)(2,1)S(1)}, u32[]{:S(2)}, u32[]{:S(2)}) collective-permute-start(bf16[2,128,256]{2,1,0:T(8,128)(2,1)S(1)} %twin.1.twin_ref), channel_id=1, source_target_pairs={{0,56},{8,48},{16,40},{24,32},{32,88},{40,80},{48,72},{56,64},{64,... | collective-permute-start | bytes 393224 | tf_op jit(solution)/shard_map/ppermute | solution.py:486
  25.3 3.8 %collective-permute-start.3 = (bf16[2,128,256]{2,1,0:T(8,128)(2,1)S(1)}, bf16[2,128,256]{2,1,0:T(8,128)(2,1)S(1)}, u32[]{:S(2)}, u32[]{:S(2)}) collective-permute-start(bf16[2,128,256]{2,1,0:T(8,128)(2,1)S(1)} %twin.1.twin_ref), channel_id=1, source_target_pairs={{0,32},{8,40},{16,48},{24,56},{32,64},{40,72},{48,80},{56,88},{64,... | collective-permute-start | bytes 393224 | tf_op jit(solution)/shard_map/ppermute | solution.py:29
  29.1 1.4 %collective-permute-start.2 = (bf16[2,128,256]{2,1,0:T(8,128)(2,1)S(1)}, bf16[2,128,256]{2,1,0:T(8,128)(2,1)S(1)}, u32[]{:S(2)}, u32[]{:S(2)}) collective-permute-start(bf16[2,128,256]{2,1,0:T(8,128)(2,1)S(1)} %twin.1.twin_ref), channel_id=1, source_target_pairs={{0,24},{8,16},{16,8},{24,0},{32,56},{40,48},{48,40},{56,32},{64,88... | collective-permute-start | bytes 393224 | tf_op jit(solution)/shard_map/ppermute | solution.py:44
  30.6 1.1 %collective-permute-done.3.below_ref = bf16[2,128,256]{2,1,0:T(8,128)(2,1)S(1)} collective-permute-done((bf16[2,128,256]{2,1,0:T(8,128)(2,1)S(1)}, bf16[2,128,256]{2,1,0:T(8,128)(2,1)S(1)}, u32[]{:S(2)}, u32[]{:S(2)}) %collective-permute-start.3) | collective-permute-done | bytes 131104 | tf_op jit(solution)/shard_map/ppermute | solution.py:29
  31.6 3.8 %collective-permute-done.2.other_ref = bf16[2,128,256]{2,1,0:T(8,128)(2,1)S(1)} collective-permute-done((bf16[2,128,256]{2,1,0:T(8,128)(2,1)S(1)}, bf16[2,128,256]{2,1,0:T(8,128)(2,1)S(1)}, u32[]{:S(2)}, u32[]{:S(2)}) %collective-permute-start.2) | collective-permute-done | bytes 131104 | tf_op jit(solution)/shard_map/ppermute | solution.py:44
  35.4 1.0 %row.1 = (f32[2,128,256]{2,1,0:T(8,128)S(1)}, bf16[2,128,256]{2,1,0:T(8,128)(2,1)S(1)}, bf16[2,128,128]{2,1,0:T(8,128)(2,1)S(1)}) custom-call(s32[8]{0:T(128)S(1)} %concatenate.3.meta, bf16[2,128,256]{2,1,0:T(8,128)(2,1)S(1)} %get-tuple-element.51.own_ref, bf16[2,128,256]{2,1,0:T(8,128)(2,1)S(1)} %collective-permute-done.1.came_ref, ...), custom_call_target="tpu_custom_call" | custom-call | flops 100000000 | bytes 1245216 | tf_op jit(solution)/shard_map/row/pallas_call | solution.py:70
  36.4 5.0 %collective-permute-start.5 = (bf16[2,128,256]{2,1,0:T(8,128)(2,1)S(1)}, bf16[2,128,256]{2,1,0:T(8,128)(2,1)S(1)}, u32[]{:S(2)}, u32[]{:S(2)}) collective-permute-start(bf16[2,128,256]{2,1,0:T(8,128)(2,1)S(1)} %get-tuple-element.53), channel_id=1, source_target_pairs={{0,32},{8,40},{16,48},{24,56},{32,64},{40,72},{48,80},{56,88},{64,... | collective-permute-start | bytes 393224 | tf_op jit(solution)/shard_map/ppermute | solution.py:29
  41.5 4.1 %collective-permute-start.6 = (bf16[2,128,128]{2,1,0:T(8,128)(2,1)S(1)}, bf16[2,128,128]{2,1,0:T(8,128)(2,1)S(1)}, u32[]{:S(2)}, u32[]{:S(2)}) collective-permute-start(bf16[2,128,128]{2,1,0:T(8,128)(2,1)S(1)} %get-tuple-element.54), channel_id=1, source_target_pairs={{0,96},{8,104},{16,112},{24,120},{32,128},{40,136},{48,144},{56,15... | collective-permute-start | bytes 196616 | tf_op jit(solution)/shard_map/ppermute | solution.py:29
  45.5 0.7 ends.1
  46.3 3.5 %collective-permute-start.8 = (bf16[272,256]{1,0:T(8,128)(2,1)S(1)}, bf16[272,256]{1,0:T(8,128)(2,1)S(1)}, u32[]{:S(2)}, u32[]{:S(2)}) collective-permute-start(bf16[272,256]{1,0:T(8,128)(2,1)S(1)} %get-tuple-element.65), channel_id=1, source_target_pairs={{0,16},{8,24},{16,0},{24,8},{32,48},{40,56},{48,32},{56,40},{64,80... | collective-permute-start | bytes 417800 | tf_op jit(solution)/shard_map/ppermute | solution.py:40
  49.8 1.8 %attend.1 = (f32[128,2048]{1,0:T(8,128)S(1)}, bf16[128,2048]{1,0:T(8,128)(2,1)S(1)}, f32[2,128,128]{2,1,0:T(8,128)S(1)}) custom-call(s32[8]{0:T(128)S(1)} %concatenate.3.meta, f32[2,128,256]{2,1,0:T(8,128)S(1)} %get-tuple-element.52.prefix_ref, bf16[2,128,256]{2,1,0:T(8,128)(2,1)S(1)} %collective-permute-done.5.wide_ref, ...), custom_call_target="tpu_custom_call" | custom-call | flops 1000000000 | bytes 3736096 | tf_op jit(solution)/shard_map/attend/pallas_call | solution.py:70
  51.8 0.8 collective-permute-done.7.refs_1_
  52.6 1.7 %collective-permute-done.8.refs_2_ = bf16[272,256]{1,0:T(8,128)(2,1)S(1)} collective-permute-done((bf16[272,256]{1,0:T(8,128)(2,1)S(1)}, bf16[272,256]{1,0:T(8,128)(2,1)S(1)}, u32[]{:S(2)}, u32[]{:S(2)}) %collective-permute-start.8) | collective-permute-done | bytes 139296 | tf_op jit(solution)/shard_map/ppermute | solution.py:40
  54.3 0.7 collective-permute-done.9.refs_3_
  55.3 0.5 collective-permute-start.11
  55.8 2.6 %collective-permute-start.12 = (bf16[32,2048]{1,0:T(8,128)(2,1)S(1)}, bf16[32,2048]{1,0:T(8,128)(2,1)S(1)}, u32[]{:S(2)}, u32[]{:S(2)}) collective-permute-start(bf16[32,2048]{1,0:T(8,128)(2,1)S(1)} %get-tuple-element.71), channel_id=1, source_target_pairs={{0,4},{2,6},{4,0},{6,2},{1,5},{3,7},{5,1},{7,3},{8,12},{10,14},{12... | collective-permute-start | bytes 393224 | tf_op jit(solution)/shard_map/ppermute | solution.py:34
  58.4 1.3 %collective-permute-start.14 = (bf16[288,128]{1,0:T(8,128)(2,1)S(1)}, bf16[288,128]{1,0:T(8,128)(2,1)S(1)}, u32[]{:S(2)}, u32[]{:S(2)}) collective-permute-start(bf16[288,128]{1,0:T(8,128)(2,1)S(1)} %state.1.pay_ref), channel_id=1, source_target_pairs={{0,128},{8,136},{16,144},{24,152},{32,160},{40,168},{48,176},{56,1... | collective-permute-start | bytes 221192 | tf_op jit(solution)/shard_map/ppermute | solution.py:44
  59.7 1.3 %collective-permute-done.11.refs_0_ = bf16[32,2048]{1,0:T(8,128)(2,1)S(1)} collective-permute-done((bf16[32,2048]{1,0:T(8,128)(2,1)S(1)}, bf16[32,2048]{1,0:T(8,128)(2,1)S(1)}, u32[]{:S(2)}, u32[]{:S(2)}) %collective-permute-start.11) | collective-permute-done | bytes 131104 | tf_op jit(solution)/shard_map/ppermute | solution.py:34
  61.0 2.1 %collective-permute-done.12.refs_1_ = bf16[32,2048]{1,0:T(8,128)(2,1)S(1)} collective-permute-done((bf16[32,2048]{1,0:T(8,128)(2,1)S(1)}, bf16[32,2048]{1,0:T(8,128)(2,1)S(1)}, u32[]{:S(2)}, u32[]{:S(2)}) %collective-permute-start.12) | collective-permute-done | bytes 131104 | tf_op jit(solution)/shard_map/ppermute | solution.py:34
  63.2 1.4 %collective-permute-done.13.refs_2_ = bf16[32,2048]{1,0:T(8,128)(2,1)S(1)} collective-permute-done((bf16[32,2048]{1,0:T(8,128)(2,1)S(1)}, bf16[32,2048]{1,0:T(8,128)(2,1)S(1)}, u32[]{:S(2)}, u32[]{:S(2)}) %collective-permute-start.13) | collective-permute-done | bytes 131104 | tf_op jit(solution)/shard_map/ppermute | solution.py:34
  64.6 0.8 norm.1
  65.3 1.6 %collective-permute-done.14.came_ref = bf16[288,128]{1,0:T(8,128)(2,1)S(1)} collective-permute-done((bf16[288,128]{1,0:T(8,128)(2,1)S(1)}, bf16[288,128]{1,0:T(8,128)(2,1)S(1)}, u32[]{:S(2)}, u32[]{:S(2)}) %collective-permute-start.14) | collective-permute-done | bytes 73760 | tf_op jit(solution)/shard_map/ppermute | solution.py:44
  67.0 0.6 columns.1
  67.6 1.1 %collective-permute-start.16 = (bf16[64,512]{1,0:T(8,128)(2,1)S(1)}, bf16[64,512]{1,0:T(8,128)(2,1)S(1)}, u32[]{:S(2)}, u32[]{:S(2)}) collective-permute-start(bf16[64,512]{1,0:T(8,128)(2,1)S(1)} %get-tuple-element.77), channel_id=1, source_target_pairs={{0,6},{2,0},{4,2},{6,4},{1,7},{3,1},{5,3},{7,5},{8,14},{10,8},{12,... | collective-permute-start | bytes 196616 | tf_op jit(solution)/shard_map/ppermute | solution.py:34
  68.8 3.4 %collective-permute-start.23 = (bf16[288,128]{1,0:T(8,128)(2,1)S(1)}, bf16[288,128]{1,0:T(8,128)(2,1)S(1)}, u32[]{:S(2)}, u32[]{:S(2)}) collective-permute-start(bf16[288,128]{1,0:T(8,128)(2,1)S(1)} %sum.1), channel_id=1, source_target_pairs={{0,224},{8,232},{16,240},{24,248},{32,0},{40,8},{48,16},{56,24},{6... | collective-permute-start | bytes 221192 | tf_op jit(solution)/shard_map/ppermute | solution.py:34
  72.2 3.6 %collective-permute-start.18 = (bf16[64,512]{1,0:T(8,128)(2,1)S(1)}, bf16[64,512]{1,0:T(8,128)(2,1)S(1)}, u32[]{:S(2)}, u32[]{:S(2)}) collective-permute-start(bf16[64,512]{1,0:T(8,128)(2,1)S(1)} %get-tuple-element.78), channel_id=1, source_target_pairs={{0,4},{2,6},{4,0},{6,2},{1,5},{3,7},{5,1},{7,3},{8,12},{10,14},{12... | collective-permute-start | bytes 196616 | tf_op jit(solution)/shard_map/ppermute | solution.py:34
  75.9 1.3 %collective-permute-start.20 = (bf16[64,512]{1,0:T(8,128)(2,1)S(1)}, bf16[64,512]{1,0:T(8,128)(2,1)S(1)}, u32[]{:S(2)}, u32[]{:S(2)}) collective-permute-start(bf16[64,512]{1,0:T(8,128)(2,1)S(1)} %get-tuple-element.79), channel_id=1, source_target_pairs={{0,2},{2,4},{4,6},{6,0},{1,3},{3,5},{5,7},{7,1},{8,10},{10,12},{12... | collective-permute-start | bytes 196616 | tf_op jit(solution)/shard_map/ppermute | solution.py:34
  77.2 0.7 convolution_convert_fusion.2
  78.1 2.3 %collective-permute-start.17 = (bf16[64,3072]{1,0:T(8,128)(2,1)S(1)}, bf16[64,3072]{1,0:T(8,128)(2,1)S(1)}, u32[]{:S(2)}, u32[]{:S(2)}) collective-permute-start(bf16[64,3072]{1,0:T(8,128)(2,1)S(1)} %convolution_convert_fusion.2), channel_id=1, source_target_pairs={{0,2},{2,4},{4,6},{6,0},{1,3},{3,5},{5,7},{7,1},{8,10},{10,12},{12... | collective-permute-start | bytes 1179656 | tf_op jit(solution)/shard_map/ppermute | solution.py:34
  80.4 0.7 convolution_convert_fusion.1
  81.0 2.3 %collective-permute-start.19 = (bf16[64,3072]{1,0:T(8,128)(2,1)S(1)}, bf16[64,3072]{1,0:T(8,128)(2,1)S(1)}, u32[]{:S(2)}, u32[]{:S(2)}) collective-permute-start(bf16[64,3072]{1,0:T(8,128)(2,1)S(1)} %convolution_convert_fusion.1), channel_id=1, source_target_pairs={{0,4},{2,6},{4,0},{6,2},{1,5},{3,7},{5,1},{7,3},{8,12},{10,14},{12... | collective-permute-start | bytes 1179656 | tf_op jit(solution)/shard_map/ppermute | solution.py:34
  83.4 0.7 convolution_convert_fusion
  84.0 0.7 collective-permute-start.21
  84.8 2.6 %collective-permute-start.27 = (bf16[288,128]{1,0:T(8,128)(2,1)S(1)}, bf16[288,128]{1,0:T(8,128)(2,1)S(1)}, u32[]{:S(2)}, u32[]{:S(2)}) collective-permute-start(bf16[288,128]{1,0:T(8,128)(2,1)S(1)} %add_add_fusion.refs_0_), channel_id=1, source_target_pairs={{0,24},{8,0},{16,8},{24,16},{32,56},{40,32},{48,40},{56,48},{64,88... | collective-permute-start | bytes 221192 | tf_op jit(solution)/shard_map/ppermute | solution.py:40
  87.4 0.7 fusion.own_ref
  88.0 4.9 %collective-permute-done.25.refs_1_ = bf16[288,128]{1,0:T(8,128)(2,1)S(1)} collective-permute-done((bf16[288,128]{1,0:T(8,128)(2,1)S(1)}, bf16[288,128]{1,0:T(8,128)(2,1)S(1)}, u32[]{:S(2)}, u32[]{:S(2)}) %collective-permute-start.25) | collective-permute-done | bytes 73760 | tf_op jit(solution)/shard_map/ppermute | solution.py:40
  92.9 2.9 %collective-permute-done.17.refs_0_ = bf16[64,3072]{1,0:T(8,128)(2,1)S(1)} collective-permute-done((bf16[64,3072]{1,0:T(8,128)(2,1)S(1)}, bf16[64,3072]{1,0:T(8,128)(2,1)S(1)}, u32[]{:S(2)}, u32[]{:S(2)}) %collective-permute-start.17) | collective-permute-done | bytes 393248 | tf_op jit(solution)/shard_map/ppermute | solution.py:34
  95.8 3.9 %collective-permute-done.21.refs_2_ = bf16[64,3072]{1,0:T(8,128)(2,1)S(1)} collective-permute-done((bf16[64,3072]{1,0:T(8,128)(2,1)S(1)}, bf16[64,3072]{1,0:T(8,128)(2,1)S(1)}, u32[]{:S(2)}, u32[]{:S(2)}) %collective-permute-start.21) | collective-permute-done | bytes 393248 | tf_op jit(solution)/shard_map/ppermute | solution.py:34
  99.8 0.9 last.1
  100.7 1.4 %finish.1 = (f32[4,256,128]{2,1,0:T(8,128)}, bf16[3,3,4,256]{3,2,1,0:T(4,128)(2,1)}) custom-call(s32[8]{0:T(128)S(1)} %concatenate.3.meta, bf16[288,128]{1,0:T(8,128)(2,1)S(1)} %add_add_fusion.refs_0_, bf16[288,128]{1,0:T(8,128)(2,1)S(1)} %collective-permute-done.25.refs_1_, bf16[288,128]{1,0:T(8,128)(2,1)S(1)} %collective-permute-done.26.refs_2_, ...), custom_call_target="tpu_custom_call" | custom-call | flops 1000000 | bytes 837664 | tf_op jit(solution)/shard_map/finish/pallas_call | solution.py:70
  (38 shorter events, 1.0 us)
Async XLA Ops:
  0.6 76.5 %copy-start = (bf16[512,3072]{1,0:T(8,128)(2,1)S(1)}, bf16[512,3072]{1,0:T(8,128)(2,1)}, u32[]{:S(2)}) copy-start(bf16[512,3072]{1,0:T(8,128)(2,1)} %param.17) | copy-start | bytes 9437188
  1.5 6.7 %collective-permute-start = (bf16[3,16,256]{2,1,0:T(8,128)(2,1)S(1)}, bf16[3,16,256]{2,1,0:T(8,128)(2,1)S(1)}, u32[]{:S(2)}, u32[]{:S(2)}) collective-permute-start(bf16[3,16,256]{2,1,0:T(8,128)(2,1)S(1)} %slice.4), channel_id=1, source_target_pairs={{0,8},{8,16},{16,24},{24,32},{32,40},{40,48},{48,56},{56,64},{64,7... | collective-permute-start | bytes 73736 | tf_op jit(solution)/shard_map/ppermute | solution.py:29
  8.3 41.5 %copy-start.3 = (bf16[256,2048]{1,0:T(8,128)(2,1)S(1)}, bf16[256,2048]{1,0:T(8,128)(2,1)}, u32[]{:S(2)}) copy-start(bf16[256,2048]{1,0:T(8,128)(2,1)} %w_ref.1) | copy-start | bytes 3145732
  8.3 41.5 %copy-start.4 = (f32[128]{0:T(128)S(1)}, f32[128]{0:T(128)}, u32[]{:S(2)}) copy-start(f32[128]{0:T(128)} %param.13) | copy-start | bytes 1540
  13.2 5.1 %collective-permute-start.1 = (bf16[2,128,256]{2,1,0:T(8,128)(2,1)S(1)}, bf16[2,128,256]{2,1,0:T(8,128)(2,1)S(1)}, u32[]{:S(2)}, u32[]{:S(2)}) collective-permute-start(bf16[2,128,256]{2,1,0:T(8,128)(2,1)S(1)} %get-tuple-element.51.own_ref), channel_id=1, source_target_pairs={{0,8},{8,0},{16,24},{24,16},{32,40},{40,32},{48,56},{56,48},{64,72... | collective-permute-start | bytes 393224 | tf_op jit(solution)/shard_map/ppermute | solution.py:44
  18.9 11.6 %collective-permute-start.4 = (bf16[2,128,256]{2,1,0:T(8,128)(2,1)S(1)}, bf16[2,128,256]{2,1,0:T(8,128)(2,1)S(1)}, u32[]{:S(2)}, u32[]{:S(2)}) collective-permute-start(bf16[2,128,256]{2,1,0:T(8,128)(2,1)S(1)} %twin.1.twin_ref), channel_id=1, source_target_pairs={{0,56},{8,48},{16,40},{24,32},{32,88},{40,80},{48,72},{56,64},{64,... | collective-permute-start | bytes 393224 | tf_op jit(solution)/shard_map/ppermute | solution.py:486
  25.3 6.3 %collective-permute-start.3 = (bf16[2,128,256]{2,1,0:T(8,128)(2,1)S(1)}, bf16[2,128,256]{2,1,0:T(8,128)(2,1)S(1)}, u32[]{:S(2)}, u32[]{:S(2)}) collective-permute-start(bf16[2,128,256]{2,1,0:T(8,128)(2,1)S(1)} %twin.1.twin_ref), channel_id=1, source_target_pairs={{0,32},{8,40},{16,48},{24,56},{32,64},{40,72},{48,80},{56,88},{64,... | collective-permute-start | bytes 393224 | tf_op jit(solution)/shard_map/ppermute | solution.py:29
  29.1 6.3 %collective-permute-start.2 = (bf16[2,128,256]{2,1,0:T(8,128)(2,1)S(1)}, bf16[2,128,256]{2,1,0:T(8,128)(2,1)S(1)}, u32[]{:S(2)}, u32[]{:S(2)}) collective-permute-start(bf16[2,128,256]{2,1,0:T(8,128)(2,1)S(1)} %twin.1.twin_ref), channel_id=1, source_target_pairs={{0,24},{8,16},{16,8},{24,0},{32,56},{40,48},{48,40},{56,32},{64,88... | collective-permute-start | bytes 393224 | tf_op jit(solution)/shard_map/ppermute | solution.py:44
  36.4 13.4 %collective-permute-start.5 = (bf16[2,128,256]{2,1,0:T(8,128)(2,1)S(1)}, bf16[2,128,256]{2,1,0:T(8,128)(2,1)S(1)}, u32[]{:S(2)}, u32[]{:S(2)}) collective-permute-start(bf16[2,128,256]{2,1,0:T(8,128)(2,1)S(1)} %get-tuple-element.53), channel_id=1, source_target_pairs={{0,32},{8,40},{16,48},{24,56},{32,64},{40,72},{48,80},{56,88},{64,... | collective-permute-start | bytes 393224 | tf_op jit(solution)/shard_map/ppermute | solution.py:29
  41.5 8.3 %collective-permute-start.6 = (bf16[2,128,128]{2,1,0:T(8,128)(2,1)S(1)}, bf16[2,128,128]{2,1,0:T(8,128)(2,1)S(1)}, u32[]{:S(2)}, u32[]{:S(2)}) collective-permute-start(bf16[2,128,128]{2,1,0:T(8,128)(2,1)S(1)} %get-tuple-element.54), channel_id=1, source_target_pairs={{0,96},{8,104},{16,112},{24,120},{32,128},{40,136},{48,144},{56,15... | collective-permute-start | bytes 196616 | tf_op jit(solution)/shard_map/ppermute | solution.py:29
  46.2 6.3 %collective-permute-start.7 = (bf16[272,256]{1,0:T(8,128)(2,1)S(1)}, bf16[272,256]{1,0:T(8,128)(2,1)S(1)}, u32[]{:S(2)}, u32[]{:S(2)}) collective-permute-start(bf16[272,256]{1,0:T(8,128)(2,1)S(1)} %get-tuple-element.64), channel_id=1, source_target_pairs={{0,8},{8,16},{16,24},{24,0},{32,40},{40,48},{48,56},{56,32},{64,72... | collective-permute-start | bytes 417800 | tf_op jit(solution)/shard_map/ppermute | solution.py:40
  46.3 8.0 %collective-permute-start.8 = (bf16[272,256]{1,0:T(8,128)(2,1)S(1)}, bf16[272,256]{1,0:T(8,128)(2,1)S(1)}, u32[]{:S(2)}, u32[]{:S(2)}) collective-permute-start(bf16[272,256]{1,0:T(8,128)(2,1)S(1)} %get-tuple-element.65), channel_id=1, source_target_pairs={{0,16},{8,24},{16,0},{24,8},{32,48},{40,56},{48,32},{56,40},{64,80... | collective-permute-start | bytes 417800 | tf_op jit(solution)/shard_map/ppermute | solution.py:40
  49.8 5.2 %collective-permute-start.9 = (bf16[272,256]{1,0:T(8,128)(2,1)S(1)}, bf16[272,256]{1,0:T(8,128)(2,1)S(1)}, u32[]{:S(2)}, u32[]{:S(2)}) collective-permute-start(bf16[272,256]{1,0:T(8,128)(2,1)S(1)} %get-tuple-element.66), channel_id=1, source_target_pairs={{0,24},{8,0},{16,8},{24,16},{32,56},{40,32},{48,40},{56,48},{64,88... | collective-permute-start | bytes 417800 | tf_op jit(solution)/shard_map/ppermute | solution.py:40
  51.7 3.5 %collective-permute-start.10 = (bf16[128,2048]{1,0:T(8,128)(2,1)S(1)}, bf16[128,2048]{1,0:T(8,128)(2,1)S(1)}, u32[]{:S(2)}, u32[]{:S(2)}) collective-permute-start(bf16[128,2048]{1,0:T(8,128)(2,1)S(1)} %get-tuple-element.68), channel_id=1, source_target_pairs={{0,1},{1,0},{2,3},{3,2},{4,5},{5,4},{6,7},{7,6},{8,9},{9,8},{10,11... | collective-permute-start | bytes 1572872 | tf_op jit(solution)/shard_map/ppermute | solution.py:34
  55.0 9.6 %copy-start.1 = (bf16[32,2048]{1,0:T(8,128)(2,1)S(1)}, bf16[32,2048]{1,0:T(8,128)(2,1)}, u32[]{:S(2)}) copy-start(bf16[32,2048]{1,0:T(8,128)(2,1)} %hidden_ref.1) | copy-start | bytes 393220
  55.0 9.6 %copy-start.2 = (f32[2048]{0:T(1024)S(1)}, f32[2048]{0:T(1024)}, u32[]{:S(2)}) copy-start(f32[2048]{0:T(1024)} %param.16) | copy-start | bytes 24580
  55.3 5.7 %collective-permute-start.11 = (bf16[32,2048]{1,0:T(8,128)(2,1)S(1)}, bf16[32,2048]{1,0:T(8,128)(2,1)S(1)}, u32[]{:S(2)}, u32[]{:S(2)}) collective-permute-start(bf16[32,2048]{1,0:T(8,128)(2,1)S(1)} %get-tuple-element.70), channel_id=1, source_target_pairs={{0,2},{2,4},{4,6},{6,0},{1,3},{3,5},{5,7},{7,1},{8,10},{10,12},{12... | collective-permute-start | bytes 393224 | tf_op jit(solution)/shard_map/ppermute | solution.py:34
  55.8 7.4 %collective-permute-start.12 = (bf16[32,2048]{1,0:T(8,128)(2,1)S(1)}, bf16[32,2048]{1,0:T(8,128)(2,1)S(1)}, u32[]{:S(2)}, u32[]{:S(2)}) collective-permute-start(bf16[32,2048]{1,0:T(8,128)(2,1)S(1)} %get-tuple-element.71), channel_id=1, source_target_pairs={{0,4},{2,6},{4,0},{6,2},{1,5},{3,7},{5,1},{7,3},{8,12},{10,14},{12... | collective-permute-start | bytes 393224 | tf_op jit(solution)/shard_map/ppermute | solution.py:34
  58.4 6.2 %collective-permute-start.13 = (bf16[32,2048]{1,0:T(8,128)(2,1)S(1)}, bf16[32,2048]{1,0:T(8,128)(2,1)S(1)}, u32[]{:S(2)}, u32[]{:S(2)}) collective-permute-start(bf16[32,2048]{1,0:T(8,128)(2,1)S(1)} %get-tuple-element.72), channel_id=1, source_target_pairs={{0,6},{2,0},{4,2},{6,4},{1,7},{3,1},{5,3},{7,5},{8,14},{10,8},{12,... | collective-permute-start | bytes 393224 | tf_op jit(solution)/shard_map/ppermute | solution.py:34
  58.4 8.6 %collective-permute-start.14 = (bf16[288,128]{1,0:T(8,128)(2,1)S(1)}, bf16[288,128]{1,0:T(8,128)(2,1)S(1)}, u32[]{:S(2)}, u32[]{:S(2)}) collective-permute-start(bf16[288,128]{1,0:T(8,128)(2,1)S(1)} %state.1.pay_ref), channel_id=1, source_target_pairs={{0,128},{8,136},{16,144},{24,152},{32,160},{40,168},{48,176},{56,1... | collective-permute-start | bytes 221192 | tf_op jit(solution)/shard_map/ppermute | solution.py:44
  65.3 1.6 %collective-permute-start.15 = (bf16[32,2048]{1,0:T(8,128)(2,1)S(1)}, bf16[32,2048]{1,0:T(8,128)(2,1)S(1)}, u32[]{:S(2)}, u32[]{:S(2)}) collective-permute-start(bf16[32,2048]{1,0:T(8,128)(2,1)S(1)} %get-tuple-element.75.mine_ref), channel_id=1, source_target_pairs={{0,1},{1,0},{2,3},{3,2},{4,5},{5,4},{6,7},{7,6},{8,9},{9,8},{10,11... | collective-permute-start | bytes 393224 | tf_op jit(solution)/shard_map/ppermute | solution.py:34
  67.6 8.3 %collective-permute-start.16 = (bf16[64,512]{1,0:T(8,128)(2,1)S(1)}, bf16[64,512]{1,0:T(8,128)(2,1)S(1)}, u32[]{:S(2)}, u32[]{:S(2)}) collective-permute-start(bf16[64,512]{1,0:T(8,128)(2,1)S(1)} %get-tuple-element.77), channel_id=1, source_target_pairs={{0,6},{2,0},{4,2},{6,4},{1,7},{3,1},{5,3},{7,5},{8,14},{10,8},{12,... | collective-permute-start | bytes 196616 | tf_op jit(solution)/shard_map/ppermute | solution.py:34
  68.7 15.4 %collective-permute-start.24 = (bf16[288,128]{1,0:T(8,128)(2,1)S(1)}, bf16[288,128]{1,0:T(8,128)(2,1)S(1)}, u32[]{:S(2)}, u32[]{:S(2)}) collective-permute-start(bf16[288,128]{1,0:T(8,128)(2,1)S(1)} %sum.1), channel_id=1, source_target_pairs={{0,64},{8,72},{16,80},{24,88},{32,96},{40,104},{48,112},{56,120},{... | collective-permute-start | bytes 221192 | tf_op jit(solution)/shard_map/ppermute | solution.py:34
  68.8 16.0 %collective-permute-start.23 = (bf16[288,128]{1,0:T(8,128)(2,1)S(1)}, bf16[288,128]{1,0:T(8,128)(2,1)S(1)}, u32[]{:S(2)}, u32[]{:S(2)}) collective-permute-start(bf16[288,128]{1,0:T(8,128)(2,1)S(1)} %sum.1), channel_id=1, source_target_pairs={{0,224},{8,232},{16,240},{24,248},{32,0},{40,8},{48,16},{56,24},{6... | collective-permute-start | bytes 221192 | tf_op jit(solution)/shard_map/ppermute | solution.py:34
  72.2 12.5 %collective-permute-start.22 = (bf16[288,128]{1,0:T(8,128)(2,1)S(1)}, bf16[288,128]{1,0:T(8,128)(2,1)S(1)}, u32[]{:S(2)}, u32[]{:S(2)}) collective-permute-start(bf16[288,128]{1,0:T(8,128)(2,1)S(1)} %sum.1), channel_id=1, source_target_pairs={{0,32},{8,40},{16,48},{24,56},{32,64},{40,72},{48,80},{56,88},{64,... | collective-permute-start | bytes 221192 | tf_op jit(solution)/shard_map/ppermute | solution.py:34
  72.2 5.9 %collective-permute-start.18 = (bf16[64,512]{1,0:T(8,128)(2,1)S(1)}, bf16[64,512]{1,0:T(8,128)(2,1)S(1)}, u32[]{:S(2)}, u32[]{:S(2)}) collective-permute-start(bf16[64,512]{1,0:T(8,128)(2,1)S(1)} %get-tuple-element.78), channel_id=1, source_target_pairs={{0,4},{2,6},{4,0},{6,2},{1,5},{3,7},{5,1},{7,3},{8,12},{10,14},{12... | collective-permute-start | bytes 196616 | tf_op jit(solution)/shard_map/ppermute | solution.py:34
  75.9 5.2 %collective-permute-start.20 = (bf16[64,512]{1,0:T(8,128)(2,1)S(1)}, bf16[64,512]{1,0:T(8,128)(2,1)S(1)}, u32[]{:S(2)}, u32[]{:S(2)}) collective-permute-start(bf16[64,512]{1,0:T(8,128)(2,1)S(1)} %get-tuple-element.79), channel_id=1, source_target_pairs={{0,2},{2,4},{4,6},{6,0},{1,3},{3,5},{5,7},{7,1},{8,10},{10,12},{12... | collective-permute-start | bytes 196616 | tf_op jit(solution)/shard_map/ppermute | solution.py:34
  78.1 17.7 %collective-permute-start.17 = (bf16[64,3072]{1,0:T(8,128)(2,1)S(1)}, bf16[64,3072]{1,0:T(8,128)(2,1)S(1)}, u32[]{:S(2)}, u32[]{:S(2)}) collective-permute-start(bf16[64,3072]{1,0:T(8,128)(2,1)S(1)} %convolution_convert_fusion.2), channel_id=1, source_target_pairs={{0,2},{2,4},{4,6},{6,0},{1,3},{3,5},{5,7},{7,1},{8,10},{10,12},{12... | collective-permute-start | bytes 1179656 | tf_op jit(solution)/shard_map/ppermute | solution.py:34
  81.0 14.8 %collective-permute-start.19 = (bf16[64,3072]{1,0:T(8,128)(2,1)S(1)}, bf16[64,3072]{1,0:T(8,128)(2,1)S(1)}, u32[]{:S(2)}, u32[]{:S(2)}) collective-permute-start(bf16[64,3072]{1,0:T(8,128)(2,1)S(1)} %convolution_convert_fusion.1), channel_id=1, source_target_pairs={{0,4},{2,6},{4,0},{6,2},{1,5},{3,7},{5,1},{7,3},{8,12},{10,14},{12... | collective-permute-start | bytes 1179656 | tf_op jit(solution)/shard_map/ppermute | solution.py:34
  84.0 15.7 %collective-permute-start.21 = (bf16[64,3072]{1,0:T(8,128)(2,1)S(1)}, bf16[64,3072]{1,0:T(8,128)(2,1)S(1)}, u32[]{:S(2)}, u32[]{:S(2)}) collective-permute-start(bf16[64,3072]{1,0:T(8,128)(2,1)S(1)} %convolution_convert_fusion), channel_id=1, source_target_pairs={{0,6},{2,0},{4,2},{6,4},{1,7},{3,1},{5,3},{7,5},{8,14},{10,8},{12,... | collective-permute-start | bytes 1179656 | tf_op jit(solution)/shard_map/ppermute | solution.py:34
  84.8 15.9 %collective-permute-start.27 = (bf16[288,128]{1,0:T(8,128)(2,1)S(1)}, bf16[288,128]{1,0:T(8,128)(2,1)S(1)}, u32[]{:S(2)}, u32[]{:S(2)}) collective-permute-start(bf16[288,128]{1,0:T(8,128)(2,1)S(1)} %add_add_fusion.refs_0_), channel_id=1, source_target_pairs={{0,24},{8,0},{16,8},{24,16},{32,56},{40,32},{48,40},{56,48},{64,88... | collective-permute-start | bytes 221192 | tf_op jit(solution)/shard_map/ppermute | solution.py:40
  87.4 5.6 %collective-permute-start.25 = (bf16[288,128]{1,0:T(8,128)(2,1)S(1)}, bf16[288,128]{1,0:T(8,128)(2,1)S(1)}, u32[]{:S(2)}, u32[]{:S(2)}) collective-permute-start(bf16[288,128]{1,0:T(8,128)(2,1)S(1)} %add_add_fusion.refs_0_), channel_id=1, source_target_pairs={{0,8},{8,16},{16,24},{24,0},{32,40},{40,48},{48,56},{56,32},{64,72... | collective-permute-start | bytes 221192 | tf_op jit(solution)/shard_map/ppermute | solution.py:40
  92.9 7.7 %collective-permute-start.26 = (bf16[288,128]{1,0:T(8,128)(2,1)S(1)}, bf16[288,128]{1,0:T(8,128)(2,1)S(1)}, u32[]{:S(2)}, u32[]{:S(2)}) collective-permute-start(bf16[288,128]{1,0:T(8,128)(2,1)S(1)} %add_add_fusion.refs_0_), channel_id=1, source_target_pairs={{0,16},{8,24},{16,0},{24,8},{32,48},{40,56},{48,32},{56,40},{64,80... | collective-permute-start | bytes 221192 | tf_op jit(solution)/shard_map/ppermute | solution.py:40

commit v9 on v8

--- a/solution.py
+++ b/solution.py
@@ -551,6 +551,7 @@
         meta, normed, peer,
         scratch=[pltpu.VMEM((wins, 2 * piece, model // wins), BF16)],
     )
+    *cols, payload = lax.optimization_barrier((*cols, payload))
     blocks = [cols[0]] + [rotate(cols[k], "win", k) for k in range(1, wins)]
 
     def partial(k):
@@ -565,8 +566,15 @@
         for bit in bits[1:]:
             payload = payload + exchange(payload, "seq", bit * ROW)
     quarters = [payload] + [row_rotate(payload, k) for k in range(1, ROW)]
-    *arrived, payload = lax.optimization_barrier((*arrived, quarters[1]))
-    quarters[1] = payload
+    final_states, conv_edges = call(
+        finish_kernel,
+        [out((REQS, heads * DK, DK), F32), out((CONV - 1, 3, REQS, width), BF16)],
+        "finish",
+        10**6,
+        meta, *quarters,
+        scratch=[pltpu.VMEM((REQS, *quarter.shape), BF16)],
+    )
+    *arrived, conv_edges = lax.optimization_barrier((*arrived, conv_edges))
     (projected,) = call(
         last_kernel,
         [out((2 * piece, w_qkv.shape[1]), BF16)],
@@ -576,14 +584,6 @@
         smem=0,
     )
 
-    final_states, conv_edges = call(
-        finish_kernel,
-        [out((REQS, heads * DK, DK), F32), out((CONV - 1, 3, REQS, width), BF16)],
-        "finish",
-        10**6,
-        meta, *quarters,
-        scratch=[pltpu.VMEM((REQS, *quarter.shape), BF16)],
-    )
     final_states = final_states.reshape(REQS, heads, DK, DK)
     conv_edges = conv_edges.transpose(2, 0, 1, 3)
     return (projected, stream_out, final_states, conv_edges)

time: 103 us -> 101 us (0.981)
  waiting for transfers between devices: 30.1 us -> 28.1 us
    ppermute x14, waiting for transfers between devices: 12 us -> 9.6 us  [rotate(): lax.ppermute(value, axis, [(s, (s + steps) % count) for s in range(count)])]
  transfers between devices with their start and end apart: 28 -> 28, of which waited for: 14 -> 16; matrix products, arithmetic and copies ran while one was open for 3% -> 3% of each run, Pallas kernels for 7% -> 7%
where the time goes in v9:
time: 101 us
  starting transfers between devices  51.7 us (51%)
  waiting for transfers between devices  28.1 us (28%)
  Pallas kernels  15.6 us (15%)
  matrix products  2.72 us (3%)
  local copies, waits for them, and re-layouts  1.66 us (2%)
    ppermute x14, starting transfers between devices, rotate(): lax.ppermute(value, axis, [(s, (s + steps) % count) for s in range(count)])  17.6 us
    ppermute x4, starting transfers between devices, shift(): lax.ppermute(value, axis, [(s, s + steps) for s in range(max(0, count - s...  16.4 us
    pallas_call x13, Pallas kernels, call(): pl.pallas_call(kernel, out_shape=outs, in_specs=[SMEM] * smem + [HBM] * h...  15.6 us
    ppermute x14, waiting for transfers between devices, rotate(): lax.ppermute(value, axis, [(s, (s + steps) % count) for s in range(count)])  9.6 us
    ppermute x3, waiting for transfers between devices, exchange(): lax.ppermute(value, axis, [(s, s ^ bit) for s in range(lax.axis_size(axis...  8.87 us
    ppermute x6, waiting for transfers between devices, row_rotate(): return lax.ppermute(value, 'seq', pairs)  8.58 us
    ppermute x6, starting transfers between devices, row_rotate(): return lax.ppermute(value, 'seq', pairs)  7.01 us
    ppermute x1, starting transfers between devices, body(): lax.ppermute(twin, 'seq', [(s, (s ^ ROW - 1) + ROW) for s in range(n_seq...  6.36 us
  transfers between devices with their start and end apart: 28, of which 16 were waited for; matrix products, arithmetic and copies ran while one was open for 3% of the time, Pallas kernels for 7%

profile of v9, /device:TPU:24, one launch (start us, length us, event | category | flops | bytes accessed | tf_op | source)
XLA Modules:
  0.0 100.7 jit_solution(11777184419671563824)
XLA Ops:
  0.6 0.9 slice.4
  1.5 3.5 %collective-permute-start = (bf16[3,16,256]{2,1,0:T(8,128)(2,1)S(1)}, bf16[3,16,256]{2,1,0:T(8,128)(2,1)S(1)}, u32[]{:S(2)}, u32[]{:S(2)}) collective-permute-start(bf16[3,16,256]{2,1,0:T(8,128)(2,1)S(1)} %slice.4), channel_id=1, source_target_pairs={{0,8},{8,16},{16,24},{24,32},{32,40},{40,48},{48,56},{56,64},{64,7... | collective-permute-start | bytes 73736 | tf_op jit(solution)/shard_map/ppermute | solution.py:29
  5.1 0.7 concatenate.3.meta
  5.8 2.4 %conv.1 = (bf16[3,256,256]{2,1,0:T(8,128)(2,1)S(1)}, bf16[3,16,256]{2,1,0:T(8,128)(2,1)S(1)}, bf16[3,16,256]{2,1,0:T(8,128)(2,1)S(1)}, f32[3,4,256]{2,1,0:T(4,128)S(1)}, f32[2,256]{1,0:T(2,128)S(1)}) custom-call(s32[8]{0:T(128)S(1)} %concatenate.3.meta, bf16[3,256,256]{2,1,0:T(8,128)(2,1)} %bitcast.20, f32[3,4,256]{2,1,0:T(4,128)} %taps_hbm.1, f32[2,256]{1,0:T(2,128)} %beta_hbm.1), custom_call_target="tpu_custom_call" | custom-call | flops 100000000 | bytes 864288 | tf_op jit(solution)/shard_map/conv/pallas_call | solution.py:70
  8.3 4.9 %prep.1 = (bf16[2,128,256]{2,1,0:T(8,128)(2,1)S(1)}, f32[2,256,256]{2,1,0:T(8,128)S(1)}, f32[2,256,128]{2,1,0:T(8,128)S(1)}, f32[2,256,128]{2,1,0:T(8,128)S(1)},...) custom-call(s32[8]{0:T(128)S(1)} %concatenate.3.meta, ...), custom_call_target="tpu_custom_call" | custom-call | flops 2000000000 | bytes 1859616 | tf_op jit(solution)/shard_map/prep/pallas_call | solution.py:70
  13.2 1.6 %collective-permute-start.1 = (bf16[2,128,256]{2,1,0:T(8,128)(2,1)S(1)}, bf16[2,128,256]{2,1,0:T(8,128)(2,1)S(1)}, u32[]{:S(2)}, u32[]{:S(2)}) collective-permute-start(bf16[2,128,256]{2,1,0:T(8,128)(2,1)S(1)} %get-tuple-element.56.own_ref), channel_id=1, source_target_pairs={{0,8},{8,0},{16,24},{24,16},{32,40},{40,32},{48,56},{56,48},{64,72... | collective-permute-start | bytes 393224 | tf_op jit(solution)/shard_map/ppermute | solution.py:44
  14.7 3.5 %collective-permute-done.1.came_ref = bf16[2,128,256]{2,1,0:T(8,128)(2,1)S(1)} collective-permute-done((bf16[2,128,256]{2,1,0:T(8,128)(2,1)S(1)}, bf16[2,128,256]{2,1,0:T(8,128)(2,1)S(1)}, u32[]{:S(2)}, u32[]{:S(2)}) %collective-permute-start.1) | collective-permute-done | bytes 131104 | tf_op jit(solution)/shard_map/ppermute | solution.py:44
  18.2 0.7 twin.1.twin_ref
  18.9 6.4 %collective-permute-start.4 = (bf16[2,128,256]{2,1,0:T(8,128)(2,1)S(1)}, bf16[2,128,256]{2,1,0:T(8,128)(2,1)S(1)}, u32[]{:S(2)}, u32[]{:S(2)}) collective-permute-start(bf16[2,128,256]{2,1,0:T(8,128)(2,1)S(1)} %twin.1.twin_ref), channel_id=1, source_target_pairs={{0,56},{8,48},{16,40},{24,32},{32,88},{40,80},{48,72},{56,64},{64,... | collective-permute-start | bytes 393224 | tf_op jit(solution)/shard_map/ppermute | solution.py:486
  25.3 3.8 %collective-permute-start.3 = (bf16[2,128,256]{2,1,0:T(8,128)(2,1)S(1)}, bf16[2,128,256]{2,1,0:T(8,128)(2,1)S(1)}, u32[]{:S(2)}, u32[]{:S(2)}) collective-permute-start(bf16[2,128,256]{2,1,0:T(8,128)(2,1)S(1)} %twin.1.twin_ref), channel_id=1, source_target_pairs={{0,32},{8,40},{16,48},{24,56},{32,64},{40,72},{48,80},{56,88},{64,... | collective-permute-start | bytes 393224 | tf_op jit(solution)/shard_map/ppermute | solution.py:29
  29.1 1.4 %collective-permute-start.2 = (bf16[2,128,256]{2,1,0:T(8,128)(2,1)S(1)}, bf16[2,128,256]{2,1,0:T(8,128)(2,1)S(1)}, u32[]{:S(2)}, u32[]{:S(2)}) collective-permute-start(bf16[2,128,256]{2,1,0:T(8,128)(2,1)S(1)} %twin.1.twin_ref), channel_id=1, source_target_pairs={{0,24},{8,16},{16,8},{24,0},{32,56},{40,48},{48,40},{56,32},{64,88... | collective-permute-start | bytes 393224 | tf_op jit(solution)/shard_map/ppermute | solution.py:44
  30.6 1.1 %collective-permute-done.3.below_ref = bf16[2,128,256]{2,1,0:T(8,128)(2,1)S(1)} collective-permute-done((bf16[2,128,256]{2,1,0:T(8,128)(2,1)S(1)}, bf16[2,128,256]{2,1,0:T(8,128)(2,1)S(1)}, u32[]{:S(2)}, u32[]{:S(2)}) %collective-permute-start.3) | collective-permute-done | bytes 131104 | tf_op jit(solution)/shard_map/ppermute | solution.py:29
  31.6 3.8 %collective-permute-done.2.other_ref = bf16[2,128,256]{2,1,0:T(8,128)(2,1)S(1)} collective-permute-done((bf16[2,128,256]{2,1,0:T(8,128)(2,1)S(1)}, bf16[2,128,256]{2,1,0:T(8,128)(2,1)S(1)}, u32[]{:S(2)}, u32[]{:S(2)}) %collective-permute-start.2) | collective-permute-done | bytes 131104 | tf_op jit(solution)/shard_map/ppermute | solution.py:44
  35.4 1.0 %row.1 = (f32[2,128,256]{2,1,0:T(8,128)S(1)}, bf16[2,128,256]{2,1,0:T(8,128)(2,1)S(1)}, bf16[2,128,128]{2,1,0:T(8,128)(2,1)S(1)}) custom-call(s32[8]{0:T(128)S(1)} %concatenate.3.meta, bf16[2,128,256]{2,1,0:T(8,128)(2,1)S(1)} %get-tuple-element.56.own_ref, bf16[2,128,256]{2,1,0:T(8,128)(2,1)S(1)} %collective-permute-done.1.came_ref, ...), custom_call_target="tpu_custom_call" | custom-call | flops 100000000 | bytes 1245216 | tf_op jit(solution)/shard_map/row/pallas_call | solution.py:70
  36.4 5.0 %collective-permute-start.5 = (bf16[2,128,256]{2,1,0:T(8,128)(2,1)S(1)}, bf16[2,128,256]{2,1,0:T(8,128)(2,1)S(1)}, u32[]{:S(2)}, u32[]{:S(2)}) collective-permute-start(bf16[2,128,256]{2,1,0:T(8,128)(2,1)S(1)} %get-tuple-element.58), channel_id=1, source_target_pairs={{0,32},{8,40},{16,48},{24,56},{32,64},{40,72},{48,80},{56,88},{64,... | collective-permute-start | bytes 393224 | tf_op jit(solution)/shard_map/ppermute | solution.py:29
  41.5 4.1 %collective-permute-start.6 = (bf16[2,128,128]{2,1,0:T(8,128)(2,1)S(1)}, bf16[2,128,128]{2,1,0:T(8,128)(2,1)S(1)}, u32[]{:S(2)}, u32[]{:S(2)}) collective-permute-start(bf16[2,128,128]{2,1,0:T(8,128)(2,1)S(1)} %get-tuple-element.59), channel_id=1, source_target_pairs={{0,96},{8,104},{16,112},{24,120},{32,128},{40,136},{48,144},{56,15... | collective-permute-start | bytes 196616 | tf_op jit(solution)/shard_map/ppermute | solution.py:29
  45.5 0.7 ends.1
  46.3 3.5 %collective-permute-start.8 = (bf16[272,256]{1,0:T(8,128)(2,1)S(1)}, bf16[272,256]{1,0:T(8,128)(2,1)S(1)}, u32[]{:S(2)}, u32[]{:S(2)}) collective-permute-start(bf16[272,256]{1,0:T(8,128)(2,1)S(1)} %get-tuple-element.70), channel_id=1, source_target_pairs={{0,16},{8,24},{16,0},{24,8},{32,48},{40,56},{48,32},{56,40},{64,80... | collective-permute-start | bytes 417800 | tf_op jit(solution)/shard_map/ppermute | solution.py:40
  49.8 1.8 %attend.1 = (f32[128,2048]{1,0:T(8,128)S(1)}, bf16[128,2048]{1,0:T(8,128)(2,1)S(1)}, f32[2,128,128]{2,1,0:T(8,128)S(1)}) custom-call(s32[8]{0:T(128)S(1)} %concatenate.3.meta, f32[2,128,256]{2,1,0:T(8,128)S(1)} %get-tuple-element.57.prefix_ref, bf16[2,128,256]{2,1,0:T(8,128)(2,1)S(1)} %collective-permute-done.5.wide_ref, ...), custom_call_target="tpu_custom_call" | custom-call | flops 1000000000 | bytes 3736096 | tf_op jit(solution)/shard_map/attend/pallas_call | solution.py:70
  51.8 0.8 collective-permute-done.7.refs_1_
  52.6 1.7 %collective-permute-done.8.refs_2_ = bf16[272,256]{1,0:T(8,128)(2,1)S(1)} collective-permute-done((bf16[272,256]{1,0:T(8,128)(2,1)S(1)}, bf16[272,256]{1,0:T(8,128)(2,1)S(1)}, u32[]{:S(2)}, u32[]{:S(2)}) %collective-permute-start.8) | collective-permute-done | bytes 139296 | tf_op jit(solution)/shard_map/ppermute | solution.py:40
  54.3 0.7 collective-permute-done.9.refs_3_
  55.8 2.6 %collective-permute-start.12 = (bf16[32,2048]{1,0:T(8,128)(2,1)S(1)}, bf16[32,2048]{1,0:T(8,128)(2,1)S(1)}, u32[]{:S(2)}, u32[]{:S(2)}) collective-permute-start(bf16[32,2048]{1,0:T(8,128)(2,1)S(1)} %get-tuple-element.76), channel_id=1, source_target_pairs={{0,4},{2,6},{4,0},{6,2},{1,5},{3,7},{5,1},{7,3},{8,12},{10,14},{12... | collective-permute-start | bytes 393224 | tf_op jit(solution)/shard_map/ppermute | solution.py:34
  58.4 1.3 %collective-permute-start.14 = (bf16[288,128]{1,0:T(8,128)(2,1)S(1)}, bf16[288,128]{1,0:T(8,128)(2,1)S(1)}, u32[]{:S(2)}, u32[]{:S(2)}) collective-permute-start(bf16[288,128]{1,0:T(8,128)(2,1)S(1)} %state.1.pay_ref), channel_id=1, source_target_pairs={{0,128},{8,136},{16,144},{24,152},{32,160},{40,168},{48,176},{56,1... | collective-permute-start | bytes 221192 | tf_op jit(solution)/shard_map/ppermute | solution.py:44
  59.7 1.3 %collective-permute-done.11.refs_0_ = bf16[32,2048]{1,0:T(8,128)(2,1)S(1)} collective-permute-done((bf16[32,2048]{1,0:T(8,128)(2,1)S(1)}, bf16[32,2048]{1,0:T(8,128)(2,1)S(1)}, u32[]{:S(2)}, u32[]{:S(2)}) %collective-permute-start.11) | collective-permute-done | bytes 131104 | tf_op jit(solution)/shard_map/ppermute | solution.py:34
  61.0 2.1 %collective-permute-done.12.refs_1_ = bf16[32,2048]{1,0:T(8,128)(2,1)S(1)} collective-permute-done((bf16[32,2048]{1,0:T(8,128)(2,1)S(1)}, bf16[32,2048]{1,0:T(8,128)(2,1)S(1)}, u32[]{:S(2)}, u32[]{:S(2)}) %collective-permute-start.12) | collective-permute-done | bytes 131104 | tf_op jit(solution)/shard_map/ppermute | solution.py:34
  63.2 1.4 %collective-permute-done.13.refs_2_ = bf16[32,2048]{1,0:T(8,128)(2,1)S(1)} collective-permute-done((bf16[32,2048]{1,0:T(8,128)(2,1)S(1)}, bf16[32,2048]{1,0:T(8,128)(2,1)S(1)}, u32[]{:S(2)}, u32[]{:S(2)}) %collective-permute-start.13) | collective-permute-done | bytes 131104 | tf_op jit(solution)/shard_map/ppermute | solution.py:34
  64.6 0.8 norm.1
  65.3 1.6 %collective-permute-done.14.came_ref = bf16[288,128]{1,0:T(8,128)(2,1)S(1)} collective-permute-done((bf16[288,128]{1,0:T(8,128)(2,1)S(1)}, bf16[288,128]{1,0:T(8,128)(2,1)S(1)}, u32[]{:S(2)}, u32[]{:S(2)}) %collective-permute-start.14) | collective-permute-done | bytes 73760 | tf_op jit(solution)/shard_map/ppermute | solution.py:44
  67.0 0.6 columns.1
  67.6 1.1 %collective-permute-start.16 = (bf16[64,512]{1,0:T(8,128)(2,1)S(1)}, bf16[64,512]{1,0:T(8,128)(2,1)S(1)}, u32[]{:S(2)}, u32[]{:S(2)}) collective-permute-start(bf16[64,512]{1,0:T(8,128)(2,1)S(1)} %get-tuple-element.87), channel_id=1, source_target_pairs={{0,6},{2,0},{4,2},{6,4},{1,7},{3,1},{5,3},{7,5},{8,14},{10,8},{12,... | collective-permute-start | bytes 196616 | tf_op jit(solution)/shard_map/ppermute | solution.py:34
  68.8 3.4 %collective-permute-start.23 = (bf16[288,128]{1,0:T(8,128)(2,1)S(1)}, bf16[288,128]{1,0:T(8,128)(2,1)S(1)}, u32[]{:S(2)}, u32[]{:S(2)}) collective-permute-start(bf16[288,128]{1,0:T(8,128)(2,1)S(1)} %sum.1), channel_id=1, source_target_pairs={{0,224},{8,232},{16,240},{24,248},{32,0},{40,8},{48,16},{56,24},{6... | collective-permute-start | bytes 221192 | tf_op jit(solution)/shard_map/ppermute | solution.py:34
  72.2 3.6 %collective-permute-start.18 = (bf16[64,512]{1,0:T(8,128)(2,1)S(1)}, bf16[64,512]{1,0:T(8,128)(2,1)S(1)}, u32[]{:S(2)}, u32[]{:S(2)}) collective-permute-start(bf16[64,512]{1,0:T(8,128)(2,1)S(1)} %get-tuple-element.88), channel_id=1, source_target_pairs={{0,4},{2,6},{4,0},{6,2},{1,5},{3,7},{5,1},{7,3},{8,12},{10,14},{12... | collective-permute-start | bytes 196616 | tf_op jit(solution)/shard_map/ppermute | solution.py:34
  75.9 1.3 %collective-permute-start.20 = (bf16[64,512]{1,0:T(8,128)(2,1)S(1)}, bf16[64,512]{1,0:T(8,128)(2,1)S(1)}, u32[]{:S(2)}, u32[]{:S(2)}) collective-permute-start(bf16[64,512]{1,0:T(8,128)(2,1)S(1)} %get-tuple-element.89), channel_id=1, source_target_pairs={{0,2},{2,4},{4,6},{6,0},{1,3},{3,5},{5,7},{7,1},{8,10},{10,12},{12... | collective-permute-start | bytes 196616 | tf_op jit(solution)/shard_map/ppermute | solution.py:34
  77.2 0.7 convolution_convert_fusion.2
  78.1 2.3 %collective-permute-start.17 = (bf16[64,3072]{1,0:T(8,128)(2,1)S(1)}, bf16[64,3072]{1,0:T(8,128)(2,1)S(1)}, u32[]{:S(2)}, u32[]{:S(2)}) collective-permute-start(bf16[64,3072]{1,0:T(8,128)(2,1)S(1)} %convolution_convert_fusion.2), channel_id=1, source_target_pairs={{0,2},{2,4},{4,6},{6,0},{1,3},{3,5},{5,7},{7,1},{8,10},{10,12},{12... | collective-permute-start | bytes 1179656 | tf_op jit(solution)/shard_map/ppermute | solution.py:34
  80.4 0.7 convolution_convert_fusion.1
  81.1 2.3 %collective-permute-start.19 = (bf16[64,3072]{1,0:T(8,128)(2,1)S(1)}, bf16[64,3072]{1,0:T(8,128)(2,1)S(1)}, u32[]{:S(2)}, u32[]{:S(2)}) collective-permute-start(bf16[64,3072]{1,0:T(8,128)(2,1)S(1)} %convolution_convert_fusion.1), channel_id=1, source_target_pairs={{0,4},{2,6},{4,0},{6,2},{1,5},{3,7},{5,1},{7,3},{8,12},{10,14},{12... | collective-permute-start | bytes 1179656 | tf_op jit(solution)/shard_map/ppermute | solution.py:34
  83.4 2.6 %collective-permute-start.27 = (bf16[288,128]{1,0:T(8,128)(2,1)S(1)}, bf16[288,128]{1,0:T(8,128)(2,1)S(1)}, u32[]{:S(2)}, u32[]{:S(2)}) collective-permute-start(bf16[288,128]{1,0:T(8,128)(2,1)S(1)} %add_add_fusion.refs_0_), channel_id=1, source_target_pairs={{0,24},{8,0},{16,8},{24,16},{32,56},{40,32},{48,40},{56,48},{64,88... | collective-permute-start | bytes 221192 | tf_op jit(solution)/shard_map/ppermute | solution.py:40
  86.0 0.7 convolution_convert_fusion
  87.5 0.5 collective-permute-done.27.refs_3_
  88.4 0.7 fusion.own_ref
  89.1 3.8 %collective-permute-done.26.refs_2_ = bf16[288,128]{1,0:T(8,128)(2,1)S(1)} collective-permute-done((bf16[288,128]{1,0:T(8,128)(2,1)S(1)}, bf16[288,128]{1,0:T(8,128)(2,1)S(1)}, u32[]{:S(2)}, u32[]{:S(2)}) %collective-permute-start.26) | collective-permute-done | bytes 73760 | tf_op jit(solution)/shard_map/ppermute | solution.py:40
  92.9 1.0 %collective-permute-done.25.refs_1_ = bf16[288,128]{1,0:T(8,128)(2,1)S(1)} collective-permute-done((bf16[288,128]{1,0:T(8,128)(2,1)S(1)}, bf16[288,128]{1,0:T(8,128)(2,1)S(1)}, u32[]{:S(2)}, u32[]{:S(2)}) %collective-permute-start.25) | collective-permute-done | bytes 73760 | tf_op jit(solution)/shard_map/ppermute | solution.py:40
  93.9 1.4 %finish.1 = (f32[4,256,128]{2,1,0:T(8,128)}, bf16[3,3,4,256]{3,2,1,0:T(4,128)(2,1)}) custom-call(s32[8]{0:T(128)S(1)} %concatenate.3.meta, bf16[288,128]{1,0:T(8,128)(2,1)S(1)} %add_add_fusion.refs_0_, bf16[288,128]{1,0:T(8,128)(2,1)S(1)} %collective-permute-done.25.refs_1_, bf16[288,128]{1,0:T(8,128)(2,1)S(1)} %collective-permute-done.26.refs_2_, ...), custom_call_target="tpu_custom_call" | custom-call | flops 1000000 | bytes 837664 | tf_op jit(solution)/shard_map/finish/pallas_call | solution.py:70
  95.3 0.5 collective-permute-done.17.refs_0_
  95.8 4.0 %collective-permute-done.21.refs_2_ = bf16[64,3072]{1,0:T(8,128)(2,1)S(1)} collective-permute-done((bf16[64,3072]{1,0:T(8,128)(2,1)S(1)}, bf16[64,3072]{1,0:T(8,128)(2,1)S(1)}, u32[]{:S(2)}, u32[]{:S(2)}) %collective-permute-start.21) | collective-permute-done | bytes 393248 | tf_op jit(solution)/shard_map/ppermute | solution.py:34
  99.8 0.9 last.1
  (38 shorter events, 2.6 us)
Async XLA Ops:
  0.6 76.5 %copy-start = (bf16[512,3072]{1,0:T(8,128)(2,1)S(1)}, bf16[512,3072]{1,0:T(8,128)(2,1)}, u32[]{:S(2)}) copy-start(bf16[512,3072]{1,0:T(8,128)(2,1)} %param.17) | copy-start | bytes 9437188
  1.5 6.7 %collective-permute-start = (bf16[3,16,256]{2,1,0:T(8,128)(2,1)S(1)}, bf16[3,16,256]{2,1,0:T(8,128)(2,1)S(1)}, u32[]{:S(2)}, u32[]{:S(2)}) collective-permute-start(bf16[3,16,256]{2,1,0:T(8,128)(2,1)S(1)} %slice.4), channel_id=1, source_target_pairs={{0,8},{8,16},{16,24},{24,32},{32,40},{40,48},{48,56},{56,64},{64,7... | collective-permute-start | bytes 73736 | tf_op jit(solution)/shard_map/ppermute | solution.py:29
  8.3 41.5 %copy-start.3 = (bf16[256,2048]{1,0:T(8,128)(2,1)S(1)}, bf16[256,2048]{1,0:T(8,128)(2,1)}, u32[]{:S(2)}) copy-start(bf16[256,2048]{1,0:T(8,128)(2,1)} %w_ref.1) | copy-start | bytes 3145732
  8.3 41.5 %copy-start.4 = (f32[128]{0:T(128)S(1)}, f32[128]{0:T(128)}, u32[]{:S(2)}) copy-start(f32[128]{0:T(128)} %param.13) | copy-start | bytes 1540
  13.2 5.1 %collective-permute-start.1 = (bf16[2,128,256]{2,1,0:T(8,128)(2,1)S(1)}, bf16[2,128,256]{2,1,0:T(8,128)(2,1)S(1)}, u32[]{:S(2)}, u32[]{:S(2)}) collective-permute-start(bf16[2,128,256]{2,1,0:T(8,128)(2,1)S(1)} %get-tuple-element.56.own_ref), channel_id=1, source_target_pairs={{0,8},{8,0},{16,24},{24,16},{32,40},{40,32},{48,56},{56,48},{64,72... | collective-permute-start | bytes 393224 | tf_op jit(solution)/shard_map/ppermute | solution.py:44
  18.9 11.6 %collective-permute-start.4 = (bf16[2,128,256]{2,1,0:T(8,128)(2,1)S(1)}, bf16[2,128,256]{2,1,0:T(8,128)(2,1)S(1)}, u32[]{:S(2)}, u32[]{:S(2)}) collective-permute-start(bf16[2,128,256]{2,1,0:T(8,128)(2,1)S(1)} %twin.1.twin_ref), channel_id=1, source_target_pairs={{0,56},{8,48},{16,40},{24,32},{32,88},{40,80},{48,72},{56,64},{64,... | collective-permute-start | bytes 393224 | tf_op jit(solution)/shard_map/ppermute | solution.py:486
  25.3 6.3 %collective-permute-start.3 = (bf16[2,128,256]{2,1,0:T(8,128)(2,1)S(1)}, bf16[2,128,256]{2,1,0:T(8,128)(2,1)S(1)}, u32[]{:S(2)}, u32[]{:S(2)}) collective-permute-start(bf16[2,128,256]{2,1,0:T(8,128)(2,1)S(1)} %twin.1.twin_ref), channel_id=1, source_target_pairs={{0,32},{8,40},{16,48},{24,56},{32,64},{40,72},{48,80},{56,88},{64,... | collective-permute-start | bytes 393224 | tf_op jit(solution)/shard_map/ppermute | solution.py:29
  29.1 6.3 %collective-permute-start.2 = (bf16[2,128,256]{2,1,0:T(8,128)(2,1)S(1)}, bf16[2,128,256]{2,1,0:T(8,128)(2,1)S(1)}, u32[]{:S(2)}, u32[]{:S(2)}) collective-permute-start(bf16[2,128,256]{2,1,0:T(8,128)(2,1)S(1)} %twin.1.twin_ref), channel_id=1, source_target_pairs={{0,24},{8,16},{16,8},{24,0},{32,56},{40,48},{48,40},{56,32},{64,88... | collective-permute-start | bytes 393224 | tf_op jit(solution)/shard_map/ppermute | solution.py:44
  36.4 13.4 %collective-permute-start.5 = (bf16[2,128,256]{2,1,0:T(8,128)(2,1)S(1)}, bf16[2,128,256]{2,1,0:T(8,128)(2,1)S(1)}, u32[]{:S(2)}, u32[]{:S(2)}) collective-permute-start(bf16[2,128,256]{2,1,0:T(8,128)(2,1)S(1)} %get-tuple-element.58), channel_id=1, source_target_pairs={{0,32},{8,40},{16,48},{24,56},{32,64},{40,72},{48,80},{56,88},{64,... | collective-permute-start | bytes 393224 | tf_op jit(solution)/shard_map/ppermute | solution.py:29
  41.5 8.3 %collective-permute-start.6 = (bf16[2,128,128]{2,1,0:T(8,128)(2,1)S(1)}, bf16[2,128,128]{2,1,0:T(8,128)(2,1)S(1)}, u32[]{:S(2)}, u32[]{:S(2)}) collective-permute-start(bf16[2,128,128]{2,1,0:T(8,128)(2,1)S(1)} %get-tuple-element.59), channel_id=1, source_target_pairs={{0,96},{8,104},{16,112},{24,120},{32,128},{40,136},{48,144},{56,15... | collective-permute-start | bytes 196616 | tf_op jit(solution)/shard_map/ppermute | solution.py:29
  46.2 6.3 %collective-permute-start.7 = (bf16[272,256]{1,0:T(8,128)(2,1)S(1)}, bf16[272,256]{1,0:T(8,128)(2,1)S(1)}, u32[]{:S(2)}, u32[]{:S(2)}) collective-permute-start(bf16[272,256]{1,0:T(8,128)(2,1)S(1)} %get-tuple-element.69), channel_id=1, source_target_pairs={{0,8},{8,16},{16,24},{24,0},{32,40},{40,48},{48,56},{56,32},{64,72... | collective-permute-start | bytes 417800 | tf_op jit(solution)/shard_map/ppermute | solution.py:40
  46.3 8.0 %collective-permute-start.8 = (bf16[272,256]{1,0:T(8,128)(2,1)S(1)}, bf16[272,256]{1,0:T(8,128)(2,1)S(1)}, u32[]{:S(2)}, u32[]{:S(2)}) collective-permute-start(bf16[272,256]{1,0:T(8,128)(2,1)S(1)} %get-tuple-element.70), channel_id=1, source_target_pairs={{0,16},{8,24},{16,0},{24,8},{32,48},{40,56},{48,32},{56,40},{64,80... | collective-permute-start | bytes 417800 | tf_op jit(solution)/shard_map/ppermute | solution.py:40
  49.8 5.2 %collective-permute-start.9 = (bf16[272,256]{1,0:T(8,128)(2,1)S(1)}, bf16[272,256]{1,0:T(8,128)(2,1)S(1)}, u32[]{:S(2)}, u32[]{:S(2)}) collective-permute-start(bf16[272,256]{1,0:T(8,128)(2,1)S(1)} %get-tuple-element.71), channel_id=1, source_target_pairs={{0,24},{8,0},{16,8},{24,16},{32,56},{40,32},{48,40},{56,48},{64,88... | collective-permute-start | bytes 417800 | tf_op jit(solution)/shard_map/ppermute | solution.py:40
  51.7 3.5 %collective-permute-start.10 = (bf16[128,2048]{1,0:T(8,128)(2,1)S(1)}, bf16[128,2048]{1,0:T(8,128)(2,1)S(1)}, u32[]{:S(2)}, u32[]{:S(2)}) collective-permute-start(bf16[128,2048]{1,0:T(8,128)(2,1)S(1)} %get-tuple-element.73), channel_id=1, source_target_pairs={{0,1},{1,0},{2,3},{3,2},{4,5},{5,4},{6,7},{7,6},{8,9},{9,8},{10,11... | collective-permute-start | bytes 1572872 | tf_op jit(solution)/shard_map/ppermute | solution.py:34
  55.0 9.6 %copy-start.1 = (bf16[32,2048]{1,0:T(8,128)(2,1)S(1)}, bf16[32,2048]{1,0:T(8,128)(2,1)}, u32[]{:S(2)}) copy-start(bf16[32,2048]{1,0:T(8,128)(2,1)} %hidden_ref.1) | copy-start | bytes 393220
  55.0 9.6 %copy-start.2 = (f32[2048]{0:T(1024)S(1)}, f32[2048]{0:T(1024)}, u32[]{:S(2)}) copy-start(f32[2048]{0:T(1024)} %param.16) | copy-start | bytes 24580
  55.3 5.7 %collective-permute-start.11 = (bf16[32,2048]{1,0:T(8,128)(2,1)S(1)}, bf16[32,2048]{1,0:T(8,128)(2,1)S(1)}, u32[]{:S(2)}, u32[]{:S(2)}) collective-permute-start(bf16[32,2048]{1,0:T(8,128)(2,1)S(1)} %get-tuple-element.75), channel_id=1, source_target_pairs={{0,2},{2,4},{4,6},{6,0},{1,3},{3,5},{5,7},{7,1},{8,10},{10,12},{12... | collective-permute-start | bytes 393224 | tf_op jit(solution)/shard_map/ppermute | solution.py:34
  55.8 7.4 %collective-permute-start.12 = (bf16[32,2048]{1,0:T(8,128)(2,1)S(1)}, bf16[32,2048]{1,0:T(8,128)(2,1)S(1)}, u32[]{:S(2)}, u32[]{:S(2)}) collective-permute-start(bf16[32,2048]{1,0:T(8,128)(2,1)S(1)} %get-tuple-element.76), channel_id=1, source_target_pairs={{0,4},{2,6},{4,0},{6,2},{1,5},{3,7},{5,1},{7,3},{8,12},{10,14},{12... | collective-permute-start | bytes 393224 | tf_op jit(solution)/shard_map/ppermute | solution.py:34
  58.4 6.2 %collective-permute-start.13 = (bf16[32,2048]{1,0:T(8,128)(2,1)S(1)}, bf16[32,2048]{1,0:T(8,128)(2,1)S(1)}, u32[]{:S(2)}, u32[]{:S(2)}) collective-permute-start(bf16[32,2048]{1,0:T(8,128)(2,1)S(1)} %get-tuple-element.77), channel_id=1, source_target_pairs={{0,6},{2,0},{4,2},{6,4},{1,7},{3,1},{5,3},{7,5},{8,14},{10,8},{12,... | collective-permute-start | bytes 393224 | tf_op jit(solution)/shard_map/ppermute | solution.py:34
  58.4 8.6 %collective-permute-start.14 = (bf16[288,128]{1,0:T(8,128)(2,1)S(1)}, bf16[288,128]{1,0:T(8,128)(2,1)S(1)}, u32[]{:S(2)}, u32[]{:S(2)}) collective-permute-start(bf16[288,128]{1,0:T(8,128)(2,1)S(1)} %state.1.pay_ref), channel_id=1, source_target_pairs={{0,128},{8,136},{16,144},{24,152},{32,160},{40,168},{48,176},{56,1... | collective-permute-start | bytes 221192 | tf_op jit(solution)/shard_map/ppermute | solution.py:44
  65.3 1.6 %collective-permute-start.15 = (bf16[32,2048]{1,0:T(8,128)(2,1)S(1)}, bf16[32,2048]{1,0:T(8,128)(2,1)S(1)}, u32[]{:S(2)}, u32[]{:S(2)}) collective-permute-start(bf16[32,2048]{1,0:T(8,128)(2,1)S(1)} %get-tuple-element.80.mine_ref), channel_id=1, source_target_pairs={{0,1},{1,0},{2,3},{3,2},{4,5},{5,4},{6,7},{7,6},{8,9},{9,8},{10,11... | collective-permute-start | bytes 393224 | tf_op jit(solution)/shard_map/ppermute | solution.py:34
  67.6 8.3 %collective-permute-start.16 = (bf16[64,512]{1,0:T(8,128)(2,1)S(1)}, bf16[64,512]{1,0:T(8,128)(2,1)S(1)}, u32[]{:S(2)}, u32[]{:S(2)}) collective-permute-start(bf16[64,512]{1,0:T(8,128)(2,1)S(1)} %get-tuple-element.87), channel_id=1, source_target_pairs={{0,6},{2,0},{4,2},{6,4},{1,7},{3,1},{5,3},{7,5},{8,14},{10,8},{12,... | collective-permute-start | bytes 196616 | tf_op jit(solution)/shard_map/ppermute | solution.py:34
  68.7 12.4 %collective-permute-start.24 = (bf16[288,128]{1,0:T(8,128)(2,1)S(1)}, bf16[288,128]{1,0:T(8,128)(2,1)S(1)}, u32[]{:S(2)}, u32[]{:S(2)}) collective-permute-start(bf16[288,128]{1,0:T(8,128)(2,1)S(1)} %sum.1), channel_id=1, source_target_pairs={{0,64},{8,72},{16,80},{24,88},{32,96},{40,104},{48,112},{56,120},{... | collective-permute-start | bytes 221192 | tf_op jit(solution)/shard_map/ppermute | solution.py:34
  68.8 14.6 %collective-permute-start.23 = (bf16[288,128]{1,0:T(8,128)(2,1)S(1)}, bf16[288,128]{1,0:T(8,128)(2,1)S(1)}, u32[]{:S(2)}, u32[]{:S(2)}) collective-permute-start(bf16[288,128]{1,0:T(8,128)(2,1)S(1)} %sum.1), channel_id=1, source_target_pairs={{0,224},{8,232},{16,240},{24,248},{32,0},{40,8},{48,16},{56,24},{6... | collective-permute-start | bytes 221192 | tf_op jit(solution)/shard_map/ppermute | solution.py:34
  72.2 11.2 %collective-permute-start.22 = (bf16[288,128]{1,0:T(8,128)(2,1)S(1)}, bf16[288,128]{1,0:T(8,128)(2,1)S(1)}, u32[]{:S(2)}, u32[]{:S(2)}) collective-permute-start(bf16[288,128]{1,0:T(8,128)(2,1)S(1)} %sum.1), channel_id=1, source_target_pairs={{0,32},{8,40},{16,48},{24,56},{32,64},{40,72},{48,80},{56,88},{64,... | collective-permute-start | bytes 221192 | tf_op jit(solution)/shard_map/ppermute | solution.py:34
  72.2 5.9 %collective-permute-start.18 = (bf16[64,512]{1,0:T(8,128)(2,1)S(1)}, bf16[64,512]{1,0:T(8,128)(2,1)S(1)}, u32[]{:S(2)}, u32[]{:S(2)}) collective-permute-start(bf16[64,512]{1,0:T(8,128)(2,1)S(1)} %get-tuple-element.88), channel_id=1, source_target_pairs={{0,4},{2,6},{4,0},{6,2},{1,5},{3,7},{5,1},{7,3},{8,12},{10,14},{12... | collective-permute-start | bytes 196616 | tf_op jit(solution)/shard_map/ppermute | solution.py:34
  75.9 10.2 %collective-permute-start.20 = (bf16[64,512]{1,0:T(8,128)(2,1)S(1)}, bf16[64,512]{1,0:T(8,128)(2,1)S(1)}, u32[]{:S(2)}, u32[]{:S(2)}) collective-permute-start(bf16[64,512]{1,0:T(8,128)(2,1)S(1)} %get-tuple-element.89), channel_id=1, source_target_pairs={{0,2},{2,4},{4,6},{6,0},{1,3},{3,5},{5,7},{7,1},{8,10},{10,12},{12... | collective-permute-start | bytes 196616 | tf_op jit(solution)/shard_map/ppermute | solution.py:34
  78.1 17.7 %collective-permute-start.17 = (bf16[64,3072]{1,0:T(8,128)(2,1)S(1)}, bf16[64,3072]{1,0:T(8,128)(2,1)S(1)}, u32[]{:S(2)}, u32[]{:S(2)}) collective-permute-start(bf16[64,3072]{1,0:T(8,128)(2,1)S(1)} %convolution_convert_fusion.2), channel_id=1, source_target_pairs={{0,2},{2,4},{4,6},{6,0},{1,3},{3,5},{5,7},{7,1},{8,10},{10,12},{12... | collective-permute-start | bytes 1179656 | tf_op jit(solution)/shard_map/ppermute | solution.py:34
  81.1 14.8 %collective-permute-start.19 = (bf16[64,3072]{1,0:T(8,128)(2,1)S(1)}, bf16[64,3072]{1,0:T(8,128)(2,1)S(1)}, u32[]{:S(2)}, u32[]{:S(2)}) collective-permute-start(bf16[64,3072]{1,0:T(8,128)(2,1)S(1)} %convolution_convert_fusion.1), channel_id=1, source_target_pairs={{0,4},{2,6},{4,0},{6,2},{1,5},{3,7},{5,1},{7,3},{8,12},{10,14},{12... | collective-permute-start | bytes 1179656 | tf_op jit(solution)/shard_map/ppermute | solution.py:34
  83.4 4.6 %collective-permute-start.27 = (bf16[288,128]{1,0:T(8,128)(2,1)S(1)}, bf16[288,128]{1,0:T(8,128)(2,1)S(1)}, u32[]{:S(2)}, u32[]{:S(2)}) collective-permute-start(bf16[288,128]{1,0:T(8,128)(2,1)S(1)} %add_add_fusion.refs_0_), channel_id=1, source_target_pairs={{0,24},{8,0},{16,8},{24,16},{32,56},{40,32},{48,40},{56,48},{64,88... | collective-permute-start | bytes 221192 | tf_op jit(solution)/shard_map/ppermute | solution.py:40
  86.7 13.1 %collective-permute-start.21 = (bf16[64,3072]{1,0:T(8,128)(2,1)S(1)}, bf16[64,3072]{1,0:T(8,128)(2,1)S(1)}, u32[]{:S(2)}, u32[]{:S(2)}) collective-permute-start(bf16[64,3072]{1,0:T(8,128)(2,1)S(1)} %convolution_convert_fusion), channel_id=1, source_target_pairs={{0,6},{2,0},{4,2},{6,4},{1,7},{3,1},{5,3},{7,5},{8,14},{10,8},{12,... | collective-permute-start | bytes 1179656 | tf_op jit(solution)/shard_map/ppermute | solution.py:34
  87.0 5.9 %collective-permute-start.26 = (bf16[288,128]{1,0:T(8,128)(2,1)S(1)}, bf16[288,128]{1,0:T(8,128)(2,1)S(1)}, u32[]{:S(2)}, u32[]{:S(2)}) collective-permute-start(bf16[288,128]{1,0:T(8,128)(2,1)S(1)} %add_add_fusion.refs_0_), channel_id=1, source_target_pairs={{0,16},{8,24},{16,0},{24,8},{32,48},{40,56},{48,32},{56,40},{64,80... | collective-permute-start | bytes 221192 | tf_op jit(solution)/shard_map/ppermute | solution.py:40
  88.0 5.9 %collective-permute-start.25 = (bf16[288,128]{1,0:T(8,128)(2,1)S(1)}, bf16[288,128]{1,0:T(8,128)(2,1)S(1)}, u32[]{:S(2)}, u32[]{:S(2)}) collective-permute-start(bf16[288,128]{1,0:T(8,128)(2,1)S(1)} %add_add_fusion.refs_0_), channel_id=1, source_target_pairs={{0,8},{8,16},{16,24},{24,0},{32,40},{40,48},{48,56},{56,32},{64,72... | collective-permute-start | bytes 221192 | tf_op jit(solution)/shard_map/ppermute | solution.py:40

commit v10 on v9

--- a/solution.py
+++ b/solution.py
@@ -542,7 +542,6 @@
     )
     peer = rotate(normed, "wout", 1)
     (payload,) = call(sum_kernel, [quarter], "sum", 10**10, payload, came, smem=0)
-    normed, payload = lax.optimization_barrier((normed, payload))
     cols = call(
         columns_kernel,
         [out((2 * piece, model // wins), BF16)] * wins,

time: 101 us -> 101 us (level)
  no operation moved by 1% of the time
where the time goes in v10:
time: 101 us
  starting transfers between devices  51.7 us (51%)
  waiting for transfers between devices  28.1 us (28%)
  Pallas kernels  15.6 us (15%)
  matrix products  2.72 us (3%)
  local copies, waits for them, and re-layouts  1.66 us (2%)
    ppermute x14, starting transfers between devices, rotate(): lax.ppermute(value, axis, [(s, (s + steps) % count) for s in range(count)])  17.6 us
    ppermute x4, starting transfers between devices, shift(): lax.ppermute(value, axis, [(s, s + steps) for s in range(max(0, count - s...  16.4 us
    pallas_call x13, Pallas kernels, call(): pl.pallas_call(kernel, out_shape=outs, in_specs=[SMEM] * smem + [HBM] * h...  15.6 us
    ppermute x14, waiting for transfers between devices, rotate(): lax.ppermute(value, axis, [(s, (s + steps) % count) for s in range(count)])  9.6 us
    ppermute x3, waiting for transfers between devices, exchange(): lax.ppermute(value, axis, [(s, s ^ bit) for s in range(lax.axis_size(axis...  8.87 us
    ppermute x6, waiting for transfers between devices, row_rotate(): return lax.ppermute(value, 'seq', pairs)  8.58 us
    ppermute x6, starting transfers between devices, row_rotate(): return lax.ppermute(value, 'seq', pairs)  7.01 us
    ppermute x1, starting transfers between devices, body(): lax.ppermute(twin, 'seq', [(s, (s ^ ROW - 1) + ROW) for s in range(n_seq...  6.36 us
  transfers between devices with their start and end apart: 28, of which 16 were waited for; matrix products, arithmetic and copies ran while one was open for 3% of the time, Pallas kernels for 7%

profile of v10, /device:TPU:24, one launch (start us, length us, event | category | flops | bytes accessed | tf_op | source)
XLA Modules:
  0.0 100.7 jit_solution(11777184419671563824)
XLA Ops:
  0.6 0.9 slice.4
  1.5 3.5 %collective-permute-start = (bf16[3,16,256]{2,1,0:T(8,128)(2,1)S(1)}, bf16[3,16,256]{2,1,0:T(8,128)(2,1)S(1)}, u32[]{:S(2)}, u32[]{:S(2)}) collective-permute-start(bf16[3,16,256]{2,1,0:T(8,128)(2,1)S(1)} %slice.4), channel_id=1, source_target_pairs={{0,8},{8,16},{16,24},{24,32},{32,40},{40,48},{48,56},{56,64},{64,7... | collective-permute-start | bytes 73736 | tf_op jit(solution)/shard_map/ppermute | solution.py:29
  5.1 0.7 concatenate.3.meta
  5.8 2.4 %conv.1 = (bf16[3,256,256]{2,1,0:T(8,128)(2,1)S(1)}, bf16[3,16,256]{2,1,0:T(8,128)(2,1)S(1)}, bf16[3,16,256]{2,1,0:T(8,128)(2,1)S(1)}, f32[3,4,256]{2,1,0:T(4,128)S(1)}, f32[2,256]{1,0:T(2,128)S(1)}) custom-call(s32[8]{0:T(128)S(1)} %concatenate.3.meta, bf16[3,256,256]{2,1,0:T(8,128)(2,1)} %bitcast.20, f32[3,4,256]{2,1,0:T(4,128)} %taps_hbm.1, f32[2,256]{1,0:T(2,128)} %beta_hbm.1), custom_call_target="tpu_custom_call" | custom-call | flops 100000000 | bytes 864288 | tf_op jit(solution)/shard_map/conv/pallas_call | solution.py:70
  8.3 4.9 %prep.1 = (bf16[2,128,256]{2,1,0:T(8,128)(2,1)S(1)}, f32[2,256,256]{2,1,0:T(8,128)S(1)}, f32[2,256,128]{2,1,0:T(8,128)S(1)}, f32[2,256,128]{2,1,0:T(8,128)S(1)},...) custom-call(s32[8]{0:T(128)S(1)} %concatenate.3.meta, ...), custom_call_target="tpu_custom_call" | custom-call | flops 2000000000 | bytes 1859616 | tf_op jit(solution)/shard_map/prep/pallas_call | solution.py:70
  13.2 1.6 %collective-permute-start.1 = (bf16[2,128,256]{2,1,0:T(8,128)(2,1)S(1)}, bf16[2,128,256]{2,1,0:T(8,128)(2,1)S(1)}, u32[]{:S(2)}, u32[]{:S(2)}) collective-permute-start(bf16[2,128,256]{2,1,0:T(8,128)(2,1)S(1)} %get-tuple-element.54.own_ref), channel_id=1, source_target_pairs={{0,8},{8,0},{16,24},{24,16},{32,40},{40,32},{48,56},{56,48},{64,72... | collective-permute-start | bytes 393224 | tf_op jit(solution)/shard_map/ppermute | solution.py:44
  14.7 3.5 %collective-permute-done.1.came_ref = bf16[2,128,256]{2,1,0:T(8,128)(2,1)S(1)} collective-permute-done((bf16[2,128,256]{2,1,0:T(8,128)(2,1)S(1)}, bf16[2,128,256]{2,1,0:T(8,128)(2,1)S(1)}, u32[]{:S(2)}, u32[]{:S(2)}) %collective-permute-start.1) | collective-permute-done | bytes 131104 | tf_op jit(solution)/shard_map/ppermute | solution.py:44
  18.2 0.7 twin.1.twin_ref
  18.9 6.4 %collective-permute-start.4 = (bf16[2,128,256]{2,1,0:T(8,128)(2,1)S(1)}, bf16[2,128,256]{2,1,0:T(8,128)(2,1)S(1)}, u32[]{:S(2)}, u32[]{:S(2)}) collective-permute-start(bf16[2,128,256]{2,1,0:T(8,128)(2,1)S(1)} %twin.1.twin_ref), channel_id=1, source_target_pairs={{0,56},{8,48},{16,40},{24,32},{32,88},{40,80},{48,72},{56,64},{64,... | collective-permute-start | bytes 393224 | tf_op jit(solution)/shard_map/ppermute | solution.py:486
  25.3 3.8 %collective-permute-start.3 = (bf16[2,128,256]{2,1,0:T(8,128)(2,1)S(1)}, bf16[2,128,256]{2,1,0:T(8,128)(2,1)S(1)}, u32[]{:S(2)}, u32[]{:S(2)}) collective-permute-start(bf16[2,128,256]{2,1,0:T(8,128)(2,1)S(1)} %twin.1.twin_ref), channel_id=1, source_target_pairs={{0,32},{8,40},{16,48},{24,56},{32,64},{40,72},{48,80},{56,88},{64,... | collective-permute-start | bytes 393224 | tf_op jit(solution)/shard_map/ppermute | solution.py:29
  29.1 1.4 %collective-permute-start.2 = (bf16[2,128,256]{2,1,0:T(8,128)(2,1)S(1)}, bf16[2,128,256]{2,1,0:T(8,128)(2,1)S(1)}, u32[]{:S(2)}, u32[]{:S(2)}) collective-permute-start(bf16[2,128,256]{2,1,0:T(8,128)(2,1)S(1)} %twin.1.twin_ref), channel_id=1, source_target_pairs={{0,24},{8,16},{16,8},{24,0},{32,56},{40,48},{48,40},{56,32},{64,88... | collective-permute-start | bytes 393224 | tf_op jit(solution)/shard_map/ppermute | solution.py:44
  30.6 1.1 %collective-permute-done.3.below_ref = bf16[2,128,256]{2,1,0:T(8,128)(2,1)S(1)} collective-permute-done((bf16[2,128,256]{2,1,0:T(8,128)(2,1)S(1)}, bf16[2,128,256]{2,1,0:T(8,128)(2,1)S(1)}, u32[]{:S(2)}, u32[]{:S(2)}) %collective-permute-start.3) | collective-permute-done | bytes 131104 | tf_op jit(solution)/shard_map/ppermute | solution.py:29
  31.6 3.8 %collective-permute-done.2.other_ref = bf16[2,128,256]{2,1,0:T(8,128)(2,1)S(1)} collective-permute-done((bf16[2,128,256]{2,1,0:T(8,128)(2,1)S(1)}, bf16[2,128,256]{2,1,0:T(8,128)(2,1)S(1)}, u32[]{:S(2)}, u32[]{:S(2)}) %collective-permute-start.2) | collective-permute-done | bytes 131104 | tf_op jit(solution)/shard_map/ppermute | solution.py:44
  35.4 1.0 %row.1 = (f32[2,128,256]{2,1,0:T(8,128)S(1)}, bf16[2,128,256]{2,1,0:T(8,128)(2,1)S(1)}, bf16[2,128,128]{2,1,0:T(8,128)(2,1)S(1)}) custom-call(s32[8]{0:T(128)S(1)} %concatenate.3.meta, bf16[2,128,256]{2,1,0:T(8,128)(2,1)S(1)} %get-tuple-element.54.own_ref, bf16[2,128,256]{2,1,0:T(8,128)(2,1)S(1)} %collective-permute-done.1.came_ref, ...), custom_call_target="tpu_custom_call" | custom-call | flops 100000000 | bytes 1245216 | tf_op jit(solution)/shard_map/row/pallas_call | solution.py:70
  36.4 5.0 %collective-permute-start.5 = (bf16[2,128,256]{2,1,0:T(8,128)(2,1)S(1)}, bf16[2,128,256]{2,1,0:T(8,128)(2,1)S(1)}, u32[]{:S(2)}, u32[]{:S(2)}) collective-permute-start(bf16[2,128,256]{2,1,0:T(8,128)(2,1)S(1)} %get-tuple-element.56), channel_id=1, source_target_pairs={{0,32},{8,40},{16,48},{24,56},{32,64},{40,72},{48,80},{56,88},{64,... | collective-permute-start | bytes 393224 | tf_op jit(solution)/shard_map/ppermute | solution.py:29
  41.5 4.1 %collective-permute-start.6 = (bf16[2,128,128]{2,1,0:T(8,128)(2,1)S(1)}, bf16[2,128,128]{2,1,0:T(8,128)(2,1)S(1)}, u32[]{:S(2)}, u32[]{:S(2)}) collective-permute-start(bf16[2,128,128]{2,1,0:T(8,128)(2,1)S(1)} %get-tuple-element.57), channel_id=1, source_target_pairs={{0,96},{8,104},{16,112},{24,120},{32,128},{40,136},{48,144},{56,15... | collective-permute-start | bytes 196616 | tf_op jit(solution)/shard_map/ppermute | solution.py:29
  45.5 0.7 ends.1
  46.3 3.5 %collective-permute-start.8 = (bf16[272,256]{1,0:T(8,128)(2,1)S(1)}, bf16[272,256]{1,0:T(8,128)(2,1)S(1)}, u32[]{:S(2)}, u32[]{:S(2)}) collective-permute-start(bf16[272,256]{1,0:T(8,128)(2,1)S(1)} %get-tuple-element.68), channel_id=1, source_target_pairs={{0,16},{8,24},{16,0},{24,8},{32,48},{40,56},{48,32},{56,40},{64,80... | collective-permute-start | bytes 417800 | tf_op jit(solution)/shard_map/ppermute | solution.py:40
  49.8 1.8 %attend.1 = (f32[128,2048]{1,0:T(8,128)S(1)}, bf16[128,2048]{1,0:T(8,128)(2,1)S(1)}, f32[2,128,128]{2,1,0:T(8,128)S(1)}) custom-call(s32[8]{0:T(128)S(1)} %concatenate.3.meta, f32[2,128,256]{2,1,0:T(8,128)S(1)} %get-tuple-element.55.prefix_ref, bf16[2,128,256]{2,1,0:T(8,128)(2,1)S(1)} %collective-permute-done.5.wide_ref, ...), custom_call_target="tpu_custom_call" | custom-call | flops 1000000000 | bytes 3736096 | tf_op jit(solution)/shard_map/attend/pallas_call | solution.py:70
  51.8 0.8 collective-permute-done.7.refs_1_
  52.6 1.7 %collective-permute-done.8.refs_2_ = bf16[272,256]{1,0:T(8,128)(2,1)S(1)} collective-permute-done((bf16[272,256]{1,0:T(8,128)(2,1)S(1)}, bf16[272,256]{1,0:T(8,128)(2,1)S(1)}, u32[]{:S(2)}, u32[]{:S(2)}) %collective-permute-start.8) | collective-permute-done | bytes 139296 | tf_op jit(solution)/shard_map/ppermute | solution.py:40
  54.3 0.7 collective-permute-done.9.refs_3_
  55.8 2.6 %collective-permute-start.12 = (bf16[32,2048]{1,0:T(8,128)(2,1)S(1)}, bf16[32,2048]{1,0:T(8,128)(2,1)S(1)}, u32[]{:S(2)}, u32[]{:S(2)}) collective-permute-start(bf16[32,2048]{1,0:T(8,128)(2,1)S(1)} %get-tuple-element.74), channel_id=1, source_target_pairs={{0,4},{2,6},{4,0},{6,2},{1,5},{3,7},{5,1},{7,3},{8,12},{10,14},{12... | collective-permute-start | bytes 393224 | tf_op jit(solution)/shard_map/ppermute | solution.py:34
  58.4 1.3 %collective-permute-start.15 = (bf16[288,128]{1,0:T(8,128)(2,1)S(1)}, bf16[288,128]{1,0:T(8,128)(2,1)S(1)}, u32[]{:S(2)}, u32[]{:S(2)}) collective-permute-start(bf16[288,128]{1,0:T(8,128)(2,1)S(1)} %state.1.pay_ref), channel_id=1, source_target_pairs={{0,128},{8,136},{16,144},{24,152},{32,160},{40,168},{48,176},{56,1... | collective-permute-start | bytes 221192 | tf_op jit(solution)/shard_map/ppermute | solution.py:44
  59.7 1.3 %collective-permute-done.11.refs_0_ = bf16[32,2048]{1,0:T(8,128)(2,1)S(1)} collective-permute-done((bf16[32,2048]{1,0:T(8,128)(2,1)S(1)}, bf16[32,2048]{1,0:T(8,128)(2,1)S(1)}, u32[]{:S(2)}, u32[]{:S(2)}) %collective-permute-start.11) | collective-permute-done | bytes 131104 | tf_op jit(solution)/shard_map/ppermute | solution.py:34
  61.0 2.1 %collective-permute-done.12.refs_1_ = bf16[32,2048]{1,0:T(8,128)(2,1)S(1)} collective-permute-done((bf16[32,2048]{1,0:T(8,128)(2,1)S(1)}, bf16[32,2048]{1,0:T(8,128)(2,1)S(1)}, u32[]{:S(2)}, u32[]{:S(2)}) %collective-permute-start.12) | collective-permute-done | bytes 131104 | tf_op jit(solution)/shard_map/ppermute | solution.py:34
  63.2 1.4 %collective-permute-done.13.refs_2_ = bf16[32,2048]{1,0:T(8,128)(2,1)S(1)} collective-permute-done((bf16[32,2048]{1,0:T(8,128)(2,1)S(1)}, bf16[32,2048]{1,0:T(8,128)(2,1)S(1)}, u32[]{:S(2)}, u32[]{:S(2)}) %collective-permute-start.13) | collective-permute-done | bytes 131104 | tf_op jit(solution)/shard_map/ppermute | solution.py:34
  64.6 0.8 norm.1
  65.3 1.6 %collective-permute-done.15.came_ref = bf16[288,128]{1,0:T(8,128)(2,1)S(1)} collective-permute-done((bf16[288,128]{1,0:T(8,128)(2,1)S(1)}, bf16[288,128]{1,0:T(8,128)(2,1)S(1)}, u32[]{:S(2)}, u32[]{:S(2)}) %collective-permute-start.15) | collective-permute-done | bytes 73760 | tf_op jit(solution)/shard_map/ppermute | solution.py:44
  67.0 0.6 columns.1
  67.6 1.1 %collective-permute-start.16 = (bf16[64,512]{1,0:T(8,128)(2,1)S(1)}, bf16[64,512]{1,0:T(8,128)(2,1)S(1)}, u32[]{:S(2)}, u32[]{:S(2)}) collective-permute-start(bf16[64,512]{1,0:T(8,128)(2,1)S(1)} %get-tuple-element.83), channel_id=1, source_target_pairs={{0,6},{2,0},{4,2},{6,4},{1,7},{3,1},{5,3},{7,5},{8,14},{10,8},{12,... | collective-permute-start | bytes 196616 | tf_op jit(solution)/shard_map/ppermute | solution.py:34
  68.8 3.4 %collective-permute-start.23 = (bf16[288,128]{1,0:T(8,128)(2,1)S(1)}, bf16[288,128]{1,0:T(8,128)(2,1)S(1)}, u32[]{:S(2)}, u32[]{:S(2)}) collective-permute-start(bf16[288,128]{1,0:T(8,128)(2,1)S(1)} %sum.1), channel_id=1, source_target_pairs={{0,224},{8,232},{16,240},{24,248},{32,0},{40,8},{48,16},{56,24},{6... | collective-permute-start | bytes 221192 | tf_op jit(solution)/shard_map/ppermute | solution.py:34
  72.2 3.6 %collective-permute-start.18 = (bf16[64,512]{1,0:T(8,128)(2,1)S(1)}, bf16[64,512]{1,0:T(8,128)(2,1)S(1)}, u32[]{:S(2)}, u32[]{:S(2)}) collective-permute-start(bf16[64,512]{1,0:T(8,128)(2,1)S(1)} %get-tuple-element.84), channel_id=1, source_target_pairs={{0,4},{2,6},{4,0},{6,2},{1,5},{3,7},{5,1},{7,3},{8,12},{10,14},{12... | collective-permute-start | bytes 196616 | tf_op jit(solution)/shard_map/ppermute | solution.py:34
  75.9 1.3 %collective-permute-start.20 = (bf16[64,512]{1,0:T(8,128)(2,1)S(1)}, bf16[64,512]{1,0:T(8,128)(2,1)S(1)}, u32[]{:S(2)}, u32[]{:S(2)}) collective-permute-start(bf16[64,512]{1,0:T(8,128)(2,1)S(1)} %get-tuple-element.85), channel_id=1, source_target_pairs={{0,2},{2,4},{4,6},{6,0},{1,3},{3,5},{5,7},{7,1},{8,10},{10,12},{12... | collective-permute-start | bytes 196616 | tf_op jit(solution)/shard_map/ppermute | solution.py:34
  77.2 0.7 convolution_convert_fusion.2
  78.1 2.3 %collective-permute-start.17 = (bf16[64,3072]{1,0:T(8,128)(2,1)S(1)}, bf16[64,3072]{1,0:T(8,128)(2,1)S(1)}, u32[]{:S(2)}, u32[]{:S(2)}) collective-permute-start(bf16[64,3072]{1,0:T(8,128)(2,1)S(1)} %convolution_convert_fusion.2), channel_id=1, source_target_pairs={{0,2},{2,4},{4,6},{6,0},{1,3},{3,5},{5,7},{7,1},{8,10},{10,12},{12... | collective-permute-start | bytes 1179656 | tf_op jit(solution)/shard_map/ppermute | solution.py:34
  80.4 0.7 convolution_convert_fusion.1
  81.1 2.3 %collective-permute-start.19 = (bf16[64,3072]{1,0:T(8,128)(2,1)S(1)}, bf16[64,3072]{1,0:T(8,128)(2,1)S(1)}, u32[]{:S(2)}, u32[]{:S(2)}) collective-permute-start(bf16[64,3072]{1,0:T(8,128)(2,1)S(1)} %convolution_convert_fusion.1), channel_id=1, source_target_pairs={{0,4},{2,6},{4,0},{6,2},{1,5},{3,7},{5,1},{7,3},{8,12},{10,14},{12... | collective-permute-start | bytes 1179656 | tf_op jit(solution)/shard_map/ppermute | solution.py:34
  83.4 2.6 %collective-permute-start.27 = (bf16[288,128]{1,0:T(8,128)(2,1)S(1)}, bf16[288,128]{1,0:T(8,128)(2,1)S(1)}, u32[]{:S(2)}, u32[]{:S(2)}) collective-permute-start(bf16[288,128]{1,0:T(8,128)(2,1)S(1)} %add_add_fusion.refs_0_), channel_id=1, source_target_pairs={{0,24},{8,0},{16,8},{24,16},{32,56},{40,32},{48,40},{56,48},{64,88... | collective-permute-start | bytes 221192 | tf_op jit(solution)/shard_map/ppermute | solution.py:40
  86.0 0.7 convolution_convert_fusion
  87.5 0.5 collective-permute-done.27.refs_3_
  88.4 0.7 fusion.own_ref
  89.1 3.8 %collective-permute-done.26.refs_2_ = bf16[288,128]{1,0:T(8,128)(2,1)S(1)} collective-permute-done((bf16[288,128]{1,0:T(8,128)(2,1)S(1)}, bf16[288,128]{1,0:T(8,128)(2,1)S(1)}, u32[]{:S(2)}, u32[]{:S(2)}) %collective-permute-start.26) | collective-permute-done | bytes 73760 | tf_op jit(solution)/shard_map/ppermute | solution.py:40
  92.9 1.0 %collective-permute-done.25.refs_1_ = bf16[288,128]{1,0:T(8,128)(2,1)S(1)} collective-permute-done((bf16[288,128]{1,0:T(8,128)(2,1)S(1)}, bf16[288,128]{1,0:T(8,128)(2,1)S(1)}, u32[]{:S(2)}, u32[]{:S(2)}) %collective-permute-start.25) | collective-permute-done | bytes 73760 | tf_op jit(solution)/shard_map/ppermute | solution.py:40
  93.9 1.4 %finish.1 = (f32[4,256,128]{2,1,0:T(8,128)}, bf16[3,3,4,256]{3,2,1,0:T(4,128)(2,1)}) custom-call(s32[8]{0:T(128)S(1)} %concatenate.3.meta, bf16[288,128]{1,0:T(8,128)(2,1)S(1)} %add_add_fusion.refs_0_, bf16[288,128]{1,0:T(8,128)(2,1)S(1)} %collective-permute-done.25.refs_1_, bf16[288,128]{1,0:T(8,128)(2,1)S(1)} %collective-permute-done.26.refs_2_, ...), custom_call_target="tpu_custom_call" | custom-call | flops 1000000 | bytes 837664 | tf_op jit(solution)/shard_map/finish/pallas_call | solution.py:70
  95.3 0.5 collective-permute-done.17.refs_0_
  95.8 4.0 %collective-permute-done.21.refs_2_ = bf16[64,3072]{1,0:T(8,128)(2,1)S(1)} collective-permute-done((bf16[64,3072]{1,0:T(8,128)(2,1)S(1)}, bf16[64,3072]{1,0:T(8,128)(2,1)S(1)}, u32[]{:S(2)}, u32[]{:S(2)}) %collective-permute-start.21) | collective-permute-done | bytes 393248 | tf_op jit(solution)/shard_map/ppermute | solution.py:34
  99.8 0.9 last.1
  (38 shorter events, 2.6 us)
Async XLA Ops:
  0.6 76.5 %copy-start = (bf16[512,3072]{1,0:T(8,128)(2,1)S(1)}, bf16[512,3072]{1,0:T(8,128)(2,1)}, u32[]{:S(2)}) copy-start(bf16[512,3072]{1,0:T(8,128)(2,1)} %param.17) | copy-start | bytes 9437188
  1.5 6.7 %collective-permute-start = (bf16[3,16,256]{2,1,0:T(8,128)(2,1)S(1)}, bf16[3,16,256]{2,1,0:T(8,128)(2,1)S(1)}, u32[]{:S(2)}, u32[]{:S(2)}) collective-permute-start(bf16[3,16,256]{2,1,0:T(8,128)(2,1)S(1)} %slice.4), channel_id=1, source_target_pairs={{0,8},{8,16},{16,24},{24,32},{32,40},{40,48},{48,56},{56,64},{64,7... | collective-permute-start | bytes 73736 | tf_op jit(solution)/shard_map/ppermute | solution.py:29
  8.3 41.5 %copy-start.3 = (bf16[256,2048]{1,0:T(8,128)(2,1)S(1)}, bf16[256,2048]{1,0:T(8,128)(2,1)}, u32[]{:S(2)}) copy-start(bf16[256,2048]{1,0:T(8,128)(2,1)} %w_ref.1) | copy-start | bytes 3145732
  8.3 41.5 %copy-start.4 = (f32[128]{0:T(128)S(1)}, f32[128]{0:T(128)}, u32[]{:S(2)}) copy-start(f32[128]{0:T(128)} %param.13) | copy-start | bytes 1540
  13.2 5.1 %collective-permute-start.1 = (bf16[2,128,256]{2,1,0:T(8,128)(2,1)S(1)}, bf16[2,128,256]{2,1,0:T(8,128)(2,1)S(1)}, u32[]{:S(2)}, u32[]{:S(2)}) collective-permute-start(bf16[2,128,256]{2,1,0:T(8,128)(2,1)S(1)} %get-tuple-element.54.own_ref), channel_id=1, source_target_pairs={{0,8},{8,0},{16,24},{24,16},{32,40},{40,32},{48,56},{56,48},{64,72... | collective-permute-start | bytes 393224 | tf_op jit(solution)/shard_map/ppermute | solution.py:44
  18.9 11.6 %collective-permute-start.4 = (bf16[2,128,256]{2,1,0:T(8,128)(2,1)S(1)}, bf16[2,128,256]{2,1,0:T(8,128)(2,1)S(1)}, u32[]{:S(2)}, u32[]{:S(2)}) collective-permute-start(bf16[2,128,256]{2,1,0:T(8,128)(2,1)S(1)} %twin.1.twin_ref), channel_id=1, source_target_pairs={{0,56},{8,48},{16,40},{24,32},{32,88},{40,80},{48,72},{56,64},{64,... | collective-permute-start | bytes 393224 | tf_op jit(solution)/shard_map/ppermute | solution.py:486
  25.3 6.3 %collective-permute-start.3 = (bf16[2,128,256]{2,1,0:T(8,128)(2,1)S(1)}, bf16[2,128,256]{2,1,0:T(8,128)(2,1)S(1)}, u32[]{:S(2)}, u32[]{:S(2)}) collective-permute-start(bf16[2,128,256]{2,1,0:T(8,128)(2,1)S(1)} %twin.1.twin_ref), channel_id=1, source_target_pairs={{0,32},{8,40},{16,48},{24,56},{32,64},{40,72},{48,80},{56,88},{64,... | collective-permute-start | bytes 393224 | tf_op jit(solution)/shard_map/ppermute | solution.py:29
  29.1 6.3 %collective-permute-start.2 = (bf16[2,128,256]{2,1,0:T(8,128)(2,1)S(1)}, bf16[2,128,256]{2,1,0:T(8,128)(2,1)S(1)}, u32[]{:S(2)}, u32[]{:S(2)}) collective-permute-start(bf16[2,128,256]{2,1,0:T(8,128)(2,1)S(1)} %twin.1.twin_ref), channel_id=1, source_target_pairs={{0,24},{8,16},{16,8},{24,0},{32,56},{40,48},{48,40},{56,32},{64,88... | collective-permute-start | bytes 393224 | tf_op jit(solution)/shard_map/ppermute | solution.py:44
  36.4 13.4 %collective-permute-start.5 = (bf16[2,128,256]{2,1,0:T(8,128)(2,1)S(1)}, bf16[2,128,256]{2,1,0:T(8,128)(2,1)S(1)}, u32[]{:S(2)}, u32[]{:S(2)}) collective-permute-start(bf16[2,128,256]{2,1,0:T(8,128)(2,1)S(1)} %get-tuple-element.56), channel_id=1, source_target_pairs={{0,32},{8,40},{16,48},{24,56},{32,64},{40,72},{48,80},{56,88},{64,... | collective-permute-start | bytes 393224 | tf_op jit(solution)/shard_map/ppermute | solution.py:29
  41.5 8.3 %collective-permute-start.6 = (bf16[2,128,128]{2,1,0:T(8,128)(2,1)S(1)}, bf16[2,128,128]{2,1,0:T(8,128)(2,1)S(1)}, u32[]{:S(2)}, u32[]{:S(2)}) collective-permute-start(bf16[2,128,128]{2,1,0:T(8,128)(2,1)S(1)} %get-tuple-element.57), channel_id=1, source_target_pairs={{0,96},{8,104},{16,112},{24,120},{32,128},{40,136},{48,144},{56,15... | collective-permute-start | bytes 196616 | tf_op jit(solution)/shard_map/ppermute | solution.py:29
  46.2 6.3 %collective-permute-start.7 = (bf16[272,256]{1,0:T(8,128)(2,1)S(1)}, bf16[272,256]{1,0:T(8,128)(2,1)S(1)}, u32[]{:S(2)}, u32[]{:S(2)}) collective-permute-start(bf16[272,256]{1,0:T(8,128)(2,1)S(1)} %get-tuple-element.67), channel_id=1, source_target_pairs={{0,8},{8,16},{16,24},{24,0},{32,40},{40,48},{48,56},{56,32},{64,72... | collective-permute-start | bytes 417800 | tf_op jit(solution)/shard_map/ppermute | solution.py:40
  46.3 8.0 %collective-permute-start.8 = (bf16[272,256]{1,0:T(8,128)(2,1)S(1)}, bf16[272,256]{1,0:T(8,128)(2,1)S(1)}, u32[]{:S(2)}, u32[]{:S(2)}) collective-permute-start(bf16[272,256]{1,0:T(8,128)(2,1)S(1)} %get-tuple-element.68), channel_id=1, source_target_pairs={{0,16},{8,24},{16,0},{24,8},{32,48},{40,56},{48,32},{56,40},{64,80... | collective-permute-start | bytes 417800 | tf_op jit(solution)/shard_map/ppermute | solution.py:40
  49.8 5.2 %collective-permute-start.9 = (bf16[272,256]{1,0:T(8,128)(2,1)S(1)}, bf16[272,256]{1,0:T(8,128)(2,1)S(1)}, u32[]{:S(2)}, u32[]{:S(2)}) collective-permute-start(bf16[272,256]{1,0:T(8,128)(2,1)S(1)} %get-tuple-element.69), channel_id=1, source_target_pairs={{0,24},{8,0},{16,8},{24,16},{32,56},{40,32},{48,40},{56,48},{64,88... | collective-permute-start | bytes 417800 | tf_op jit(solution)/shard_map/ppermute | solution.py:40
  51.7 3.5 %collective-permute-start.10 = (bf16[128,2048]{1,0:T(8,128)(2,1)S(1)}, bf16[128,2048]{1,0:T(8,128)(2,1)S(1)}, u32[]{:S(2)}, u32[]{:S(2)}) collective-permute-start(bf16[128,2048]{1,0:T(8,128)(2,1)S(1)} %get-tuple-element.71), channel_id=1, source_target_pairs={{0,1},{1,0},{2,3},{3,2},{4,5},{5,4},{6,7},{7,6},{8,9},{9,8},{10,11... | collective-permute-start | bytes 1572872 | tf_op jit(solution)/shard_map/ppermute | solution.py:34
  55.0 9.6 %copy-start.1 = (bf16[32,2048]{1,0:T(8,128)(2,1)S(1)}, bf16[32,2048]{1,0:T(8,128)(2,1)}, u32[]{:S(2)}) copy-start(bf16[32,2048]{1,0:T(8,128)(2,1)} %hidden_ref.1) | copy-start | bytes 393220
  55.0 9.6 %copy-start.2 = (f32[2048]{0:T(1024)S(1)}, f32[2048]{0:T(1024)}, u32[]{:S(2)}) copy-start(f32[2048]{0:T(1024)} %param.16) | copy-start | bytes 24580
  55.3 5.7 %collective-permute-start.11 = (bf16[32,2048]{1,0:T(8,128)(2,1)S(1)}, bf16[32,2048]{1,0:T(8,128)(2,1)S(1)}, u32[]{:S(2)}, u32[]{:S(2)}) collective-permute-start(bf16[32,2048]{1,0:T(8,128)(2,1)S(1)} %get-tuple-element.73), channel_id=1, source_target_pairs={{0,2},{2,4},{4,6},{6,0},{1,3},{3,5},{5,7},{7,1},{8,10},{10,12},{12... | collective-permute-start | bytes 393224 | tf_op jit(solution)/shard_map/ppermute | solution.py:34
  55.8 7.4 %collective-permute-start.12 = (bf16[32,2048]{1,0:T(8,128)(2,1)S(1)}, bf16[32,2048]{1,0:T(8,128)(2,1)S(1)}, u32[]{:S(2)}, u32[]{:S(2)}) collective-permute-start(bf16[32,2048]{1,0:T(8,128)(2,1)S(1)} %get-tuple-element.74), channel_id=1, source_target_pairs={{0,4},{2,6},{4,0},{6,2},{1,5},{3,7},{5,1},{7,3},{8,12},{10,14},{12... | collective-permute-start | bytes 393224 | tf_op jit(solution)/shard_map/ppermute | solution.py:34
  58.4 6.2 %collective-permute-start.13 = (bf16[32,2048]{1,0:T(8,128)(2,1)S(1)}, bf16[32,2048]{1,0:T(8,128)(2,1)S(1)}, u32[]{:S(2)}, u32[]{:S(2)}) collective-permute-start(bf16[32,2048]{1,0:T(8,128)(2,1)S(1)} %get-tuple-element.75), channel_id=1, source_target_pairs={{0,6},{2,0},{4,2},{6,4},{1,7},{3,1},{5,3},{7,5},{8,14},{10,8},{12,... | collective-permute-start | bytes 393224 | tf_op jit(solution)/shard_map/ppermute | solution.py:34
  58.4 8.6 %collective-permute-start.15 = (bf16[288,128]{1,0:T(8,128)(2,1)S(1)}, bf16[288,128]{1,0:T(8,128)(2,1)S(1)}, u32[]{:S(2)}, u32[]{:S(2)}) collective-permute-start(bf16[288,128]{1,0:T(8,128)(2,1)S(1)} %state.1.pay_ref), channel_id=1, source_target_pairs={{0,128},{8,136},{16,144},{24,152},{32,160},{40,168},{48,176},{56,1... | collective-permute-start | bytes 221192 | tf_op jit(solution)/shard_map/ppermute | solution.py:44
  65.3 1.6 %collective-permute-start.14 = (bf16[32,2048]{1,0:T(8,128)(2,1)S(1)}, bf16[32,2048]{1,0:T(8,128)(2,1)S(1)}, u32[]{:S(2)}, u32[]{:S(2)}) collective-permute-start(bf16[32,2048]{1,0:T(8,128)(2,1)S(1)} %get-tuple-element.76.mine_ref), channel_id=1, source_target_pairs={{0,1},{1,0},{2,3},{3,2},{4,5},{5,4},{6,7},{7,6},{8,9},{9,8},{10,11... | collective-permute-start | bytes 393224 | tf_op jit(solution)/shard_map/ppermute | solution.py:34
  67.6 8.3 %collective-permute-start.16 = (bf16[64,512]{1,0:T(8,128)(2,1)S(1)}, bf16[64,512]{1,0:T(8,128)(2,1)S(1)}, u32[]{:S(2)}, u32[]{:S(2)}) collective-permute-start(bf16[64,512]{1,0:T(8,128)(2,1)S(1)} %get-tuple-element.83), channel_id=1, source_target_pairs={{0,6},{2,0},{4,2},{6,4},{1,7},{3,1},{5,3},{7,5},{8,14},{10,8},{12,... | collective-permute-start | bytes 196616 | tf_op jit(solution)/shard_map/ppermute | solution.py:34
  68.7 12.4 %collective-permute-start.24 = (bf16[288,128]{1,0:T(8,128)(2,1)S(1)}, bf16[288,128]{1,0:T(8,128)(2,1)S(1)}, u32[]{:S(2)}, u32[]{:S(2)}) collective-permute-start(bf16[288,128]{1,0:T(8,128)(2,1)S(1)} %sum.1), channel_id=1, source_target_pairs={{0,64},{8,72},{16,80},{24,88},{32,96},{40,104},{48,112},{56,120},{... | collective-permute-start | bytes 221192 | tf_op jit(solution)/shard_map/ppermute | solution.py:34
  68.8 14.6 %collective-permute-start.23 = (bf16[288,128]{1,0:T(8,128)(2,1)S(1)}, bf16[288,128]{1,0:T(8,128)(2,1)S(1)}, u32[]{:S(2)}, u32[]{:S(2)}) collective-permute-start(bf16[288,128]{1,0:T(8,128)(2,1)S(1)} %sum.1), channel_id=1, source_target_pairs={{0,224},{8,232},{16,240},{24,248},{32,0},{40,8},{48,16},{56,24},{6... | collective-permute-start | bytes 221192 | tf_op jit(solution)/shard_map/ppermute | solution.py:34
  72.2 11.2 %collective-permute-start.22 = (bf16[288,128]{1,0:T(8,128)(2,1)S(1)}, bf16[288,128]{1,0:T(8,128)(2,1)S(1)}, u32[]{:S(2)}, u32[]{:S(2)}) collective-permute-start(bf16[288,128]{1,0:T(8,128)(2,1)S(1)} %sum.1), channel_id=1, source_target_pairs={{0,32},{8,40},{16,48},{24,56},{32,64},{40,72},{48,80},{56,88},{64,... | collective-permute-start | bytes 221192 | tf_op jit(solution)/shard_map/ppermute | solution.py:34
  72.2 5.9 %collective-permute-start.18 = (bf16[64,512]{1,0:T(8,128)(2,1)S(1)}, bf16[64,512]{1,0:T(8,128)(2,1)S(1)}, u32[]{:S(2)}, u32[]{:S(2)}) collective-permute-start(bf16[64,512]{1,0:T(8,128)(2,1)S(1)} %get-tuple-element.84), channel_id=1, source_target_pairs={{0,4},{2,6},{4,0},{6,2},{1,5},{3,7},{5,1},{7,3},{8,12},{10,14},{12... | collective-permute-start | bytes 196616 | tf_op jit(solution)/shard_map/ppermute | solution.py:34
  75.9 10.2 %collective-permute-start.20 = (bf16[64,512]{1,0:T(8,128)(2,1)S(1)}, bf16[64,512]{1,0:T(8,128)(2,1)S(1)}, u32[]{:S(2)}, u32[]{:S(2)}) collective-permute-start(bf16[64,512]{1,0:T(8,128)(2,1)S(1)} %get-tuple-element.85), channel_id=1, source_target_pairs={{0,2},{2,4},{4,6},{6,0},{1,3},{3,5},{5,7},{7,1},{8,10},{10,12},{12... | collective-permute-start | bytes 196616 | tf_op jit(solution)/shard_map/ppermute | solution.py:34
  78.1 17.7 %collective-permute-start.17 = (bf16[64,3072]{1,0:T(8,128)(2,1)S(1)}, bf16[64,3072]{1,0:T(8,128)(2,1)S(1)}, u32[]{:S(2)}, u32[]{:S(2)}) collective-permute-start(bf16[64,3072]{1,0:T(8,128)(2,1)S(1)} %convolution_convert_fusion.2), channel_id=1, source_target_pairs={{0,2},{2,4},{4,6},{6,0},{1,3},{3,5},{5,7},{7,1},{8,10},{10,12},{12... | collective-permute-start | bytes 1179656 | tf_op jit(solution)/shard_map/ppermute | solution.py:34
  81.1 14.8 %collective-permute-start.19 = (bf16[64,3072]{1,0:T(8,128)(2,1)S(1)}, bf16[64,3072]{1,0:T(8,128)(2,1)S(1)}, u32[]{:S(2)}, u32[]{:S(2)}) collective-permute-start(bf16[64,3072]{1,0:T(8,128)(2,1)S(1)} %convolution_convert_fusion.1), channel_id=1, source_target_pairs={{0,4},{2,6},{4,0},{6,2},{1,5},{3,7},{5,1},{7,3},{8,12},{10,14},{12... | collective-permute-start | bytes 1179656 | tf_op jit(solution)/shard_map/ppermute | solution.py:34
  83.4 4.6 %collective-permute-start.27 = (bf16[288,128]{1,0:T(8,128)(2,1)S(1)}, bf16[288,128]{1,0:T(8,128)(2,1)S(1)}, u32[]{:S(2)}, u32[]{:S(2)}) collective-permute-start(bf16[288,128]{1,0:T(8,128)(2,1)S(1)} %add_add_fusion.refs_0_), channel_id=1, source_target_pairs={{0,24},{8,0},{16,8},{24,16},{32,56},{40,32},{48,40},{56,48},{64,88... | collective-permute-start | bytes 221192 | tf_op jit(solution)/shard_map/ppermute | solution.py:40
  86.7 13.1 %collective-permute-start.21 = (bf16[64,3072]{1,0:T(8,128)(2,1)S(1)}, bf16[64,3072]{1,0:T(8,128)(2,1)S(1)}, u32[]{:S(2)}, u32[]{:S(2)}) collective-permute-start(bf16[64,3072]{1,0:T(8,128)(2,1)S(1)} %convolution_convert_fusion), channel_id=1, source_target_pairs={{0,6},{2,0},{4,2},{6,4},{1,7},{3,1},{5,3},{7,5},{8,14},{10,8},{12,... | collective-permute-start | bytes 1179656 | tf_op jit(solution)/shard_map/ppermute | solution.py:34
  87.0 5.9 %collective-permute-start.26 = (bf16[288,128]{1,0:T(8,128)(2,1)S(1)}, bf16[288,128]{1,0:T(8,128)(2,1)S(1)}, u32[]{:S(2)}, u32[]{:S(2)}) collective-permute-start(bf16[288,128]{1,0:T(8,128)(2,1)S(1)} %add_add_fusion.refs_0_), channel_id=1, source_target_pairs={{0,16},{8,24},{16,0},{24,8},{32,48},{40,56},{48,32},{56,40},{64,80... | collective-permute-start | bytes 221192 | tf_op jit(solution)/shard_map/ppermute | solution.py:40
  88.0 5.9 %collective-permute-start.25 = (bf16[288,128]{1,0:T(8,128)(2,1)S(1)}, bf16[288,128]{1,0:T(8,128)(2,1)S(1)}, u32[]{:S(2)}, u32[]{:S(2)}) collective-permute-start(bf16[288,128]{1,0:T(8,128)(2,1)S(1)} %add_add_fusion.refs_0_), channel_id=1, source_target_pairs={{0,8},{8,16},{16,24},{24,0},{32,40},{40,48},{48,56},{56,32},{64,72... | collective-permute-start | bytes 221192 | tf_op jit(solution)/shard_map/ppermute | solution.py:40
